TPU v7x, 32 devices: a whole 2x2x4 slice. The times are simulated.
32 devices in a mesh: item: 8 (over z, x), bucket: 4 (over y, core).
Axes of the slice: x: 2, y: 2, z: 4, core: 2. Of those that a mesh axis runs over, the one named last changes fastest.
Arguments:
- code_rows: bfloat16 [8192, 64], P('item'), may hold values from -6 to 6
- centroids: bfloat16 [32768, 64], P('bucket'), may hold values from -0.5 to 0.5
Outputs:
- grad_codes: float32 [8192, 64], P('item')
- new_centroids: float32 [32768, 64], P('bucket')
All inputs are finite; a program needn't handle non-finite values.
Results may differ from a plain program's by a relative error of at most 0.0032.
Values sent between devices are 32-bit elements; how exact they have to be, the bound alone decides.
No kernel may reach another device: no remote copies, remote signals or barrier semaphores. Data moves between devices by JAX's collectives and lax.ppermute only.
A program may use at most 128 MiB of HBM per device.

v0:
```python
import jax
import jax.numpy as jnp
from jax import lax
from jax.sharding import PartitionSpec as P

BUCKETS = 32768
ITERS = 3


score_scale = 20.0
step_rate = 0.2
epsilon = 1e-06


def joined(value, axis, join):
    pieces = jax.tree.map(lambda part: lax.all_gather(part, axis), value)
    head = jax.tree.map(lambda part: part[0], pieces)
    tail = jax.tree.map(lambda part: part[1:], pieces)
    so_far, _ = lax.scan(lambda so_far, piece: (join(so_far, piece), None), head, tail)
    return so_far


def scores_of(code_rows, centroids):
    return score_scale * lax.dot_general(
        code_rows, centroids, (((1,), (1,)), ((), ())), preferred_element_type=jnp.float32
    )


def lse_pair(first, second):
    highest = jnp.maximum(first[0], second[0])
    return (
        highest,
        first[1] * jnp.exp(first[0] - highest) + second[1] * jnp.exp(second[0] - highest),
    )


def stats_triple(first, second):
    highest = jnp.maximum(first[0], second[0])
    return (
        highest,
        first[1] * jnp.exp(first[0] - highest) + second[1] * jnp.exp(second[0] - highest),
        first[2] + second[2],
    )


def reduce_rows(values):
    highest = jnp.max(values, axis=1)
    summed = jnp.sum(jnp.exp(values - highest[:, None]), axis=1)
    highest, summed = joined((highest, summed), "bucket", lse_pair)
    return highest + jnp.log(summed)


def reduce_cols(values):
    highest = jnp.max(values, axis=0)
    summed = jnp.sum(jnp.exp(values - highest[None, :]), axis=0)
    highest, summed = joined((highest, summed), "item", lse_pair)
    return highest + jnp.log(summed)


def rescale(own_rows, gradient):
    moved = own_rows.astype(jnp.float32) - step_rate * gradient
    return moved * lax.rsqrt(jnp.mean(moved * moved, axis=1, keepdims=True) + epsilon)


def body(code_rows, centroids):
    rows_total = code_rows.shape[0] * lax.axis_size("item")
    log_rows = jnp.log(jnp.float32(rows_total))
    log_buckets = jnp.log(jnp.float32(BUCKETS))
    potential_col = jnp.zeros((centroids.shape[0],), jnp.float32)
    potential_row = jnp.zeros((code_rows.shape[0],), jnp.float32)
    for iteration in range(ITERS):
        potential_row = -log_rows - reduce_rows(
            scores_of(code_rows, centroids) + potential_col[None, :]
        )
        potential_col = -log_buckets - reduce_cols(
            scores_of(code_rows, centroids) + potential_row[:, None]
        )
    scores = scores_of(code_rows, centroids)
    plan = jnp.exp(scores + potential_row[:, None] + potential_col[None, :] + log_rows)
    masses = jnp.sum(plan, axis=1)
    highest = jnp.max(scores, axis=1)
    totals = jnp.sum(jnp.exp(scores - highest[:, None]), axis=1)
    highest, totals, masses = joined((highest, totals, masses), "bucket", stats_triple)
    delta = (masses[:, None] * jnp.exp(scores - highest[:, None]) / totals[:, None] - plan).astype(
        jnp.bfloat16
    )
    grad_codes = lax.psum(
        score_scale * jnp.dot(delta, centroids, preferred_element_type=jnp.float32), "bucket"
    )
    local_grad = score_scale * lax.dot_general(
        delta, code_rows, (((0,), (0,)), ((), ())), preferred_element_type=jnp.float32
    )
    gradient = lax.psum(local_grad, "item")
    new_centroids = rescale(centroids, gradient)
    return (grad_codes, new_centroids)


def solution(mesh):
    return jax.shard_map(
        body,
        mesh=mesh,
        in_specs=(P("item", None), P("bucket", None)),
        out_specs=(P("item", None), P("bucket", None)),
        check_vma=False,
    )
```

profile of v0, /device:TPU:0, one launch (start us, length us, event | category | flops | bytes accessed | tf_op | source)
XLA Modules:
  0.0 586.0 jit_solution(3918211216739394180)
XLA Ops:
  8.1 14.3 %fusion.2 = (f32[1024]{0:T(1024)S(1)}, f32[1024,8192]{1,0:T(8,128)}) fusion(bf16[1024,64]{0,1:T(8,128)(2,1)S(1)} %copy-done, bf16[8192,64]{0,1:T(8,128)(2,1)} %param.17), kind=kOutput, calls=%fused_computation.49 | convolution fusion | flops 1090518016 | bytes 34738176 | tf_op jit(solution)/shard_map/dot_general | solution.py:24
  22.4 6.2 %all-gather = f32[4096]{0:T(1024)S(1)} all-gather(f32[1024]{0:T(1024)S(1)} %get-tuple-element.326), channel_id=2, replica_groups=mesh['item'=8,'bucket'=4] {'bucket'}, dimensions={0}, use_global_device_ids=true | all-gather | bytes 20480 | tf_op jit(solution)/shard_map/all_gather | solution.py:16
  28.6 13.6 %exponential_reduce_fusion.5 = f32[1024]{0:T(1024)S(1)} fusion(f32[1024,8192]{1,0:T(8,128)} %get-tuple-element.327, f32[1024]{0:T(1024)S(1)} %get-tuple-element.326), kind=kLoop, calls=%fused_computation.29 | loop fusion | flops 16776192 | bytes 33562624 | tf_op jit(solution)/shard_map/reduce_sum | solution.py:82
  42.3 5.4 all-gather.1
  47.9 12.5 %add_reduce_fusion.3 = f32[8192]{0:T(1024)S(1)} fusion(f32[1024,8192]{1,0:T(8,128)} %get-tuple-element.327, f32[1024]{0:T(1024)S(1)} %add_subtract_fusion.5), kind=kLoop, calls=%fused_computation.33 | loop fusion | flops 16769024 | bytes 33591296 | tf_op jit(solution)/shard_map/reduce_max | solution.py:54
  60.4 14.0 %exponential_reduce_fusion.4 = f32[8192]{0:T(1024)S(1)} fusion(f32[1024,8192]{1,0:T(8,128)} %get-tuple-element.327, f32[8192]{0:T(1024)S(1)} %add_reduce_fusion.3, f32[1024]{0:T(1024)S(1)} %add_subtract_fusion.5), kind=kLoop, calls=%fused_computation.28 | loop fusion | flops 25157632 | bytes 33624064 | tf_op jit(solution)/shard_map/reduce_sum | solution.py:55
  74.4 31.4 %all-gather.2 = f32[65536]{0:T(1024)S(1)} all-gather(f32[8192]{0:T(1024)S(1)} %add_reduce_fusion.3), channel_id=4, replica_groups=mesh['item'=8,'bucket'=4] {'item'}, dimensions={0}, use_global_device_ids=true | all-gather | bytes 294912 | tf_op jit(solution)/shard_map/all_gather | solution.py:16
  105.8 30.7 %all-gather.3 = f32[65536]{0:T(1024)S(1)} all-gather(f32[8192]{0:T(1024)S(1)} %exponential_reduce_fusion.4), channel_id=5, replica_groups=mesh['item'=8,'bucket'=4] {'item'}, dimensions={0}, use_global_device_ids=true | all-gather | bytes 294912 | tf_op jit(solution)/shard_map/all_gather | solution.py:16
  137.6 12.2 %add_reduce_fusion.2 = f32[1024]{0:T(1024)S(1)} fusion(f32[1024,8192]{1,0:T(8,128)} %get-tuple-element.327, f32[8192]{0:T(1024)S(1)} %add_subtract_fusion.2), kind=kLoop, calls=%fused_computation.32 | loop fusion | flops 16776192 | bytes 33591296 | tf_op jit(solution)/shard_map/reduce_max | solution.py:47
  149.8 14.3 %exponential_reduce_fusion.3 = f32[1024]{0:T(1024)S(1)} fusion(f32[1024,8192]{1,0:T(8,128)} %get-tuple-element.327, f32[1024]{0:T(1024)S(1)} %add_reduce_fusion.2, f32[8192]{0:T(1024)S(1)} %add_subtract_fusion.2), kind=kLoop, calls=%fused_computation.27 | loop fusion | flops 25164800 | bytes 33595392 | tf_op jit(solution)/shard_map/reduce_sum | solution.py:48
  164.1 5.2 all-gather.4
  169.3 5.2 all-gather.5
  174.7 12.5 %add_reduce_fusion.1 = f32[8192]{0:T(1024)S(1)} fusion(f32[1024,8192]{1,0:T(8,128)} %get-tuple-element.327, f32[1024]{0:T(1024)S(1)} %add_subtract_fusion.4), kind=kLoop, calls=%fused_computation.31 | loop fusion | flops 16769024 | bytes 33591296 | tf_op jit(solution)/shard_map/reduce_max | solution.py:54
  187.2 14.0 %exponential_reduce_fusion.2 = f32[8192]{0:T(1024)S(1)} fusion(f32[1024,8192]{1,0:T(8,128)} %get-tuple-element.327, f32[8192]{0:T(1024)S(1)} %add_reduce_fusion.1, f32[1024]{0:T(1024)S(1)} %add_subtract_fusion.4), kind=kLoop, calls=%fused_computation.26 | loop fusion | flops 25157632 | bytes 33624064 | tf_op jit(solution)/shard_map/reduce_sum | solution.py:55
  201.2 30.9 %all-gather.6 = f32[65536]{0:T(1024)S(1)} all-gather(f32[8192]{0:T(1024)S(1)} %add_reduce_fusion.1), channel_id=8, replica_groups=mesh['item'=8,'bucket'=4] {'item'}, dimensions={0}, use_global_device_ids=true | all-gather | bytes 294912 | tf_op jit(solution)/shard_map/all_gather | solution.py:16
  232.1 30.7 %all-gather.7 = f32[65536]{0:T(1024)S(1)} all-gather(f32[8192]{0:T(1024)S(1)} %exponential_reduce_fusion.2), channel_id=9, replica_groups=mesh['item'=8,'bucket'=4] {'item'}, dimensions={0}, use_global_device_ids=true | all-gather | bytes 294912 | tf_op jit(solution)/shard_map/all_gather | solution.py:16
  263.9 12.2 %add_reduce_fusion = f32[1024]{0:T(1024)S(1)} fusion(f32[1024,8192]{1,0:T(8,128)} %get-tuple-element.327, f32[8192]{0:T(1024)S(1)} %add_subtract_fusion.1), kind=kLoop, calls=%fused_computation.30 | loop fusion | flops 16776192 | bytes 33591296 | tf_op jit(solution)/shard_map/reduce_max | solution.py:47
  276.1 14.3 %exponential_reduce_fusion.1 = f32[1024]{0:T(1024)S(1)} fusion(f32[1024,8192]{1,0:T(8,128)} %get-tuple-element.327, f32[1024]{0:T(1024)S(1)} %add_reduce_fusion, f32[8192]{0:T(1024)S(1)} %add_subtract_fusion.1), kind=kLoop, calls=%fused_computation.25 | loop fusion | flops 25164800 | bytes 33595392 | tf_op jit(solution)/shard_map/reduce_sum | solution.py:48
  290.4 5.2 all-gather.8
  295.6 5.4 all-gather.9
  301.2 12.5 %add_reduce_fusion.4 = f32[8192]{0:T(1024)S(1)} fusion(f32[1024,8192]{1,0:T(8,128)} %get-tuple-element.327, f32[1024]{0:T(1024)S(1)} %add_subtract_fusion.3), kind=kLoop, calls=%fused_computation.34 | loop fusion | flops 16769024 | bytes 33591296 | tf_op jit(solution)/shard_map/reduce_max | solution.py:54
  313.7 14.0 %exponential_reduce_fusion = f32[8192]{0:T(1024)S(1)} fusion(f32[1024,8192]{1,0:T(8,128)} %get-tuple-element.327, f32[8192]{0:T(1024)S(1)} %add_reduce_fusion.4, f32[1024]{0:T(1024)S(1)} %add_subtract_fusion.3), kind=kLoop, calls=%fused_computation.24 | loop fusion | flops 25157632 | bytes 33624064 | tf_op jit(solution)/shard_map/reduce_sum | solution.py:55
  327.7 30.9 %all-gather.10 = f32[65536]{0:T(1024)S(1)} all-gather(f32[8192]{0:T(1024)S(1)} %add_reduce_fusion.4), channel_id=12, replica_groups=mesh['item'=8,'bucket'=4] {'item'}, dimensions={0}, use_global_device_ids=true | all-gather | bytes 294912 | tf_op jit(solution)/shard_map/all_gather | solution.py:16
  358.6 30.7 %all-gather.11 = f32[65536]{0:T(1024)S(1)} all-gather(f32[8192]{0:T(1024)S(1)} %exponential_reduce_fusion), channel_id=13, replica_groups=mesh['item'=8,'bucket'=4] {'item'}, dimensions={0}, use_global_device_ids=true | all-gather | bytes 294912 | tf_op jit(solution)/shard_map/all_gather | solution.py:16
  390.4 14.8 %fusion = f32[1024]{0:T(1024)S(1)} fusion(f32[1024,8192]{1,0:T(8,128)} %get-tuple-element.327, f32[8192]{0:T(1024)S(1)} %add_subtract_fusion, f32[1024]{0:T(1024)S(1)} %add_subtract_fusion.3), kind=kLoop, calls=%fused_computation.35 | loop fusion | flops 33553408 | bytes 33595392 | tf_op jit(solution)/shard_map/reduce_sum | solution.py:80
  405.2 5.2 all-gather.12
  410.7 18.8 %subtract_convert_fusion = bf16[1024,8192]{1,0:T(8,128)(2,1)S(1)} fusion(f32[1024,8192]{1,0:T(8,128)} %get-tuple-element.327, f32[1024]{0:T(1024)S(1)} %get-tuple-element.223, f32[1024]{0:T(1024)S(1)} %get-tuple-element.222, f32[1024]{0:T(1024)S(1)} %get-tuple-element.221, f32[8192]{0:T(1024)S(1)} %add_subtract_fusion, f32[1024]{0:T(1024)S(1)} %add_subtract_fusion.3), kind=kLoop, calls=%fused_computation.22 | loop fusion | flops 67108864 | bytes 50380800 | tf_op jit(solution)/shard_map/convert_element_type | solution.py:84
  429.5 5.7 copy-done.1
  435.2 4.3 convolution_multiply_fusion
  439.8 11.7 %convolution_multiply_fusion.1 = f32[1024,64]{0,1:T(8,128)} fusion(bf16[1024,8192]{1,0:T(8,128)(2,1)} %copy-done.1, bf16[8192,64]{0,1:T(8,128)(2,1)S(1)} %copy-done.2), kind=kOutput, calls=%fused_computation.41 | convolution fusion | flops 1073807360 | bytes 18087936 | tf_op jit(solution)/shard_map/dot_general | solution.py:88
  451.5 91.4 %all-reduce.5.cloned.1.call-done = f32[8192,64]{0,1:T(8,128)} async-done(((f32[8192,64]{0,1:T(8,128)}), f32[8192,64]{0,1:T(8,128)}) %all-reduce.5.cloned.1.call-update) | async-done | bytes 2097168 | tf_op jit(solution)/shard_map/psum | solution.py:93
  548.2 29.2 %all-reduce.3.cloned.1.call-done = f32[1024,64]{0,1:T(8,128)} async-done(((f32[1024,64]{0,1:T(8,128)}), f32[1024,64]{0,1:T(8,128)}) %all-reduce.3.cloned.1.call-update) | async-done | bytes 262160 | tf_op jit(solution)/shard_map/psum | solution.py:87
  (139 shorter events, 14.7 us)
Async XLA Ops:
  7.2 0.9 copy-start
  7.2 535.8 %all-reduce.5.cloned.1.call-start = ((), (), s32[]{:S(2)}) async-start(), calls=%async_computation.1 | async-start | bytes 4194304 | tf_op jit(solution)/shard_map/psum | solution.py:93
  410.6 29.2 %copy-start.2 = (bf16[8192,64]{0,1:T(8,128)(2,1)S(1)}, bf16[8192,64]{0,1:T(8,128)(2,1)}, u32[]{:S(2)}) copy-start(bf16[8192,64]{0,1:T(8,128)(2,1)} %param.17) | copy-start | bytes 3145732
  429.5 5.7 copy-start.1
  439.5 137.9 %all-reduce.3.cloned.1.call-start = ((), (), s32[]{:S(2)}) async-start(), calls=%async_computation | async-start | bytes 524288 | tf_op jit(solution)/shard_map/psum | solution.py:87
Sparse Core Ops, SparseCore 0:
  439.7 103.2 all-reduce.4
  545.9 31.5 all-reduce.2
where the time goes:
time: 588 us; the launch traced here: 586 us
  blocking collectives  223 us (38%)
  other arithmetic  186 us (32%)
  waiting for transfers between devices  121 us (21%)
  matrix products  30.3 us (5%)
  between operations  14.4 us (2%)
  local copies, waits for them, and re-layouts  10.4 us (2%)
    all_gather x13, blocking collectives, joined(): pieces = jax.tree.map(lambda part: lax.all_gather(part, axis), value)  223 us
    psum x1, waiting for transfers between devices, body(): gradient = lax.psum(local_grad, 'item')  91.4 us
    reduce_sum x3, other arithmetic, reduce_cols(): summed = jnp.sum(jnp.exp(values - highest[None, :]), axis=0)  41.9 us
    reduce_max x3, other arithmetic, reduce_cols(): highest = jnp.max(values, axis=0)  37.4 us
    psum x1, waiting for transfers between devices, body(): lax.psum(score_scale * jnp.dot(delta, centroids, preferred_element_type=j...  29.2 us
    reduce_sum x2, other arithmetic, reduce_rows(): summed = jnp.sum(jnp.exp(values - highest[:, None]), axis=1)  28.6 us
    reduce_max x2, other arithmetic, reduce_rows(): highest = jnp.max(values, axis=1)  24.3 us
    convert_element_type x1, other arithmetic, body(): (masses[:, None] * jnp.exp(scores - highest[:, None]) / totals[:, None] -...  18.8 us
  transfers between devices with their start and end apart: 2, of which 2 were waited for; matrix products, arithmetic and copies ran while one was open for 3% of the time, Pallas kernels for 0%

commit v1 on v0

v1 whole, which is shorter than its diff:
```python
import functools
import math

import jax
import jax.numpy as jnp
from jax import lax
from jax.experimental import pallas as pl
from jax.experimental.pallas import tpu as pltpu
from jax.sharding import PartitionSpec as P

ITERS = 3

score_scale = 20.0
step_rate = 0.2
epsilon = 1e-06

CHUNK = 512
LANES = 128
POTS = 16


def swap(value, axis, bit):
    size = lax.axis_size(axis)
    return lax.ppermute(value, axis, [(k, k ^ bit) for k in range(size)])


def bits_of(axis):
    size = lax.axis_size(axis)
    return [1 << k for k in range(size.bit_length() - 1)]


def add_over(value, axis):
    for bit in bits_of(axis):
        value = value + swap(value, axis, bit)
    return value


def gather_blocks(value, axis):
    held = {0: value}
    for bit in reversed(bits_of(axis)):
        held.update({key | bit: swap(block, axis, bit) for key, block in list(held.items())})
    return held


def weights(w_ref, columns, repeat):
    tile = w_ref[:, columns]
    return [tile] * repeat


def thirds(value):
    high = value.astype(jnp.bfloat16).astype(jnp.float32)
    middle = (value - high).astype(jnp.bfloat16).astype(jnp.float32)
    return high, middle, value - high - middle


def left_pots(column, shape):
    lane = lax.broadcasted_iota(jnp.int32, shape, 1)
    high, middle, low = thirds(column)
    out = jnp.where(lane < 3, 1.0, 0.0)
    out = jnp.where(lane == 3, high, out)
    out = jnp.where(lane == 4, middle, out)
    out = jnp.where(lane == 5, low, out)
    return out.astype(jnp.bfloat16)


def right_pots(row, width):
    sub = lax.broadcasted_iota(jnp.int32, (POTS, width), 0)
    high, middle, low = thirds(row)
    out = jnp.where((sub >= 3) & (sub < 6), 1.0, 0.0)
    out = jnp.where(sub == 0, high, out)
    out = jnp.where(sub == 1, middle, out)
    out = jnp.where(sub == 2, low, out)
    return out.astype(jnp.bfloat16)


def column_of(rows):
    return jnp.transpose(rows)


def row_of(column):
    wide = jnp.broadcast_to(column, (column.shape[0], LANES))
    return jnp.transpose(wide)[0:8, :]


def slices(value):
    return [value[:, k * LANES : (k + 1) * LANES] for k in range(value.shape[1] // LANES)]


def folded(values, op):
    values = list(values)
    while len(values) > 1:
        values = [op(*values[k : k + 2]) if k + 1 < len(values) else values[k] for k in range(0, len(values), 2)]
    return values[0]


def lse_kernel(l_ref, w_ref, out_ref, y_ref, part_ref, *, repeat):
    block, width = y_ref.shape
    left = l_ref[...]
    part_ref[...] = jnp.full(part_ref.shape, -jnp.inf, jnp.float32)

    @pl.loop(0, width // CHUNK)
    def _(step):
        at = pl.ds(pl.multiple_of(step * CHUNK, CHUNK), CHUNK)
        right = jnp.concatenate(weights(w_ref, at, repeat), axis=0)
        y = jnp.dot(left, right, preferred_element_type=jnp.float32)
        y_ref[:, at] = y
        part_ref[...] = jnp.maximum(part_ref[...], folded(slices(y), jnp.maximum))

    highest = jnp.max(part_ref[...], axis=1, keepdims=True)
    part_ref[...] = jnp.zeros(part_ref.shape, jnp.float32)
    wide = jnp.broadcast_to(highest, (block, LANES))

    @pl.loop(0, width // CHUNK)
    def _(step):
        at = pl.ds(pl.multiple_of(step * CHUNK, CHUNK), CHUNK)
        terms = [jnp.exp(piece - wide) for piece in slices(y_ref[:, at])]
        part_ref[...] += folded(terms, jnp.add)

    summed = jnp.sum(part_ref[...], axis=1, keepdims=True)
    lane = lax.broadcasted_iota(jnp.int32, (block, LANES), 1)
    both = jnp.where(lane == 0, highest, summed)
    out_ref[...] = jnp.transpose(both)[0:8, :]


def sink_kernel(
    l_ref, p_ref, w_ref, q_ref, sums_ref, pot_ref, row_ref, y_ref, part_ref, wide_ref, wpot_ref, acc_ref,
    *, first, rows_total, buckets_total, repeat
):
    block, width = y_ref.shape
    step_id = pl.program_id(0)

    @pl.when(step_id == 0)
    def _():
        acc_ref[...] = jnp.zeros(acc_ref.shape, jnp.float32)

        @pl.loop(0, width // CHUNK)
        def _(step):
            at = pl.ds(pl.multiple_of(step * CHUNK, CHUNK), CHUNK)
            row = q_ref[0:1, at]
            if not first:
                row = row - jnp.log(q_ref[1:2, at] * float(rows_total))
            row_ref[0:1, at] = row
            wpot_ref[:, at] = right_pots(row, CHUNK)

    if first:
        old = jnp.zeros((block, 1), jnp.float32)
    else:
        old = column_of(p_ref[...])[:, 0:1]
    left = jnp.concatenate([l_ref[...], left_pots(old, (block, LANES))], axis=1)[:, : LANES + POTS]
    part_ref[...] = jnp.full(part_ref.shape, -jnp.inf if first else 0.0, jnp.float32)

    @pl.loop(0, width // CHUNK)
    def _(step):
        at = pl.ds(pl.multiple_of(step * CHUNK, CHUNK), CHUNK)
        right = jnp.concatenate(weights(w_ref, at, repeat) + [wpot_ref[:, at]], axis=0)
        y = jnp.dot(left, right, preferred_element_type=jnp.float32)
        if first:
            y_ref[:, at] = y
            part_ref[...] = jnp.maximum(part_ref[...], folded(slices(y), jnp.maximum))
        else:
            y = jnp.exp(y)
            y_ref[:, at] = y
            part_ref[...] += folded(slices(y), jnp.add)

    if first:
        highest = jnp.max(part_ref[...], axis=1, keepdims=True)
        wide_ref[...] = jnp.broadcast_to(highest, (block, LANES))
        part_ref[...] = jnp.zeros(part_ref.shape, jnp.float32)

        @pl.loop(0, width // CHUNK)
        def _(step):
            at = pl.ds(pl.multiple_of(step * CHUNK, CHUNK), CHUNK)
            terms = [jnp.exp(piece - wide_ref[...]) for piece in slices(y_ref[:, at])]
            y_ref[:, at] = jnp.concatenate(terms, axis=1)
            part_ref[...] += folded(terms, jnp.add)

    summed = jnp.sum(part_ref[...], axis=1, keepdims=True)
    if first:
        new = -math.log(buckets_total) - (highest + jnp.log(summed))
    else:
        new = old - jnp.log(summed * float(buckets_total))
    pot_ref[...] = row_of(new)
    wide_ref[...] = jnp.broadcast_to(1.0 / (summed * float(buckets_total)), (block, LANES))

    @pl.loop(0, width // CHUNK)
    def _(step):
        at = pl.ds(pl.multiple_of(step * CHUNK, CHUNK), CHUNK)
        sums = [
            jnp.sum((piece * wide_ref[...]).reshape(block // 8, 8, LANES), axis=0) for piece in slices(y_ref[:, at])
        ]
        acc_ref[:, at] += jnp.concatenate(sums, axis=1)

    @pl.when(step_id == pl.num_programs(0) - 1)
    def _():
        sums_ref[...] = jnp.sum(acc_ref[...], axis=0, keepdims=True)


def final_kernel(
    l_ref, p_ref, w_ref, q_ref, r_ref, *rest, repeat, update
):
    if update:
        own_ref, out_ref, wide_ref, wpot_ref, acc_ref = rest
    else:
        out_ref, wide_ref, wpot_ref, acc_ref = rest
    block = l_ref.shape[0]
    width = w_ref.shape[1]

    @pl.when(pl.program_id(0) == 0)
    def _():
        @pl.loop(0, width // CHUNK)
        def _(step):
            at = pl.ds(pl.multiple_of(step * CHUNK, CHUNK), CHUNK)
            wpot_ref[:, at] = right_pots(q_ref[0:1, at], CHUNK)

    columns = column_of(p_ref[...])
    left = jnp.concatenate([l_ref[...], left_pots(columns[:, 0:1], (block, LANES))], axis=1)[:, : LANES + POTS]
    wide_ref[...] = jnp.broadcast_to(columns[:, 1:2], (block, LANES))
    acc_ref[...] = jnp.zeros(acc_ref.shape, jnp.float32)

    @pl.loop(0, width // CHUNK)
    def _(step):
        at = pl.ds(pl.multiple_of(step * CHUNK, CHUNK), CHUNK)
        right = jnp.concatenate(weights(w_ref, at, repeat) + [wpot_ref[:, at]], axis=0)
        y = jnp.dot(left, right, preferred_element_type=jnp.float32)
        scale = q_ref[1:2, at]
        delta = jnp.concatenate(
            [
                (jnp.exp(piece) * (wide_ref[...] * factor - 1.0)).astype(jnp.bfloat16)
                for piece, factor in zip(slices(y), slices(scale))
            ],
            axis=1,
        )
        acc_ref[...] += lax.dot_general(
            delta, r_ref[:, at], (((1,), (1,)), ((), ())), preferred_element_type=jnp.float32
        )

    gradient = score_scale * acc_ref[...]
    if not update:
        out_ref[...] = gradient
    else:
        moved = own_ref[...].astype(jnp.float32) - step_rate * gradient
        scaled = moved * lax.rsqrt(jnp.mean(moved * moved, axis=1, keepdims=True) + epsilon)
        half = block // 2
        out_ref[...] = jnp.concatenate([scaled[:half], scaled[half:]], axis=1)


VMEM = functools.partial(pltpu.VMEM)


def block_of(count, width):
    return min(count, 256 if width <= 16384 else 128)


def params():
    return pltpu.CompilerParams(dimension_semantics=("arbitrary",), vmem_limit_bytes=60 * 1024 * 1024)


def cost(count, width, passes):
    return pl.CostEstimate(
        flops=2 * count * width * 256 * passes, transcendentals=count * width, bytes_accessed=width * 256 * 2
    )


def full(array):
    return pl.BlockSpec(array.shape, lambda k: (0, 0))


def lse(left, right, repeat):
    count, width = left.shape[0], right.shape[1]
    block = block_of(count, width)
    return pl.pallas_call(
        functools.partial(lse_kernel, repeat=repeat),
        grid=(count // block,),
        in_specs=[pl.BlockSpec((block, LANES), lambda k: (k, 0)), full(right)],
        out_specs=pl.BlockSpec((8, block), lambda k: (0, k)),
        out_shape=jax.ShapeDtypeStruct((8, count), jnp.float32),
        scratch_shapes=[VMEM((block, width), jnp.float32), VMEM((block, LANES), jnp.float32)],
        compiler_params=params(),
        cost_estimate=cost(count, width, 1),
        name="row_lse",
    )(left, right)


def sink(left, p_rows, right, q_rows, first, rows_total, buckets_total):
    count, width = left.shape[0], right.shape[1]
    block = block_of(count, width)
    return pl.pallas_call(
        functools.partial(
            sink_kernel, first=first, rows_total=rows_total, buckets_total=buckets_total, repeat=1
        ),
        grid=(count // block,),
        in_specs=[
            pl.BlockSpec((block, LANES), lambda k: (k, 0)),
            pl.BlockSpec((8, block), lambda k: (0, k)),
            full(right),
            full(q_rows),
        ],
        out_specs=[
            pl.BlockSpec((1, width), lambda k: (0, 0)),
            pl.BlockSpec((8, block), lambda k: (0, k)),
            pl.BlockSpec((1, width), lambda k: (0, 0)),
        ],
        out_shape=[
            jax.ShapeDtypeStruct((1, width), jnp.float32),
            jax.ShapeDtypeStruct((8, count), jnp.float32),
            jax.ShapeDtypeStruct((1, width), jnp.float32),
        ],
        scratch_shapes=[
            VMEM((block, width), jnp.float32),
            VMEM((block, LANES), jnp.float32),
            VMEM((block, LANES), jnp.float32),
            VMEM((POTS, width), jnp.bfloat16),
            VMEM((8, width), jnp.float32),
        ],
        compiler_params=params(),
        cost_estimate=cost(count, width, 1),
        name="sinkhorn_first" if first else "sinkhorn_next",
    )(left, p_rows, right, q_rows)


def final(left, p_rows, right, q_rows, other, repeat, own=None):
    count, width = left.shape[0], right.shape[1]
    block = block_of(count, width)
    update = own is not None
    dim = other.shape[0]
    in_specs = [
        pl.BlockSpec((block, LANES), lambda k: (k, 0)),
        pl.BlockSpec((8, block), lambda k: (0, k)),
        full(right),
        full(q_rows),
        full(other),
    ]
    args = [left, p_rows, right, q_rows, other]
    if update:
        in_specs.append(pl.BlockSpec((block, dim), lambda k: (k, 0)))
        args.append(own)
        out_spec = pl.BlockSpec((block // 2, 2 * dim), lambda k: (k, 0))
        out_shape = jax.ShapeDtypeStruct((count // 2, 2 * dim), jnp.float32)
    else:
        out_spec = pl.BlockSpec((block, dim), lambda k: (k, 0))
        out_shape = jax.ShapeDtypeStruct((count, dim), jnp.float32)
    out = pl.pallas_call(
        functools.partial(final_kernel, repeat=repeat, update=update),
        grid=(count // block,),
        in_specs=in_specs,
        out_specs=out_spec,
        out_shape=out_shape,
        scratch_shapes=[
            VMEM((block, LANES), jnp.float32),
            VMEM((POTS, width), jnp.bfloat16),
            VMEM((block, dim), jnp.float32),
        ],
        compiler_params=params(),
        cost_estimate=cost(count, width, 2),
        name="centroid_update" if update else "code_gradient",
    )(*args)
    return out, block


def halves(scaled):
    high = lax.reduce_precision(scaled, 8, 7)
    return high.astype(jnp.bfloat16), (scaled - high).astype(jnp.bfloat16)


def eight(*rows):
    rows = [row.reshape(1, -1) for row in rows]
    return jnp.concatenate(rows + [jnp.zeros((8 - len(rows), rows[0].shape[1]), jnp.float32)], axis=0)


def body(code_rows, centroids):
    items = lax.axis_size("item")
    item = lax.axis_index("item")
    rows_own, dim = code_rows.shape
    rows_total = rows_own * items
    buckets_own = centroids.shape[0]
    buckets_total = buckets_own * lax.axis_size("bucket")
    share = buckets_own // items
    log_rows = math.log(rows_total)

    codes_f32 = code_rows.astype(jnp.float32)
    row_left = jnp.concatenate(halves(score_scale * codes_f32), axis=1)
    centroids_t = centroids.T
    stats = lse(row_left, centroids_t, 2)[0:2]
    codes_t = codes_f32.T

    blocks = gather_blocks(codes_t, "item")
    table = jnp.zeros((items,) + codes_t.shape, jnp.float32)
    for key, block in blocks.items():
        table = lax.dynamic_update_slice(table, block[None], (item ^ key, 0, 0))
    table = table.transpose(1, 0, 2).reshape(dim, rows_total)
    high, low = halves(score_scale * table)
    all_right = jnp.concatenate([high, low], axis=0)
    all_other = table.astype(jnp.bfloat16)
    own = lax.dynamic_slice_in_dim(centroids, item * share, share, axis=0)
    own_left = jnp.concatenate([own, own], axis=1)

    for bit in bits_of("bucket"):
        other = swap(stats, "bucket", bit)
        highest = jnp.maximum(stats[0], other[0])
        summed = stats[1] * jnp.exp(stats[0] - highest) + other[1] * jnp.exp(other[0] - highest)
        stats = jnp.stack([highest, summed])
    first_own = -log_rows - (stats[0] + jnp.log(stats[1]))
    row_first = lax.dynamic_update_slice(jnp.zeros((rows_total,), jnp.float32), first_own, (item * rows_own,))
    row_first = add_over(row_first, "item")

    p_rows = jnp.zeros((8, share), jnp.float32)
    q_rows = eight(row_first)
    sums = None
    for iteration in range(ITERS):
        sums, p_rows, row = sink(own_left, p_rows, all_right, q_rows, iteration == 0, rows_total, buckets_total)
        sums = add_over(sums, "bucket")
        if iteration < ITERS - 1:
            sums = add_over(sums, "item")
            q_rows = eight(row, sums)

    col_own = p_rows[0]
    col = lax.dynamic_update_slice(jnp.zeros((buckets_own,), jnp.float32), col_own, (item * share,))
    if buckets_own == rows_total:
        both = add_over(jnp.concatenate([sums, col.reshape(1, -1)], axis=0), "item")
        sums, col = both[0], both[1]
    else:
        sums, col = add_over(sums.reshape(-1), "item"), add_over(col, "item")
    mass = sums.reshape(-1) * float(rows_total)
    row = row.reshape(-1)
    row_pot = row + log_rows
    row_scale = mass * jnp.exp(row_first - row)

    update, block = final(
        own_left, eight(col_own, jnp.exp(-col_own)), all_right, eight(row_pot, row_scale), all_other, 1, own
    )

    def mine(values):
        return lax.dynamic_slice_in_dim(values, item * rows_own, rows_own, axis=0)

    grad, _ = final(
        row_left, eight(mine(row_pot), mine(row_scale)), centroids_t, eight(col, jnp.exp(-col)), centroids_t, 2
    )

    new_centroids = jnp.zeros((items, share, dim), jnp.float32)
    for key, piece in gather_blocks(update, "item").items():
        piece = piece.reshape(share // block, block // 2, 2, dim).transpose(0, 2, 1, 3).reshape(1, share, dim)
        new_centroids = lax.dynamic_update_slice(new_centroids, piece, (item ^ key, 0, 0))
    grad_codes = add_over(grad, "bucket")
    return (grad_codes, new_centroids.reshape(buckets_own, dim))


def solution(mesh):
    return jax.shard_map(
        body,
        mesh=mesh,
        in_specs=(P("item", None), P("bucket", None)),
        out_specs=(P("item", None), P("bucket", None)),
        check_vma=False,
    )
```

time: 588 us -> 337 us (0.57)
  blocking collectives: 223 us -> 0 us
  other arithmetic: 186 us -> 16.4 us
  Pallas kernels: 0 us -> 155 us
  waiting for transfers between devices: 121 us -> 53 us
  local copies, waits for them, and re-layouts: 10.4 us -> 65.2 us
  starting transfers between devices: 0.3 us -> 43.8 us
  matrix products: 30.3 us -> 0 us
  between operations: 14.4 us -> 1.32 us
    all_gather x13 -> x0, blocking collectives: 223 us -> none  [joined(): pieces = jax.tree.map(lambda part: lax.all_gather(part, axis), value)]
    pallas_call x0 -> x6, Pallas kernels: none -> 155 us  [the longest x3 75.3 us: sink(): pl.pallas_call(functools.partial(sink_kernel, first=first, rows_total=row...]
    psum x2 -> x0, waiting for transfers between devices: 121 us -> none  [the longest x1 91.4 us: body(): gradient = lax.psum(local_grad, 'item')]
    reduce_sum x8 -> x0, other arithmetic: 101 us -> none  [the longest x3 41.9 us: reduce_cols(): summed = jnp.sum(jnp.exp(values - highest[None, :]), axis=0)]
    reduce_max x5 -> x0, other arithmetic: 61.7 us -> none  [the longest x3 37.4 us: reduce_cols(): highest = jnp.max(values, axis=0)]
    ppermute x0 -> x36, waiting for transfers between devices: none -> 53 us  [swap(): return lax.ppermute(value, axis, [(k, k ^ bit) for k in range(size)])]
    ppermute x0 -> x36, starting transfers between devices: none -> 43.8 us  [swap(): return lax.ppermute(value, axis, [(k, k ^ bit) for k in range(size)])]
    dynamic_update_slice x0 -> x16, local copies, waits for them, and re-layouts: none -> 31.5 us  [the longest x8 18.1 us: body(): lax.dynamic_update_slice(new_centroids, piece, (item ^ key, 0, 0))]
  transfers between devices with their start and end apart: 2 -> 36, of which waited for: 2 -> 19; matrix products, arithmetic and copies ran while one was open for 3% -> 18% of each run, Pallas kernels for 0% -> 8%
where the time goes in v1:
time: 337 us; the launch traced here: 334 us
  Pallas kernels  155 us (46%)
  local copies, waits for them, and re-layouts  65.2 us (19%)
  waiting for transfers between devices  53 us (16%)
  starting transfers between devices  43.8 us (13%)
  other arithmetic  16.4 us (5%)
    pallas_call x3, Pallas kernels, sink(): pl.pallas_call(functools.partial(sink_kernel, first=first, rows_total=row...  75.3 us
    pallas_call x2, Pallas kernels, final(): pl.pallas_call(functools.partial(final_kernel, repeat=repeat, update=upda...  57.5 us
    ppermute x36, waiting for transfers between devices, swap(): return lax.ppermute(value, axis, [(k, k ^ bit) for k in range(size)])  53 us
    ppermute x36, starting transfers between devices, swap(): return lax.ppermute(value, axis, [(k, k ^ bit) for k in range(size)])  43.8 us
    pallas_call x1, Pallas kernels, lse(): pl.pallas_call(functools.partial(lse_kernel, repeat=repeat), grid=(count...  22 us
    dynamic_update_slice x8, local copies, waits for them, and re-layouts, body(): lax.dynamic_update_slice(new_centroids, piece, (item ^ key, 0, 0))  18.1 us
    dynamic_update_slice x8, local copies, waits for them, and re-layouts, body(): table = lax.dynamic_update_slice(table, block[None], (item ^ key, 0, 0))  13.4 us
    broadcast_in_dim x8, local copies, waits for them, and re-layouts, body(): table = lax.dynamic_update_slice(table, block[None], (item ^ key, 0, 0))  7.87 us
  transfers between devices with their start and end apart: 36, of which 19 were waited for; matrix products, arithmetic and copies ran while one was open for 18% of the time, Pallas kernels for 8%

profile of v1, /device:TPU:0, one launch (start us, length us, event | category | flops | bytes accessed | tf_op | source)
XLA Modules:
  0.0 334.5 jit_solution(1065716625479970117)
XLA Ops:
  2.6 22.0 %row_lse.1 = f32[8,1024]{1,0:T(8,128)} custom-call(bf16[1024,128]{1,0:T(8,128)(2,1)} %pad_maximum_fusion.1.l_ref, bf16[64,8192]{1,0:T(8,128)(2,1)} %bitcast.97), custom_call_target="tpu_custom_call" | custom-call | flops 4294967296 | bytes 4194304 | tf_op jit(solution)/shard_map/row_lse/pallas_call | solution.py:271
  26.6 3.6 %collective-permute-start = (f32[64,1024]{1,0:T(8,128)}, f32[64,1024]{1,0:T(8,128)S(1)}, u32[]{:S(2)}, u32[]{:S(2)}) collective-permute-start(f32[64,1024]{1,0:T(8,128)} %get-tuple-element.34), channel_id=1, source_target_pairs={{0,16},{4,20},{8,24},{12,28},{16,0},{20,4},{24,8},{28,12},{1,17},{... | collective-permute-start | bytes 786440 | tf_op jit(solution)/shard_map/ppermute | solution.py:24
  34.2 8.9 %collective-permute-done = f32[64,1024]{1,0:T(8,128)S(1)} collective-permute-done((f32[64,1024]{1,0:T(8,128)}, f32[64,1024]{1,0:T(8,128)S(1)}, u32[]{:S(2)}, u32[]{:S(2)}) %collective-permute-start) | collective-permute-done | bytes 262176 | tf_op jit(solution)/shard_map/ppermute | solution.py:24
  48.0 3.2 collective-permute-done.2
  54.9 1.8 collective-permute-done.10
  56.7 2.5 collective-permute-start.11
  86.5 27.8 %sinkhorn_first.1 = (f32[1,8192]{1,0:T(1,128)}, f32[8,1024]{1,0:T(8,128)}, f32[1,8192]{1,0:T(1,128)}) custom-call(bf16[1024,128]{1,0:T(8,128)(2,1)} %pad_maximum_fusion.2.l_ref, f32[8,1024]{1,0:T(8,128)} %broadcast_in_dim.34.p_ref, bf16[128,8192]{1,0:T(8,128)(2,1)} %pad_maximum_fusion.w_ref, f32[8,8192]{1,0:T(8,128)} %concatenate.36.q_ref), custom_call_target="tpu_custom_call" | custom-call | flops 4294967296 | bytes 4194304 | tf_op jit(solution)/shard_map/sinkhorn_first/pallas_call | solution.py:287
  118.1 2.4 collective-permute-done.13
  121.2 3.4 %collective-permute-done.14 = f32[1,8192]{1,0:T(1,128)S(1)} collective-permute-done((f32[1,8192]{1,0:T(1,128)S(1)}, f32[1,8192]{1,0:T(1,128)S(1)}, u32[]{:S(2)}, u32[]{:S(2)}) %collective-permute-start.14) | collective-permute-done | bytes 32800 | tf_op jit(solution)/shard_map/ppermute | solution.py:24
  124.6 1.8 collective-permute-start.15
  126.4 2.2 collective-permute-done.15
  128.6 1.8 collective-permute-start.16
  130.5 3.0 collective-permute-done.16
  135.1 23.8 %sinkhorn_next.2 = (f32[1,8192]{1,0:T(1,128)}, f32[8,1024]{1,0:T(8,128)}, f32[1,8192]{1,0:T(1,128)}) custom-call(bf16[1024,128]{1,0:T(8,128)(2,1)} %pad_maximum_fusion.2.l_ref, f32[8,1024]{1,0:T(8,128)} %get-tuple-element.11.p_ref, bf16[128,8192]{1,0:T(8,128)(2,1)} %pad_maximum_fusion.w_ref, f32[8,8192]{1,0:T(8,128)} %maximum_maximum_fusion.q_ref), custom_call_target="tpu_custom_call" | custom-call | flops 4294967296 | bytes 4194304 | tf_op jit(solution)/shard_map/sinkhorn_next/pallas_call | solution.py:287
  162.7 2.4 collective-permute-done.18
  165.8 3.3 collective-permute-done.19
  169.1 2.0 collective-permute-start.20
  171.1 2.0 collective-permute-done.20
  173.2 1.9 collective-permute-start.21
  175.0 3.0 collective-permute-done.21
  179.6 23.8 %sinkhorn_next.3 = (f32[1,8192]{1,0:T(1,128)}, f32[8,1024]{1,0:T(8,128)}, f32[1,8192]{1,0:T(1,128)}) custom-call(bf16[1024,128]{1,0:T(8,128)(2,1)} %pad_maximum_fusion.2.l_ref, f32[8,1024]{1,0:T(8,128)} %get-tuple-element.14.p_ref, bf16[128,8192]{1,0:T(8,128)(2,1)} %pad_maximum_fusion.w_ref, f32[8,8192]{1,0:T(8,128)} %maximum_maximum_fusion.1.q_ref), custom_call_target="tpu_custom_call" | custom-call | flops 4294967296 | bytes 4194304 | tf_op jit(solution)/shard_map/sinkhorn_next/pallas_call | solution.py:287
  212.0 2.1 collective-permute-done.24
  214.2 2.0 collective-permute-start.25
  216.2 2.4 collective-permute-done.25
  220.5 3.4 %collective-permute-done.26 = f32[2,8192]{1,0:T(2,128)S(1)} collective-permute-done((f32[2,8192]{1,0:T(2,128)S(1)}, f32[2,8192]{1,0:T(2,128)S(1)}, u32[]{:S(2)}, u32[]{:S(2)}) %collective-permute-start.26) | collective-permute-done | bytes 65568 | tf_op jit(solution)/shard_map/ppermute | solution.py:24
  225.7 29.2 %centroid_update.1 = f32[512,128]{1,0:T(8,128)} custom-call(bf16[1024,128]{1,0:T(8,128)(2,1)} %pad_maximum_fusion.2.l_ref, f32[8,1024]{1,0:T(8,128)} %get-tuple-element.52.p_ref, bf16[128,8192]{1,0:T(8,128)(2,1)} %pad_maximum_fusion.w_ref, f32[8,8192]{1,0:T(8,128)} %get-tuple-element.50.q_ref, bf16[64,8192]{1,0:T(8,128)(2,1)} %bitcast.80, ...), custom_call_target="tpu_custom_call" | custom-call | flops 8589934592 | bytes 4194304 | tf_op jit(solution)/shard_map/centroid_update/pallas_call | solution.py:342
  256.7 2.1 collective-permute-start.30
  258.8 28.2 %code_gradient.1 = f32[1024,64]{1,0:T(8,128)} custom-call(bf16[1024,128]{1,0:T(8,128)(2,1)} %pad_maximum_fusion.1.l_ref, f32[8,1024]{1,0:T(8,128)} %get-tuple-element.53.p_ref, bf16[64,8192]{1,0:T(8,128)(2,1)} %bitcast.98, f32[8,8192]{1,0:T(8,128)} %get-tuple-element.51.q_ref, bf16[64,8192]{1,0:T(8,128)(2,1)} %bitcast.99), custom_call_target="tpu_custom_call" | custom-call | flops 8589934592 | bytes 4194304 | tf_op jit(solution)/shard_map/code_gradient/pallas_call | solution.py:342
  292.4 3.7 %collective-permute-done.31 = f32[512,128]{1,0:T(8,128)} collective-permute-done((f32[512,128]{1,0:T(8,128)}, f32[512,128]{1,0:T(8,128)}, u32[]{:S(2)}, u32[]{:S(2)}) %collective-permute-start.31) | collective-permute-done | bytes 262176 | tf_op jit(solution)/shard_map/ppermute | solution.py:24
  317.4 4.0 %dynamic_update_slice.71 = f32[8,1024,64]{1,0,2:T(8,128)S(1)} dynamic-update-slice(f32[8,1024,64]{1,0,2:T(8,128)S(1)} %dynamic_update_slice.70, f32[1,1024,64]{1,0,2:T(1,128)} %bitcast.73, s32[]{:T(128)S(6)} %select_n.43, s32[]{:T(128)} %constant.22.clone.1, s32[]{:T(128)} %constant.22.clone.1) | dynamic-update-slice | bytes 524292 | tf_op jit(solution)/shard_map/dynamic_update_slice | solution.py:442
  323.1 4.0 %dynamic_update_slice.73 = f32[8,1024,64]{1,0,2:T(8,128)S(1)} dynamic-update-slice(f32[8,1024,64]{1,0,2:T(8,128)S(1)} %dynamic_update_slice.72, f32[1,1024,64]{1,0,2:T(1,128)} %bitcast.74, s32[]{:T(128)S(6)} %select_n.45, s32[]{:T(128)} %constant.22.clone.1, s32[]{:T(128)} %constant.22.clone.1) | dynamic-update-slice | bytes 524292 | tf_op jit(solution)/shard_map/dynamic_update_slice | solution.py:442
  332.0 2.5 copy.88
  (160 shorter events, 103.0 us)
Async XLA Ops:
  25.3 4.8 %collective-permute-start.7 = (f32[2,1024]{1,0:T(2,128)S(1)}, f32[2,1024]{1,0:T(2,128)S(1)}, u32[]{:S(2)}, u32[]{:S(2)}) collective-permute-start(f32[2,1024]{1,0:T(2,128)S(1)} %slice.46), channel_id=1, source_target_pairs={{0,1},{1,0},{2,3},{3,2},{4,5},{5,4},{6,7},{7,6},{8,9},{9,8},{10,11... | collective-permute-start | bytes 24584 | tf_op jit(solution)/shard_map/ppermute | solution.py:24
  26.6 16.5 %collective-permute-start = (f32[64,1024]{1,0:T(8,128)}, f32[64,1024]{1,0:T(8,128)S(1)}, u32[]{:S(2)}, u32[]{:S(2)}) collective-permute-start(f32[64,1024]{1,0:T(8,128)} %get-tuple-element.34), channel_id=1, source_target_pairs={{0,16},{4,20},{8,24},{12,28},{16,0},{20,4},{24,8},{28,12},{1,17},{... | collective-permute-start | bytes 786440 | tf_op jit(solution)/shard_map/ppermute | solution.py:24
  31.1 12.8 %collective-permute-start.8 = (f32[2,1024]{1,0:T(2,128)S(1)}, f32[2,1024]{1,0:T(2,128)S(1)}, u32[]{:S(2)}, u32[]{:S(2)}) collective-permute-start(f32[2,1024]{1,0:T(2,128)S(1)} %pad_maximum_fusion.4), channel_id=1, source_target_pairs={{0,2},{1,3},{2,0},{3,1},{4,6},{5,7},{6,4},{7,5},{8,10},{9,11},{10,... | collective-permute-start | bytes 24584 | tf_op jit(solution)/shard_map/ppermute | solution.py:24
  32.6 14.9 %collective-permute-start.1 = (f32[64,1024]{1,0:T(8,128)}, f32[64,1024]{1,0:T(8,128)}, u32[]{:S(2)}, u32[]{:S(2)}) collective-permute-start(f32[64,1024]{1,0:T(8,128)} %get-tuple-element.34), channel_id=1, source_target_pairs={{0,8},{4,12},{8,0},{12,4},{16,24},{20,28},{24,16},{28,20},{1,9},{5... | collective-permute-start | bytes 786440 | tf_op jit(solution)/shard_map/ppermute | solution.py:24
  43.1 8.2 %collective-permute-start.2 = (f32[64,1024]{1,0:T(8,128)S(1)}, f32[64,1024]{1,0:T(8,128)}, u32[]{:S(2)}, u32[]{:S(2)}) collective-permute-start(f32[64,1024]{1,0:T(8,128)S(1)} %collective-permute-done), channel_id=1, source_target_pairs={{0,8},{4,12},{8,0},{12,4},{16,24},{20,28},{24,16},{28,20},{1,9},{5... | collective-permute-start | bytes 786440 | tf_op jit(solution)/shard_map/ppermute | solution.py:24
  43.9 8.8 %collective-permute-start.9 = (f32[8192]{0:T(1024)S(1)}, f32[8192]{0:T(1024)S(1)}, u32[]{:S(2)}, u32[]{:S(2)}) collective-permute-start(f32[8192]{0:T(1024)S(1)} %get-tuple-element.26), channel_id=1, source_target_pairs={{0,4},{4,0},{8,12},{12,8},{16,20},{20,16},{24,28},{28,24},{1,5},{5... | collective-permute-start | bytes 98312 | tf_op jit(solution)/shard_map/ppermute | solution.py:24
  45.5 19.1 %collective-permute-start.3 = (f32[64,1024]{1,0:T(8,128)}, f32[64,1024]{1,0:T(8,128)}, u32[]{:S(2)}, u32[]{:S(2)}) collective-permute-start(f32[64,1024]{1,0:T(8,128)} %get-tuple-element.34), channel_id=1, source_target_pairs={{0,4},{4,0},{8,12},{12,8},{16,20},{20,16},{24,28},{28,24},{1,5},{5... | collective-permute-start | bytes 786440 | tf_op jit(solution)/shard_map/ppermute | solution.py:24
  46.0 24.4 %collective-permute-start.4 = (f32[64,1024]{1,0:T(8,128)S(1)}, f32[64,1024]{1,0:T(8,128)}, u32[]{:S(2)}, u32[]{:S(2)}) collective-permute-start(f32[64,1024]{1,0:T(8,128)S(1)} %collective-permute-done), channel_id=1, source_target_pairs={{0,4},{4,0},{8,12},{12,8},{16,20},{20,16},{24,28},{28,24},{1,5},{5... | collective-permute-start | bytes 786440 | tf_op jit(solution)/shard_map/ppermute | solution.py:24
  47.5 24.1 %collective-permute-start.5 = (f32[64,1024]{1,0:T(8,128)}, f32[64,1024]{1,0:T(8,128)}, u32[]{:S(2)}, u32[]{:S(2)}) collective-permute-start(f32[64,1024]{1,0:T(8,128)} %collective-permute-done.1), channel_id=1, source_target_pairs={{0,4},{4,0},{8,12},{12,8},{16,20},{20,16},{24,28},{28,24},{1,5},{5... | collective-permute-start | bytes 786440 | tf_op jit(solution)/shard_map/ppermute | solution.py:24
  51.3 28.3 %collective-permute-start.6 = (f32[64,1024]{1,0:T(8,128)}, f32[64,1024]{1,0:T(8,128)}, u32[]{:S(2)}, u32[]{:S(2)}) collective-permute-start(f32[64,1024]{1,0:T(8,128)} %collective-permute-done.2), channel_id=1, source_target_pairs={{0,4},{4,0},{8,12},{12,8},{16,20},{20,16},{24,28},{28,24},{1,5},{5... | collective-permute-start | bytes 786440 | tf_op jit(solution)/shard_map/ppermute | solution.py:24
  52.8 3.9 %collective-permute-start.10 = (f32[8192]{0:T(1024)S(1)}, f32[8192]{0:T(1024)S(1)}, u32[]{:S(2)}, u32[]{:S(2)}) collective-permute-start(f32[8192]{0:T(1024)S(1)} %add_dynamic-update-slice_fusion), channel_id=1, source_target_pairs={{0,8},{4,12},{8,0},{12,4},{16,24},{20,28},{24,16},{28,20},{1,9},{5... | collective-permute-start | bytes 98312 | tf_op jit(solution)/shard_map/ppermute | solution.py:24
  56.7 5.6 %collective-permute-start.11 = (f32[8192]{0:T(1024)S(1)}, f32[8192]{0:T(1024)S(1)}, u32[]{:S(2)}, u32[]{:S(2)}) collective-permute-start(f32[8192]{0:T(1024)S(1)} %add.139), channel_id=1, source_target_pairs={{0,16},{4,20},{8,24},{12,28},{16,0},{20,4},{24,8},{28,12},{1,17},{... | collective-permute-start | bytes 98312 | tf_op jit(solution)/shard_map/ppermute | solution.py:24
  116.5 4.0 %collective-permute-start.13 = (f32[1,8192]{1,0:T(1,128)S(1)}, f32[1,8192]{1,0:T(1,128)S(1)}, u32[]{:S(2)}, u32[]{:S(2)}) collective-permute-start(f32[1,8192]{1,0:T(1,128)S(1)} %add.141), channel_id=1, source_target_pairs={{0,2},{1,3},{2,0},{3,1},{4,6},{5,7},{6,4},{7,5},{8,10},{9,11},{10,... | collective-permute-start | bytes 98312 | tf_op jit(solution)/shard_map/ppermute | solution.py:24
  120.6 4.0 %collective-permute-start.14 = (f32[1,8192]{1,0:T(1,128)S(1)}, f32[1,8192]{1,0:T(1,128)S(1)}, u32[]{:S(2)}, u32[]{:S(2)}) collective-permute-start(f32[1,8192]{1,0:T(1,128)S(1)} %add.142), channel_id=1, source_target_pairs={{0,4},{4,0},{8,12},{12,8},{16,20},{20,16},{24,28},{28,24},{1,5},{5... | collective-permute-start | bytes 98312 | tf_op jit(solution)/shard_map/ppermute | solution.py:24
  124.6 4.0 %collective-permute-start.15 = (f32[1,8192]{1,0:T(1,128)S(1)}, f32[1,8192]{1,0:T(1,128)S(1)}, u32[]{:S(2)}, u32[]{:S(2)}) collective-permute-start(f32[1,8192]{1,0:T(1,128)S(1)} %add.143), channel_id=1, source_target_pairs={{0,8},{4,12},{8,0},{12,4},{16,24},{20,28},{24,16},{28,20},{1,9},{5... | collective-permute-start | bytes 98312 | tf_op jit(solution)/shard_map/ppermute | solution.py:24
  128.6 4.9 %collective-permute-start.16 = (f32[1,8192]{1,0:T(1,128)S(1)}, f32[1,8192]{1,0:T(1,128)S(1)}, u32[]{:S(2)}, u32[]{:S(2)}) collective-permute-start(f32[1,8192]{1,0:T(1,128)S(1)} %add.144), channel_id=1, source_target_pairs={{0,16},{4,20},{8,24},{12,28},{16,0},{20,4},{24,8},{28,12},{1,17},{... | collective-permute-start | bytes 98312 | tf_op jit(solution)/shard_map/ppermute | solution.py:24
  161.1 4.0 %collective-permute-start.18 = (f32[1,8192]{1,0:T(1,128)S(1)}, f32[1,8192]{1,0:T(1,128)S(1)}, u32[]{:S(2)}, u32[]{:S(2)}) collective-permute-start(f32[1,8192]{1,0:T(1,128)S(1)} %add.146), channel_id=1, source_target_pairs={{0,2},{1,3},{2,0},{3,1},{4,6},{5,7},{6,4},{7,5},{8,10},{9,11},{10,... | collective-permute-start | bytes 98312 | tf_op jit(solution)/shard_map/ppermute | solution.py:24
  165.1 4.0 %collective-permute-start.19 = (f32[1,8192]{1,0:T(1,128)S(1)}, f32[1,8192]{1,0:T(1,128)S(1)}, u32[]{:S(2)}, u32[]{:S(2)}) collective-permute-start(f32[1,8192]{1,0:T(1,128)S(1)} %add.147), channel_id=1, source_target_pairs={{0,4},{4,0},{8,12},{12,8},{16,20},{20,16},{24,28},{28,24},{1,5},{5... | collective-permute-start | bytes 98312 | tf_op jit(solution)/shard_map/ppermute | solution.py:24
  169.1 4.0 %collective-permute-start.20 = (f32[1,8192]{1,0:T(1,128)S(1)}, f32[1,8192]{1,0:T(1,128)S(1)}, u32[]{:S(2)}, u32[]{:S(2)}) collective-permute-start(f32[1,8192]{1,0:T(1,128)S(1)} %add.148), channel_id=1, source_target_pairs={{0,8},{4,12},{8,0},{12,4},{16,24},{20,28},{24,16},{28,20},{1,9},{5... | collective-permute-start | bytes 98312 | tf_op jit(solution)/shard_map/ppermute | solution.py:24
  173.2 4.9 %collective-permute-start.21 = (f32[1,8192]{1,0:T(1,128)S(1)}, f32[1,8192]{1,0:T(1,128)S(1)}, u32[]{:S(2)}, u32[]{:S(2)}) collective-permute-start(f32[1,8192]{1,0:T(1,128)S(1)} %add.149), channel_id=1, source_target_pairs={{0,16},{4,20},{8,24},{12,28},{16,0},{20,4},{24,8},{28,12},{1,17},{... | collective-permute-start | bytes 98312 | tf_op jit(solution)/shard_map/ppermute | solution.py:24
  205.7 4.0 %collective-permute-start.23 = (f32[1,8192]{1,0:T(1,128)S(1)}, f32[1,8192]{1,0:T(1,128)S(1)}, u32[]{:S(2)}, u32[]{:S(2)}) collective-permute-start(f32[1,8192]{1,0:T(1,128)S(1)} %add.153), channel_id=1, source_target_pairs={{0,2},{1,3},{2,0},{3,1},{4,6},{5,7},{6,4},{7,5},{8,10},{9,11},{10,... | collective-permute-start | bytes 98312 | tf_op jit(solution)/shard_map/ppermute | solution.py:24
  209.8 4.3 %collective-permute-start.24 = (f32[2,8192]{1,0:T(2,128)S(1)}, f32[2,8192]{1,0:T(2,128)S(1)}, u32[]{:S(2)}, u32[]{:S(2)}) collective-permute-start(f32[2,8192]{1,0:T(2,128)S(1)} %pad_maximum_fusion.3), channel_id=1, source_target_pairs={{0,4},{4,0},{8,12},{12,8},{16,20},{20,16},{24,28},{28,24},{1,5},{5... | collective-permute-start | bytes 196616 | tf_op jit(solution)/shard_map/ppermute | solution.py:24
  214.2 4.4 %collective-permute-start.25 = (f32[2,8192]{1,0:T(2,128)S(1)}, f32[2,8192]{1,0:T(2,128)S(1)}, u32[]{:S(2)}, u32[]{:S(2)}) collective-permute-start(f32[2,8192]{1,0:T(2,128)S(1)} %fusion.6), channel_id=1, source_target_pairs={{0,8},{4,12},{8,0},{12,4},{16,24},{20,28},{24,16},{28,20},{1,9},{5... | collective-permute-start | bytes 196616 | tf_op jit(solution)/shard_map/ppermute | solution.py:24
  218.7 5.2 %collective-permute-start.26 = (f32[2,8192]{1,0:T(2,128)S(1)}, f32[2,8192]{1,0:T(2,128)S(1)}, u32[]{:S(2)}, u32[]{:S(2)}) collective-permute-start(f32[2,8192]{1,0:T(2,128)S(1)} %fusion.12), channel_id=1, source_target_pairs={{0,16},{4,20},{8,24},{12,28},{16,0},{20,4},{24,8},{28,12},{1,17},{... | collective-permute-start | bytes 196616 | tf_op jit(solution)/shard_map/ppermute | solution.py:24
  254.9 32.1 %collective-permute-start.29 = (f32[512,128]{1,0:T(8,128)}, f32[512,128]{1,0:T(8,128)}, u32[]{:S(2)}, u32[]{:S(2)}) collective-permute-start(f32[512,128]{1,0:T(8,128)} %centroid_update.1), channel_id=1, source_target_pairs={{0,16},{4,20},{8,24},{12,28},{16,0},{20,4},{24,8},{28,12},{1,17},{... | collective-permute-start | bytes 786440 | tf_op jit(solution)/shard_map/ppermute | solution.py:24
  256.7 32.6 %collective-permute-start.30 = (f32[512,128]{1,0:T(8,128)}, f32[512,128]{1,0:T(8,128)}, u32[]{:S(2)}, u32[]{:S(2)}) collective-permute-start(f32[512,128]{1,0:T(8,128)} %centroid_update.1), channel_id=1, source_target_pairs={{0,8},{4,12},{8,0},{12,4},{16,24},{20,28},{24,16},{28,20},{1,9},{5... | collective-permute-start | bytes 786440 | tf_op jit(solution)/shard_map/ppermute | solution.py:24
  287.1 9.0 %collective-permute-start.31 = (f32[512,128]{1,0:T(8,128)}, f32[512,128]{1,0:T(8,128)}, u32[]{:S(2)}, u32[]{:S(2)}) collective-permute-start(f32[512,128]{1,0:T(8,128)} %collective-permute-done.29), channel_id=1, source_target_pairs={{0,8},{4,12},{8,0},{12,4},{16,24},{20,28},{24,16},{28,20},{1,9},{5... | collective-permute-start | bytes 786440 | tf_op jit(solution)/shard_map/ppermute | solution.py:24
  287.1 15.6 %collective-permute-start.32 = (f32[512,128]{1,0:T(8,128)}, f32[512,128]{1,0:T(8,128)}, u32[]{:S(2)}, u32[]{:S(2)}) collective-permute-start(f32[512,128]{1,0:T(8,128)} %centroid_update.1), channel_id=1, source_target_pairs={{0,4},{4,0},{8,12},{12,8},{16,20},{20,16},{24,28},{28,24},{1,5},{5... | collective-permute-start | bytes 786440 | tf_op jit(solution)/shard_map/ppermute | solution.py:24
  287.7 23.5 %collective-permute-start.33 = (f32[512,128]{1,0:T(8,128)}, f32[512,128]{1,0:T(8,128)}, u32[]{:S(2)}, u32[]{:S(2)}) collective-permute-start(f32[512,128]{1,0:T(8,128)} %collective-permute-done.29), channel_id=1, source_target_pairs={{0,4},{4,0},{8,12},{12,8},{16,20},{20,16},{24,28},{28,24},{1,5},{5... | collective-permute-start | bytes 786440 | tf_op jit(solution)/shard_map/ppermute | solution.py:24
  289.2 24.1 %collective-permute-start.34 = (f32[512,128]{1,0:T(8,128)}, f32[512,128]{1,0:T(8,128)}, u32[]{:S(2)}, u32[]{:S(2)}) collective-permute-start(f32[512,128]{1,0:T(8,128)} %collective-permute-done.30), channel_id=1, source_target_pairs={{0,4},{4,0},{8,12},{12,8},{16,20},{20,16},{24,28},{28,24},{1,5},{5... | collective-permute-start | bytes 786440 | tf_op jit(solution)/shard_map/ppermute | solution.py:24
  290.9 24.5 %collective-permute-start.28 = (f32[1024,64]{1,0:T(8,128)S(1)}, f32[1024,64]{1,0:T(8,128)}, u32[]{:S(2)}, u32[]{:S(2)}) collective-permute-start(f32[1024,64]{1,0:T(8,128)S(1)} %add.158), channel_id=1, source_target_pairs={{0,2},{1,3},{2,0},{3,1},{4,6},{5,7},{6,4},{7,5},{8,10},{9,11},{10,... | collective-permute-start | bytes 786440 | tf_op jit(solution)/shard_map/ppermute | solution.py:24
  296.1 32.8 %collective-permute-start.35 = (f32[512,128]{1,0:T(8,128)}, f32[512,128]{1,0:T(8,128)}, u32[]{:S(2)}, u32[]{:S(2)}) collective-permute-start(f32[512,128]{1,0:T(8,128)} %collective-permute-done.31), channel_id=1, source_target_pairs={{0,4},{4,0},{8,12},{12,8},{16,20},{20,16},{24,28},{28,24},{1,5},{5... | collective-permute-start | bytes 786440 | tf_op jit(solution)/shard_map/ppermute | solution.py:24
  (8 other events, 59.0 us)

commit v2 on v0

v2 whole, which is shorter than its diff:
```python
import functools
import math

import jax
import jax.numpy as jnp
from jax import lax
from jax.experimental import pallas as pl
from jax.experimental.pallas import tpu as pltpu
from jax.sharding import PartitionSpec as P

ITERS = 3

score_scale = 20.0
step_rate = 0.2
epsilon = 1e-06

CHUNK = 2048
LANES = 128
POTS = 16


def swap(value, axis, bit):
    size = lax.axis_size(axis)
    return lax.ppermute(value, axis, [(k, k ^ bit) for k in range(size)])


def bits_of(axis):
    size = lax.axis_size(axis)
    return [1 << k for k in range(size.bit_length() - 1)]


def add_over(value, axis):
    for bit in bits_of(axis):
        value = value + swap(value, axis, bit)
    return value


def gather_blocks(value, axis):
    held = {0: value}
    for bit in reversed(bits_of(axis)):
        held.update({key | bit: swap(block, axis, bit) for key, block in list(held.items())})
    return held


def thirds(value):
    high = value.astype(jnp.bfloat16).astype(jnp.float32)
    middle = (value - high).astype(jnp.bfloat16).astype(jnp.float32)
    return high, middle, value - high - middle


def pots(row, width, at):
    sub = lax.broadcasted_iota(jnp.int32, (POTS, width), 0)
    high, middle, low = thirds(row)
    out = jnp.where(sub < 6, 1.0, 0.0)
    out = jnp.where(sub == at, high, out)
    out = jnp.where(sub == at + 1, middle, out)
    out = jnp.where(sub == at + 2, low, out)
    return out.astype(jnp.bfloat16)


def left_pots(row, width):
    return jnp.transpose(pots(row, width, 3).astype(jnp.float32)).astype(jnp.bfloat16)


def row_of(column):
    wide = jnp.broadcast_to(column, (column.shape[0], LANES))
    return jnp.transpose(wide)[0:8, :]


def slices(value):
    return [value[:, k * LANES : (k + 1) * LANES] for k in range(value.shape[1] // LANES)]


def folded(values, op):
    values = list(values)
    while len(values) > 1:
        values = [op(*values[k : k + 2]) if k + 1 < len(values) else values[k] for k in range(0, len(values), 2)]
    return values[0]


def own_pieces(item_ref, key, width):
    return pl.ds(pl.multiple_of((item_ref[0] ^ key) * width, width), width)


def table_kernel(item_ref, *refs, keys):
    pieces, (right_ref, other_ref) = refs[: len(keys)], refs[len(keys) :]
    dim = other_ref.shape[0]
    for key, piece_ref in zip(keys, pieces):
        at = own_pieces(item_ref, key, piece_ref.shape[1])
        piece = piece_ref[...]
        scaled = score_scale * piece
        high = scaled.astype(jnp.bfloat16)
        right_ref[0:dim, at] = high
        right_ref[dim : 2 * dim, at] = (scaled - high.astype(jnp.float32)).astype(jnp.bfloat16)
        other_ref[:, at] = piece.astype(jnp.bfloat16)


def spread_kernel(item_ref, *refs, keys, half):
    pieces, out_ref = refs[: len(keys)], refs[len(keys)]
    for key, piece_ref in zip(keys, pieces):
        count, twice = piece_ref.shape
        for part in range(count // half):
            piece = piece_ref[part * half : (part + 1) * half, :]
            for side in range(2):
                start = (item_ref[0] ^ key) * (2 * count) + (2 * part + side) * half
                at = pl.ds(pl.multiple_of(start, half), half)
                out_ref[at, :] = piece[:, side * (twice // 2) : (side + 1) * (twice // 2)]


def chunk_of(width):
    return min(width, CHUNK)


def chunks(width, run):
    size = chunk_of(width)

    @pl.loop(0, width // size)
    def _(step):
        run(pl.ds(pl.multiple_of(step * size, size), size))


def cases(count, run):
    step = pl.program_id(0)

    @pl.when(step == 0)
    def _():
        run(True, False)

    if count > 1:

        @pl.when((step > 0) & (step < count))
        def _():
            run(True, True)

    @pl.when(step == count)
    def _():
        run(False, True)


def lse_kernel(l_ref, w_ref, out_ref, y_ref, part_ref, sum_ref, wide_ref, *, repeat, count):
    block, width = y_ref.shape

    def run(new, old):
        if old:
            highest = jnp.max(part_ref[...], axis=1, keepdims=True)
            wide_ref[...] = jnp.broadcast_to(highest, (block, LANES))
            sum_ref[...] = jnp.zeros(sum_ref.shape, jnp.float32)
        if new:
            part_ref[...] = jnp.full(part_ref.shape, -jnp.inf, jnp.float32)

        def chunk(at):
            if old:
                terms = [jnp.exp(piece - wide_ref[...]) for piece in slices(y_ref[:, at])]
                sum_ref[...] += folded(terms, jnp.add)
            if new:
                right = jnp.concatenate([w_ref[:, at]] * repeat, axis=0)
                y = jnp.dot(l_ref[...], right, preferred_element_type=jnp.float32)
                y_ref[:, at] = y
                part_ref[...] = jnp.maximum(part_ref[...], folded(slices(y), jnp.maximum))

        chunks(width, chunk)
        if old:
            summed = jnp.sum(sum_ref[...], axis=1, keepdims=True)
            lane = lax.broadcasted_iota(jnp.int32, (block, LANES), 1)
            both = jnp.where(lane == 0, wide_ref[...], summed)
            out_ref[...] = jnp.transpose(both)[0:8, :]

    cases(count, run)


def sink_kernel(
    l_ref, p_ref, w_ref, q_ref, *rest, first, rows_total, buckets_total, count
):
    if not first:
        one_ref, two_ref, *rest = rest
    sums_ref, pot_ref, row_ref, y_ref, part_ref, high_ref, wide_ref, wpot_ref, acc_ref = rest
    block, width = y_ref.shape

    def run(new, old):
        if new and not old:
            acc_ref[...] = jnp.zeros(acc_ref.shape, jnp.float32)

            def prepare(at):
                row = q_ref[0:1, at]
                if not first:
                    row = row - jnp.log((one_ref[0:1, at] + two_ref[0:1, at]) * float(rows_total))
                row_ref[0:1, at] = row
                wpot_ref[:, at] = pots(row, chunk_of(width), 0)

            chunks(width, prepare)
        if new:
            was = jnp.zeros((1, block), jnp.float32) if first else p_ref[0:1, :]
            left = jnp.concatenate([l_ref[...], left_pots(was, block)], axis=1)
            part_ref[...] = jnp.full(part_ref.shape, -jnp.inf if first else 0.0, jnp.float32)

        def chunk(at):
            if old:
                sums = [
                    jnp.sum((piece * wide_ref[...]).reshape(block // 8, 8, LANES), axis=0)
                    for piece in slices(y_ref[:, at])
                ]
                acc_ref[:, at] += jnp.concatenate(sums, axis=1)
            if new:
                right = jnp.concatenate([w_ref[:, at], wpot_ref[:, at]], axis=0)
                y = jnp.dot(left, right, preferred_element_type=jnp.float32)
                if first:
                    y_ref[:, at] = y
                    part_ref[...] = jnp.maximum(part_ref[...], folded(slices(y), jnp.maximum))
                else:
                    y = jnp.exp(y)
                    y_ref[:, at] = y
                    part_ref[...] += folded(slices(y), jnp.add)

        chunks(width, chunk)
        if new and first:
            highest = jnp.max(part_ref[...], axis=1, keepdims=True)
            high_ref[...] = jnp.broadcast_to(highest, (block, LANES))
            part_ref[...] = jnp.zeros(part_ref.shape, jnp.float32)

            def again(at):
                terms = [jnp.exp(piece - high_ref[...]) for piece in slices(y_ref[:, at])]
                y_ref[:, at] = jnp.concatenate(terms, axis=1)
                part_ref[...] += folded(terms, jnp.add)

            chunks(width, again)
        if new:
            summed = jnp.sum(part_ref[...], axis=1, keepdims=True) * float(buckets_total)
            wide_ref[...] = jnp.broadcast_to(1.0 / summed, (block, LANES))
            summed = row_of(summed)
            if first:
                pot_ref[...] = -(row_of(high_ref[...]) + jnp.log(summed))
            else:
                pot_ref[...] = was - jnp.log(summed)
        if not new:
            sums_ref[...] = jnp.sum(acc_ref[...], axis=0, keepdims=True)

    cases(count, run)


def final_kernel(l_ref, p_ref, u_ref, w_ref, q_ref, v_ref, r_ref, *rest, repeat, update):
    if update:
        own_ref, out_ref, wide_ref, wpot_ref, acc_ref = rest
    else:
        out_ref, wide_ref, wpot_ref, acc_ref = rest
    block = l_ref.shape[0]
    width = w_ref.shape[1]

    @pl.when(pl.program_id(0) == 0)
    def _():
        def prepare(at):
            wpot_ref[:, at] = pots(q_ref[0:1, at], chunk_of(width), 0)

        chunks(width, prepare)

    left = jnp.concatenate([l_ref[...], left_pots(p_ref[0:1, :], block)], axis=1)
    wide_ref[...] = jnp.transpose(jnp.broadcast_to(u_ref[0:1, :], (LANES, block)))
    acc_ref[...] = jnp.zeros(acc_ref.shape, jnp.float32)

    def chunk(at):
        right = jnp.concatenate([w_ref[:, at]] * repeat + [wpot_ref[:, at]], axis=0)
        y = jnp.dot(left, right, preferred_element_type=jnp.float32)
        delta = jnp.concatenate(
            [
                (jnp.exp(piece) * (wide_ref[...] * factor - 1.0)).astype(jnp.bfloat16)
                for piece, factor in zip(slices(y), slices(v_ref[0:1, at]))
            ],
            axis=1,
        )
        acc_ref[...] += lax.dot_general(
            delta, r_ref[:, at], (((1,), (1,)), ((), ())), preferred_element_type=jnp.float32
        )

    chunks(width, chunk)
    gradient = score_scale * acc_ref[...]
    if not update:
        out_ref[...] = gradient
    else:
        moved = own_ref[...].astype(jnp.float32) - step_rate * gradient
        scaled = moved * lax.rsqrt(jnp.mean(moved * moved, axis=1, keepdims=True) + epsilon)
        half = block // 2
        out_ref[...] = jnp.concatenate([scaled[:half], scaled[half:]], axis=1)


VMEM = functools.partial(pltpu.VMEM)


def block_of(count, width):
    return min(count, 256 if width <= 16384 else 128)


def params():
    return pltpu.CompilerParams(dimension_semantics=("arbitrary",), vmem_limit_bytes=60 * 1024 * 1024)


def cost(count, width, passes):
    return pl.CostEstimate(
        flops=2 * count * width * 256 * passes, transcendentals=count * width, bytes_accessed=width * 256 * 2
    )


def full(array):
    return pl.BlockSpec(array.shape, lambda k: (0, 0))


def lse(left, right, repeat):
    rows, width = left.shape[0], right.shape[1]
    block = block_of(rows, width)
    count = rows // block
    return pl.pallas_call(
        functools.partial(lse_kernel, repeat=repeat, count=count),
        grid=(count + 1,),
        in_specs=[pl.BlockSpec((block, LANES), lambda k: (jnp.minimum(k, count - 1), 0)), full(right)],
        out_specs=pl.BlockSpec((8, block), lambda k: (0, jnp.maximum(k - 1, 0))),
        out_shape=jax.ShapeDtypeStruct((8, rows), jnp.float32),
        scratch_shapes=[VMEM((block, width), jnp.float32)] + [VMEM((block, LANES), jnp.float32)] * 3,
        compiler_params=params(),
        cost_estimate=cost(rows, width, 1),
        name="row_lse",
    )(left, right)


def sink(left, p_rows, right, row, sums, rows_total, buckets_total):
    rows, width = left.shape[0], right.shape[1]
    block = block_of(rows, width)
    count = rows // block
    first = sums is None
    line = pl.BlockSpec((1, width), lambda k: (0, 0))
    lines = [row] if first else [row, *sums]
    pot_spec = pl.BlockSpec((8, block), lambda k: (0, jnp.minimum(k, count - 1)))
    return pl.pallas_call(
        functools.partial(
            sink_kernel, first=first, rows_total=rows_total, buckets_total=buckets_total, count=count
        ),
        grid=(count + 1,),
        in_specs=[
            pl.BlockSpec((block, LANES), lambda k: (jnp.minimum(k, count - 1), 0)),
            pot_spec,
            full(right),
        ]
        + [line] * len(lines),
        out_specs=[line, pot_spec, line],
        out_shape=[
            jax.ShapeDtypeStruct((1, width), jnp.float32),
            jax.ShapeDtypeStruct((8, rows), jnp.float32),
            jax.ShapeDtypeStruct((1, width), jnp.float32),
        ],
        scratch_shapes=[VMEM((block, width), jnp.float32)]
        + [VMEM((block, LANES), jnp.float32)] * 3
        + [VMEM((POTS, width), jnp.bfloat16), VMEM((8, width), jnp.float32)],
        compiler_params=params(),
        cost_estimate=cost(rows, width, 1),
        name="sinkhorn_first" if first else "sinkhorn_next",
    )(left, p_rows, right, *lines)


def final(left, p_row, u_row, right, q_row, v_row, other, repeat, own=None):
    rows, width = left.shape[0], right.shape[1]
    block = block_of(rows, width)
    update = own is not None
    dim = other.shape[0]
    line = pl.BlockSpec((1, width), lambda k: (0, 0))
    part = pl.BlockSpec((1, block), lambda k: (0, k))
    in_specs = [pl.BlockSpec((block, LANES), lambda k: (k, 0)), part, part, full(right), line, line, full(other)]
    args = [left, p_row, u_row, right, q_row, v_row, other]
    if update:
        in_specs.append(pl.BlockSpec((block, dim), lambda k: (k, 0)))
        args.append(own)
        out_spec = pl.BlockSpec((block // 2, 2 * dim), lambda k: (k, 0))
        out_shape = jax.ShapeDtypeStruct((rows // 2, 2 * dim), jnp.float32)
    else:
        out_spec = pl.BlockSpec((block, dim), lambda k: (k, 0))
        out_shape = jax.ShapeDtypeStruct((rows, dim), jnp.float32)
    out = pl.pallas_call(
        functools.partial(final_kernel, repeat=repeat, update=update),
        grid=(rows // block,),
        in_specs=in_specs,
        out_specs=out_spec,
        out_shape=out_shape,
        scratch_shapes=[
            VMEM((block, LANES), jnp.float32),
            VMEM((POTS, width), jnp.bfloat16),
            VMEM((block, dim), jnp.float32),
        ],
        compiler_params=params(),
        cost_estimate=cost(rows, width, 2),
        name="centroid_update" if update else "code_gradient",
    )(*args)
    return out, block


def by_item(kernel, item, blocks, out_shape, name, **settings):
    keys = sorted(blocks)
    several = isinstance(out_shape, list)
    whole = lambda shape: pl.BlockSpec(shape, lambda k, item: (0, 0))
    shapes = out_shape if several else [out_shape]
    specs = [whole(one.shape) for one in shapes]
    return pl.pallas_call(
        functools.partial(kernel, keys=keys, **settings),
        grid_spec=pltpu.PrefetchScalarGridSpec(
            num_scalar_prefetch=1,
            grid=(1,),
            in_specs=[whole(blocks[key].shape) for key in keys],
            out_specs=specs if several else specs[0],
        ),
        out_shape=out_shape,
        compiler_params=params(),
        cost_estimate=pl.CostEstimate(flops=0, transcendentals=0, bytes_accessed=6 << 20),
        name=name,
    )(item.reshape(1).astype(jnp.int32), *[blocks[key] for key in keys])


def halves(scaled):
    high = lax.reduce_precision(scaled, 8, 7)
    return high.astype(jnp.bfloat16), (scaled - high).astype(jnp.bfloat16)


def body(code_rows, centroids):
    items = lax.axis_size("item")
    item = lax.axis_index("item")
    rows_own, dim = code_rows.shape
    rows_total = rows_own * items
    buckets_own = centroids.shape[0]
    buckets_total = buckets_own * lax.axis_size("bucket")
    share = buckets_own // items
    log_rows = math.log(rows_total)

    codes_f32 = code_rows.astype(jnp.float32)
    row_left = jnp.concatenate(halves(score_scale * codes_f32), axis=1)
    centroids_t = centroids.T
    stats = lse(row_left, centroids_t, 2)[0:2]

    right, other = by_item(
        table_kernel,
        item,
        gather_blocks(codes_f32.T, "item"),
        [
            jax.ShapeDtypeStruct((2 * dim, rows_total), jnp.bfloat16),
            jax.ShapeDtypeStruct((dim, rows_total), jnp.bfloat16),
        ],
        "table",
    )
    own = lax.dynamic_slice_in_dim(centroids, item * share, share, axis=0)
    own_left = jnp.concatenate([own, own], axis=1)

    for bit in bits_of("bucket"):
        received = swap(stats, "bucket", bit)
        highest = jnp.maximum(stats[0], received[0])
        summed = stats[1] * jnp.exp(stats[0] - highest) + received[1] * jnp.exp(received[0] - highest)
        stats = jnp.stack([highest, summed])
    first_own = -log_rows - (stats[0:1] + jnp.log(stats[1:2]))
    row_first = lax.dynamic_update_slice(jnp.zeros((1, rows_total), jnp.float32), first_own, (0, item * rows_own))
    row = row_first = add_over(row_first, "item")

    cols = jnp.zeros((8, share), jnp.float32)
    sums = None
    for iteration in range(ITERS):
        total, cols, row = sink(own_left, cols, right, row, sums, rows_total, buckets_total)
        total = add_over(total, "bucket")
        if iteration < ITERS - 1:
            for bit in bits_of("item")[:-1]:
                total = total + swap(total, "item", bit)
            sums = (total, swap(total, "item", bits_of("item")[-1]))

    col_own = cols[0:1]
    col = lax.dynamic_update_slice(jnp.zeros((1, buckets_own), jnp.float32), col_own, (0, item * share))
    if buckets_own == rows_total:
        both = add_over(jnp.concatenate([total, col], axis=0), "item")
        total, col = both[0:1], both[1:2]
    else:
        total, col = add_over(total, "item"), add_over(col, "item")
    row_scale = total * float(rows_total) * jnp.exp(row_first - row)
    row = row + log_rows

    update, block = final(own_left, col_own, jnp.exp(-col_own), right, row, row_scale, other, 1, own)

    def mine(values):
        return lax.dynamic_slice_in_dim(values, item * rows_own, rows_own, axis=1)

    grad, _ = final(row_left, mine(row), mine(row_scale), centroids_t, col, jnp.exp(-col), centroids_t, 2)

    new_centroids = by_item(
        spread_kernel,
        item,
        gather_blocks(update, "item"),
        jax.ShapeDtypeStruct((buckets_own, dim), jnp.float32),
        "spread",
        half=block // 2,
    )
    grad_codes = add_over(grad, "bucket")
    return (grad_codes, new_centroids)


def solution(mesh):
    return jax.shard_map(
        body,
        mesh=mesh,
        in_specs=(P("item", None), P("bucket", None)),
        out_specs=(P("item", None), P("bucket", None)),
        check_vma=False,
    )
```

time: 588 us -> 243 us (0.41)
  blocking collectives: 223 us -> 0 us
  other arithmetic: 186 us -> 10.4 us
  Pallas kernels: 0 us -> 93.3 us
  starting transfers between devices: 0.3 us -> 44 us
  waiting for transfers between devices: 121 us -> 81.8 us
  matrix products: 30.3 us -> 0 us
  between operations: 14.4 us -> 0.94 us
    all_gather x13 -> x0, blocking collectives: 223 us -> none  [joined(): pieces = jax.tree.map(lambda part: lax.all_gather(part, axis), value)]
    psum x2 -> x0, waiting for transfers between devices: 121 us -> none  [the longest x1 91.4 us: body(): gradient = lax.psum(local_grad, 'item')]
    reduce_sum x8 -> x0, other arithmetic: 101 us -> none  [the longest x3 41.9 us: reduce_cols(): summed = jnp.sum(jnp.exp(values - highest[None, :]), axis=0)]
    pallas_call x0 -> x8, Pallas kernels: none -> 93.3 us  [the longest x3 41.6 us: sink(): pl.pallas_call(functools.partial(sink_kernel, first=first, rows_total=row...]
    ppermute x0 -> x36, waiting for transfers between devices: none -> 81.8 us  [swap(): return lax.ppermute(value, axis, [(k, k ^ bit) for k in range(size)])]
    reduce_max x5 -> x0, other arithmetic: 61.7 us -> none  [the longest x3 37.4 us: reduce_cols(): highest = jnp.max(values, axis=0)]
    ppermute x0 -> x36, starting transfers between devices: none -> 44 us  [swap(): return lax.ppermute(value, axis, [(k, k ^ bit) for k in range(size)])]
    dot_general x3 -> x0, matrix products: 30.3 us -> none  [the longest x1 14.3 us: scores_of(): lax.dot_general(code_rows, centroids, (((1,), (1,)), ((), ())), preferred...]
  transfers between devices with their start and end apart: 2 -> 36, of which waited for: 2 -> 27; matrix products, arithmetic and copies ran while one was open for 3% -> 3% of each run, Pallas kernels for 0% -> 6%
where the time goes in v2:
time: 243 us; the launch traced here: 242 us
  Pallas kernels  93.3 us (38%)
  waiting for transfers between devices  81.8 us (34%)
  starting transfers between devices  44 us (18%)
  local copies, waits for them, and re-layouts  11.5 us (5%)
  other arithmetic  10.4 us (4%)
    ppermute x36, waiting for transfers between devices, swap(): return lax.ppermute(value, axis, [(k, k ^ bit) for k in range(size)])  81.8 us
    ppermute x36, starting transfers between devices, swap(): return lax.ppermute(value, axis, [(k, k ^ bit) for k in range(size)])  44 us
    pallas_call x3, Pallas kernels, sink(): pl.pallas_call(functools.partial(sink_kernel, first=first, rows_total=row...  41.6 us
    pallas_call x2, Pallas kernels, final(): pl.pallas_call(functools.partial(final_kernel, repeat=repeat, update=upda...  32.7 us
    pallas_call x1, Pallas kernels, lse(): pl.pallas_call(functools.partial(lse_kernel, repeat=repeat, count=count),...  11.2 us
    pallas_call x2, Pallas kernels, by_item(): pl.pallas_call(functools.partial(kernel, keys=keys, **settings), grid_spe...  7.87 us
    unnamed x53, local copies, waits for them, and re-layouts  7.48 us
  transfers between devices with their start and end apart: 36, of which 27 were waited for; matrix products, arithmetic and copies ran while one was open for 3% of the time, Pallas kernels for 6%

profile of v2, /device:TPU:0, one launch (start us, length us, event | category | flops | bytes accessed | tf_op | source)
XLA Modules:
  0.0 241.9 jit_solution(11115075749580908997)
XLA Ops:
  2.6 11.2 %row_lse.1 = f32[8,1024]{1,0:T(8,128)} custom-call(bf16[1024,128]{1,0:T(8,128)(2,1)} %pad_maximum_fusion.l_ref, bf16[64,8192]{1,0:T(8,128)(2,1)} %bitcast.4), custom_call_target="tpu_custom_call" | custom-call | flops 4294967296 | bytes 4194304 | tf_op jit(solution)/shard_map/row_lse/pallas_call | solution.py:309
  15.1 3.7 %collective-permute-start.3 = (f32[64,1024]{1,0:T(8,128)S(1)}, f32[64,1024]{1,0:T(8,128)S(1)}, u32[]{:S(2)}, u32[]{:S(2)}) collective-permute-start(f32[64,1024]{1,0:T(8,128)S(1)} %convert_bitcast_fusion.refs_0_), channel_id=1, source_target_pairs={{0,16},{4,20},{8,24},{12,28},{16,0},{20,4},{24,8},{28,12},{1,17},{... | collective-permute-start | bytes 786440 | tf_op jit(solution)/shard_map/ppermute | solution.py:24
  22.8 8.7 %collective-permute-done.3.refs_4_ = f32[64,1024]{1,0:T(8,128)S(1)} collective-permute-done((f32[64,1024]{1,0:T(8,128)S(1)}, f32[64,1024]{1,0:T(8,128)S(1)}, u32[]{:S(2)}, u32[]{:S(2)}) %collective-permute-start.3) | collective-permute-done | bytes 262176 | tf_op jit(solution)/shard_map/ppermute | solution.py:24
  36.4 3.2 %collective-permute-done.5.refs_6_ = f32[64,1024]{1,0:T(8,128)S(1)} collective-permute-done((f32[64,1024]{1,0:T(8,128)S(1)}, f32[64,1024]{1,0:T(8,128)S(1)}, u32[]{:S(2)}, u32[]{:S(2)}) %collective-permute-start.5) | collective-permute-done | bytes 262176 | tf_op jit(solution)/shard_map/ppermute | solution.py:24
  45.0 2.6 %collective-permute-start.11 = (f32[1,8192]{1,0:T(1,128)S(1)}, f32[1,8192]{1,0:T(1,128)S(1)}, u32[]{:S(2)}, u32[]{:S(2)}) collective-permute-start(f32[1,8192]{1,0:T(1,128)S(1)} %add.87), channel_id=1, source_target_pairs={{0,16},{4,20},{8,24},{12,28},{16,0},{20,4},{24,8},{28,12},{1,17},{... | collective-permute-start | bytes 98312 | tf_op jit(solution)/shard_map/ppermute | solution.py:24
  50.6 3.6 %collective-permute-done.2.refs_3_ = f32[64,1024]{1,0:T(8,128)S(1)} collective-permute-done((f32[64,1024]{1,0:T(8,128)S(1)}, f32[64,1024]{1,0:T(8,128)S(1)}, u32[]{:S(2)}, u32[]{:S(2)}) %collective-permute-start.2) | collective-permute-done | bytes 262176 | tf_op jit(solution)/shard_map/ppermute | solution.py:24
  54.2 4.5 %collective-permute-done.6.refs_7_ = f32[64,1024]{1,0:T(8,128)S(1)} collective-permute-done((f32[64,1024]{1,0:T(8,128)S(1)}, f32[64,1024]{1,0:T(8,128)S(1)}, u32[]{:S(2)}, u32[]{:S(2)}) %collective-permute-start.6) | collective-permute-done | bytes 262176 | tf_op jit(solution)/shard_map/ppermute | solution.py:24
  59.4 3.8 %table.1 = (bf16[128,8192]{1,0:T(8,128)(2,1)}, bf16[64,8192]{1,0:T(8,128)(2,1)}) custom-call(s32[1]{0:T(128)} %bitcast.item_ref, f32[64,1024]{1,0:T(8,128)} %copy-done, f32[64,1024]{1,0:T(8,128)} %copy-done.8, f32[64,1024]{1,0:T(8,128)} %copy-done.4, f32[64,1024]{1,0:T(8,128)} %copy-done.11, f32[64,1024]{1,0:T(8,128)} %copy-done.3, f32[64,1024]{1,0:T(8,128)} %copy-done.9, ...), custom_call_target="tpu_custom_call" | custom-call | bytes 6291456 | tf_op jit(solution)/shard_map/table/pallas_call | solution.py:397
  63.8 17.4 %sinkhorn_first.1 = (f32[1,8192]{1,0:T(1,128)}, f32[8,1024]{1,0:T(8,128)}, f32[1,8192]{1,0:T(1,128)}) custom-call(bf16[1024,128]{1,0:T(8,128)(2,1)} %pad_maximum_fusion.1.l_ref, f32[8,1024]{1,0:T(8,128)} %broadcast_in_dim.3.p_ref, bf16[128,8192]{1,0:T(8,128)(2,1)} %get-tuple-element.13.w_ref, f32[1,8192]{1,0:T(1,128)} %add.88.q_ref), custom_call_target="tpu_custom_call" | custom-call | flops 4294967296 | bytes 4194304 | tf_op jit(solution)/shard_map/sinkhorn_first/pallas_call | solution.py:330
  85.1 2.4 collective-permute-done.13
  88.2 3.3 %collective-permute-done.14 = f32[1,8192]{1,0:T(1,128)S(1)} collective-permute-done((f32[1,8192]{1,0:T(1,128)S(1)}, f32[1,8192]{1,0:T(1,128)S(1)}, u32[]{:S(2)}, u32[]{:S(2)}) %collective-permute-start.14) | collective-permute-done | bytes 32800 | tf_op jit(solution)/shard_map/ppermute | solution.py:24
  92.6 3.0 %collective-permute-done.15 = f32[1,8192]{1,0:T(1,128)S(1)} collective-permute-done((f32[1,8192]{1,0:T(1,128)S(1)}, f32[1,8192]{1,0:T(1,128)S(1)}, u32[]{:S(2)}, u32[]{:S(2)}) %collective-permute-start.15) | collective-permute-done | bytes 32800 | tf_op jit(solution)/shard_map/ppermute | solution.py:24
  95.6 3.4 %collective-permute-start.16 = (f32[1,8192]{1,0:T(1,128)S(1)}, f32[1,8192]{1,0:T(1,128)S(1)}, u32[]{:S(2)}, u32[]{:S(2)}) collective-permute-start(f32[1,8192]{1,0:T(1,128)S(1)} %add.92.rest_0_), channel_id=1, source_target_pairs={{0,16},{4,20},{8,24},{12,28},{16,0},{20,4},{24,8},{28,12},{1,17},{... | collective-permute-start | bytes 98312 | tf_op jit(solution)/shard_map/ppermute | solution.py:24
  101.8 12.0 %sinkhorn_next.2 = (f32[1,8192]{1,0:T(1,128)}, f32[8,1024]{1,0:T(8,128)}, f32[1,8192]{1,0:T(1,128)}) custom-call(bf16[1024,128]{1,0:T(8,128)(2,1)} %pad_maximum_fusion.1.l_ref, f32[8,1024]{1,0:T(8,128)} %get-tuple-element.14.p_ref, bf16[128,8192]{1,0:T(8,128)(2,1)} %get-tuple-element.13.w_ref, f32[1,8192]{1,0:T(1,128)} %get-tuple-element.15.q_ref, ...), custom_call_target="tpu_custom_call" | custom-call | flops 4294967296 | bytes 4194304 | tf_op jit(solution)/shard_map/sinkhorn_next/pallas_call | solution.py:330
  117.6 2.4 collective-permute-done.18
  120.8 3.2 %collective-permute-done.19 = f32[1,8192]{1,0:T(1,128)S(1)} collective-permute-done((f32[1,8192]{1,0:T(1,128)S(1)}, f32[1,8192]{1,0:T(1,128)S(1)}, u32[]{:S(2)}, u32[]{:S(2)}) %collective-permute-start.19) | collective-permute-done | bytes 32800 | tf_op jit(solution)/shard_map/ppermute | solution.py:24
  124.4 3.7 %collective-permute-done.20 = f32[1,8192]{1,0:T(1,128)S(1)} collective-permute-done((f32[1,8192]{1,0:T(1,128)S(1)}, f32[1,8192]{1,0:T(1,128)S(1)}, u32[]{:S(2)}, u32[]{:S(2)}) %collective-permute-start.20) | collective-permute-done | bytes 32800 | tf_op jit(solution)/shard_map/ppermute | solution.py:24
  128.1 2.7 %collective-permute-start.21 = (f32[1,8192]{1,0:T(1,128)S(1)}, f32[1,8192]{1,0:T(1,128)S(1)}, u32[]{:S(2)}, u32[]{:S(2)}) collective-permute-start(f32[1,8192]{1,0:T(1,128)S(1)} %add.96.rest_0_), channel_id=1, source_target_pairs={{0,16},{4,20},{8,24},{12,28},{16,0},{20,4},{24,8},{28,12},{1,17},{... | collective-permute-start | bytes 98312 | tf_op jit(solution)/shard_map/ppermute | solution.py:24
  133.6 12.1 %sinkhorn_next.3 = (f32[1,8192]{1,0:T(1,128)}, f32[8,1024]{1,0:T(8,128)}, f32[1,8192]{1,0:T(1,128)}) custom-call(bf16[1024,128]{1,0:T(8,128)(2,1)} %pad_maximum_fusion.1.l_ref, f32[8,1024]{1,0:T(8,128)} %get-tuple-element.17.p_ref, bf16[128,8192]{1,0:T(8,128)(2,1)} %get-tuple-element.13.w_ref, f32[1,8192]{1,0:T(1,128)} %get-tuple-element.18.q_ref, ...), custom_call_target="tpu_custom_call" | custom-call | flops 4294967296 | bytes 4194304 | tf_op jit(solution)/shard_map/sinkhorn_next/pallas_call | solution.py:330
  152.9 3.4 %collective-permute-done.24 = f32[2,8192]{1,0:T(2,128)S(1)} collective-permute-done((f32[2,8192]{1,0:T(2,128)S(1)}, f32[2,8192]{1,0:T(2,128)S(1)}, u32[]{:S(2)}, u32[]{:S(2)}) %collective-permute-start.24) | collective-permute-done | bytes 65568 | tf_op jit(solution)/shard_map/ppermute | solution.py:24
  156.7 4.1 %collective-permute-done.25 = f32[2,8192]{1,0:T(2,128)S(1)} collective-permute-done((f32[2,8192]{1,0:T(2,128)S(1)}, f32[2,8192]{1,0:T(2,128)S(1)}, u32[]{:S(2)}, u32[]{:S(2)}) %collective-permute-start.25) | collective-permute-done | bytes 65568 | tf_op jit(solution)/shard_map/ppermute | solution.py:24
  160.8 2.7 %collective-permute-start.26 = (f32[2,8192]{1,0:T(2,128)S(1)}, f32[2,8192]{1,0:T(2,128)S(1)}, u32[]{:S(2)}, u32[]{:S(2)}) collective-permute-start(f32[2,8192]{1,0:T(2,128)S(1)} %fusion.7), channel_id=1, source_target_pairs={{0,16},{4,20},{8,24},{12,28},{16,0},{20,4},{24,8},{28,12},{1,17},{... | collective-permute-start | bytes 196616 | tf_op jit(solution)/shard_map/ppermute | solution.py:24
  163.5 2.9 %collective-permute-done.26 = f32[2,8192]{1,0:T(2,128)S(1)} collective-permute-done((f32[2,8192]{1,0:T(2,128)S(1)}, f32[2,8192]{1,0:T(2,128)S(1)}, u32[]{:S(2)}, u32[]{:S(2)}) %collective-permute-start.26) | collective-permute-done | bytes 65568 | tf_op jit(solution)/shard_map/ppermute | solution.py:24
  168.6 17.0 %centroid_update.1.refs_0_ = f32[512,128]{1,0:T(8,128)} custom-call(bf16[1024,128]{1,0:T(8,128)(2,1)} %pad_maximum_fusion.1.l_ref, f32[1,1024]{1,0:T(1,128)} %get-tuple-element.38.p_ref, f32[1,1024]{1,0:T(1,128)} %get-tuple-element.36.u_ref, bf16[128,8192]{1,0:T(8,128)(2,1)} %get-tuple-element.13.w_ref, f32[1,8192]{1,0:T(1,128)} %copy-done.20, ...), custom_call_target="tpu_custom_call" | custom-call | flops 8589934592 | bytes 4194304 | tf_op jit(solution)/shard_map/centroid_update/pallas_call | solution.py:373
  187.8 15.7 %code_gradient.1 = f32[1024,64]{1,0:T(8,128)} custom-call(bf16[1024,128]{1,0:T(8,128)(2,1)} %pad_maximum_fusion.l_ref, f32[1,1024]{1,0:T(1,128)} %get-tuple-element.39.p_ref, f32[1,1024]{1,0:T(1,128)} %get-tuple-element.40.u_ref, bf16[64,8192]{1,0:T(8,128)(2,1)} %bitcast.5, f32[1,8192]{1,0:T(1,128)} %get-tuple-element.33.q_ref, ...), custom_call_target="tpu_custom_call" | custom-call | flops 8589934592 | bytes 4194304 | tf_op jit(solution)/shard_map/code_gradient/pallas_call | solution.py:373
  210.4 2.4 collective-permute-done.30.refs_2_
  213.4 4.5 %collective-permute-done.34.refs_6_ = f32[512,128]{1,0:T(8,128)S(1)} collective-permute-done((f32[512,128]{1,0:T(8,128)S(1)}, f32[512,128]{1,0:T(8,128)S(1)}, u32[]{:S(2)}, u32[]{:S(2)}) %collective-permute-start.34) | collective-permute-done | bytes 262176 | tf_op jit(solution)/shard_map/ppermute | solution.py:24
  218.5 2.3 collective-permute-done.28
  223.2 5.6 %collective-permute-done.31.refs_3_ = f32[512,128]{1,0:T(8,128)S(1)} collective-permute-done((f32[512,128]{1,0:T(8,128)S(1)}, f32[512,128]{1,0:T(8,128)S(1)}, u32[]{:S(2)}, u32[]{:S(2)}) %collective-permute-start.31) | collective-permute-done | bytes 262176 | tf_op jit(solution)/shard_map/ppermute | solution.py:24
  228.8 4.5 %collective-permute-done.35.refs_7_ = f32[512,128]{1,0:T(8,128)S(1)} collective-permute-done((f32[512,128]{1,0:T(8,128)S(1)}, f32[512,128]{1,0:T(8,128)S(1)}, u32[]{:S(2)}, u32[]{:S(2)}) %collective-permute-start.35) | collective-permute-done | bytes 262176 | tf_op jit(solution)/shard_map/ppermute | solution.py:24
  234.1 4.1 %spread.1 = f32[8192,64]{1,0:T(8,128)} custom-call(s32[1]{0:T(128)} %bitcast.item_ref, f32[512,128]{1,0:T(8,128)} %centroid_update.1.refs_0_, f32[512,128]{1,0:T(8,128)} %copy-done.14, f32[512,128]{1,0:T(8,128)} %copy-done.10, f32[512,128]{1,0:T(8,128)} %copy-done.16, f32[512,128]{1,0:T(8,128)} %copy-done.7, f32[512,128]{1,0:T(8,128)} %copy-done.15, ...), custom_call_target="tpu_custom_call" | custom-call | bytes 6291456 | tf_op jit(solution)/shard_map/spread/pallas_call | solution.py:397
  238.1 3.8 %copy.19 = f32[8192,64]{0,1:T(8,128)} copy(f32[8192,64]{1,0:T(8,128)} %spread.1) | data formatting | bytes 4194304
  (136 shorter events, 61.3 us)
Async XLA Ops:
  14.6 4.2 %collective-permute-start.7 = (f32[2,1024]{1,0:T(2,128)S(1)}, f32[2,1024]{1,0:T(2,128)S(1)}, u32[]{:S(2)}, u32[]{:S(2)}) collective-permute-start(f32[2,1024]{1,0:T(2,128)S(1)} %slice.46), channel_id=1, source_target_pairs={{0,1},{1,0},{2,3},{3,2},{4,5},{5,4},{6,7},{7,6},{8,9},{9,8},{10,11... | collective-permute-start | bytes 24584 | tf_op jit(solution)/shard_map/ppermute | solution.py:24
  15.1 16.4 %collective-permute-start.3 = (f32[64,1024]{1,0:T(8,128)S(1)}, f32[64,1024]{1,0:T(8,128)S(1)}, u32[]{:S(2)}, u32[]{:S(2)}) collective-permute-start(f32[64,1024]{1,0:T(8,128)S(1)} %convert_bitcast_fusion.refs_0_), channel_id=1, source_target_pairs={{0,16},{4,20},{8,24},{12,28},{16,0},{20,4},{24,8},{28,12},{1,17},{... | collective-permute-start | bytes 786440 | tf_op jit(solution)/shard_map/ppermute | solution.py:24
  19.6 12.5 %collective-permute-start.8 = (f32[2,1024]{1,0:T(2,128)S(1)}, f32[2,1024]{1,0:T(2,128)S(1)}, u32[]{:S(2)}, u32[]{:S(2)}) collective-permute-start(f32[2,1024]{1,0:T(2,128)S(1)} %pad_maximum_fusion.3), channel_id=1, source_target_pairs={{0,2},{1,3},{2,0},{3,1},{4,6},{5,7},{6,4},{7,5},{8,10},{9,11},{10,... | collective-permute-start | bytes 24584 | tf_op jit(solution)/shard_map/ppermute | solution.py:24
  21.2 14.6 %collective-permute-start.1 = (f32[64,1024]{1,0:T(8,128)S(1)}, f32[64,1024]{1,0:T(8,128)S(1)}, u32[]{:S(2)}, u32[]{:S(2)}) collective-permute-start(f32[64,1024]{1,0:T(8,128)S(1)} %convert_bitcast_fusion.refs_0_), channel_id=1, source_target_pairs={{0,8},{4,12},{8,0},{12,4},{16,24},{20,28},{24,16},{28,20},{1,9},{5... | collective-permute-start | bytes 786440 | tf_op jit(solution)/shard_map/ppermute | solution.py:24
  31.5 8.1 %collective-permute-start.5 = (f32[64,1024]{1,0:T(8,128)S(1)}, f32[64,1024]{1,0:T(8,128)S(1)}, u32[]{:S(2)}, u32[]{:S(2)}) collective-permute-start(f32[64,1024]{1,0:T(8,128)S(1)} %collective-permute-done.3.refs_4_), channel_id=1, source_target_pairs={{0,8},{4,12},{8,0},{12,4},{16,24},{20,28},{24,16},{28,20},{1,9},{5... | collective-permute-start | bytes 786440 | tf_op jit(solution)/shard_map/ppermute | solution.py:24
  32.2 8.8 %collective-permute-start.9 = (f32[1,8192]{1,0:T(1,128)S(1)}, f32[1,8192]{1,0:T(1,128)S(1)}, u32[]{:S(2)}, u32[]{:S(2)}) collective-permute-start(f32[1,8192]{1,0:T(1,128)S(1)} %constant_dynamic-update-slice_fusion.1), channel_id=1, source_target_pairs={{0,4},{4,0},{8,12},{12,8},{16,20},{20,16},{24,28},{28,24},{1,5},{5... | collective-permute-start | bytes 98312 | tf_op jit(solution)/shard_map/ppermute | solution.py:24
  33.8 16.8 %collective-permute-start = (f32[64,1024]{1,0:T(8,128)S(1)}, f32[64,1024]{1,0:T(8,128)S(1)}, u32[]{:S(2)}, u32[]{:S(2)}) collective-permute-start(f32[64,1024]{1,0:T(8,128)S(1)} %convert_bitcast_fusion.refs_0_), channel_id=1, source_target_pairs={{0,4},{4,0},{8,12},{12,8},{16,20},{20,16},{24,28},{28,24},{1,5},{5... | collective-permute-start | bytes 786440 | tf_op jit(solution)/shard_map/ppermute | solution.py:24
  34.3 16.3 %collective-permute-start.4 = (f32[64,1024]{1,0:T(8,128)S(1)}, f32[64,1024]{1,0:T(8,128)S(1)}, u32[]{:S(2)}, u32[]{:S(2)}) collective-permute-start(f32[64,1024]{1,0:T(8,128)S(1)} %collective-permute-done.3.refs_4_), channel_id=1, source_target_pairs={{0,4},{4,0},{8,12},{12,8},{16,20},{20,16},{24,28},{28,24},{1,5},{5... | collective-permute-start | bytes 786440 | tf_op jit(solution)/shard_map/ppermute | solution.py:24
  35.8 18.4 %collective-permute-start.2 = (f32[64,1024]{1,0:T(8,128)S(1)}, f32[64,1024]{1,0:T(8,128)S(1)}, u32[]{:S(2)}, u32[]{:S(2)}) collective-permute-start(f32[64,1024]{1,0:T(8,128)S(1)} %collective-permute-done.1.refs_2_), channel_id=1, source_target_pairs={{0,4},{4,0},{8,12},{12,8},{16,20},{20,16},{24,28},{28,24},{1,5},{5... | collective-permute-start | bytes 786440 | tf_op jit(solution)/shard_map/ppermute | solution.py:24
  39.6 19.1 %collective-permute-start.6 = (f32[64,1024]{1,0:T(8,128)S(1)}, f32[64,1024]{1,0:T(8,128)S(1)}, u32[]{:S(2)}, u32[]{:S(2)}) collective-permute-start(f32[64,1024]{1,0:T(8,128)S(1)} %collective-permute-done.5.refs_6_), channel_id=1, source_target_pairs={{0,4},{4,0},{8,12},{12,8},{16,20},{20,16},{24,28},{28,24},{1,5},{5... | collective-permute-start | bytes 786440 | tf_op jit(solution)/shard_map/ppermute | solution.py:24
  41.0 4.0 %collective-permute-start.10 = (f32[1,8192]{1,0:T(1,128)S(1)}, f32[1,8192]{1,0:T(1,128)S(1)}, u32[]{:S(2)}, u32[]{:S(2)}) collective-permute-start(f32[1,8192]{1,0:T(1,128)S(1)} %add_dynamic-update-slice_fusion), channel_id=1, source_target_pairs={{0,8},{4,12},{8,0},{12,4},{16,24},{20,28},{24,16},{28,20},{1,9},{5... | collective-permute-start | bytes 98312 | tf_op jit(solution)/shard_map/ppermute | solution.py:24
  45.0 4.9 %collective-permute-start.11 = (f32[1,8192]{1,0:T(1,128)S(1)}, f32[1,8192]{1,0:T(1,128)S(1)}, u32[]{:S(2)}, u32[]{:S(2)}) collective-permute-start(f32[1,8192]{1,0:T(1,128)S(1)} %add.87), channel_id=1, source_target_pairs={{0,16},{4,20},{8,24},{12,28},{16,0},{20,4},{24,8},{28,12},{1,17},{... | collective-permute-start | bytes 98312 | tf_op jit(solution)/shard_map/ppermute | solution.py:24
  83.5 4.0 %collective-permute-start.13 = (f32[1,8192]{1,0:T(1,128)S(1)}, f32[1,8192]{1,0:T(1,128)S(1)}, u32[]{:S(2)}, u32[]{:S(2)}) collective-permute-start(f32[1,8192]{1,0:T(1,128)S(1)} %add.89), channel_id=1, source_target_pairs={{0,2},{1,3},{2,0},{3,1},{4,6},{5,7},{6,4},{7,5},{8,10},{9,11},{10,... | collective-permute-start | bytes 98312 | tf_op jit(solution)/shard_map/ppermute | solution.py:24
  87.5 4.0 %collective-permute-start.14 = (f32[1,8192]{1,0:T(1,128)S(1)}, f32[1,8192]{1,0:T(1,128)S(1)}, u32[]{:S(2)}, u32[]{:S(2)}) collective-permute-start(f32[1,8192]{1,0:T(1,128)S(1)} %add.90), channel_id=1, source_target_pairs={{0,4},{4,0},{8,12},{12,8},{16,20},{20,16},{24,28},{28,24},{1,5},{5... | collective-permute-start | bytes 98312 | tf_op jit(solution)/shard_map/ppermute | solution.py:24
  91.5 4.0 %collective-permute-start.15 = (f32[1,8192]{1,0:T(1,128)S(1)}, f32[1,8192]{1,0:T(1,128)S(1)}, u32[]{:S(2)}, u32[]{:S(2)}) collective-permute-start(f32[1,8192]{1,0:T(1,128)S(1)} %add.91), channel_id=1, source_target_pairs={{0,8},{4,12},{8,0},{12,4},{16,24},{20,28},{24,16},{28,20},{1,9},{5... | collective-permute-start | bytes 98312 | tf_op jit(solution)/shard_map/ppermute | solution.py:24
  95.6 5.6 %collective-permute-start.16 = (f32[1,8192]{1,0:T(1,128)S(1)}, f32[1,8192]{1,0:T(1,128)S(1)}, u32[]{:S(2)}, u32[]{:S(2)}) collective-permute-start(f32[1,8192]{1,0:T(1,128)S(1)} %add.92.rest_0_), channel_id=1, source_target_pairs={{0,16},{4,20},{8,24},{12,28},{16,0},{20,4},{24,8},{28,12},{1,17},{... | collective-permute-start | bytes 98312 | tf_op jit(solution)/shard_map/ppermute | solution.py:24
  116.0 4.0 %collective-permute-start.18 = (f32[1,8192]{1,0:T(1,128)S(1)}, f32[1,8192]{1,0:T(1,128)S(1)}, u32[]{:S(2)}, u32[]{:S(2)}) collective-permute-start(f32[1,8192]{1,0:T(1,128)S(1)} %add.93), channel_id=1, source_target_pairs={{0,2},{1,3},{2,0},{3,1},{4,6},{5,7},{6,4},{7,5},{8,10},{9,11},{10,... | collective-permute-start | bytes 98312 | tf_op jit(solution)/shard_map/ppermute | solution.py:24
  120.1 4.0 %collective-permute-start.19 = (f32[1,8192]{1,0:T(1,128)S(1)}, f32[1,8192]{1,0:T(1,128)S(1)}, u32[]{:S(2)}, u32[]{:S(2)}) collective-permute-start(f32[1,8192]{1,0:T(1,128)S(1)} %add.94), channel_id=1, source_target_pairs={{0,4},{4,0},{8,12},{12,8},{16,20},{20,16},{24,28},{28,24},{1,5},{5... | collective-permute-start | bytes 98312 | tf_op jit(solution)/shard_map/ppermute | solution.py:24
  124.1 4.0 %collective-permute-start.20 = (f32[1,8192]{1,0:T(1,128)S(1)}, f32[1,8192]{1,0:T(1,128)S(1)}, u32[]{:S(2)}, u32[]{:S(2)}) collective-permute-start(f32[1,8192]{1,0:T(1,128)S(1)} %add.95), channel_id=1, source_target_pairs={{0,8},{4,12},{8,0},{12,4},{16,24},{20,28},{24,16},{28,20},{1,9},{5... | collective-permute-start | bytes 98312 | tf_op jit(solution)/shard_map/ppermute | solution.py:24
  128.1 4.9 %collective-permute-start.21 = (f32[1,8192]{1,0:T(1,128)S(1)}, f32[1,8192]{1,0:T(1,128)S(1)}, u32[]{:S(2)}, u32[]{:S(2)}) collective-permute-start(f32[1,8192]{1,0:T(1,128)S(1)} %add.96.rest_0_), channel_id=1, source_target_pairs={{0,16},{4,20},{8,24},{12,28},{16,0},{20,4},{24,8},{28,12},{1,17},{... | collective-permute-start | bytes 98312 | tf_op jit(solution)/shard_map/ppermute | solution.py:24
  147.9 4.0 %collective-permute-start.23 = (f32[1,8192]{1,0:T(1,128)S(1)}, f32[1,8192]{1,0:T(1,128)S(1)}, u32[]{:S(2)}, u32[]{:S(2)}) collective-permute-start(f32[1,8192]{1,0:T(1,128)S(1)} %add.99), channel_id=1, source_target_pairs={{0,2},{1,3},{2,0},{3,1},{4,6},{5,7},{6,4},{7,5},{8,10},{9,11},{10,... | collective-permute-start | bytes 98312 | tf_op jit(solution)/shard_map/ppermute | solution.py:24
  152.0 4.3 %collective-permute-start.24 = (f32[2,8192]{1,0:T(2,128)S(1)}, f32[2,8192]{1,0:T(2,128)S(1)}, u32[]{:S(2)}, u32[]{:S(2)}) collective-permute-start(f32[2,8192]{1,0:T(2,128)S(1)} %pad_maximum_fusion.2), channel_id=1, source_target_pairs={{0,4},{4,0},{8,12},{12,8},{16,20},{20,16},{24,28},{28,24},{1,5},{5... | collective-permute-start | bytes 196616 | tf_op jit(solution)/shard_map/ppermute | solution.py:24
  156.4 4.3 %collective-permute-start.25 = (f32[2,8192]{1,0:T(2,128)S(1)}, f32[2,8192]{1,0:T(2,128)S(1)}, u32[]{:S(2)}, u32[]{:S(2)}) collective-permute-start(f32[2,8192]{1,0:T(2,128)S(1)} %fusion.6), channel_id=1, source_target_pairs={{0,8},{4,12},{8,0},{12,4},{16,24},{20,28},{24,16},{28,20},{1,9},{5... | collective-permute-start | bytes 196616 | tf_op jit(solution)/shard_map/ppermute | solution.py:24
  160.8 5.6 %collective-permute-start.26 = (f32[2,8192]{1,0:T(2,128)S(1)}, f32[2,8192]{1,0:T(2,128)S(1)}, u32[]{:S(2)}, u32[]{:S(2)}) collective-permute-start(f32[2,8192]{1,0:T(2,128)S(1)} %fusion.7), channel_id=1, source_target_pairs={{0,16},{4,20},{8,24},{12,28},{16,0},{20,4},{24,8},{28,12},{1,17},{... | collective-permute-start | bytes 196616 | tf_op jit(solution)/shard_map/ppermute | solution.py:24
  185.6 18.1 %collective-permute-start.32 = (f32[512,128]{1,0:T(8,128)}, f32[512,128]{1,0:T(8,128)S(1)}, u32[]{:S(2)}, u32[]{:S(2)}) collective-permute-start(f32[512,128]{1,0:T(8,128)} %centroid_update.1.refs_0_), channel_id=1, source_target_pairs={{0,16},{4,20},{8,24},{12,28},{16,0},{20,4},{24,8},{28,12},{1,17},{... | collective-permute-start | bytes 786440 | tf_op jit(solution)/shard_map/ppermute | solution.py:24
  203.6 9.2 %collective-permute-start.30 = (f32[512,128]{1,0:T(8,128)S(1)}, f32[512,128]{1,0:T(8,128)S(1)}, u32[]{:S(2)}, u32[]{:S(2)}) collective-permute-start(f32[512,128]{1,0:T(8,128)S(1)} %copy-done.6), channel_id=1, source_target_pairs={{0,8},{4,12},{8,0},{12,4},{16,24},{20,28},{24,16},{28,20},{1,9},{5... | collective-permute-start | bytes 786440 | tf_op jit(solution)/shard_map/ppermute | solution.py:24
  203.7 14.2 %collective-permute-start.34 = (f32[512,128]{1,0:T(8,128)S(1)}, f32[512,128]{1,0:T(8,128)S(1)}, u32[]{:S(2)}, u32[]{:S(2)}) collective-permute-start(f32[512,128]{1,0:T(8,128)S(1)} %collective-permute-done.32.refs_4_), channel_id=1, source_target_pairs={{0,8},{4,12},{8,0},{12,4},{16,24},{20,28},{24,16},{28,20},{1,9},{5... | collective-permute-start | bytes 786440 | tf_op jit(solution)/shard_map/ppermute | solution.py:24
  206.8 14.0 %collective-permute-start.28 = (f32[1024,64]{1,0:T(8,128)S(1)}, f32[1024,64]{1,0:T(8,128)S(1)}, u32[]{:S(2)}, u32[]{:S(2)}) collective-permute-start(f32[1024,64]{1,0:T(8,128)S(1)} %add.104), channel_id=1, source_target_pairs={{0,2},{1,3},{2,0},{3,1},{4,6},{5,7},{6,4},{7,5},{8,10},{9,11},{10,... | collective-permute-start | bytes 786440 | tf_op jit(solution)/shard_map/ppermute | solution.py:24
  208.4 13.4 %collective-permute-start.29 = (f32[512,128]{1,0:T(8,128)S(1)}, f32[512,128]{1,0:T(8,128)S(1)}, u32[]{:S(2)}, u32[]{:S(2)}) collective-permute-start(f32[512,128]{1,0:T(8,128)S(1)} %copy-done.6), channel_id=1, source_target_pairs={{0,4},{4,0},{8,12},{12,8},{16,20},{20,16},{24,28},{28,24},{1,5},{5... | collective-permute-start | bytes 786440 | tf_op jit(solution)/shard_map/ppermute | solution.py:24
  209.0 14.2 %collective-permute-start.33 = (f32[512,128]{1,0:T(8,128)S(1)}, f32[512,128]{1,0:T(8,128)S(1)}, u32[]{:S(2)}, u32[]{:S(2)}) collective-permute-start(f32[512,128]{1,0:T(8,128)S(1)} %collective-permute-done.32.refs_4_), channel_id=1, source_target_pairs={{0,4},{4,0},{8,12},{12,8},{16,20},{20,16},{24,28},{28,24},{1,5},{5... | collective-permute-start | bytes 786440 | tf_op jit(solution)/shard_map/ppermute | solution.py:24
  212.8 16.0 %collective-permute-start.31 = (f32[512,128]{1,0:T(8,128)S(1)}, f32[512,128]{1,0:T(8,128)S(1)}, u32[]{:S(2)}, u32[]{:S(2)}) collective-permute-start(f32[512,128]{1,0:T(8,128)S(1)} %collective-permute-done.30.refs_2_), channel_id=1, source_target_pairs={{0,4},{4,0},{8,12},{12,8},{16,20},{20,16},{24,28},{28,24},{1,5},{5... | collective-permute-start | bytes 786440 | tf_op jit(solution)/shard_map/ppermute | solution.py:24
  217.9 15.4 %collective-permute-start.35 = (f32[512,128]{1,0:T(8,128)S(1)}, f32[512,128]{1,0:T(8,128)S(1)}, u32[]{:S(2)}, u32[]{:S(2)}) collective-permute-start(f32[512,128]{1,0:T(8,128)S(1)} %collective-permute-done.34.refs_6_), channel_id=1, source_target_pairs={{0,4},{4,0},{8,12},{12,8},{16,20},{20,16},{24,28},{28,24},{1,5},{5... | collective-permute-start | bytes 786440 | tf_op jit(solution)/shard_map/ppermute | solution.py:24
  (29 other events, 345.3 us)

commit v3 on v2

--- a/solution.py
+++ b/solution.py
@@ -8,6 +8,7 @@
 from jax.experimental.pallas import tpu as pltpu
 from jax.sharding import PartitionSpec as P
 
+
 ITERS = 3
 
 score_scale = 20.0
@@ -38,7 +39,8 @@
 def gather_blocks(value, axis):
     held = {0: value}
     for bit in reversed(bits_of(axis)):
-        held.update({key | bit: swap(block, axis, bit) for key, block in list(held.items())})
+        for key, block in list(held.items()):
+            held[key | bit] = swap(block, axis, bit)
     return held
 
 
@@ -78,33 +80,35 @@
     return values[0]
 
 
-def own_pieces(item_ref, key, width):
-    return pl.ds(pl.multiple_of((item_ref[0] ^ key) * width, width), width)
-
-
-def table_kernel(item_ref, *refs, keys):
-    pieces, (right_ref, other_ref) = refs[: len(keys)], refs[len(keys) :]
-    dim = other_ref.shape[0]
+def place_kernel(item_ref, *refs, keys):
+    pieces, out_ref = refs[: len(keys)], refs[len(keys)]
     for key, piece_ref in zip(keys, pieces):
-        at = own_pieces(item_ref, key, piece_ref.shape[1])
+        width = piece_ref.shape[1]
+        at = pl.ds(pl.multiple_of((item_ref[0] ^ key) * width, width), width)
+        out_ref[:, at] = piece_ref[...]
+
+
+def table_kernel(core_ref, mine_ref, other_ref, right_ref, codes_ref):
+    dim, width = mine_ref.shape
+    for piece_ref, half in ((mine_ref, core_ref[0]), (other_ref, 1 - core_ref[0])):
+        at = pl.ds(pl.multiple_of(half * width, width), width)
         piece = piece_ref[...]
         scaled = score_scale * piece
         high = scaled.astype(jnp.bfloat16)
         right_ref[0:dim, at] = high
         right_ref[dim : 2 * dim, at] = (scaled - high.astype(jnp.float32)).astype(jnp.bfloat16)
-        other_ref[:, at] = piece.astype(jnp.bfloat16)
-
-
-def spread_kernel(item_ref, *refs, keys, half):
-    pieces, out_ref = refs[: len(keys)], refs[len(keys)]
-    for key, piece_ref in zip(keys, pieces):
-        count, twice = piece_ref.shape
-        for part in range(count // half):
-            piece = piece_ref[part * half : (part + 1) * half, :]
-            for side in range(2):
-                start = (item_ref[0] ^ key) * (2 * count) + (2 * part + side) * half
-                at = pl.ds(pl.multiple_of(start, half), half)
-                out_ref[at, :] = piece[:, side * (twice // 2) : (side + 1) * (twice // 2)]
+        codes_ref[:, at] = piece.astype(jnp.bfloat16)
+
+
+def left_of(l_ref, split):
+    rows = jnp.transpose(l_ref[...].astype(jnp.float32))
+    if split:
+        rows = score_scale * rows
+        high = rows.astype(jnp.bfloat16)
+        low = (rows - high.astype(jnp.float32)).astype(jnp.bfloat16)
+    else:
+        high = low = rows.astype(jnp.bfloat16)
+    return jnp.concatenate([high, low], axis=1)
 
 
 def chunk_of(width):
@@ -147,6 +151,7 @@
             sum_ref[...] = jnp.zeros(sum_ref.shape, jnp.float32)
         if new:
             part_ref[...] = jnp.full(part_ref.shape, -jnp.inf, jnp.float32)
+            left = left_of(l_ref, True)
 
         def chunk(at):
             if old:
@@ -154,7 +159,7 @@
                 sum_ref[...] += folded(terms, jnp.add)
             if new:
                 right = jnp.concatenate([w_ref[:, at]] * repeat, axis=0)
-                y = jnp.dot(l_ref[...], right, preferred_element_type=jnp.float32)
+                y = jnp.dot(left, right, preferred_element_type=jnp.float32)
                 y_ref[:, at] = y
                 part_ref[...] = jnp.maximum(part_ref[...], folded(slices(y), jnp.maximum))
 
@@ -190,7 +195,7 @@
             chunks(width, prepare)
         if new:
             was = jnp.zeros((1, block), jnp.float32) if first else p_ref[0:1, :]
-            left = jnp.concatenate([l_ref[...], left_pots(was, block)], axis=1)
+            left = jnp.concatenate([left_of(l_ref, False), left_pots(was, block)], axis=1)
             part_ref[...] = jnp.full(part_ref.shape, -jnp.inf if first else 0.0, jnp.float32)
 
         def chunk(at):
@@ -238,11 +243,8 @@
 
 
 def final_kernel(l_ref, p_ref, u_ref, w_ref, q_ref, v_ref, r_ref, *rest, repeat, update):
-    if update:
-        own_ref, out_ref, wide_ref, wpot_ref, acc_ref = rest
-    else:
-        out_ref, wide_ref, wpot_ref, acc_ref = rest
-    block = l_ref.shape[0]
+    out_ref, wide_ref, wpot_ref, acc_ref = rest
+    block = l_ref.shape[1]
     width = w_ref.shape[1]
 
     @pl.when(pl.program_id(0) == 0)
@@ -252,7 +254,7 @@
 
         chunks(width, prepare)
 
-    left = jnp.concatenate([l_ref[...], left_pots(p_ref[0:1, :], block)], axis=1)
+    left = jnp.concatenate([left_of(l_ref, not update), left_pots(p_ref[0:1, :], block)], axis=1)
     wide_ref[...] = jnp.transpose(jnp.broadcast_to(u_ref[0:1, :], (LANES, block)))
     acc_ref[...] = jnp.zeros(acc_ref.shape, jnp.float32)
 
@@ -271,17 +273,14 @@
         )
 
     chunks(width, chunk)
-    gradient = score_scale * acc_ref[...]
-    if not update:
-        out_ref[...] = gradient
-    else:
-        moved = own_ref[...].astype(jnp.float32) - step_rate * gradient
-        scaled = moved * lax.rsqrt(jnp.mean(moved * moved, axis=1, keepdims=True) + epsilon)
-        half = block // 2
-        out_ref[...] = jnp.concatenate([scaled[:half], scaled[half:]], axis=1)
-
-
-VMEM = functools.partial(pltpu.VMEM)
+    gradient = score_scale * jnp.transpose(acc_ref[...])
+    if update:
+        moved = l_ref[...].astype(jnp.float32) - step_rate * gradient
+        gradient = moved * lax.rsqrt(jnp.mean(moved * moved, axis=0, keepdims=True) + epsilon)
+    out_ref[...] = gradient
+
+
+VMEM = pltpu.VMEM
 
 
 def block_of(count, width):
@@ -303,13 +302,13 @@
 
 
 def lse(left, right, repeat):
-    rows, width = left.shape[0], right.shape[1]
+    (dim, rows), width = left.shape, right.shape[1]
     block = block_of(rows, width)
     count = rows // block
     return pl.pallas_call(
         functools.partial(lse_kernel, repeat=repeat, count=count),
         grid=(count + 1,),
-        in_specs=[pl.BlockSpec((block, LANES), lambda k: (jnp.minimum(k, count - 1), 0)), full(right)],
+        in_specs=[pl.BlockSpec((dim, block), lambda k: (0, jnp.minimum(k, count - 1))), full(right)],
         out_specs=pl.BlockSpec((8, block), lambda k: (0, jnp.maximum(k - 1, 0))),
         out_shape=jax.ShapeDtypeStruct((8, rows), jnp.float32),
         scratch_shapes=[VMEM((block, width), jnp.float32)] + [VMEM((block, LANES), jnp.float32)] * 3,
@@ -320,7 +319,7 @@
 
 
 def sink(left, p_rows, right, row, sums, rows_total, buckets_total):
-    rows, width = left.shape[0], right.shape[1]
+    (dim, rows), width = left.shape, right.shape[1]
     block = block_of(rows, width)
     count = rows // block
     first = sums is None
@@ -333,7 +332,7 @@
         ),
         grid=(count + 1,),
         in_specs=[
-            pl.BlockSpec((block, LANES), lambda k: (jnp.minimum(k, count - 1), 0)),
+            pl.BlockSpec((dim, block), lambda k: (0, jnp.minimum(k, count - 1))),
             pot_spec,
             full(right),
         ]
@@ -353,29 +352,18 @@
     )(left, p_rows, right, *lines)
 
 
-def final(left, p_row, u_row, right, q_row, v_row, other, repeat, own=None):
-    rows, width = left.shape[0], right.shape[1]
+def final(left, p_row, u_row, right, q_row, v_row, other, repeat, update):
+    (dim, rows), width = left.shape, right.shape[1]
     block = block_of(rows, width)
-    update = own is not None
-    dim = other.shape[0]
     line = pl.BlockSpec((1, width), lambda k: (0, 0))
     part = pl.BlockSpec((1, block), lambda k: (0, k))
-    in_specs = [pl.BlockSpec((block, LANES), lambda k: (k, 0)), part, part, full(right), line, line, full(other)]
-    args = [left, p_row, u_row, right, q_row, v_row, other]
-    if update:
-        in_specs.append(pl.BlockSpec((block, dim), lambda k: (k, 0)))
-        args.append(own)
-        out_spec = pl.BlockSpec((block // 2, 2 * dim), lambda k: (k, 0))
-        out_shape = jax.ShapeDtypeStruct((rows // 2, 2 * dim), jnp.float32)
-    else:
-        out_spec = pl.BlockSpec((block, dim), lambda k: (k, 0))
-        out_shape = jax.ShapeDtypeStruct((rows, dim), jnp.float32)
-    out = pl.pallas_call(
+    piece = pl.BlockSpec((dim, block), lambda k: (0, k))
+    return pl.pallas_call(
         functools.partial(final_kernel, repeat=repeat, update=update),
         grid=(rows // block,),
-        in_specs=in_specs,
-        out_specs=out_spec,
-        out_shape=out_shape,
+        in_specs=[piece, part, part, full(right), line, line, full(other)],
+        out_specs=piece,
+        out_shape=jax.ShapeDtypeStruct((dim, rows), jnp.float32),
         scratch_shapes=[
             VMEM((block, LANES), jnp.float32),
             VMEM((POTS, width), jnp.bfloat16),
@@ -384,77 +372,96 @@
         compiler_params=params(),
         cost_estimate=cost(rows, width, 2),
         name="centroid_update" if update else "code_gradient",
-    )(*args)
-    return out, block
-
-
-def by_item(kernel, item, blocks, out_shape, name, **settings):
-    keys = sorted(blocks)
+    )(left, p_row, u_row, right, q_row, v_row, other)
+
+
+def small(kernel, index, arrays, out_shape, **settings):
     several = isinstance(out_shape, list)
-    whole = lambda shape: pl.BlockSpec(shape, lambda k, item: (0, 0))
-    shapes = out_shape if several else [out_shape]
-    specs = [whole(one.shape) for one in shapes]
+    whole = lambda shape: pl.BlockSpec(shape, lambda k, index: (0, 0))
+    specs = [whole(one.shape) for one in (out_shape if several else [out_shape])]
     return pl.pallas_call(
-        functools.partial(kernel, keys=keys, **settings),
+        functools.partial(kernel, **settings),
         grid_spec=pltpu.PrefetchScalarGridSpec(
             num_scalar_prefetch=1,
             grid=(1,),
-            in_specs=[whole(blocks[key].shape) for key in keys],
+            in_specs=[whole(one.shape) for one in arrays],
             out_specs=specs if several else specs[0],
         ),
         out_shape=out_shape,
         compiler_params=params(),
-        cost_estimate=pl.CostEstimate(flops=0, transcendentals=0, bytes_accessed=6 << 20),
-        name=name,
-    )(item.reshape(1).astype(jnp.int32), *[blocks[key] for key in keys])
-
-
-def halves(scaled):
-    high = lax.reduce_precision(scaled, 8, 7)
-    return high.astype(jnp.bfloat16), (scaled - high).astype(jnp.bfloat16)
-
-
-def body(code_rows, centroids):
+        cost_estimate=pl.CostEstimate(flops=0, transcendentals=0, bytes_accessed=4 << 20),
+    )(index.reshape(1).astype(jnp.int32), *arrays)
+
+
+def place(blocks, item):
+    keys = sorted(blocks)
+    dim, width = blocks[0].shape
+    shape = jax.ShapeDtypeStruct((dim, width * len(keys)), jnp.float32)
+    return small(place_kernel, item, [blocks[key] for key in keys], shape, keys=keys)
+
+
+def step(code_rows, centroids):
     items = lax.axis_size("item")
     item = lax.axis_index("item")
+    core = lax.axis_index("bucket") & 1
     rows_own, dim = code_rows.shape
     rows_total = rows_own * items
+    rows_half = rows_own // 2
     buckets_own = centroids.shape[0]
     buckets_total = buckets_own * lax.axis_size("bucket")
     share = buckets_own // items
     log_rows = math.log(rows_total)
-
-    codes_f32 = code_rows.astype(jnp.float32)
-    row_left = jnp.concatenate(halves(score_scale * codes_f32), axis=1)
+    codes_t = code_rows.T
     centroids_t = centroids.T
-    stats = lse(row_left, centroids_t, 2)[0:2]
-
-    right, other = by_item(
-        table_kernel,
-        item,
-        gather_blocks(codes_f32.T, "item"),
-        [
-            jax.ShapeDtypeStruct((2 * dim, rows_total), jnp.bfloat16),
-            jax.ShapeDtypeStruct((dim, rows_total), jnp.bfloat16),
-        ],
-        "table",
-    )
-    own = lax.dynamic_slice_in_dim(centroids, item * share, share, axis=0)
-    own_left = jnp.concatenate([own, own], axis=1)
-
+
+    def spread_rows(values):
+        out = jnp.zeros((1, rows_total), jnp.float32)
+        for half in range(2):
+            piece = values[:, half * rows_half : (half + 1) * rows_half]
+            out = lax.dynamic_update_slice(out, piece, (0, half * (rows_total // 2) + item * rows_half))
+        return out
+
+    def own_rows(values):
+        return jnp.concatenate(
+            [
+                lax.dynamic_slice_in_dim(values, half * (rows_total // 2) + item * rows_half, rows_half, axis=1)
+                for half in range(2)
+            ],
+            axis=1,
+        )
+
+    own_half = lax.dynamic_slice_in_dim(codes_t, core * rows_half, rows_half, axis=1).astype(jnp.float32)
+    pieces = gather_blocks(own_half, "item")
+
+    stats = []
+    for part in range(2):
+        stats.append(lse(codes_t[:, part * rows_half : (part + 1) * rows_half], centroids_t, 2)[0:2])
+    stats = jnp.concatenate(stats, axis=1)
     for bit in bits_of("bucket"):
         received = swap(stats, "bucket", bit)
         highest = jnp.maximum(stats[0], received[0])
         summed = stats[1] * jnp.exp(stats[0] - highest) + received[1] * jnp.exp(received[0] - highest)
         stats = jnp.stack([highest, summed])
     first_own = -log_rows - (stats[0:1] + jnp.log(stats[1:2]))
-    row_first = lax.dynamic_update_slice(jnp.zeros((1, rows_total), jnp.float32), first_own, (0, item * rows_own))
-    row = row_first = add_over(row_first, "item")
-
+
+    mine = place(pieces, item)
+    theirs = swap(mine, "bucket", 1)
+    right, other = small(
+        table_kernel,
+        core,
+        [mine, theirs],
+        [
+            jax.ShapeDtypeStruct((2 * dim, rows_total), jnp.bfloat16),
+            jax.ShapeDtypeStruct((dim, rows_total), jnp.bfloat16),
+        ],
+    )
+    row = row_first = add_over(spread_rows(first_own), "item")
+
+    own = lax.dynamic_slice_in_dim(centroids_t, item * share, share, axis=1)
     cols = jnp.zeros((8, share), jnp.float32)
     sums = None
     for iteration in range(ITERS):
-        total, cols, row = sink(own_left, cols, right, row, sums, rows_total, buckets_total)
+        total, cols, row = sink(own, cols, right, row, sums, rows_total, buckets_total)
         total = add_over(total, "bucket")
         if iteration < ITERS - 1:
             for bit in bits_of("item")[:-1]:
@@ -471,28 +478,28 @@
     row_scale = total * float(rows_total) * jnp.exp(row_first - row)
     row = row + log_rows
 
-    update, block = final(own_left, col_own, jnp.exp(-col_own), right, row, row_scale, other, 1, own)
-
-    def mine(values):
-        return lax.dynamic_slice_in_dim(values, item * rows_own, rows_own, axis=1)
-
-    grad, _ = final(row_left, mine(row), mine(row_scale), centroids_t, col, jnp.exp(-col), centroids_t, 2)
-
-    new_centroids = by_item(
-        spread_kernel,
-        item,
-        gather_blocks(update, "item"),
-        jax.ShapeDtypeStruct((buckets_own, dim), jnp.float32),
-        "spread",
-        half=block // 2,
-    )
-    grad_codes = add_over(grad, "bucket")
-    return (grad_codes, new_centroids)
+    update = final(own, col_own, jnp.exp(-col_own), right, row, row_scale, other, 1, True)
+    pieces = gather_blocks(update, "item")
+
+    rows_pot, rows_scale, cols_scale = own_rows(row), own_rows(row_scale), jnp.exp(-col)
+    grads = []
+    for part in range(4):
+        at = slice(part * rows_own // 4, (part + 1) * rows_own // 4)
+        grads.append(
+            final(
+                codes_t[:, at], rows_pot[:, at], rows_scale[:, at], centroids_t, col, cols_scale, centroids_t, 2, False
+            )
+        )
+    new_centroids = place(pieces, item)
+    grad_codes = jnp.concatenate(grads, axis=1)
+    for bit in bits_of("bucket"):
+        grad_codes = grad_codes + swap(grad_codes, "bucket", bit)
+    return (grad_codes.T, new_centroids.T)
 
 
 def solution(mesh):
     return jax.shard_map(
-        body,
+        step,
         mesh=mesh,
         in_specs=(P("item", None), P("bucket", None)),
         out_specs=(P("item", None), P("bucket", None)),

time: 243 us -> 243 us (level)
  waiting for transfers between devices: 81.8 us -> 66.6 us
  Pallas kernels: 93.3 us -> 107 us
  starting transfers between devices: 44 us -> 46.8 us
    ppermute x36 -> x37, waiting for transfers between devices: 81.8 us -> 66.6 us  [swap(): return lax.ppermute(value, axis, [(k, k ^ bit) for k in range(size)])]
    pallas_call x2 -> x5, Pallas kernels: 32.7 us -> 40.1 us  [final(): pl.pallas_call(functools.partial(final_kernel, repeat=repeat, update=upda...]
    slice x1 -> x5, local copies, waits for them, and re-layouts: 0.76 us -> 4.94 us  [the longest x1 1.52 us: step(): codes_t[:, part * rows_half:(part + 1) * rows_half]]
    unnamed x53 -> x52, local copies, waits for them, and re-layouts: 7.48 us -> 3.68 us
    pallas_call x1 -> x2, Pallas kernels: 11.2 us -> 14.6 us  [lse(): pl.pallas_call(functools.partial(lse_kernel, repeat=repeat, count=count),...]
    ppermute x36 -> x37, starting transfers between devices: 44 us -> 46.8 us  [swap(): return lax.ppermute(value, axis, [(k, k ^ bit) for k in range(size)])]
    pallas_call x2 -> x3, Pallas kernels: 7.87 us -> 9.13 us  [small(): pl.pallas_call(functools.partial(kernel, **settings), grid_spec=pltpu.Pre...]
  transfers between devices with their start and end apart: 36 -> 37, of which waited for: 27 -> 24; matrix products, arithmetic and copies ran while one was open for 3% -> 5% of each run, Pallas kernels for 6% -> 17%
where the time goes in v3:
time: 243 us; the launch traced here: 242 us
  Pallas kernels  107 us (44%)
  waiting for transfers between devices  66.6 us (27%)
  starting transfers between devices  46.8 us (19%)
  local copies, waits for them, and re-layouts  10.9 us (4%)
  other arithmetic  9.93 us (4%)
    ppermute x37, waiting for transfers between devices, swap(): return lax.ppermute(value, axis, [(k, k ^ bit) for k in range(size)])  66.6 us
    ppermute x37, starting transfers between devices, swap(): return lax.ppermute(value, axis, [(k, k ^ bit) for k in range(size)])  46.8 us
    pallas_call x3, Pallas kernels, sink(): pl.pallas_call(functools.partial(sink_kernel, first=first, rows_total=row...  42.9 us
    pallas_call x5, Pallas kernels, final(): pl.pallas_call(functools.partial(final_kernel, repeat=repeat, update=upda...  40.1 us
    pallas_call x2, Pallas kernels, lse(): pl.pallas_call(functools.partial(lse_kernel, repeat=repeat, count=count),...  14.6 us
    pallas_call x3, Pallas kernels, small(): pl.pallas_call(functools.partial(kernel, **settings), grid_spec=pltpu.Pre...  9.13 us
  transfers between devices with their start and end apart: 37, of which 24 were waited for; matrix products, arithmetic and copies ran while one was open for 5% of the time, Pallas kernels for 17%

profile of v3, /device:TPU:0, one launch (start us, length us, event | category | flops | bytes accessed | tf_op | source)
XLA Modules:
  0.0 241.9 jit_solution(16435360296440650471)
XLA Ops:
  1.5 4.1 %collective-permute-start.3 = (f32[64,512]{1,0:T(8,128)S(1)}, f32[64,512]{1,0:T(8,128)S(1)}, u32[]{:S(2)}, u32[]{:S(2)}) collective-permute-start(f32[64,512]{1,0:T(8,128)S(1)} %convert_bitcast_fusion.refs_0_), channel_id=1, source_target_pairs={{0,16},{4,20},{8,24},{12,28},{16,0},{20,4},{24,8},{28,12},{1,17},{... | collective-permute-start | bytes 393224 | tf_op jit(solution)/shard_map/ppermute | solution.py:25
  12.7 7.3 %row_lse.2 = f32[8,512]{1,0:T(8,128)} custom-call(bf16[64,512]{1,0:T(8,128)(2,1)} %get-tuple-element.30.l_ref, bf16[64,8192]{1,0:T(8,128)(2,1)} %bitcast.14), custom_call_target="tpu_custom_call" | custom-call | flops 2147483648 | bytes 4194304 | tf_op jit(solution)/shard_map/row_lse/pallas_call | solution.py:308
  23.5 7.3 %row_lse.3 = f32[8,512]{1,0:T(8,128)} custom-call(bf16[64,512]{1,0:T(8,128)(2,1)} %get-tuple-element.31.l_ref, bf16[64,8192]{1,0:T(8,128)(2,1)} %bitcast.15), custom_call_target="tpu_custom_call" | custom-call | flops 2147483648 | bytes 4194304 | tf_op jit(solution)/shard_map/row_lse/pallas_call | solution.py:308
  33.0 2.3 shard_map.41.mine_ref
  40.3 3.4 %collective-permute-done.10 = f32[1,8192]{1,0:T(1,128)S(1)} collective-permute-done((f32[1,8192]{1,0:T(1,128)S(1)}, f32[1,8192]{1,0:T(1,128)S(1)}, u32[]{:S(2)}, u32[]{:S(2)}) %collective-permute-start.10) | collective-permute-done | bytes 32800 | tf_op jit(solution)/shard_map/ppermute | solution.py:25
  45.3 2.5 %collective-permute-done.11 = f32[1,8192]{1,0:T(1,128)S(1)} collective-permute-done((f32[1,8192]{1,0:T(1,128)S(1)}, f32[1,8192]{1,0:T(1,128)S(1)}, u32[]{:S(2)}, u32[]{:S(2)}) %collective-permute-start.11) | collective-permute-done | bytes 32800 | tf_op jit(solution)/shard_map/ppermute | solution.py:25
  47.8 3.4 %collective-permute-start.12 = (f32[1,8192]{1,0:T(1,128)S(1)}, f32[1,8192]{1,0:T(1,128)S(1)}, u32[]{:S(2)}, u32[]{:S(2)}) collective-permute-start(f32[1,8192]{1,0:T(1,128)S(1)} %add.107), channel_id=1, source_target_pairs={{0,16},{4,20},{8,24},{12,28},{16,0},{20,4},{24,8},{28,12},{1,17},{... | collective-permute-start | bytes 98312 | tf_op jit(solution)/shard_map/ppermute | solution.py:25
  54.7 3.8 %shard_map.42 = (bf16[128,8192]{1,0:T(8,128)(2,1)}, bf16[64,8192]{1,0:T(8,128)(2,1)}) custom-call(s32[1]{0:T(128)} %bitcast.2.core_ref, f32[64,4096]{1,0:T(8,128)} %shard_map.41.mine_ref, f32[64,4096]{1,0:T(8,128)} %copy-done), custom_call_target="tpu_custom_call" | custom-call | bytes 4194304 | tf_op jit(solution)/shard_map/pallas_call | solution.py:382
  59.2 17.9 %sinkhorn_first.1 = (f32[1,8192]{1,0:T(1,128)}, f32[8,1024]{1,0:T(8,128)}, f32[1,8192]{1,0:T(1,128)}) custom-call(bf16[64,1024]{1,0:T(8,128)(2,1)} %dynamic-slice_bitcast_fusion.l_ref, f32[8,1024]{1,0:T(8,128)} %broadcast_in_dim.3.p_ref, bf16[128,8192]{1,0:T(8,128)(2,1)} %get-tuple-element.13.w_ref, f32[1,8192]{1,0:T(1,128)} %add.108.q_ref), custom_call_target="tpu_custom_call" | custom-call | flops 4294967296 | bytes 4194304 | tf_op jit(solution)/shard_map/sinkhorn_first/pallas_call | solution.py:329
  80.9 2.4 collective-permute-done.14
  83.9 3.4 %collective-permute-done.15 = f32[1,8192]{1,0:T(1,128)S(1)} collective-permute-done((f32[1,8192]{1,0:T(1,128)S(1)}, f32[1,8192]{1,0:T(1,128)S(1)}, u32[]{:S(2)}, u32[]{:S(2)}) %collective-permute-start.15) | collective-permute-done | bytes 32800 | tf_op jit(solution)/shard_map/ppermute | solution.py:25
  88.4 2.9 %collective-permute-done.16 = f32[1,8192]{1,0:T(1,128)S(1)} collective-permute-done((f32[1,8192]{1,0:T(1,128)S(1)}, f32[1,8192]{1,0:T(1,128)S(1)}, u32[]{:S(2)}, u32[]{:S(2)}) %collective-permute-start.16) | collective-permute-done | bytes 32800 | tf_op jit(solution)/shard_map/ppermute | solution.py:25
  91.4 3.0 %collective-permute-start.17 = (f32[1,8192]{1,0:T(1,128)S(1)}, f32[1,8192]{1,0:T(1,128)S(1)}, u32[]{:S(2)}, u32[]{:S(2)}) collective-permute-start(f32[1,8192]{1,0:T(1,128)S(1)} %add.112.rest_0_), channel_id=1, source_target_pairs={{0,16},{4,20},{8,24},{12,28},{16,0},{20,4},{24,8},{28,12},{1,17},{... | collective-permute-start | bytes 98312 | tf_op jit(solution)/shard_map/ppermute | solution.py:25
  96.9 12.5 %sinkhorn_next.2 = (f32[1,8192]{1,0:T(1,128)}, f32[8,1024]{1,0:T(8,128)}, f32[1,8192]{1,0:T(1,128)}) custom-call(bf16[64,1024]{1,0:T(8,128)(2,1)} %dynamic-slice_bitcast_fusion.l_ref, f32[8,1024]{1,0:T(8,128)} %get-tuple-element.14.p_ref, bf16[128,8192]{1,0:T(8,128)(2,1)} %get-tuple-element.13.w_ref, f32[1,8192]{1,0:T(1,128)} %get-tuple-element.15.q_ref, ...), custom_call_target="tpu_custom_call" | custom-call | flops 4294967296 | bytes 4194304 | tf_op jit(solution)/shard_map/sinkhorn_next/pallas_call | solution.py:329
  113.1 2.4 collective-permute-done.19
  116.2 3.4 %collective-permute-done.20 = f32[1,8192]{1,0:T(1,128)S(1)} collective-permute-done((f32[1,8192]{1,0:T(1,128)S(1)}, f32[1,8192]{1,0:T(1,128)S(1)}, u32[]{:S(2)}, u32[]{:S(2)}) %collective-permute-start.20) | collective-permute-done | bytes 32800 | tf_op jit(solution)/shard_map/ppermute | solution.py:25
  120.7 2.9 %collective-permute-done.21 = f32[1,8192]{1,0:T(1,128)S(1)} collective-permute-done((f32[1,8192]{1,0:T(1,128)S(1)}, f32[1,8192]{1,0:T(1,128)S(1)}, u32[]{:S(2)}, u32[]{:S(2)}) %collective-permute-start.21) | collective-permute-done | bytes 32800 | tf_op jit(solution)/shard_map/ppermute | solution.py:25
  123.6 3.0 %collective-permute-start.22 = (f32[1,8192]{1,0:T(1,128)S(1)}, f32[1,8192]{1,0:T(1,128)S(1)}, u32[]{:S(2)}, u32[]{:S(2)}) collective-permute-start(f32[1,8192]{1,0:T(1,128)S(1)} %add.116.rest_0_), channel_id=1, source_target_pairs={{0,16},{4,20},{8,24},{12,28},{16,0},{20,4},{24,8},{28,12},{1,17},{... | collective-permute-start | bytes 98312 | tf_op jit(solution)/shard_map/ppermute | solution.py:25
  129.1 12.5 %sinkhorn_next.3 = (f32[1,8192]{1,0:T(1,128)}, f32[8,1024]{1,0:T(8,128)}, f32[1,8192]{1,0:T(1,128)}) custom-call(bf16[64,1024]{1,0:T(8,128)(2,1)} %dynamic-slice_bitcast_fusion.l_ref, f32[8,1024]{1,0:T(8,128)} %get-tuple-element.17.p_ref, bf16[128,8192]{1,0:T(8,128)(2,1)} %get-tuple-element.13.w_ref, f32[1,8192]{1,0:T(1,128)} %get-tuple-element.18.q_ref, ...), custom_call_target="tpu_custom_call" | custom-call | flops 4294967296 | bytes 4194304 | tf_op jit(solution)/shard_map/sinkhorn_next/pallas_call | solution.py:329
  148.6 3.7 %collective-permute-done.25 = f32[2,8192]{1,0:T(2,128)S(1)} collective-permute-done((f32[2,8192]{1,0:T(2,128)S(1)}, f32[2,8192]{1,0:T(2,128)S(1)}, u32[]{:S(2)}, u32[]{:S(2)}) %collective-permute-start.25) | collective-permute-done | bytes 65568 | tf_op jit(solution)/shard_map/ppermute | solution.py:25
  153.5 3.3 %collective-permute-done.26 = f32[2,8192]{1,0:T(2,128)S(1)} collective-permute-done((f32[2,8192]{1,0:T(2,128)S(1)}, f32[2,8192]{1,0:T(2,128)S(1)}, u32[]{:S(2)}, u32[]{:S(2)}) %collective-permute-start.26) | collective-permute-done | bytes 65568 | tf_op jit(solution)/shard_map/ppermute | solution.py:25
  156.8 3.0 %collective-permute-start.27 = (f32[2,8192]{1,0:T(2,128)S(1)}, f32[2,8192]{1,0:T(2,128)S(1)}, u32[]{:S(2)}, u32[]{:S(2)}) collective-permute-start(f32[2,8192]{1,0:T(2,128)S(1)} %fusion.12), channel_id=1, source_target_pairs={{0,16},{4,20},{8,24},{12,28},{16,0},{20,4},{24,8},{28,12},{1,17},{... | collective-permute-start | bytes 196616 | tf_op jit(solution)/shard_map/ppermute | solution.py:25
  164.4 16.9 %centroid_update.1.refs_0_ = f32[64,1024]{1,0:T(8,128)} custom-call(bf16[64,1024]{1,0:T(8,128)(2,1)} %dynamic-slice_bitcast_fusion.l_ref, f32[1,1024]{1,0:T(1,128)} %get-tuple-element.38.p_ref, f32[1,1024]{1,0:T(1,128)} %get-tuple-element.36.u_ref, bf16[128,8192]{1,0:T(8,128)(2,1)} %get-tuple-element.13.w_ref, f32[1,8192]{1,0:T(1,128)} %get-tuple-element.35.q_ref, ...), custom_call_target="tpu_custom_call" | custom-call | flops 8589934592 | bytes 4194304 | tf_op jit(solution)/shard_map/centroid_update/pallas_call | solution.py:361
  184.8 5.8 %code_gradient.4 = f32[64,256]{1,0:T(8,128)} custom-call(bf16[64,256]{1,0:T(8,128)(2,1)} %get-tuple-element.26.l_ref, f32[1,256]{1,0:T(1,128)} %get-tuple-element.50.p_ref, f32[1,256]{1,0:T(1,128)} %get-tuple-element.39.u_ref, bf16[64,8192]{1,0:T(8,128)(2,1)} %bitcast.16, f32[1,8192]{1,0:T(1,128)} %get-tuple-element.33.q_ref, ...), custom_call_target="tpu_custom_call" | custom-call | flops 2147483648 | bytes 4194304 | tf_op jit(solution)/shard_map/code_gradient/pallas_call | solution.py:361
  190.6 5.8 %code_gradient.5 = f32[64,256]{1,0:T(8,128)} custom-call(bf16[64,256]{1,0:T(8,128)(2,1)} %get-tuple-element.29.l_ref, f32[1,256]{1,0:T(1,128)} %get-tuple-element.47.p_ref, f32[1,256]{1,0:T(1,128)} %get-tuple-element.42.u_ref, bf16[64,8192]{1,0:T(8,128)(2,1)} %bitcast.18, f32[1,8192]{1,0:T(1,128)} %get-tuple-element.33.q_ref, ...), custom_call_target="tpu_custom_call" | custom-call | flops 2147483648 | bytes 4194304 | tf_op jit(solution)/shard_map/code_gradient/pallas_call | solution.py:361
  196.4 5.8 %code_gradient.6 = f32[64,256]{1,0:T(8,128)} custom-call(bf16[64,256]{1,0:T(8,128)(2,1)} %get-tuple-element.28.l_ref, f32[1,256]{1,0:T(1,128)} %get-tuple-element.49.p_ref, f32[1,256]{1,0:T(1,128)} %get-tuple-element.40.u_ref, bf16[64,8192]{1,0:T(8,128)(2,1)} %bitcast.20, f32[1,8192]{1,0:T(1,128)} %get-tuple-element.33.q_ref, ...), custom_call_target="tpu_custom_call" | custom-call | flops 2147483648 | bytes 4194304 | tf_op jit(solution)/shard_map/code_gradient/pallas_call | solution.py:361
  202.2 5.9 %code_gradient.7 = f32[64,256]{1,0:T(8,128)} custom-call(bf16[64,256]{1,0:T(8,128)(2,1)} %get-tuple-element.27.l_ref, f32[1,256]{1,0:T(1,128)} %get-tuple-element.48.p_ref, f32[1,256]{1,0:T(1,128)} %get-tuple-element.41.u_ref, bf16[64,8192]{1,0:T(8,128)(2,1)} %bitcast.22, f32[1,8192]{1,0:T(1,128)} %get-tuple-element.33.q_ref, ...), custom_call_target="tpu_custom_call" | custom-call | flops 2147483648 | bytes 4194304 | tf_op jit(solution)/shard_map/code_gradient/pallas_call | solution.py:361
  215.6 2.7 %collective-permute-done.31.refs_2_ = f32[64,1024]{1,0:T(8,128)S(1)} collective-permute-done((f32[64,1024]{1,0:T(8,128)S(1)}, f32[64,1024]{1,0:T(8,128)S(1)}, u32[]{:S(2)}, u32[]{:S(2)}) %collective-permute-start.31) | collective-permute-done | bytes 262176 | tf_op jit(solution)/shard_map/ppermute | solution.py:25
  218.8 4.5 %collective-permute-done.35.refs_6_ = f32[64,1024]{1,0:T(8,128)S(1)} collective-permute-done((f32[64,1024]{1,0:T(8,128)S(1)}, f32[64,1024]{1,0:T(8,128)S(1)}, u32[]{:S(2)}, u32[]{:S(2)}) %collective-permute-start.35) | collective-permute-done | bytes 262176 | tf_op jit(solution)/shard_map/ppermute | solution.py:25
  224.6 9.4 %collective-permute-done.32.refs_3_ = f32[64,1024]{1,0:T(8,128)S(1)} collective-permute-done((f32[64,1024]{1,0:T(8,128)S(1)}, f32[64,1024]{1,0:T(8,128)S(1)}, u32[]{:S(2)}, u32[]{:S(2)}) %collective-permute-start.32) | collective-permute-done | bytes 262176 | tf_op jit(solution)/shard_map/ppermute | solution.py:25
  234.0 4.2 %collective-permute-done.36.refs_7_ = f32[64,1024]{1,0:T(8,128)S(1)} collective-permute-done((f32[64,1024]{1,0:T(8,128)S(1)}, f32[64,1024]{1,0:T(8,128)S(1)}, u32[]{:S(2)}, u32[]{:S(2)}) %collective-permute-start.36) | collective-permute-done | bytes 262176 | tf_op jit(solution)/shard_map/ppermute | solution.py:25
  239.0 3.0 %shard_map.43 = f32[64,8192]{1,0:T(8,128)} custom-call(s32[1]{0:T(128)} %bitcast.3.item_ref, f32[64,1024]{1,0:T(8,128)} %centroid_update.1.refs_0_, f32[64,1024]{1,0:T(8,128)} %copy-done.7, f32[64,1024]{1,0:T(8,128)} %copy-done.5, f32[64,1024]{1,0:T(8,128)} %copy-done.9, f32[64,1024]{1,0:T(8,128)} %copy-done.4, f32[64,1024]{1,0:T(8,128)} %copy-done.8, ...), custom_call_target="tpu_custom_call" | custom-call | bytes 4194304 | tf_op jit(solution)/shard_map/pallas_call | solution.py:382
  (145 shorter events, 66.7 us)
Async XLA Ops:
  1.5 10.5 %collective-permute-start.3 = (f32[64,512]{1,0:T(8,128)S(1)}, f32[64,512]{1,0:T(8,128)S(1)}, u32[]{:S(2)}, u32[]{:S(2)}) collective-permute-start(f32[64,512]{1,0:T(8,128)S(1)} %convert_bitcast_fusion.refs_0_), channel_id=1, source_target_pairs={{0,16},{4,20},{8,24},{12,28},{16,0},{20,4},{24,8},{28,12},{1,17},{... | collective-permute-start | bytes 393224 | tf_op jit(solution)/shard_map/ppermute | solution.py:25
  5.6 15.8 %collective-permute-start.1 = (f32[64,512]{1,0:T(8,128)S(1)}, f32[64,512]{1,0:T(8,128)S(1)}, u32[]{:S(2)}, u32[]{:S(2)}) collective-permute-start(f32[64,512]{1,0:T(8,128)S(1)} %convert_bitcast_fusion.refs_0_), channel_id=1, source_target_pairs={{0,8},{4,12},{8,0},{12,4},{16,24},{20,28},{24,16},{28,20},{1,9},{5... | collective-permute-start | bytes 393224 | tf_op jit(solution)/shard_map/ppermute | solution.py:25
  7.2 25.0 %collective-permute-start = (f32[64,512]{1,0:T(8,128)S(1)}, f32[64,512]{1,0:T(8,128)S(1)}, u32[]{:S(2)}, u32[]{:S(2)}) collective-permute-start(f32[64,512]{1,0:T(8,128)S(1)} %convert_bitcast_fusion.refs_0_), channel_id=1, source_target_pairs={{0,4},{4,0},{8,12},{12,8},{16,20},{20,16},{24,28},{28,24},{1,5},{5... | collective-permute-start | bytes 393224 | tf_op jit(solution)/shard_map/ppermute | solution.py:25
  12.0 10.0 %collective-permute-start.5 = (f32[64,512]{1,0:T(8,128)S(1)}, f32[64,512]{1,0:T(8,128)S(1)}, u32[]{:S(2)}, u32[]{:S(2)}) collective-permute-start(f32[64,512]{1,0:T(8,128)S(1)} %collective-permute-done.3.refs_4_), channel_id=1, source_target_pairs={{0,8},{4,12},{8,0},{12,4},{16,24},{20,28},{24,16},{28,20},{1,9},{5... | collective-permute-start | bytes 393224 | tf_op jit(solution)/shard_map/ppermute | solution.py:25
  20.0 12.3 %collective-permute-start.4 = (f32[64,512]{1,0:T(8,128)S(1)}, f32[64,512]{1,0:T(8,128)S(1)}, u32[]{:S(2)}, u32[]{:S(2)}) collective-permute-start(f32[64,512]{1,0:T(8,128)S(1)} %collective-permute-done.3.refs_4_), channel_id=1, source_target_pairs={{0,4},{4,0},{8,12},{12,8},{16,20},{20,16},{24,28},{28,24},{1,5},{5... | collective-permute-start | bytes 393224 | tf_op jit(solution)/shard_map/ppermute | solution.py:25
  21.5 10.8 %collective-permute-start.2 = (f32[64,512]{1,0:T(8,128)S(1)}, f32[64,512]{1,0:T(8,128)S(1)}, u32[]{:S(2)}, u32[]{:S(2)}) collective-permute-start(f32[64,512]{1,0:T(8,128)S(1)} %collective-permute-done.1.refs_2_), channel_id=1, source_target_pairs={{0,4},{4,0},{8,12},{12,8},{16,20},{20,16},{24,28},{28,24},{1,5},{5... | collective-permute-start | bytes 393224 | tf_op jit(solution)/shard_map/ppermute | solution.py:25
  22.0 10.3 %collective-permute-start.6 = (f32[64,512]{1,0:T(8,128)S(1)}, f32[64,512]{1,0:T(8,128)S(1)}, u32[]{:S(2)}, u32[]{:S(2)}) collective-permute-start(f32[64,512]{1,0:T(8,128)S(1)} %collective-permute-done.5.refs_6_), channel_id=1, source_target_pairs={{0,4},{4,0},{8,12},{12,8},{16,20},{20,16},{24,28},{28,24},{1,5},{5... | collective-permute-start | bytes 393224 | tf_op jit(solution)/shard_map/ppermute | solution.py:25
  35.4 18.4 %collective-permute-start.7 = (f32[64,4096]{1,0:T(8,128)}, f32[64,4096]{1,0:T(8,128)S(1)}, u32[]{:S(2)}, u32[]{:S(2)}) collective-permute-start(f32[64,4096]{1,0:T(8,128)} %shard_map.41.mine_ref), channel_id=1, source_target_pairs={{0,1},{1,0},{2,3},{3,2},{4,5},{5,4},{6,7},{7,6},{8,9},{9,8},{10,11... | collective-permute-start | bytes 3145736 | tf_op jit(solution)/shard_map/ppermute | solution.py:25
  35.9 3.7 %collective-permute-start.9 = (f32[2,1024]{1,0:T(2,128)S(1)}, f32[2,1024]{1,0:T(2,128)S(1)}, u32[]{:S(2)}, u32[]{:S(2)}) collective-permute-start(f32[2,1024]{1,0:T(2,128)S(1)} %pad_maximum_fusion.3), channel_id=1, source_target_pairs={{0,2},{1,3},{2,0},{3,1},{4,6},{5,7},{6,4},{7,5},{8,10},{9,11},{10,... | collective-permute-start | bytes 24584 | tf_op jit(solution)/shard_map/ppermute | solution.py:25
  39.7 4.0 %collective-permute-start.10 = (f32[1,8192]{1,0:T(1,128)S(1)}, f32[1,8192]{1,0:T(1,128)S(1)}, u32[]{:S(2)}, u32[]{:S(2)}) collective-permute-start(f32[1,8192]{1,0:T(1,128)S(1)} %constant_dynamic-update-slice_fusion.1), channel_id=1, source_target_pairs={{0,4},{4,0},{8,12},{12,8},{16,20},{20,16},{24,28},{28,24},{1,5},{5... | collective-permute-start | bytes 98312 | tf_op jit(solution)/shard_map/ppermute | solution.py:25
  43.8 4.0 %collective-permute-start.11 = (f32[1,8192]{1,0:T(1,128)S(1)}, f32[1,8192]{1,0:T(1,128)S(1)}, u32[]{:S(2)}, u32[]{:S(2)}) collective-permute-start(f32[1,8192]{1,0:T(1,128)S(1)} %add.106), channel_id=1, source_target_pairs={{0,8},{4,12},{8,0},{12,4},{16,24},{20,28},{24,16},{28,20},{1,9},{5... | collective-permute-start | bytes 98312 | tf_op jit(solution)/shard_map/ppermute | solution.py:25
  47.8 5.3 %collective-permute-start.12 = (f32[1,8192]{1,0:T(1,128)S(1)}, f32[1,8192]{1,0:T(1,128)S(1)}, u32[]{:S(2)}, u32[]{:S(2)}) collective-permute-start(f32[1,8192]{1,0:T(1,128)S(1)} %add.107), channel_id=1, source_target_pairs={{0,16},{4,20},{8,24},{12,28},{16,0},{20,4},{24,8},{28,12},{1,17},{... | collective-permute-start | bytes 98312 | tf_op jit(solution)/shard_map/ppermute | solution.py:25
  79.3 4.0 %collective-permute-start.14 = (f32[1,8192]{1,0:T(1,128)S(1)}, f32[1,8192]{1,0:T(1,128)S(1)}, u32[]{:S(2)}, u32[]{:S(2)}) collective-permute-start(f32[1,8192]{1,0:T(1,128)S(1)} %add.109), channel_id=1, source_target_pairs={{0,2},{1,3},{2,0},{3,1},{4,6},{5,7},{6,4},{7,5},{8,10},{9,11},{10,... | collective-permute-start | bytes 98312 | tf_op jit(solution)/shard_map/ppermute | solution.py:25
  83.3 4.0 %collective-permute-start.15 = (f32[1,8192]{1,0:T(1,128)S(1)}, f32[1,8192]{1,0:T(1,128)S(1)}, u32[]{:S(2)}, u32[]{:S(2)}) collective-permute-start(f32[1,8192]{1,0:T(1,128)S(1)} %add.110), channel_id=1, source_target_pairs={{0,4},{4,0},{8,12},{12,8},{16,20},{20,16},{24,28},{28,24},{1,5},{5... | collective-permute-start | bytes 98312 | tf_op jit(solution)/shard_map/ppermute | solution.py:25
  87.4 4.0 %collective-permute-start.16 = (f32[1,8192]{1,0:T(1,128)S(1)}, f32[1,8192]{1,0:T(1,128)S(1)}, u32[]{:S(2)}, u32[]{:S(2)}) collective-permute-start(f32[1,8192]{1,0:T(1,128)S(1)} %add.111), channel_id=1, source_target_pairs={{0,8},{4,12},{8,0},{12,4},{16,24},{20,28},{24,16},{28,20},{1,9},{5... | collective-permute-start | bytes 98312 | tf_op jit(solution)/shard_map/ppermute | solution.py:25
  91.4 4.9 %collective-permute-start.17 = (f32[1,8192]{1,0:T(1,128)S(1)}, f32[1,8192]{1,0:T(1,128)S(1)}, u32[]{:S(2)}, u32[]{:S(2)}) collective-permute-start(f32[1,8192]{1,0:T(1,128)S(1)} %add.112.rest_0_), channel_id=1, source_target_pairs={{0,16},{4,20},{8,24},{12,28},{16,0},{20,4},{24,8},{28,12},{1,17},{... | collective-permute-start | bytes 98312 | tf_op jit(solution)/shard_map/ppermute | solution.py:25
  111.5 4.0 %collective-permute-start.19 = (f32[1,8192]{1,0:T(1,128)S(1)}, f32[1,8192]{1,0:T(1,128)S(1)}, u32[]{:S(2)}, u32[]{:S(2)}) collective-permute-start(f32[1,8192]{1,0:T(1,128)S(1)} %add.113), channel_id=1, source_target_pairs={{0,2},{1,3},{2,0},{3,1},{4,6},{5,7},{6,4},{7,5},{8,10},{9,11},{10,... | collective-permute-start | bytes 98312 | tf_op jit(solution)/shard_map/ppermute | solution.py:25
  115.6 4.0 %collective-permute-start.20 = (f32[1,8192]{1,0:T(1,128)S(1)}, f32[1,8192]{1,0:T(1,128)S(1)}, u32[]{:S(2)}, u32[]{:S(2)}) collective-permute-start(f32[1,8192]{1,0:T(1,128)S(1)} %add.114), channel_id=1, source_target_pairs={{0,4},{4,0},{8,12},{12,8},{16,20},{20,16},{24,28},{28,24},{1,5},{5... | collective-permute-start | bytes 98312 | tf_op jit(solution)/shard_map/ppermute | solution.py:25
  119.6 4.0 %collective-permute-start.21 = (f32[1,8192]{1,0:T(1,128)S(1)}, f32[1,8192]{1,0:T(1,128)S(1)}, u32[]{:S(2)}, u32[]{:S(2)}) collective-permute-start(f32[1,8192]{1,0:T(1,128)S(1)} %add.115), channel_id=1, source_target_pairs={{0,8},{4,12},{8,0},{12,4},{16,24},{20,28},{24,16},{28,20},{1,9},{5... | collective-permute-start | bytes 98312 | tf_op jit(solution)/shard_map/ppermute | solution.py:25
  123.6 4.9 %collective-permute-start.22 = (f32[1,8192]{1,0:T(1,128)S(1)}, f32[1,8192]{1,0:T(1,128)S(1)}, u32[]{:S(2)}, u32[]{:S(2)}) collective-permute-start(f32[1,8192]{1,0:T(1,128)S(1)} %add.116.rest_0_), channel_id=1, source_target_pairs={{0,16},{4,20},{8,24},{12,28},{16,0},{20,4},{24,8},{28,12},{1,17},{... | collective-permute-start | bytes 98312 | tf_op jit(solution)/shard_map/ppermute | solution.py:25
  143.9 4.0 %collective-permute-start.24 = (f32[1,8192]{1,0:T(1,128)S(1)}, f32[1,8192]{1,0:T(1,128)S(1)}, u32[]{:S(2)}, u32[]{:S(2)}) collective-permute-start(f32[1,8192]{1,0:T(1,128)S(1)} %add.119), channel_id=1, source_target_pairs={{0,2},{1,3},{2,0},{3,1},{4,6},{5,7},{6,4},{7,5},{8,10},{9,11},{10,... | collective-permute-start | bytes 98312 | tf_op jit(solution)/shard_map/ppermute | solution.py:25
  148.0 4.3 %collective-permute-start.25 = (f32[2,8192]{1,0:T(2,128)S(1)}, f32[2,8192]{1,0:T(2,128)S(1)}, u32[]{:S(2)}, u32[]{:S(2)}) collective-permute-start(f32[2,8192]{1,0:T(2,128)S(1)} %pad_maximum_fusion.1), channel_id=1, source_target_pairs={{0,4},{4,0},{8,12},{12,8},{16,20},{20,16},{24,28},{28,24},{1,5},{5... | collective-permute-start | bytes 196616 | tf_op jit(solution)/shard_map/ppermute | solution.py:25
  152.4 4.3 %collective-permute-start.26 = (f32[2,8192]{1,0:T(2,128)S(1)}, f32[2,8192]{1,0:T(2,128)S(1)}, u32[]{:S(2)}, u32[]{:S(2)}) collective-permute-start(f32[2,8192]{1,0:T(2,128)S(1)} %fusion.8), channel_id=1, source_target_pairs={{0,8},{4,12},{8,0},{12,4},{16,24},{20,28},{24,16},{28,20},{1,9},{5... | collective-permute-start | bytes 196616 | tf_op jit(solution)/shard_map/ppermute | solution.py:25
  156.8 5.9 %collective-permute-start.27 = (f32[2,8192]{1,0:T(2,128)S(1)}, f32[2,8192]{1,0:T(2,128)S(1)}, u32[]{:S(2)}, u32[]{:S(2)}) collective-permute-start(f32[2,8192]{1,0:T(2,128)S(1)} %fusion.12), channel_id=1, source_target_pairs={{0,16},{4,20},{8,24},{12,28},{16,0},{20,4},{24,8},{28,12},{1,17},{... | collective-permute-start | bytes 196616 | tf_op jit(solution)/shard_map/ppermute | solution.py:25
  181.2 27.9 %collective-permute-start.33 = (f32[64,1024]{1,0:T(8,128)}, f32[64,1024]{1,0:T(8,128)S(1)}, u32[]{:S(2)}, u32[]{:S(2)}) collective-permute-start(f32[64,1024]{1,0:T(8,128)} %centroid_update.1.refs_0_), channel_id=1, source_target_pairs={{0,16},{4,20},{8,24},{12,28},{16,0},{20,4},{24,8},{28,12},{1,17},{... | collective-permute-start | bytes 786440 | tf_op jit(solution)/shard_map/ppermute | solution.py:25
  209.0 9.2 %collective-permute-start.31 = (f32[64,1024]{1,0:T(8,128)S(1)}, f32[64,1024]{1,0:T(8,128)S(1)}, u32[]{:S(2)}, u32[]{:S(2)}) collective-permute-start(f32[64,1024]{1,0:T(8,128)S(1)} %copy-done.3), channel_id=1, source_target_pairs={{0,8},{4,12},{8,0},{12,4},{16,24},{20,28},{24,16},{28,20},{1,9},{5... | collective-permute-start | bytes 786440 | tf_op jit(solution)/shard_map/ppermute | solution.py:25
  209.1 14.2 %collective-permute-start.35 = (f32[64,1024]{1,0:T(8,128)S(1)}, f32[64,1024]{1,0:T(8,128)S(1)}, u32[]{:S(2)}, u32[]{:S(2)}) collective-permute-start(f32[64,1024]{1,0:T(8,128)S(1)} %collective-permute-done.33.refs_4_), channel_id=1, source_target_pairs={{0,8},{4,12},{8,0},{12,4},{16,24},{20,28},{24,16},{28,20},{1,9},{5... | collective-permute-start | bytes 786440 | tf_op jit(solution)/shard_map/ppermute | solution.py:25
  212.0 11.9 %collective-permute-start.29 = (f32[64,1024]{1,0:T(8,128)S(1)}, f32[64,1024]{1,0:T(8,128)S(1)}, u32[]{:S(2)}, u32[]{:S(2)}) collective-permute-start(f32[64,1024]{1,0:T(8,128)S(1)} %fusion.9), channel_id=1, source_target_pairs={{0,2},{1,3},{2,0},{3,1},{4,6},{5,7},{6,4},{7,5},{8,10},{9,11},{10,... | collective-permute-start | bytes 786440 | tf_op jit(solution)/shard_map/ppermute | solution.py:25
  213.6 11.0 %collective-permute-start.30 = (f32[64,1024]{1,0:T(8,128)S(1)}, f32[64,1024]{1,0:T(8,128)S(1)}, u32[]{:S(2)}, u32[]{:S(2)}) collective-permute-start(f32[64,1024]{1,0:T(8,128)S(1)} %copy-done.3), channel_id=1, source_target_pairs={{0,4},{4,0},{8,12},{12,8},{16,20},{20,16},{24,28},{28,24},{1,5},{5... | collective-permute-start | bytes 786440 | tf_op jit(solution)/shard_map/ppermute | solution.py:25
  214.1 19.9 %collective-permute-start.34 = (f32[64,1024]{1,0:T(8,128)S(1)}, f32[64,1024]{1,0:T(8,128)S(1)}, u32[]{:S(2)}, u32[]{:S(2)}) collective-permute-start(f32[64,1024]{1,0:T(8,128)S(1)} %collective-permute-done.33.refs_4_), channel_id=1, source_target_pairs={{0,4},{4,0},{8,12},{12,8},{16,20},{20,16},{24,28},{28,24},{1,5},{5... | collective-permute-start | bytes 786440 | tf_op jit(solution)/shard_map/ppermute | solution.py:25
  218.3 15.7 %collective-permute-start.32 = (f32[64,1024]{1,0:T(8,128)S(1)}, f32[64,1024]{1,0:T(8,128)S(1)}, u32[]{:S(2)}, u32[]{:S(2)}) collective-permute-start(f32[64,1024]{1,0:T(8,128)S(1)} %collective-permute-done.31.refs_2_), channel_id=1, source_target_pairs={{0,4},{4,0},{8,12},{12,8},{16,20},{20,16},{24,28},{28,24},{1,5},{5... | collective-permute-start | bytes 786440 | tf_op jit(solution)/shard_map/ppermute | solution.py:25
  223.3 14.9 %collective-permute-start.36 = (f32[64,1024]{1,0:T(8,128)S(1)}, f32[64,1024]{1,0:T(8,128)S(1)}, u32[]{:S(2)}, u32[]{:S(2)}) collective-permute-start(f32[64,1024]{1,0:T(8,128)S(1)} %collective-permute-done.35.refs_6_), channel_id=1, source_target_pairs={{0,4},{4,0},{8,12},{12,8},{16,20},{20,16},{24,28},{28,24},{1,5},{5... | collective-permute-start | bytes 786440 | tf_op jit(solution)/shard_map/ppermute | solution.py:25
  (31 other events, 245.1 us)

commit v4 on v3

--- a/solution.py
+++ b/solution.py
@@ -30,9 +30,28 @@
     return [1 << k for k in range(size.bit_length() - 1)]
 
 
-def add_over(value, axis):
-    for bit in bits_of(axis):
-        value = value + swap(value, axis, bit)
+def odd_swap(value, axis, bit):
+    items, buckets = lax.axis_size("item"), lax.axis_size("bucket")
+    pairs = []
+    for item in range(items):
+        for bucket in range(1, buckets, 2):
+            other = (item ^ bit, bucket) if axis == "item" else (item, bucket ^ bit)
+            pairs.append((item * buckets + bucket, other[0] * buckets + other[1]))
+    return lax.ppermute(value, ("item", "bucket"), pairs)
+
+
+def up(value):
+    return lax.ppermute(value, "bucket", [(k, k + 1) for k in range(0, lax.axis_size("bucket"), 2)])
+
+
+def down(value):
+    return lax.ppermute(value, "bucket", [(k + 1, k) for k in range(0, lax.axis_size("bucket"), 2)])
+
+
+def odd_add(value, axis, bits):
+    for bit in bits:
+        received = odd_swap(value, axis, bit)
+        value = value + received
     return value
 
 
@@ -141,7 +160,8 @@
         run(False, True)
 
 
-def lse_kernel(l_ref, w_ref, out_ref, y_ref, part_ref, sum_ref, wide_ref, *, repeat, count):
+def lse_kernel(l_ref, w_ref, *rest, repeat, count):
+    out_ref, y_ref, part_ref, sum_ref, wide_ref = rest[-5:]
     block, width = y_ref.shape
 
     def run(new, old):
@@ -168,16 +188,16 @@
             summed = jnp.sum(sum_ref[...], axis=1, keepdims=True)
             lane = lax.broadcasted_iota(jnp.int32, (block, LANES), 1)
             both = jnp.where(lane == 0, wide_ref[...], summed)
-            out_ref[...] = jnp.transpose(both)[0:8, :]
+            out_ref[...] = jnp.transpose(both)[0:2, :]
 
     cases(count, run)
 
 
 def sink_kernel(
-    l_ref, p_ref, w_ref, q_ref, *rest, first, rows_total, buckets_total, count
+    l_ref, w_ref, one_ref, two_ref, *rest, first, rows_total, buckets_total, count
 ):
     if not first:
-        one_ref, two_ref, *rest = rest
+        p_ref, q_ref, *rest = rest
     sums_ref, pot_ref, row_ref, y_ref, part_ref, high_ref, wide_ref, wpot_ref, acc_ref = rest
     block, width = y_ref.shape
 
@@ -186,9 +206,9 @@
             acc_ref[...] = jnp.zeros(acc_ref.shape, jnp.float32)
 
             def prepare(at):
-                row = q_ref[0:1, at]
+                row = one_ref[0:1, at] + two_ref[0:1, at]
                 if not first:
-                    row = row - jnp.log((one_ref[0:1, at] + two_ref[0:1, at]) * float(rows_total))
+                    row = q_ref[0:1, at] - jnp.log(row * float(rows_total))
                 row_ref[0:1, at] = row
                 wpot_ref[:, at] = pots(row, chunk_of(width), 0)
 
@@ -242,20 +262,33 @@
     cases(count, run)
 
 
-def final_kernel(l_ref, p_ref, u_ref, w_ref, q_ref, v_ref, r_ref, *rest, repeat, update):
-    out_ref, wide_ref, wpot_ref, acc_ref = rest
+def final_kernel(l_ref, p_ref, w_ref, *rest, repeat, update, rows_total):
+    out_ref, wide_ref, wpot_ref, v_ref, acc_ref = rest[-5:]
+    if update:
+        row_ref, start_ref, one_ref, two_ref, r_ref = rest[:5]
+    else:
+        col_ref, r_ref = rest[0], w_ref
     block = l_ref.shape[1]
     width = w_ref.shape[1]
 
     @pl.when(pl.program_id(0) == 0)
     def _():
         def prepare(at):
-            wpot_ref[:, at] = pots(q_ref[0:1, at], chunk_of(width), 0)
+            if update:
+                row = row_ref[0:1, at]
+                mass = (one_ref[0:1, at] + two_ref[0:1, at]) * float(rows_total)
+                v_ref[0:1, at] = mass * jnp.exp(start_ref[0:1, at] - row)
+                row = row + math.log(rows_total)
+            else:
+                row = col_ref[0:1, at]
+                v_ref[0:1, at] = jnp.exp(-row)
+            wpot_ref[:, at] = pots(row, chunk_of(width), 0)
 
         chunks(width, prepare)
 
+    factor_p = jnp.exp(-p_ref[0:1, :]) if update else p_ref[1:2, :]
     left = jnp.concatenate([left_of(l_ref, not update), left_pots(p_ref[0:1, :], block)], axis=1)
-    wide_ref[...] = jnp.transpose(jnp.broadcast_to(u_ref[0:1, :], (LANES, block)))
+    wide_ref[...] = jnp.transpose(jnp.broadcast_to(factor_p, (LANES, block)))
     acc_ref[...] = jnp.zeros(acc_ref.shape, jnp.float32)
 
     def chunk(at):
@@ -301,30 +334,32 @@
     return pl.BlockSpec(array.shape, lambda k: (0, 0))
 
 
-def lse(left, right, repeat):
+def lse(left, right, repeat, part, parts, before):
+    (dim, rows), width = left.shape, right.shape[1]
+    block = min(block_of(rows, width), rows // parts)
+    count = rows // parts // block
+    lead = part * count
+    return pl.pallas_call(
+        functools.partial(lse_kernel, repeat=repeat, count=count),
+        grid=(count + 1,),
+        in_specs=[pl.BlockSpec((dim, block), lambda k: (0, lead + jnp.minimum(k, count - 1))), full(right)]
+        + [pl.BlockSpec(memory_space=pl.ANY)] * len(before),
+        out_specs=pl.BlockSpec((2, block), lambda k: (0, lead + jnp.maximum(k - 1, 0))),
+        out_shape=jax.ShapeDtypeStruct((2, rows), jnp.float32),
+        scratch_shapes=[VMEM((block, width), jnp.float32)] + [VMEM((block, LANES), jnp.float32)] * 3,
+        input_output_aliases={2: 0} if before else {},
+        compiler_params=params(),
+        cost_estimate=cost(rows // parts, width, 1),
+        name="row_lse",
+    )(left, right, *before)
+
+
+def sink(left, right, one, two, old, rows_total, buckets_total):
     (dim, rows), width = left.shape, right.shape[1]
     block = block_of(rows, width)
     count = rows // block
-    return pl.pallas_call(
-        functools.partial(lse_kernel, repeat=repeat, count=count),
-        grid=(count + 1,),
-        in_specs=[pl.BlockSpec((dim, block), lambda k: (0, jnp.minimum(k, count - 1))), full(right)],
-        out_specs=pl.BlockSpec((8, block), lambda k: (0, jnp.maximum(k - 1, 0))),
-        out_shape=jax.ShapeDtypeStruct((8, rows), jnp.float32),
-        scratch_shapes=[VMEM((block, width), jnp.float32)] + [VMEM((block, LANES), jnp.float32)] * 3,
-        compiler_params=params(),
-        cost_estimate=cost(rows, width, 1),
-        name="row_lse",
-    )(left, right)
-
-
-def sink(left, p_rows, right, row, sums, rows_total, buckets_total):
-    (dim, rows), width = left.shape, right.shape[1]
-    block = block_of(rows, width)
-    count = rows // block
-    first = sums is None
+    first = not old
     line = pl.BlockSpec((1, width), lambda k: (0, 0))
-    lines = [row] if first else [row, *sums]
     pot_spec = pl.BlockSpec((8, block), lambda k: (0, jnp.minimum(k, count - 1)))
     return pl.pallas_call(
         functools.partial(
@@ -333,10 +368,11 @@
         grid=(count + 1,),
         in_specs=[
             pl.BlockSpec((dim, block), lambda k: (0, jnp.minimum(k, count - 1))),
-            pot_spec,
             full(right),
+            line,
+            line,
         ]
-        + [line] * len(lines),
+        + ([] if first else [pot_spec, line]),
         out_specs=[line, pot_spec, line],
         out_shape=[
             jax.ShapeDtypeStruct((1, width), jnp.float32),
@@ -349,30 +385,39 @@
         compiler_params=params(),
         cost_estimate=cost(rows, width, 1),
         name="sinkhorn_first" if first else "sinkhorn_next",
-    )(left, p_rows, right, *lines)
-
-
-def final(left, p_row, u_row, right, q_row, v_row, other, repeat, update):
+    )(left, right, one, two, *old)
+
+
+def final(left, p_rows, right, lines, codes, repeat, update, rows_total, lead, steps, total, before):
     (dim, rows), width = left.shape, right.shape[1]
     block = block_of(rows, width)
     line = pl.BlockSpec((1, width), lambda k: (0, 0))
-    part = pl.BlockSpec((1, block), lambda k: (0, k))
-    piece = pl.BlockSpec((dim, block), lambda k: (0, k))
+    into = total - steps if before else 0
+    extra = [codes] if update else []
     return pl.pallas_call(
-        functools.partial(final_kernel, repeat=repeat, update=update),
-        grid=(rows // block,),
-        in_specs=[piece, part, part, full(right), line, line, full(other)],
-        out_specs=piece,
-        out_shape=jax.ShapeDtypeStruct((dim, rows), jnp.float32),
+        functools.partial(final_kernel, repeat=repeat, update=update, rows_total=rows_total),
+        grid=(steps,),
+        in_specs=[
+            pl.BlockSpec((dim, block), lambda k: (0, lead + k)),
+            pl.BlockSpec((p_rows.shape[0], block), lambda k: (0, lead + k)),
+            full(right),
+        ]
+        + [line] * len(lines)
+        + [full(one) for one in extra]
+        + [pl.BlockSpec(memory_space=pl.ANY)] * len(before),
+        out_specs=pl.BlockSpec((dim, block), lambda k: (0, into + k)),
+        out_shape=jax.ShapeDtypeStruct((dim, total * block), jnp.float32),
         scratch_shapes=[
             VMEM((block, LANES), jnp.float32),
             VMEM((POTS, width), jnp.bfloat16),
+            VMEM((8, width), jnp.float32),
             VMEM((block, dim), jnp.float32),
         ],
+        input_output_aliases={3 + len(lines) + len(extra): 0} if before else {},
         compiler_params=params(),
-        cost_estimate=cost(rows, width, 2),
+        cost_estimate=cost(steps * block, width, 2),
         name="centroid_update" if update else "code_gradient",
-    )(left, p_row, u_row, right, q_row, v_row, other)
+    )(left, p_rows, right, *lines, *extra, *before)
 
 
 def small(kernel, index, arrays, out_shape, **settings):
@@ -430,23 +475,30 @@
             axis=1,
         )
 
+    odd = core == 1
+    bucket_bits, item_bits = bits_of("bucket")[1:], bits_of("item")
+
+    def shared(value):
+        return jnp.where(odd, value, 0.0), down(value)
+
     own_half = lax.dynamic_slice_in_dim(codes_t, core * rows_half, rows_half, axis=1).astype(jnp.float32)
     pieces = gather_blocks(own_half, "item")
 
-    stats = []
+    held = []
     for part in range(2):
-        stats.append(lse(codes_t[:, part * rows_half : (part + 1) * rows_half], centroids_t, 2)[0:2])
-    stats = jnp.concatenate(stats, axis=1)
-    for bit in bits_of("bucket"):
-        received = swap(stats, "bucket", bit)
-        highest = jnp.maximum(stats[0], received[0])
-        summed = stats[1] * jnp.exp(stats[0] - highest) + received[1] * jnp.exp(received[0] - highest)
-        stats = jnp.stack([highest, summed])
+        held = [lse(codes_t, centroids_t, 2, part, 2, held)]
+    stats = held[0]
+    for step_bit in [1] + bucket_bits:
+        received = up(stats) if step_bit == 1 else odd_swap(stats, "bucket", step_bit)
+        highest = jnp.maximum(stats[0:1], received[0:1])
+        summed = stats[1:2] * jnp.exp(stats[0:1] - highest) + received[1:2] * jnp.exp(received[0:1] - highest)
+        stats = jnp.concatenate([highest, summed], axis=0)
     first_own = -log_rows - (stats[0:1] + jnp.log(stats[1:2]))
+    one, two = shared(odd_add(spread_rows(first_own), "item", item_bits))
 
     mine = place(pieces, item)
     theirs = swap(mine, "bucket", 1)
-    right, other = small(
+    right, codes = small(
         table_kernel,
         core,
         [mine, theirs],
@@ -455,46 +507,53 @@
             jax.ShapeDtypeStruct((dim, rows_total), jnp.bfloat16),
         ],
     )
-    row = row_first = add_over(spread_rows(first_own), "item")
 
     own = lax.dynamic_slice_in_dim(centroids_t, item * share, share, axis=1)
-    cols = jnp.zeros((8, share), jnp.float32)
-    sums = None
+    old = []
+    row_first = None
     for iteration in range(ITERS):
-        total, cols, row = sink(own, cols, right, row, sums, rows_total, buckets_total)
-        total = add_over(total, "bucket")
+        total, cols, row = sink(own, right, one, two, old, rows_total, buckets_total)
+        old = [cols, row]
+        if row_first is None:
+            row_first = row
         if iteration < ITERS - 1:
-            for bit in bits_of("item")[:-1]:
-                total = total + swap(total, "item", bit)
-            sums = (total, swap(total, "item", bits_of("item")[-1]))
-
-    col_own = cols[0:1]
-    col = lax.dynamic_update_slice(jnp.zeros((1, buckets_own), jnp.float32), col_own, (0, item * share))
-    if buckets_own == rows_total:
-        both = add_over(jnp.concatenate([total, col], axis=0), "item")
-        total, col = both[0:1], both[1:2]
-    else:
-        total, col = add_over(total, "item"), add_over(col, "item")
-    row_scale = total * float(rows_total) * jnp.exp(row_first - row)
-    row = row + log_rows
-
-    update = final(own, col_own, jnp.exp(-col_own), right, row, row_scale, other, 1, True)
+            total = total + up(total)
+            total = odd_add(odd_add(total, "bucket", bucket_bits), "item", item_bits)
+            one, two = shared(total)
+
+    col = lax.dynamic_update_slice(jnp.zeros((1, buckets_own), jnp.float32), cols[0:1], (0, item * share))
+    received = up(jnp.concatenate([total, col], axis=1))
+    total = odd_add(total + received[:, :rows_total], "bucket", bucket_bits)
+    both = odd_add(jnp.concatenate([total, received[:, rows_total:], col], axis=1), "item", item_bits)
+    lower = down(both[:, : rows_total + buckets_own])
+    total = jnp.where(odd, both[:, :rows_total], 0.0)
+
+    blocks = share // block_of(share, rows_total)
+    update = final(own, cols, right, [row, row_first, total, lower], codes, 1, True, rows_total, 0, blocks, blocks, [])
     pieces = gather_blocks(update, "item")
 
-    rows_pot, rows_scale, cols_scale = own_rows(row), own_rows(row_scale), jnp.exp(-col)
-    grads = []
-    for part in range(4):
-        at = slice(part * rows_own // 4, (part + 1) * rows_own // 4)
-        grads.append(
-            final(
-                codes_t[:, at], rows_pot[:, at], rows_scale[:, at], centroids_t, col, cols_scale, centroids_t, 2, False
-            )
-        )
+    mass = (total + lower[:, :rows_total]) * float(rows_total)
+    col = jnp.where(odd, both[:, rows_total + buckets_own :], lower[:, rows_total:])
+    p_rows = own_rows(jnp.concatenate([row + log_rows, mass * jnp.exp(row_first - row)], axis=0))
+    blocks = rows_own // block_of(rows_own, buckets_own)
+    halves = []
+    for half in range(2):
+        held = []
+        for part in range(2):
+            steps = blocks // 4
+            held = [
+                final(
+                    codes_t, p_rows, centroids_t, [col], None, 2, False, rows_total,
+                    (2 * half + part) * steps, steps, 2 * steps, held,
+                )
+            ]
+        grad = held[0]
+        for bit in bits_of("bucket"):
+            received = swap(grad, "bucket", bit)
+            grad = grad + received
+        halves.append(grad)
     new_centroids = place(pieces, item)
-    grad_codes = jnp.concatenate(grads, axis=1)
-    for bit in bits_of("bucket"):
-        grad_codes = grad_codes + swap(grad_codes, "bucket", bit)
-    return (grad_codes.T, new_centroids.T)
+    return (jnp.concatenate(halves, axis=1).T, new_centroids.T)
 
 
 def solution(mesh):

time: 243 us -> 268 us (1.10)
  waiting for transfers between devices: 66.6 us -> 85.7 us
  starting transfers between devices: 46.8 us -> 57.6 us
  local copies, waits for them, and re-layouts: 10.9 us -> 6.61 us
    ppermute x0 -> x24, waiting for transfers between devices: none -> 60.8 us  [the longest x4 56.9 us: down(): lax.ppermute(value, 'bucket', [(k + 1, k) for k in range(0, lax.axis_size...]
    ppermute x37 -> x19, waiting for transfers between devices: 66.6 us -> 24.9 us  [swap(): return lax.ppermute(value, axis, [(k, k ^ bit) for k in range(size)])]
    ppermute x0 -> x24, starting transfers between devices: none -> 25.4 us  [the longest x16 10.6 us: odd_swap(): return lax.ppermute(value, ('item', 'bucket'), pairs)]
    ppermute x37 -> x19, starting transfers between devices: 46.8 us -> 32.2 us  [swap(): return lax.ppermute(value, axis, [(k, k ^ bit) for k in range(size)])]
    slice x5 -> x1, local copies, waits for them, and re-layouts: 4.94 us -> 0.01 us  [step(): lower = down(both[:, :rows_total + buckets_own])]
    exp x2 -> x0, other arithmetic: 2.91 us -> none  [the longest x1 1.54 us: step(): jnp.exp(-col)]
  transfers between devices with their start and end apart: 37 -> 43, of which waited for: 24 -> 13; matrix products, arithmetic and copies ran while one was open for 5% -> 2% of each run, Pallas kernels for 17% -> 10%
where the time goes in v4:
time: 268 us; the launch traced here: 267 us
  Pallas kernels  105 us (39%)
  waiting for transfers between devices  85.7 us (32%)
  starting transfers between devices  57.6 us (21%)
  other arithmetic  10.7 us (4%)
  local copies, waits for them, and re-layouts  6.61 us (2%)
    ppermute x4, waiting for transfers between devices, down(): lax.ppermute(value, 'bucket', [(k + 1, k) for k in range(0, lax.axis_size...  56.9 us
    pallas_call x3, Pallas kernels, sink(): pl.pallas_call(functools.partial(sink_kernel, first=first, rows_total=row...  42.8 us
    pallas_call x5, Pallas kernels, final(): pl.pallas_call(functools.partial(final_kernel, repeat=repeat, update=upda...  38.3 us
    ppermute x19, starting transfers between devices, swap(): return lax.ppermute(value, axis, [(k, k ^ bit) for k in range(size)])  32.2 us
    ppermute x19, waiting for transfers between devices, swap(): return lax.ppermute(value, axis, [(k, k ^ bit) for k in range(size)])  24.9 us
    pallas_call x2, Pallas kernels, lse(): pl.pallas_call(functools.partial(lse_kernel, repeat=repeat, count=count),...  14.6 us
    ppermute x16, starting transfers between devices, odd_swap(): return lax.ppermute(value, ('item', 'bucket'), pairs)  10.6 us
    ppermute x4, starting transfers between devices, up(): lax.ppermute(value, 'bucket', [(k, k + 1) for k in range(0, lax.axis_size...  9.71 us
  transfers between devices with their start and end apart: 43, of which 13 were waited for; matrix products, arithmetic and copies ran while one was open for 2% of the time, Pallas kernels for 10%

profile of v4, /device:TPU:0, one launch (start us, length us, event | category | flops | bytes accessed | tf_op | source)
XLA Modules:
  0.0 266.8 jit_solution(4838599297643003776)
XLA Ops:
  0.6 7.3 %row_lse.2.rest_0_ = f32[2,1024]{1,0:T(2,128)} custom-call(bf16[64,1024]{1,0:T(8,128)(2,1)} %bitcast.12, bf16[64,8192]{1,0:T(8,128)(2,1)} %bitcast.18), custom_call_target="tpu_custom_call" | custom-call | flops 2147483648 | bytes 4194304 | tf_op jit(solution)/shard_map/row_lse/pallas_call | solution.py:342
  7.9 7.3 %row_lse.3 = f32[2,1024]{1,0:T(2,128)} custom-call(bf16[64,1024]{1,0:T(8,128)(2,1)} %bitcast.13, bf16[64,8192]{1,0:T(8,128)(2,1)} %bitcast.19, f32[2,1024]{1,0:T(2,128)} %row_lse.2.rest_0_), custom_call_target="tpu_custom_call", output_to_operand_aliasing={{}: (2, {})} | custom-call | flops 2147483648 | bytes 4194304 | tf_op jit(solution)/shard_map/row_lse/pallas_call | solution.py:342
  15.3 2.4 collective-permute-start.8
  20.2 3.5 %collective-permute-start.3 = (f32[64,512]{1,0:T(8,128)S(1)}, f32[64,512]{1,0:T(8,128)S(1)}, u32[]{:S(2)}, u32[]{:S(2)}) collective-permute-start(f32[64,512]{1,0:T(8,128)S(1)} %convert_bitcast_fusion.refs_0_), channel_id=1, source_target_pairs={{0,16},{4,20},{8,24},{12,28},{16,0},{20,4},{24,8},{28,12},{1,17},{... | collective-permute-start | bytes 393224 | tf_op jit(solution)/shard_map/ppermute | solution.py:25
  23.7 1.6 collective-permute-start.1
  26.8 4.4 %collective-permute-start.5 = (f32[64,512]{1,0:T(8,128)S(1)}, f32[64,512]{1,0:T(8,128)S(1)}, u32[]{:S(2)}, u32[]{:S(2)}) collective-permute-start(f32[64,512]{1,0:T(8,128)S(1)} %collective-permute-done.3.refs_4_), channel_id=1, source_target_pairs={{0,8},{4,12},{8,0},{12,4},{16,24},{20,28},{24,16},{28,20},{1,9},{5... | collective-permute-start | bytes 393224 | tf_op jit(solution)/shard_map/ppermute | solution.py:25
  33.3 1.7 collective-permute-done.5.refs_6_
  38.5 1.9 collective-permute-done.2.refs_3_
  40.5 2.7 %collective-permute-done.6.refs_7_ = f32[64,512]{1,0:T(8,128)S(1)} collective-permute-done((f32[64,512]{1,0:T(8,128)S(1)}, f32[64,512]{1,0:T(8,128)S(1)}, u32[]{:S(2)}, u32[]{:S(2)}) %collective-permute-start.6) | collective-permute-done | bytes 131104 | tf_op jit(solution)/shard_map/ppermute | solution.py:25
  43.8 2.3 shard_map.41.mine_ref
  46.1 9.1 %collective-permute-start.7 = (f32[64,4096]{1,0:T(8,128)}, f32[64,4096]{1,0:T(8,128)S(1)}, u32[]{:S(2)}, u32[]{:S(2)}) collective-permute-start(f32[64,4096]{1,0:T(8,128)} %shard_map.41.mine_ref), channel_id=1, source_target_pairs={{0,1},{1,0},{2,3},{3,2},{4,5},{5,4},{6,7},{7,6},{8,9},{9,8},{10,11... | collective-permute-start | bytes 3145736 | tf_op jit(solution)/shard_map/ppermute | solution.py:25
  57.2 1.6 dynamic-slice_bitcast_fusion.l_ref
  59.8 3.8 %shard_map.42 = (bf16[128,8192]{1,0:T(8,128)(2,1)}, bf16[64,8192]{1,0:T(8,128)(2,1)}) custom-call(s32[1]{0:T(128)} %bitcast.2.core_ref, f32[64,4096]{1,0:T(8,128)} %shard_map.41.mine_ref, f32[64,4096]{1,0:T(8,128)} %copy-done), custom_call_target="tpu_custom_call" | custom-call | bytes 4194304 | tf_op jit(solution)/shard_map/pallas_call | solution.py:427
  64.2 17.9 %sinkhorn_first.1 = (f32[1,8192]{1,0:T(1,128)}, f32[8,1024]{1,0:T(8,128)}, f32[1,8192]{1,0:T(1,128)}) custom-call(bf16[64,1024]{1,0:T(8,128)(2,1)} %dynamic-slice_bitcast_fusion.l_ref, bf16[128,8192]{1,0:T(8,128)(2,1)} %get-tuple-element.13.w_ref, f32[1,8192]{1,0:T(1,128)} %get-tuple-element.30.one_ref, f32[1,8192]{1,0:T(1,128)} %copy-done.21), custom_call_target="tpu_custom_call" | custom-call | flops 4294967296 | bytes 4194304 | tf_op jit(solution)/shard_map/sinkhorn_first/pallas_call | solution.py:364
  82.2 3.0 %collective-permute-start.14 = (f32[1,8192]{1,0:T(1,128)}, f32[1,8192]{1,0:T(1,128)S(1)}, u32[]{:S(2)}, u32[]{:S(2)}) collective-permute-start(f32[1,8192]{1,0:T(1,128)} %get-tuple-element.14), channel_id=1, source_target_pairs={{0,1},{2,3},{4,5},{6,7},{8,9},{10,11},{12,13},{14,15},{16,17},{18,... | collective-permute-start | bytes 98312 | tf_op jit(solution)/shard_map/ppermute | solution.py:44
  91.9 18.2 %collective-permute-done.19.two_ref = f32[1,8192]{1,0:T(1,128)S(1)} collective-permute-done((f32[1,8192]{1,0:T(1,128)S(1)}, f32[1,8192]{1,0:T(1,128)S(1)}, u32[]{:S(2)}, u32[]{:S(2)}) %collective-permute-start.19) | collective-permute-done | bytes 32800 | tf_op jit(solution)/shard_map/ppermute | solution.py:48
  110.6 12.4 %sinkhorn_next.2 = (f32[1,8192]{1,0:T(1,128)}, f32[8,1024]{1,0:T(8,128)}, f32[1,8192]{1,0:T(1,128)}) custom-call(bf16[64,1024]{1,0:T(8,128)(2,1)} %dynamic-slice_bitcast_fusion.l_ref, bf16[128,8192]{1,0:T(8,128)(2,1)} %get-tuple-element.13.w_ref, f32[1,8192]{1,0:T(1,128)} %get-tuple-element.28.one_ref, f32[1,8192]{1,0:T(1,128)} %copy-done.23, ...), custom_call_target="tpu_custom_call" | custom-call | flops 4294967296 | bytes 4194304 | tf_op jit(solution)/shard_map/sinkhorn_next/pallas_call | solution.py:364
  123.1 2.1 collective-permute-start.20
  131.8 18.0 %collective-permute-done.25.two_ref = f32[1,8192]{1,0:T(1,128)S(1)} collective-permute-done((f32[1,8192]{1,0:T(1,128)S(1)}, f32[1,8192]{1,0:T(1,128)S(1)}, u32[]{:S(2)}, u32[]{:S(2)}) %collective-permute-start.25) | collective-permute-done | bytes 32800 | tf_op jit(solution)/shard_map/ppermute | solution.py:48
  150.4 12.5 %sinkhorn_next.3 = (f32[1,8192]{1,0:T(1,128)}, f32[8,1024]{1,0:T(8,128)}, f32[1,8192]{1,0:T(1,128)}) custom-call(bf16[64,1024]{1,0:T(8,128)(2,1)} %dynamic-slice_bitcast_fusion.l_ref, bf16[128,8192]{1,0:T(8,128)(2,1)} %get-tuple-element.13.w_ref, f32[1,8192]{1,0:T(1,128)} %get-tuple-element.26.one_ref, f32[1,8192]{1,0:T(1,128)} %copy-done.22, ...), custom_call_target="tpu_custom_call" | custom-call | flops 4294967296 | bytes 4194304 | tf_op jit(solution)/shard_map/sinkhorn_next/pallas_call | solution.py:364
  164.4 2.3 collective-permute-start.26
  172.8 20.7 %collective-permute-done.31.rest_3_ = f32[1,16384]{1,0:T(1,128)S(1)} collective-permute-done((f32[1,16384]{1,0:T(1,128)S(1)}, f32[1,16384]{1,0:T(1,128)S(1)}, u32[]{:S(2)}, u32[]{:S(2)}) %collective-permute-start.31) | collective-permute-done | bytes 65568 | tf_op jit(solution)/shard_map/ppermute | solution.py:48
  195.1 16.6 %centroid_update.1.refs_0_ = f32[64,1024]{1,0:T(8,128)} custom-call(bf16[64,1024]{1,0:T(8,128)(2,1)} %dynamic-slice_bitcast_fusion.l_ref, f32[8,1024]{1,0:T(8,128)} %get-tuple-element.22.p_ref, bf16[128,8192]{1,0:T(8,128)(2,1)} %get-tuple-element.13.w_ref, f32[1,8192]{1,0:T(1,128)} %get-tuple-element.20.rest_0_, f32[1,8192]{1,0:T(1,128)} %get-tuple-element.16.rest_1_, ...), custom_call_target="tpu_custom_call" | custom-call | flops 8589934592 | bytes 4194304 | tf_op jit(solution)/shard_map/centroid_update/pallas_call | solution.py:397
  212.5 5.4 %code_gradient.4.rest_1_ = f32[64,512]{1,0:T(8,128)} custom-call(bf16[64,1024]{1,0:T(8,128)(2,1)} %bitcast.14, f32[2,1024]{1,0:T(2,128)} %pad_maximum_fusion.3.p_ref, bf16[64,8192]{1,0:T(8,128)(2,1)} %bitcast.20, f32[1,8192]{1,0:T(1,128)} %get-tuple-element.34.rest_0_), custom_call_target="tpu_custom_call" | custom-call | flops 2147483648 | bytes 4194304 | tf_op jit(solution)/shard_map/code_gradient/pallas_call | solution.py:397
  217.9 5.4 %code_gradient.5 = f32[64,512]{1,0:T(8,128)} custom-call(bf16[64,1024]{1,0:T(8,128)(2,1)} %bitcast.15, f32[2,1024]{1,0:T(2,128)} %pad_maximum_fusion.3.p_ref, bf16[64,8192]{1,0:T(8,128)(2,1)} %bitcast.21, f32[1,8192]{1,0:T(1,128)} %get-tuple-element.34.rest_0_, f32[64,512]{1,0:T(8,128)} %code_gradient.4.rest_1_), custom_call_target="tpu_custom_call", output_to_operand_aliasing={{}: (4, {})} | custom-call | flops 2147483648 | bytes 4194304 | tf_op jit(solution)/shard_map/code_gradient/pallas_call | solution.py:397
  223.4 5.4 %code_gradient.6.rest_1_ = f32[64,512]{1,0:T(8,128)} custom-call(bf16[64,1024]{1,0:T(8,128)(2,1)} %bitcast.16, f32[2,1024]{1,0:T(2,128)} %pad_maximum_fusion.3.p_ref, bf16[64,8192]{1,0:T(8,128)(2,1)} %bitcast.22, f32[1,8192]{1,0:T(1,128)} %get-tuple-element.34.rest_0_), custom_call_target="tpu_custom_call" | custom-call | flops 2147483648 | bytes 4194304 | tf_op jit(solution)/shard_map/code_gradient/pallas_call | solution.py:397
  228.9 1.9 collective-permute-start.41
  230.8 5.4 %code_gradient.7 = f32[64,512]{1,0:T(8,128)} custom-call(bf16[64,1024]{1,0:T(8,128)(2,1)} %bitcast.17, f32[2,1024]{1,0:T(2,128)} %pad_maximum_fusion.3.p_ref, bf16[64,8192]{1,0:T(8,128)(2,1)} %bitcast.23, f32[1,8192]{1,0:T(1,128)} %get-tuple-element.34.rest_0_, f32[64,512]{1,0:T(8,128)} %code_gradient.6.rest_1_), custom_call_target="tpu_custom_call", output_to_operand_aliasing={{}: (4, {})} | custom-call | flops 2147483648 | bytes 4194304 | tf_op jit(solution)/shard_map/code_gradient/pallas_call | solution.py:397
  243.7 4.3 %collective-permute-done.35 = f32[64,512]{1,0:T(8,128)S(1)} collective-permute-done((f32[64,512]{1,0:T(8,128)S(1)}, f32[64,512]{1,0:T(8,128)S(1)}, u32[]{:S(2)}, u32[]{:S(2)}) %collective-permute-start.35) | collective-permute-done | bytes 131104 | tf_op jit(solution)/shard_map/ppermute | solution.py:25
  248.8 9.6 %collective-permute-done.38.refs_3_ = f32[64,1024]{1,0:T(8,128)S(1)} collective-permute-done((f32[64,1024]{1,0:T(8,128)S(1)}, f32[64,1024]{1,0:T(8,128)S(1)}, u32[]{:S(2)}, u32[]{:S(2)}) %collective-permute-start.38) | collective-permute-done | bytes 262176 | tf_op jit(solution)/shard_map/ppermute | solution.py:25
  258.5 4.6 %collective-permute-done.42.refs_7_ = f32[64,1024]{1,0:T(8,128)S(1)} collective-permute-done((f32[64,1024]{1,0:T(8,128)S(1)}, f32[64,1024]{1,0:T(8,128)S(1)}, u32[]{:S(2)}, u32[]{:S(2)}) %collective-permute-start.42) | collective-permute-done | bytes 262176 | tf_op jit(solution)/shard_map/ppermute | solution.py:25
  263.9 3.0 %shard_map.43 = f32[64,8192]{1,0:T(8,128)} custom-call(s32[1]{0:T(128)} %bitcast.3.item_ref, f32[64,1024]{1,0:T(8,128)} %centroid_update.1.refs_0_, f32[64,1024]{1,0:T(8,128)} %copy-done.6, f32[64,1024]{1,0:T(8,128)} %copy-done.4, f32[64,1024]{1,0:T(8,128)} %copy-done.8, f32[64,1024]{1,0:T(8,128)} %copy-done.3, f32[64,1024]{1,0:T(8,128)} %copy-done.7, ...), custom_call_target="tpu_custom_call" | custom-call | bytes 4194304 | tf_op jit(solution)/shard_map/pallas_call | solution.py:427
  (154 shorter events, 47.1 us)
Async XLA Ops:
  15.3 3.4 %collective-permute-start.8 = (f32[2,1024]{1,0:T(2,128)}, f32[2,1024]{1,0:T(2,128)S(1)}, u32[]{:S(2)}, u32[]{:S(2)}) collective-permute-start(f32[2,1024]{1,0:T(2,128)} %row_lse.3), channel_id=1, source_target_pairs={{0,1},{2,3},{4,5},{6,7},{8,9},{10,11},{12,13},{14,15},{16,17},{18,... | collective-permute-start | bytes 24584 | tf_op jit(solution)/shard_map/ppermute | solution.py:44
  19.5 7.3 %collective-permute-start.9 = (f32[2,1024]{1,0:T(2,128)S(1)}, f32[2,1024]{1,0:T(2,128)S(1)}, u32[]{:S(2)}, u32[]{:S(2)}) collective-permute-start(f32[2,1024]{1,0:T(2,128)S(1)} %pad_maximum_fusion.2), channel_id=1, source_target_pairs={{1,3},{3,1},{5,7},{7,5},{9,11},{11,9},{13,15},{15,13},{17,19},{19,... | collective-permute-start | bytes 24584 | tf_op jit(solution)/shard_map/ppermute | solution.py:40
  20.2 6.6 %collective-permute-start.3 = (f32[64,512]{1,0:T(8,128)S(1)}, f32[64,512]{1,0:T(8,128)S(1)}, u32[]{:S(2)}, u32[]{:S(2)}) collective-permute-start(f32[64,512]{1,0:T(8,128)S(1)} %convert_bitcast_fusion.refs_0_), channel_id=1, source_target_pairs={{0,16},{4,20},{8,24},{12,28},{16,0},{20,4},{24,8},{28,12},{1,17},{... | collective-permute-start | bytes 393224 | tf_op jit(solution)/shard_map/ppermute | solution.py:25
  23.7 9.1 %collective-permute-start.1 = (f32[64,512]{1,0:T(8,128)S(1)}, f32[64,512]{1,0:T(8,128)S(1)}, u32[]{:S(2)}, u32[]{:S(2)}) collective-permute-start(f32[64,512]{1,0:T(8,128)S(1)} %convert_bitcast_fusion.refs_0_), channel_id=1, source_target_pairs={{0,8},{4,12},{8,0},{12,4},{16,24},{20,28},{24,16},{28,20},{1,9},{5... | collective-permute-start | bytes 393224 | tf_op jit(solution)/shard_map/ppermute | solution.py:25
  25.3 13.2 %collective-permute-start = (f32[64,512]{1,0:T(8,128)S(1)}, f32[64,512]{1,0:T(8,128)S(1)}, u32[]{:S(2)}, u32[]{:S(2)}) collective-permute-start(f32[64,512]{1,0:T(8,128)S(1)} %convert_bitcast_fusion.refs_0_), channel_id=1, source_target_pairs={{0,4},{4,0},{8,12},{12,8},{16,20},{20,16},{24,28},{28,24},{1,5},{5... | collective-permute-start | bytes 393224 | tf_op jit(solution)/shard_map/ppermute | solution.py:25
  26.8 8.2 %collective-permute-start.5 = (f32[64,512]{1,0:T(8,128)S(1)}, f32[64,512]{1,0:T(8,128)S(1)}, u32[]{:S(2)}, u32[]{:S(2)}) collective-permute-start(f32[64,512]{1,0:T(8,128)S(1)} %collective-permute-done.3.refs_4_), channel_id=1, source_target_pairs={{0,8},{4,12},{8,0},{12,4},{16,24},{20,28},{24,16},{28,20},{1,9},{5... | collective-permute-start | bytes 393224 | tf_op jit(solution)/shard_map/ppermute | solution.py:25
  31.2 7.3 %collective-permute-start.4 = (f32[64,512]{1,0:T(8,128)S(1)}, f32[64,512]{1,0:T(8,128)S(1)}, u32[]{:S(2)}, u32[]{:S(2)}) collective-permute-start(f32[64,512]{1,0:T(8,128)S(1)} %collective-permute-done.3.refs_4_), channel_id=1, source_target_pairs={{0,4},{4,0},{8,12},{12,8},{16,20},{20,16},{24,28},{28,24},{1,5},{5... | collective-permute-start | bytes 393224 | tf_op jit(solution)/shard_map/ppermute | solution.py:25
  32.8 7.7 %collective-permute-start.2 = (f32[64,512]{1,0:T(8,128)S(1)}, f32[64,512]{1,0:T(8,128)S(1)}, u32[]{:S(2)}, u32[]{:S(2)}) collective-permute-start(f32[64,512]{1,0:T(8,128)S(1)} %collective-permute-done.1.refs_2_), channel_id=1, source_target_pairs={{0,4},{4,0},{8,12},{12,8},{16,20},{20,16},{24,28},{28,24},{1,5},{5... | collective-permute-start | bytes 393224 | tf_op jit(solution)/shard_map/ppermute | solution.py:25
  35.0 8.2 %collective-permute-start.6 = (f32[64,512]{1,0:T(8,128)S(1)}, f32[64,512]{1,0:T(8,128)S(1)}, u32[]{:S(2)}, u32[]{:S(2)}) collective-permute-start(f32[64,512]{1,0:T(8,128)S(1)} %collective-permute-done.5.refs_6_), channel_id=1, source_target_pairs={{0,4},{4,0},{8,12},{12,8},{16,20},{20,16},{24,28},{28,24},{1,5},{5... | collective-permute-start | bytes 393224 | tf_op jit(solution)/shard_map/ppermute | solution.py:25
  37.8 17.5 %collective-permute-start.12 = (f32[1,8192]{1,0:T(1,128)S(1)}, f32[1,8192]{1,0:T(1,128)S(1)}, u32[]{:S(2)}, u32[]{:S(2)}) collective-permute-start(f32[1,8192]{1,0:T(1,128)S(1)} %add.114), channel_id=1, source_target_pairs={{1,17},{3,19},{5,21},{7,23},{9,25},{11,27},{13,29},{15,31},{17,1},... | collective-permute-start | bytes 98312 | tf_op jit(solution)/shard_map/ppermute | solution.py:40
  46.1 12.7 %collective-permute-start.7 = (f32[64,4096]{1,0:T(8,128)}, f32[64,4096]{1,0:T(8,128)S(1)}, u32[]{:S(2)}, u32[]{:S(2)}) collective-permute-start(f32[64,4096]{1,0:T(8,128)} %shard_map.41.mine_ref), channel_id=1, source_target_pairs={{0,1},{1,0},{2,3},{3,2},{4,5},{5,4},{6,7},{7,6},{8,9},{9,8},{10,11... | collective-permute-start | bytes 3145736 | tf_op jit(solution)/shard_map/ppermute | solution.py:25
  56.0 7.7 %collective-permute-start.13 = (f32[1,8192]{1,0:T(1,128)S(1)}, f32[1,8192]{1,0:T(1,128)S(1)}, u32[]{:S(2)}, u32[]{:S(2)}) collective-permute-start(f32[1,8192]{1,0:T(1,128)S(1)} %get-tuple-element.31), channel_id=1, source_target_pairs={{1,0},{3,2},{5,4},{7,6},{9,8},{11,10},{13,12},{15,14},{17,16},{19,... | collective-permute-start | bytes 98312 | tf_op jit(solution)/shard_map/ppermute | solution.py:48
  82.2 4.1 %collective-permute-start.14 = (f32[1,8192]{1,0:T(1,128)}, f32[1,8192]{1,0:T(1,128)S(1)}, u32[]{:S(2)}, u32[]{:S(2)}) collective-permute-start(f32[1,8192]{1,0:T(1,128)} %get-tuple-element.14), channel_id=1, source_target_pairs={{0,1},{2,3},{4,5},{6,7},{8,9},{10,11},{12,13},{14,15},{16,17},{18,... | collective-permute-start | bytes 98312 | tf_op jit(solution)/shard_map/ppermute | solution.py:44
  90.6 19.5 %collective-permute-start.19 = (f32[1,8192]{1,0:T(1,128)S(1)}, f32[1,8192]{1,0:T(1,128)S(1)}, u32[]{:S(2)}, u32[]{:S(2)}) collective-permute-start(f32[1,8192]{1,0:T(1,128)S(1)} %get-tuple-element.29), channel_id=1, source_target_pairs={{1,0},{3,2},{5,4},{7,6},{9,8},{11,10},{13,12},{15,14},{17,16},{19,... | collective-permute-start | bytes 98312 | tf_op jit(solution)/shard_map/ppermute | solution.py:48
  123.1 3.1 %collective-permute-start.20 = (f32[1,8192]{1,0:T(1,128)}, f32[1,8192]{1,0:T(1,128)S(1)}, u32[]{:S(2)}, u32[]{:S(2)}) collective-permute-start(f32[1,8192]{1,0:T(1,128)} %get-tuple-element.17), channel_id=1, source_target_pairs={{0,1},{2,3},{4,5},{6,7},{8,9},{10,11},{12,13},{14,15},{16,17},{18,... | collective-permute-start | bytes 98312 | tf_op jit(solution)/shard_map/ppermute | solution.py:44
  130.5 19.3 %collective-permute-start.25 = (f32[1,8192]{1,0:T(1,128)S(1)}, f32[1,8192]{1,0:T(1,128)S(1)}, u32[]{:S(2)}, u32[]{:S(2)}) collective-permute-start(f32[1,8192]{1,0:T(1,128)S(1)} %get-tuple-element.27), channel_id=1, source_target_pairs={{1,0},{3,2},{5,4},{7,6},{9,8},{11,10},{13,12},{15,14},{17,16},{19,... | collective-permute-start | bytes 98312 | tf_op jit(solution)/shard_map/ppermute | solution.py:48
  164.4 3.0 %collective-permute-start.26 = (f32[1,16384]{1,0:T(1,128)S(1)}, f32[1,16384]{1,0:T(1,128)S(1)}, u32[]{:S(2)}, u32[]{:S(2)}) collective-permute-start(f32[1,16384]{1,0:T(1,128)S(1)} %pad_maximum_fusion.1), channel_id=1, source_target_pairs={{0,1},{2,3},{4,5},{6,7},{8,9},{10,11},{12,13},{14,15},{16,17},{18,... | collective-permute-start | bytes 196616 | tf_op jit(solution)/shard_map/ppermute | solution.py:44
  169.0 0.7 collective-permute-start.28
  169.9 0.7 collective-permute-start.29
  170.7 0.7 collective-permute-start.30
  171.5 22.0 %collective-permute-start.31 = (f32[1,16384]{1,0:T(1,128)S(1)}, f32[1,16384]{1,0:T(1,128)S(1)}, u32[]{:S(2)}, u32[]{:S(2)}) collective-permute-start(f32[1,16384]{1,0:T(1,128)S(1)} %slice.78), channel_id=1, source_target_pairs={{1,0},{3,2},{5,4},{7,6},{9,8},{11,10},{13,12},{15,14},{17,16},{19,... | collective-permute-start | bytes 196616 | tf_op jit(solution)/shard_map/ppermute | solution.py:48
  211.7 17.2 %collective-permute-start.39 = (f32[64,1024]{1,0:T(8,128)}, f32[64,1024]{1,0:T(8,128)S(1)}, u32[]{:S(2)}, u32[]{:S(2)}) collective-permute-start(f32[64,1024]{1,0:T(8,128)} %centroid_update.1.refs_0_), channel_id=1, source_target_pairs={{0,16},{4,20},{8,24},{12,28},{16,0},{20,4},{24,8},{28,12},{1,17},{... | collective-permute-start | bytes 786440 | tf_op jit(solution)/shard_map/ppermute | solution.py:25
  211.7 28.4 %collective-permute-start.37 = (f32[64,1024]{1,0:T(8,128)}, f32[64,1024]{1,0:T(8,128)S(1)}, u32[]{:S(2)}, u32[]{:S(2)}) collective-permute-start(f32[64,1024]{1,0:T(8,128)} %centroid_update.1.refs_0_), channel_id=1, source_target_pairs={{0,8},{4,12},{8,0},{12,4},{16,24},{20,28},{24,16},{28,20},{1,9},{5... | collective-permute-start | bytes 786440 | tf_op jit(solution)/shard_map/ppermute | solution.py:25
  223.3 13.2 %collective-permute-start.32 = (f32[64,512]{1,0:T(8,128)}, f32[64,512]{1,0:T(8,128)S(1)}, u32[]{:S(2)}, u32[]{:S(2)}) collective-permute-start(f32[64,512]{1,0:T(8,128)} %code_gradient.5), channel_id=1, source_target_pairs={{0,1},{1,0},{2,3},{3,2},{4,5},{5,4},{6,7},{7,6},{8,9},{9,8},{10,11... | collective-permute-start | bytes 393224 | tf_op jit(solution)/shard_map/ppermute | solution.py:25
  228.9 12.6 %collective-permute-start.41 = (f32[64,1024]{1,0:T(8,128)S(1)}, f32[64,1024]{1,0:T(8,128)S(1)}, u32[]{:S(2)}, u32[]{:S(2)}) collective-permute-start(f32[64,1024]{1,0:T(8,128)S(1)} %collective-permute-done.39.refs_4_), channel_id=1, source_target_pairs={{0,8},{4,12},{8,0},{12,4},{16,24},{20,28},{24,16},{28,20},{1,9},{5... | collective-permute-start | bytes 786440 | tf_op jit(solution)/shard_map/ppermute | solution.py:25
  236.2 3.2 %collective-permute-start.34 = (f32[64,512]{1,0:T(8,128)}, f32[64,512]{1,0:T(8,128)S(1)}, u32[]{:S(2)}, u32[]{:S(2)}) collective-permute-start(f32[64,512]{1,0:T(8,128)} %code_gradient.7), channel_id=1, source_target_pairs={{0,1},{1,0},{2,3},{3,2},{4,5},{5,4},{6,7},{7,6},{8,9},{9,8},{10,11... | collective-permute-start | bytes 393224 | tf_op jit(solution)/shard_map/ppermute | solution.py:25
  236.5 6.6 %collective-permute-start.33 = (f32[64,512]{1,0:T(8,128)S(1)}, f32[64,512]{1,0:T(8,128)S(1)}, u32[]{:S(2)}, u32[]{:S(2)}) collective-permute-start(f32[64,512]{1,0:T(8,128)S(1)} %add.134), channel_id=1, source_target_pairs={{0,2},{1,3},{2,0},{3,1},{4,6},{5,7},{6,4},{7,5},{8,10},{9,11},{10,... | collective-permute-start | bytes 393224 | tf_op jit(solution)/shard_map/ppermute | solution.py:25
  238.0 10.8 %collective-permute-start.36 = (f32[64,1024]{1,0:T(8,128)S(1)}, f32[64,1024]{1,0:T(8,128)S(1)}, u32[]{:S(2)}, u32[]{:S(2)}) collective-permute-start(f32[64,1024]{1,0:T(8,128)S(1)} %copy-done.2), channel_id=1, source_target_pairs={{0,4},{4,0},{8,12},{12,8},{16,20},{20,16},{24,28},{28,24},{1,5},{5... | collective-permute-start | bytes 786440 | tf_op jit(solution)/shard_map/ppermute | solution.py:25
  239.5 19.0 %collective-permute-start.40 = (f32[64,1024]{1,0:T(8,128)S(1)}, f32[64,1024]{1,0:T(8,128)S(1)}, u32[]{:S(2)}, u32[]{:S(2)}) collective-permute-start(f32[64,1024]{1,0:T(8,128)S(1)} %collective-permute-done.39.refs_4_), channel_id=1, source_target_pairs={{0,4},{4,0},{8,12},{12,8},{16,20},{20,16},{24,28},{28,24},{1,5},{5... | collective-permute-start | bytes 786440 | tf_op jit(solution)/shard_map/ppermute | solution.py:25
  240.1 18.4 %collective-permute-start.38 = (f32[64,1024]{1,0:T(8,128)S(1)}, f32[64,1024]{1,0:T(8,128)S(1)}, u32[]{:S(2)}, u32[]{:S(2)}) collective-permute-start(f32[64,1024]{1,0:T(8,128)S(1)} %collective-permute-done.37.refs_2_), channel_id=1, source_target_pairs={{0,4},{4,0},{8,12},{12,8},{16,20},{20,16},{24,28},{28,24},{1,5},{5... | collective-permute-start | bytes 786440 | tf_op jit(solution)/shard_map/ppermute | solution.py:25
  241.5 21.6 %collective-permute-start.42 = (f32[64,1024]{1,0:T(8,128)S(1)}, f32[64,1024]{1,0:T(8,128)S(1)}, u32[]{:S(2)}, u32[]{:S(2)}) collective-permute-start(f32[64,1024]{1,0:T(8,128)S(1)} %collective-permute-done.41.refs_6_), channel_id=1, source_target_pairs={{0,4},{4,0},{8,12},{12,8},{16,20},{20,16},{24,28},{28,24},{1,5},{5... | collective-permute-start | bytes 786440 | tf_op jit(solution)/shard_map/ppermute | solution.py:25
  243.1 5.0 %collective-permute-start.35 = (f32[64,512]{1,0:T(8,128)S(1)}, f32[64,512]{1,0:T(8,128)S(1)}, u32[]{:S(2)}, u32[]{:S(2)}) collective-permute-start(f32[64,512]{1,0:T(8,128)S(1)} %add.136), channel_id=1, source_target_pairs={{0,2},{1,3},{2,0},{3,1},{4,6},{5,7},{6,4},{7,5},{8,10},{9,11},{10,... | collective-permute-start | bytes 393224 | tf_op jit(solution)/shard_map/ppermute | solution.py:25
  (35 other events, 234.1 us)

commit v5 on v4

--- a/solution.py
+++ b/solution.py
@@ -30,29 +30,34 @@
     return [1 << k for k in range(size.bit_length() - 1)]
 
 
-def odd_swap(value, axis, bit):
+def joint_swap(value, flips):
     items, buckets = lax.axis_size("item"), lax.axis_size("bucket")
-    pairs = []
-    for item in range(items):
-        for bucket in range(1, buckets, 2):
-            other = (item ^ bit, bucket) if axis == "item" else (item, bucket ^ bit)
-            pairs.append((item * buckets + bucket, other[0] * buckets + other[1]))
+    item_bits = sum(bit for axis, bit in flips if axis == "item")
+    bucket_bits = sum(bit for axis, bit in flips if axis == "bucket")
+    pairs = [
+        (item * buckets + bucket, (item ^ item_bits) * buckets + (bucket ^ bucket_bits))
+        for item in range(items)
+        for bucket in range(buckets)
+    ]
     return lax.ppermute(value, ("item", "bucket"), pairs)
 
 
-def up(value):
-    return lax.ppermute(value, "bucket", [(k, k + 1) for k in range(0, lax.axis_size("bucket"), 2)])
-
-
-def down(value):
-    return lax.ppermute(value, "bucket", [(k + 1, k) for k in range(0, lax.axis_size("bucket"), 2)])
-
-
-def odd_add(value, axis, bits):
-    for bit in bits:
-        received = odd_swap(value, axis, bit)
-        value = value + received
-    return value
+def groups_of(flips):
+    pairs = [flips[k : k + 2] for k in range(0, len(flips), 2)]
+    return [[[pair[0]]] if len(pair) == 1 else [[pair[0]], [pair[1]], pair] for pair in pairs]
+
+
+def joined(terms):
+    if len(terms) == 4:
+        return (terms[0] + terms[1]) + (terms[2] + terms[3])
+    return terms[0] + terms[1]
+
+
+def exchanged(value, group):
+    terms = [value]
+    for flips in group:
+        terms.append(joint_swap(value, flips))
+    return terms
 
 
 def gather_blocks(value, axis):
@@ -194,8 +199,9 @@
 
 
 def sink_kernel(
-    l_ref, w_ref, one_ref, two_ref, *rest, first, rows_total, buckets_total, count
+    l_ref, w_ref, *rest, first, rows_total, buckets_total, count, terms
 ):
+    term_refs, rest = rest[:terms], rest[terms:]
     if not first:
         p_ref, q_ref, *rest = rest
     sums_ref, pot_ref, row_ref, y_ref, part_ref, high_ref, wide_ref, wpot_ref, acc_ref = rest
@@ -206,7 +212,7 @@
             acc_ref[...] = jnp.zeros(acc_ref.shape, jnp.float32)
 
             def prepare(at):
-                row = one_ref[0:1, at] + two_ref[0:1, at]
+                row = joined([term_ref[0:1, at] for term_ref in term_refs])
                 if not first:
                     row = q_ref[0:1, at] - jnp.log(row * float(rows_total))
                 row_ref[0:1, at] = row
@@ -262,10 +268,11 @@
     cases(count, run)
 
 
-def final_kernel(l_ref, p_ref, w_ref, *rest, repeat, update, rows_total):
+def final_kernel(l_ref, p_ref, w_ref, *rest, repeat, update, rows_total, terms):
     out_ref, wide_ref, wpot_ref, v_ref, acc_ref = rest[-5:]
     if update:
-        row_ref, start_ref, one_ref, two_ref, r_ref = rest[:5]
+        row_ref, start_ref, *term_refs = rest[: 2 + terms]
+        r_ref = rest[2 + terms]
     else:
         col_ref, r_ref = rest[0], w_ref
     block = l_ref.shape[1]
@@ -276,7 +283,7 @@
         def prepare(at):
             if update:
                 row = row_ref[0:1, at]
-                mass = (one_ref[0:1, at] + two_ref[0:1, at]) * float(rows_total)
+                mass = joined([term_ref[0:1, at] for term_ref in term_refs]) * float(rows_total)
                 v_ref[0:1, at] = mass * jnp.exp(start_ref[0:1, at] - row)
                 row = row + math.log(rows_total)
             else:
@@ -354,7 +361,7 @@
     )(left, right, *before)
 
 
-def sink(left, right, one, two, old, rows_total, buckets_total):
+def sink(left, right, terms, old, rows_total, buckets_total):
     (dim, rows), width = left.shape, right.shape[1]
     block = block_of(rows, width)
     count = rows // block
@@ -363,15 +370,15 @@
     pot_spec = pl.BlockSpec((8, block), lambda k: (0, jnp.minimum(k, count - 1)))
     return pl.pallas_call(
         functools.partial(
-            sink_kernel, first=first, rows_total=rows_total, buckets_total=buckets_total, count=count
+            sink_kernel, first=first, rows_total=rows_total, buckets_total=buckets_total, count=count,
+            terms=len(terms),
         ),
         grid=(count + 1,),
         in_specs=[
             pl.BlockSpec((dim, block), lambda k: (0, jnp.minimum(k, count - 1))),
             full(right),
-            line,
-            line,
         ]
+        + [line] * len(terms)
         + ([] if first else [pot_spec, line]),
         out_specs=[line, pot_spec, line],
         out_shape=[
@@ -385,7 +392,7 @@
         compiler_params=params(),
         cost_estimate=cost(rows, width, 1),
         name="sinkhorn_first" if first else "sinkhorn_next",
-    )(left, right, one, two, *old)
+    )(left, right, *terms, *old)
 
 
 def final(left, p_rows, right, lines, codes, repeat, update, rows_total, lead, steps, total, before):
@@ -395,7 +402,9 @@
     into = total - steps if before else 0
     extra = [codes] if update else []
     return pl.pallas_call(
-        functools.partial(final_kernel, repeat=repeat, update=update, rows_total=rows_total),
+        functools.partial(
+            final_kernel, repeat=repeat, update=update, rows_total=rows_total, terms=len(lines) - 2
+        ),
         grid=(steps,),
         in_specs=[
             pl.BlockSpec((dim, block), lambda k: (0, lead + k)),
@@ -459,7 +468,7 @@
     codes_t = code_rows.T
     centroids_t = centroids.T
 
-    def spread_rows(values):
+    def spread_rows(values, item):
         out = jnp.zeros((1, rows_total), jnp.float32)
         for half in range(2):
             piece = values[:, half * rows_half : (half + 1) * rows_half]
@@ -475,11 +484,8 @@
             axis=1,
         )
 
-    odd = core == 1
-    bucket_bits, item_bits = bits_of("bucket")[1:], bits_of("item")
-
-    def shared(value):
-        return jnp.where(odd, value, 0.0), down(value)
+    side_bits = [("bucket", bit) for bit in bits_of("bucket")[1:]]
+    item_bits = [("item", bit) for bit in bits_of("item")]
 
     own_half = lax.dynamic_slice_in_dim(codes_t, core * rows_half, rows_half, axis=1).astype(jnp.float32)
     pieces = gather_blocks(own_half, "item")
@@ -487,14 +493,25 @@
     held = []
     for part in range(2):
         held = [lse(codes_t, centroids_t, 2, part, 2, held)]
+
+    def merged(first, second):
+        highest = jnp.maximum(first[0:1], second[0:1])
+        summed = first[1:2] * jnp.exp(first[0:1] - highest) + second[1:2] * jnp.exp(second[0:1] - highest)
+        return jnp.concatenate([highest, summed], axis=0)
+
+    def potential(stats):
+        return -log_rows - (stats[0:1] + jnp.log(stats[1:2]))
+
     stats = held[0]
-    for step_bit in [1] + bucket_bits:
-        received = up(stats) if step_bit == 1 else odd_swap(stats, "bucket", step_bit)
-        highest = jnp.maximum(stats[0:1], received[0:1])
-        summed = stats[1:2] * jnp.exp(stats[0:1] - highest) + received[1:2] * jnp.exp(received[0:1] - highest)
-        stats = jnp.concatenate([highest, summed], axis=0)
-    first_own = -log_rows - (stats[0:1] + jnp.log(stats[1:2]))
-    one, two = shared(odd_add(spread_rows(first_own), "item", item_bits))
+    for flips in [[("bucket", 1)]] + [[flip] for flip in side_bits[:-1]]:
+        stats = merged(stats, joint_swap(stats, flips))
+    terms = exchanged(stats, groups_of([side_bits[-1], item_bits[0]])[0])
+    rows = spread_rows(potential(merged(terms[0], terms[1])), item)
+    rows = rows + spread_rows(potential(merged(terms[2], terms[3])), item ^ 1)
+    groups = groups_of(item_bits[1:])
+    for group in groups[:-1]:
+        rows = joined(exchanged(rows, group))
+    terms = exchanged(rows, groups[-1])
 
     mine = place(pieces, item)
     theirs = swap(mine, "bucket", 1)
@@ -512,41 +529,52 @@
     old = []
     row_first = None
     for iteration in range(ITERS):
-        total, cols, row = sink(own, right, one, two, old, rows_total, buckets_total)
+        total, cols, row = sink(own, right, terms, old, rows_total, buckets_total)
         old = [cols, row]
         if row_first is None:
             row_first = row
         if iteration < ITERS - 1:
-            total = total + up(total)
-            total = odd_add(odd_add(total, "bucket", bucket_bits), "item", item_bits)
-            one, two = shared(total)
+            total = total + swap(total, "bucket", 1)
+            groups = groups_of(side_bits + item_bits)
+            for group in groups[:-1]:
+                total = joined(exchanged(total, group))
+            terms = exchanged(total, groups[-1])
 
     col = lax.dynamic_update_slice(jnp.zeros((1, buckets_own), jnp.float32), cols[0:1], (0, item * share))
-    received = up(jnp.concatenate([total, col], axis=1))
-    total = odd_add(total + received[:, :rows_total], "bucket", bucket_bits)
-    both = odd_add(jnp.concatenate([total, received[:, rows_total:], col], axis=1), "item", item_bits)
-    lower = down(both[:, : rows_total + buckets_own])
-    total = jnp.where(odd, both[:, :rows_total], 0.0)
+    total = total + swap(total, "bucket", 1)
+    groups = groups_of(side_bits + item_bits)
+    for group in groups[:-1]:
+        sums, held_cols = [total], [col]
+        for flips in group:
+            alone = any(axis == "bucket" for axis, _ in flips)
+            sent = total if alone else jnp.concatenate([total, col], axis=1)
+            received = joint_swap(sent, flips)
+            sums.append(received[:, :rows_total])
+            if not alone:
+                held_cols.append(received[:, rows_total:])
+        total = joined(sums)
+        col = functools.reduce(jnp.add, held_cols)
+    terms = exchanged(jnp.concatenate([total, col], axis=1), groups[-1])
 
     blocks = share // block_of(share, rows_total)
-    update = final(own, cols, right, [row, row_first, total, lower], codes, 1, True, rows_total, 0, blocks, blocks, [])
+    update = final(
+        own, cols, right, [row, row_first, *terms], codes, 1, True, rows_total, 0, blocks, blocks, []
+    )
     pieces = gather_blocks(update, "item")
 
-    mass = (total + lower[:, :rows_total]) * float(rows_total)
-    col = jnp.where(odd, both[:, rows_total + buckets_own :], lower[:, rows_total:])
+    both = joined(terms)
+    mass, col = both[:, :rows_total] * float(rows_total), both[:, rows_total:]
     p_rows = own_rows(jnp.concatenate([row + log_rows, mass * jnp.exp(row_first - row)], axis=0))
     blocks = rows_own // block_of(rows_own, buckets_own)
     halves = []
-    for half in range(2):
+    done = 0
+    for sizes in [[blocks // 2], [blocks // 4, blocks // 4]]:
         held = []
-        for part in range(2):
-            steps = blocks // 4
+        for steps in sizes:
             held = [
-                final(
-                    codes_t, p_rows, centroids_t, [col], None, 2, False, rows_total,
-                    (2 * half + part) * steps, steps, 2 * steps, held,
-                )
+                final(codes_t, p_rows, centroids_t, [col], None, 2, False, rows_total, done, steps, sum(sizes), held)
             ]
+            done += steps
         grad = held[0]
         for bit in bits_of("bucket"):
             received = swap(grad, "bucket", bit)

time: 268 us -> 226 us (0.84)
  waiting for transfers between devices: 85.7 us -> 51.7 us
  starting transfers between devices: 57.6 us -> 52.4 us
    ppermute x24 -> x25, waiting for transfers between devices: 60.8 us -> 22.2 us  [joint_swap(): return lax.ppermute(value, ('item', 'bucket'), pairs)]
    ppermute x19 -> x22, starting transfers between devices: 32.2 us -> 20.2 us  [swap(): return lax.ppermute(value, axis, [(k, k ^ bit) for k in range(size)])]
    ppermute x24 -> x25, starting transfers between devices: 25.4 us -> 32.2 us  [joint_swap(): return lax.ppermute(value, ('item', 'bucket'), pairs)]
    ppermute x19 -> x22, waiting for transfers between devices: 24.9 us -> 29.5 us  [swap(): return lax.ppermute(value, axis, [(k, k ^ bit) for k in range(size)])]
    pallas_call x5 -> x4, Pallas kernels: 38.3 us -> 36.5 us  [final(): pl.pallas_call(functools.partial(final_kernel, repeat=repeat, update=upda...]
  transfers between devices with their start and end apart: 43 -> 47, of which waited for: 13 -> 24; matrix products, arithmetic and copies ran while one was open for 2% -> 3% of each run, Pallas kernels for 10% -> 18%
where the time goes in v5:
time: 226 us; the launch traced here: 225 us
  Pallas kernels  103 us (46%)
  starting transfers between devices  52.4 us (23%)
  waiting for transfers between devices  51.7 us (23%)
  other arithmetic  9.35 us (4%)
  local copies, waits for them, and re-layouts  7.24 us (3%)
    pallas_call x3, Pallas kernels, sink(): pl.pallas_call(functools.partial(sink_kernel, first=first, rows_total=row...  43 us
    pallas_call x4, Pallas kernels, final(): pl.pallas_call(functools.partial(final_kernel, repeat=repeat, update=upda...  36.5 us
    ppermute x25, starting transfers between devices, joint_swap(): return lax.ppermute(value, ('item', 'bucket'), pairs)  32.2 us
    ppermute x22, waiting for transfers between devices, swap(): return lax.ppermute(value, axis, [(k, k ^ bit) for k in range(size)])  29.5 us
    ppermute x25, waiting for transfers between devices, joint_swap(): return lax.ppermute(value, ('item', 'bucket'), pairs)  22.2 us
    ppermute x22, starting transfers between devices, swap(): return lax.ppermute(value, axis, [(k, k ^ bit) for k in range(size)])  20.2 us
    pallas_call x2, Pallas kernels, lse(): pl.pallas_call(functools.partial(lse_kernel, repeat=repeat, count=count),...  14.6 us
    pallas_call x3, Pallas kernels, small(): pl.pallas_call(functools.partial(kernel, **settings), grid_spec=pltpu.Pre...  9.06 us
  transfers between devices with their start and end apart: 47, of which 24 were waited for; matrix products, arithmetic and copies ran while one was open for 3% of the time, Pallas kernels for 18%

profile of v5, /device:TPU:0, one launch (start us, length us, event | category | flops | bytes accessed | tf_op | source)
XLA Modules:
  0.0 224.9 jit_solution(774817988565039355)
XLA Ops:
  1.5 4.1 %collective-permute-start.3 = (f32[64,512]{1,0:T(8,128)S(1)}, f32[64,512]{1,0:T(8,128)S(1)}, u32[]{:S(2)}, u32[]{:S(2)}) collective-permute-start(f32[64,512]{1,0:T(8,128)S(1)} %convert_bitcast_fusion.refs_0_), channel_id=1, source_target_pairs={{0,16},{4,20},{8,24},{12,28},{16,0},{20,4},{24,8},{28,12},{1,17},{... | collective-permute-start | bytes 393224 | tf_op jit(solution)/shard_map/ppermute | solution.py:25
  5.6 7.3 %row_lse.2.rest_0_ = f32[2,1024]{1,0:T(2,128)} custom-call(bf16[64,1024]{1,0:T(8,128)(2,1)} %bitcast.12, bf16[64,8192]{1,0:T(8,128)(2,1)} %bitcast.17), custom_call_target="tpu_custom_call" | custom-call | flops 2147483648 | bytes 4194304 | tf_op jit(solution)/shard_map/row_lse/pallas_call | solution.py:349
  12.9 7.3 %row_lse.3 = f32[2,1024]{1,0:T(2,128)} custom-call(bf16[64,1024]{1,0:T(8,128)(2,1)} %bitcast.13, bf16[64,8192]{1,0:T(8,128)(2,1)} %bitcast.18, f32[2,1024]{1,0:T(2,128)} %row_lse.2.rest_0_), custom_call_target="tpu_custom_call", output_to_operand_aliasing={{}: (2, {})} | custom-call | flops 2147483648 | bytes 4194304 | tf_op jit(solution)/shard_map/row_lse/pallas_call | solution.py:349
  31.9 3.7 %collective-permute-done.4.refs_5_ = f32[64,512]{1,0:T(8,128)S(1)} collective-permute-done((f32[64,512]{1,0:T(8,128)S(1)}, f32[64,512]{1,0:T(8,128)S(1)}, u32[]{:S(2)}, u32[]{:S(2)}) %collective-permute-start.4) | collective-permute-done | bytes 131104 | tf_op jit(solution)/shard_map/ppermute | solution.py:25
  35.6 2.5 %collective-permute-done.2.refs_3_ = f32[64,512]{1,0:T(8,128)S(1)} collective-permute-done((f32[64,512]{1,0:T(8,128)S(1)}, f32[64,512]{1,0:T(8,128)S(1)}, u32[]{:S(2)}, u32[]{:S(2)}) %collective-permute-start.2) | collective-permute-done | bytes 131104 | tf_op jit(solution)/shard_map/ppermute | solution.py:25
  40.2 2.3 %shard_map.41.mine_ref = f32[64,4096]{1,0:T(8,128)} custom-call(s32[1]{0:T(128)} %bitcast.3.item_ref, f32[64,512]{1,0:T(8,128)} %copy-done.1, f32[64,512]{1,0:T(8,128)} %copy-done.13, f32[64,512]{1,0:T(8,128)} %copy-done.11, f32[64,512]{1,0:T(8,128)} %copy-done.15, f32[64,512]{1,0:T(8,128)} %copy-done.10, f32[64,512]{1,0:T(8,128)} %copy-done.14, ...), custom_call_target="tpu_custom_call" | custom-call | bytes 4194304 | tf_op jit(solution)/shard_map/pallas_call | solution.py:436
  42.7 1.6 collective-permute-start.12
  44.7 2.5 %collective-permute-start.14 = (f32[1,8192]{1,0:T(1,128)S(1)}, f32[1,8192]{1,0:T(1,128)S(1)}, u32[]{:S(2)}, u32[]{:S(2)}) collective-permute-start(f32[1,8192]{1,0:T(1,128)S(1)} %add.130.rest_0_), channel_id=1, source_target_pairs={{0,24},{1,25},{2,26},{3,27},{4,28},{5,29},{6,30},{7,31},{8,16},{9,... | collective-permute-start | bytes 98312 | tf_op jit(solution)/shard_map/ppermute | solution.py:42
  49.7 3.8 %shard_map.42 = (bf16[128,8192]{1,0:T(8,128)(2,1)}, bf16[64,8192]{1,0:T(8,128)(2,1)}) custom-call(s32[1]{0:T(128)} %bitcast.2.core_ref, f32[64,4096]{1,0:T(8,128)} %shard_map.41.mine_ref, f32[64,4096]{1,0:T(8,128)} %copy-done), custom_call_target="tpu_custom_call" | custom-call | bytes 4194304 | tf_op jit(solution)/shard_map/pallas_call | solution.py:436
  54.1 18.0 %sinkhorn_first.1 = (f32[1,8192]{1,0:T(1,128)}, f32[8,1024]{1,0:T(8,128)}, f32[1,8192]{1,0:T(1,128)}) custom-call(bf16[64,1024]{1,0:T(8,128)(2,1)} %dynamic-slice_bitcast_fusion.l_ref, bf16[128,8192]{1,0:T(8,128)(2,1)} %get-tuple-element.13.w_ref, f32[1,8192]{1,0:T(1,128)} %copy-done.24, f32[1,8192]{1,0:T(1,128)} %copy-done.27, f32[1,8192]{1,0:T(1,128)} %copy-done.28, ...), custom_call_target="tpu_custom_call" | custom-call | flops 4294967296 | bytes 4194304 | tf_op jit(solution)/shard_map/sinkhorn_first/pallas_call | solution.py:371
  79.1 2.2 collective-permute-done.18
  83.3 2.5 %collective-permute-start.21 = (f32[1,8192]{1,0:T(1,128)S(1)}, f32[1,8192]{1,0:T(1,128)S(1)}, u32[]{:S(2)}, u32[]{:S(2)}) collective-permute-start(f32[1,8192]{1,0:T(1,128)S(1)} %add_add_fusion.2.rest_0_), channel_id=1, source_target_pairs={{0,24},{1,25},{2,26},{3,27},{4,28},{5,29},{6,30},{7,31},{8,16},{9,... | collective-permute-start | bytes 98312 | tf_op jit(solution)/shard_map/ppermute | solution.py:42
  86.9 2.1 collective-permute-done.21.rest_3_
  89.6 12.5 %sinkhorn_next.2 = (f32[1,8192]{1,0:T(1,128)}, f32[8,1024]{1,0:T(8,128)}, f32[1,8192]{1,0:T(1,128)}) custom-call(bf16[64,1024]{1,0:T(8,128)(2,1)} %dynamic-slice_bitcast_fusion.l_ref, bf16[128,8192]{1,0:T(8,128)(2,1)} %get-tuple-element.13.w_ref, f32[1,8192]{1,0:T(1,128)} %copy-done.26, f32[1,8192]{1,0:T(1,128)} %copy-done.31, f32[1,8192]{1,0:T(1,128)} %copy-done.33, ...), custom_call_target="tpu_custom_call" | custom-call | flops 4294967296 | bytes 4194304 | tf_op jit(solution)/shard_map/sinkhorn_next/pallas_call | solution.py:371
  104.4 1.6 collective-permute-start.23
  111.5 3.0 %collective-permute-start.27 = (f32[1,8192]{1,0:T(1,128)S(1)}, f32[1,8192]{1,0:T(1,128)S(1)}, u32[]{:S(2)}, u32[]{:S(2)}) collective-permute-start(f32[1,8192]{1,0:T(1,128)S(1)} %add_add_fusion.1.rest_0_), channel_id=1, source_target_pairs={{0,16},{1,17},{2,18},{3,19},{4,20},{5,21},{6,22},{7,23},{8,24},{9,... | collective-permute-start | bytes 98312 | tf_op jit(solution)/shard_map/ppermute | solution.py:42
  116.4 3.8 %collective-permute-done.28.rest_3_ = f32[1,8192]{1,0:T(1,128)S(1)} collective-permute-done((f32[1,8192]{1,0:T(1,128)S(1)}, f32[1,8192]{1,0:T(1,128)S(1)}, u32[]{:S(2)}, u32[]{:S(2)}) %collective-permute-start.28) | collective-permute-done | bytes 32800 | tf_op jit(solution)/shard_map/ppermute | solution.py:42
  120.8 12.5 %sinkhorn_next.3 = (f32[1,8192]{1,0:T(1,128)}, f32[8,1024]{1,0:T(8,128)}, f32[1,8192]{1,0:T(1,128)}) custom-call(bf16[64,1024]{1,0:T(8,128)(2,1)} %dynamic-slice_bitcast_fusion.l_ref, bf16[128,8192]{1,0:T(8,128)(2,1)} %get-tuple-element.13.w_ref, f32[1,8192]{1,0:T(1,128)} %copy-done.25, f32[1,8192]{1,0:T(1,128)} %copy-done.30, f32[1,8192]{1,0:T(1,128)} %copy-done.32, ...), custom_call_target="tpu_custom_call" | custom-call | flops 4294967296 | bytes 4194304 | tf_op jit(solution)/shard_map/sinkhorn_next/pallas_call | solution.py:371
  139.2 2.3 %collective-permute-done.30 = f32[1,8192]{1,0:T(1,128)S(1)} collective-permute-done((f32[1,8192]{1,0:T(1,128)S(1)}, f32[1,8192]{1,0:T(1,128)S(1)}, u32[]{:S(2)}, u32[]{:S(2)}) %collective-permute-start.30) | collective-permute-done | bytes 32800 | tf_op jit(solution)/shard_map/ppermute | solution.py:42
  143.6 1.9 collective-permute-start.34
  145.5 2.5 %collective-permute-start.35 = (f32[1,16384]{1,0:T(1,128)S(1)}, f32[1,16384]{1,0:T(1,128)S(1)}, u32[]{:S(2)}, u32[]{:S(2)}) collective-permute-start(f32[1,16384]{1,0:T(1,128)S(1)} %pad_maximum_fusion.1.rest_2_), channel_id=1, source_target_pairs={{0,24},{1,25},{2,26},{3,27},{4,28},{5,29},{6,30},{7,31},{8,16},{9,... | collective-permute-start | bytes 196616 | tf_op jit(solution)/shard_map/ppermute | solution.py:42
  149.3 2.3 %collective-permute-done.35.rest_5_ = f32[1,16384]{1,0:T(1,128)S(1)} collective-permute-done((f32[1,16384]{1,0:T(1,128)S(1)}, f32[1,16384]{1,0:T(1,128)S(1)}, u32[]{:S(2)}, u32[]{:S(2)}) %collective-permute-start.35) | collective-permute-done | bytes 65568 | tf_op jit(solution)/shard_map/ppermute | solution.py:42
  152.1 16.7 %centroid_update.1.refs_0_ = f32[64,1024]{1,0:T(8,128)} custom-call(bf16[64,1024]{1,0:T(8,128)(2,1)} %dynamic-slice_bitcast_fusion.l_ref, f32[8,1024]{1,0:T(8,128)} %get-tuple-element.22.p_ref, bf16[128,8192]{1,0:T(8,128)(2,1)} %get-tuple-element.13.w_ref, f32[1,8192]{1,0:T(1,128)} %get-tuple-element.20.rest_0_, ...), custom_call_target="tpu_custom_call" | custom-call | flops 8589934592 | bytes 4194304 | tf_op jit(solution)/shard_map/centroid_update/pallas_call | solution.py:404
  168.9 3.0 %collective-permute-start.41 = (f32[64,1024]{1,0:T(8,128)}, f32[64,1024]{1,0:T(8,128)S(1)}, u32[]{:S(2)}, u32[]{:S(2)}) collective-permute-start(f32[64,1024]{1,0:T(8,128)} %centroid_update.1.refs_0_), channel_id=1, source_target_pairs={{0,8},{4,12},{8,0},{12,4},{16,24},{20,28},{24,16},{28,20},{1,9},{5... | collective-permute-start | bytes 786440 | tf_op jit(solution)/shard_map/ppermute | solution.py:25
  174.3 8.9 %code_gradient.3 = f32[64,512]{1,0:T(8,128)} custom-call(bf16[64,1024]{1,0:T(8,128)(2,1)} %bitcast.14, f32[2,1024]{1,0:T(2,128)} %pad_maximum_fusion.3.p_ref, bf16[64,8192]{1,0:T(8,128)(2,1)} %bitcast.19, f32[1,8192]{1,0:T(1,128)} %get-tuple-element.26.rest_0_), custom_call_target="tpu_custom_call" | custom-call | flops 4294967296 | bytes 4194304 | tf_op jit(solution)/shard_map/code_gradient/pallas_call | solution.py:404
  183.2 5.4 %code_gradient.4.rest_1_ = f32[64,512]{1,0:T(8,128)} custom-call(bf16[64,1024]{1,0:T(8,128)(2,1)} %bitcast.15, f32[2,1024]{1,0:T(2,128)} %pad_maximum_fusion.3.p_ref, bf16[64,8192]{1,0:T(8,128)(2,1)} %bitcast.20, f32[1,8192]{1,0:T(1,128)} %get-tuple-element.26.rest_0_), custom_call_target="tpu_custom_call" | custom-call | flops 2147483648 | bytes 4194304 | tf_op jit(solution)/shard_map/code_gradient/pallas_call | solution.py:404
  188.7 5.5 %code_gradient.5 = f32[64,512]{1,0:T(8,128)} custom-call(bf16[64,1024]{1,0:T(8,128)(2,1)} %bitcast.16, f32[2,1024]{1,0:T(2,128)} %pad_maximum_fusion.3.p_ref, bf16[64,8192]{1,0:T(8,128)(2,1)} %bitcast.21, f32[1,8192]{1,0:T(1,128)} %get-tuple-element.26.rest_0_, f32[64,512]{1,0:T(8,128)} %code_gradient.4.rest_1_), custom_call_target="tpu_custom_call", output_to_operand_aliasing={{}: (4, {})} | custom-call | flops 2147483648 | bytes 4194304 | tf_op jit(solution)/shard_map/code_gradient/pallas_call | solution.py:404
  194.8 1.6 collective-permute-start.37
  202.0 4.4 %collective-permute-done.39 = f32[64,512]{1,0:T(8,128)S(1)} collective-permute-done((f32[64,512]{1,0:T(8,128)S(1)}, f32[64,512]{1,0:T(8,128)S(1)}, u32[]{:S(2)}, u32[]{:S(2)}) %collective-permute-start.39) | collective-permute-done | bytes 131104 | tf_op jit(solution)/shard_map/ppermute | solution.py:25
  207.2 9.6 %collective-permute-done.42.refs_3_ = f32[64,1024]{1,0:T(8,128)S(1)} collective-permute-done((f32[64,1024]{1,0:T(8,128)S(1)}, f32[64,1024]{1,0:T(8,128)S(1)}, u32[]{:S(2)}, u32[]{:S(2)}) %collective-permute-start.42) | collective-permute-done | bytes 262176 | tf_op jit(solution)/shard_map/ppermute | solution.py:25
  216.8 4.4 %collective-permute-done.46.refs_7_ = f32[64,1024]{1,0:T(8,128)S(1)} collective-permute-done((f32[64,1024]{1,0:T(8,128)S(1)}, f32[64,1024]{1,0:T(8,128)S(1)}, u32[]{:S(2)}, u32[]{:S(2)}) %collective-permute-start.46) | collective-permute-done | bytes 262176 | tf_op jit(solution)/shard_map/ppermute | solution.py:25
  221.9 3.0 %shard_map.43 = f32[64,8192]{1,0:T(8,128)} custom-call(s32[1]{0:T(128)} %bitcast.3.item_ref, f32[64,1024]{1,0:T(8,128)} %centroid_update.1.refs_0_, f32[64,1024]{1,0:T(8,128)} %copy-done.6, f32[64,1024]{1,0:T(8,128)} %copy-done.4, f32[64,1024]{1,0:T(8,128)} %copy-done.8, f32[64,1024]{1,0:T(8,128)} %copy-done.3, f32[64,1024]{1,0:T(8,128)} %copy-done.7, ...), custom_call_target="tpu_custom_call" | custom-call | bytes 4194304 | tf_op jit(solution)/shard_map/pallas_call | solution.py:436
  (179 shorter events, 59.0 us)
Async XLA Ops:
  1.5 20.3 %collective-permute-start.3 = (f32[64,512]{1,0:T(8,128)S(1)}, f32[64,512]{1,0:T(8,128)S(1)}, u32[]{:S(2)}, u32[]{:S(2)}) collective-permute-start(f32[64,512]{1,0:T(8,128)S(1)} %convert_bitcast_fusion.refs_0_), channel_id=1, source_target_pairs={{0,16},{4,20},{8,24},{12,28},{16,0},{20,4},{24,8},{28,12},{1,17},{... | collective-permute-start | bytes 393224 | tf_op jit(solution)/shard_map/ppermute | solution.py:25
  20.2 9.6 %collective-permute-start.1 = (f32[64,512]{1,0:T(8,128)S(1)}, f32[64,512]{1,0:T(8,128)S(1)}, u32[]{:S(2)}, u32[]{:S(2)}) collective-permute-start(f32[64,512]{1,0:T(8,128)S(1)} %convert_bitcast_fusion.refs_0_), channel_id=1, source_target_pairs={{0,8},{4,12},{8,0},{12,4},{16,24},{20,28},{24,16},{28,20},{1,9},{5... | collective-permute-start | bytes 393224 | tf_op jit(solution)/shard_map/ppermute | solution.py:25
  21.8 9.5 %collective-permute-start.5 = (f32[64,512]{1,0:T(8,128)S(1)}, f32[64,512]{1,0:T(8,128)S(1)}, u32[]{:S(2)}, u32[]{:S(2)}) collective-permute-start(f32[64,512]{1,0:T(8,128)S(1)} %collective-permute-done.3.refs_4_), channel_id=1, source_target_pairs={{0,8},{4,12},{8,0},{12,4},{16,24},{20,28},{24,16},{28,20},{1,9},{5... | collective-permute-start | bytes 393224 | tf_op jit(solution)/shard_map/ppermute | solution.py:25
  26.1 5.8 %collective-permute-start = (f32[64,512]{1,0:T(8,128)S(1)}, f32[64,512]{1,0:T(8,128)S(1)}, u32[]{:S(2)}, u32[]{:S(2)}) collective-permute-start(f32[64,512]{1,0:T(8,128)S(1)} %convert_bitcast_fusion.refs_0_), channel_id=1, source_target_pairs={{0,4},{4,0},{8,12},{12,8},{16,20},{20,16},{24,28},{28,24},{1,5},{5... | collective-permute-start | bytes 393224 | tf_op jit(solution)/shard_map/ppermute | solution.py:25
  27.6 15.0 %collective-permute-start.9 = (f32[2,1024]{1,0:T(2,128)S(1)}, f32[2,1024]{1,0:T(2,128)S(1)}, u32[]{:S(2)}, u32[]{:S(2)}) collective-permute-start(f32[2,1024]{1,0:T(2,128)S(1)} %pad_maximum_fusion.2), channel_id=1, source_target_pairs={{0,2},{1,3},{2,0},{3,1},{4,6},{5,7},{6,4},{7,5},{8,10},{9,11},{10,... | collective-permute-start | bytes 24584 | tf_op jit(solution)/shard_map/ppermute | solution.py:42
  29.2 6.4 %collective-permute-start.4 = (f32[64,512]{1,0:T(8,128)S(1)}, f32[64,512]{1,0:T(8,128)S(1)}, u32[]{:S(2)}, u32[]{:S(2)}) collective-permute-start(f32[64,512]{1,0:T(8,128)S(1)} %collective-permute-done.3.refs_4_), channel_id=1, source_target_pairs={{0,4},{4,0},{8,12},{12,8},{16,20},{20,16},{24,28},{28,24},{1,5},{5... | collective-permute-start | bytes 393224 | tf_op jit(solution)/shard_map/ppermute | solution.py:25
  29.8 8.3 %collective-permute-start.2 = (f32[64,512]{1,0:T(8,128)S(1)}, f32[64,512]{1,0:T(8,128)S(1)}, u32[]{:S(2)}, u32[]{:S(2)}) collective-permute-start(f32[64,512]{1,0:T(8,128)S(1)} %collective-permute-done.1.refs_2_), channel_id=1, source_target_pairs={{0,4},{4,0},{8,12},{12,8},{16,20},{20,16},{24,28},{28,24},{1,5},{5... | collective-permute-start | bytes 393224 | tf_op jit(solution)/shard_map/ppermute | solution.py:25
  31.3 8.2 %collective-permute-start.6 = (f32[64,512]{1,0:T(8,128)S(1)}, f32[64,512]{1,0:T(8,128)S(1)}, u32[]{:S(2)}, u32[]{:S(2)}) collective-permute-start(f32[64,512]{1,0:T(8,128)S(1)} %collective-permute-done.5.refs_6_), channel_id=1, source_target_pairs={{0,4},{4,0},{8,12},{12,8},{16,20},{20,16},{24,28},{28,24},{1,5},{5... | collective-permute-start | bytes 393224 | tf_op jit(solution)/shard_map/ppermute | solution.py:25
  42.5 6.2 %collective-permute-start.7 = (f32[64,4096]{1,0:T(8,128)}, f32[64,4096]{1,0:T(8,128)S(1)}, u32[]{:S(2)}, u32[]{:S(2)}) collective-permute-start(f32[64,4096]{1,0:T(8,128)} %shard_map.41.mine_ref), channel_id=1, source_target_pairs={{0,1},{1,0},{2,3},{3,2},{4,5},{5,4},{6,7},{7,6},{8,9},{9,8},{10,11... | collective-permute-start | bytes 3145736 | tf_op jit(solution)/shard_map/ppermute | solution.py:25
  42.7 10.8 %collective-permute-start.12 = (f32[1,8192]{1,0:T(1,128)S(1)}, f32[1,8192]{1,0:T(1,128)S(1)}, u32[]{:S(2)}, u32[]{:S(2)}) collective-permute-start(f32[1,8192]{1,0:T(1,128)S(1)} %add.130.rest_0_), channel_id=1, source_target_pairs={{0,8},{1,9},{2,10},{3,11},{4,12},{5,13},{6,14},{7,15},{8,0},{9,1},... | collective-permute-start | bytes 98312 | tf_op jit(solution)/shard_map/ppermute | solution.py:42
  44.4 9.1 %collective-permute-start.13 = (f32[1,8192]{1,0:T(1,128)S(1)}, f32[1,8192]{1,0:T(1,128)S(1)}, u32[]{:S(2)}, u32[]{:S(2)}) collective-permute-start(f32[1,8192]{1,0:T(1,128)S(1)} %add.130.rest_0_), channel_id=1, source_target_pairs={{0,16},{1,17},{2,18},{3,19},{4,20},{5,21},{6,22},{7,23},{8,24},{9,... | collective-permute-start | bytes 98312 | tf_op jit(solution)/shard_map/ppermute | solution.py:42
  44.7 8.8 %collective-permute-start.14 = (f32[1,8192]{1,0:T(1,128)S(1)}, f32[1,8192]{1,0:T(1,128)S(1)}, u32[]{:S(2)}, u32[]{:S(2)}) collective-permute-start(f32[1,8192]{1,0:T(1,128)S(1)} %add.130.rest_0_), channel_id=1, source_target_pairs={{0,24},{1,25},{2,26},{3,27},{4,28},{5,29},{6,30},{7,31},{8,16},{9,... | collective-permute-start | bytes 98312 | tf_op jit(solution)/shard_map/ppermute | solution.py:42
  76.4 4.8 %collective-permute-start.18 = (f32[1,8192]{1,0:T(1,128)S(1)}, f32[1,8192]{1,0:T(1,128)S(1)}, u32[]{:S(2)}, u32[]{:S(2)}) collective-permute-start(f32[1,8192]{1,0:T(1,128)S(1)} %add.131), channel_id=1, source_target_pairs={{0,6},{1,7},{2,4},{3,5},{4,2},{5,3},{6,0},{7,1},{8,14},{9,15},{10,... | collective-permute-start | bytes 98312 | tf_op jit(solution)/shard_map/ppermute | solution.py:42
  82.0 4.8 %collective-permute-start.20 = (f32[1,8192]{1,0:T(1,128)S(1)}, f32[1,8192]{1,0:T(1,128)S(1)}, u32[]{:S(2)}, u32[]{:S(2)}) collective-permute-start(f32[1,8192]{1,0:T(1,128)S(1)} %add_add_fusion.2.rest_0_), channel_id=1, source_target_pairs={{0,16},{1,17},{2,18},{3,19},{4,20},{5,21},{6,22},{7,23},{8,24},{9,... | collective-permute-start | bytes 98312 | tf_op jit(solution)/shard_map/ppermute | solution.py:42
  83.3 5.7 %collective-permute-start.21 = (f32[1,8192]{1,0:T(1,128)S(1)}, f32[1,8192]{1,0:T(1,128)S(1)}, u32[]{:S(2)}, u32[]{:S(2)}) collective-permute-start(f32[1,8192]{1,0:T(1,128)S(1)} %add_add_fusion.2.rest_0_), channel_id=1, source_target_pairs={{0,24},{1,25},{2,26},{3,27},{4,28},{5,29},{6,30},{7,31},{8,16},{9,... | collective-permute-start | bytes 98312 | tf_op jit(solution)/shard_map/ppermute | solution.py:42
  106.5 4.8 %collective-permute-start.25 = (f32[1,8192]{1,0:T(1,128)S(1)}, f32[1,8192]{1,0:T(1,128)S(1)}, u32[]{:S(2)}, u32[]{:S(2)}) collective-permute-start(f32[1,8192]{1,0:T(1,128)S(1)} %add.135), channel_id=1, source_target_pairs={{0,6},{1,7},{2,4},{3,5},{4,2},{5,3},{6,0},{7,1},{8,14},{9,15},{10,... | collective-permute-start | bytes 98312 | tf_op jit(solution)/shard_map/ppermute | solution.py:42
  111.5 4.9 %collective-permute-start.27 = (f32[1,8192]{1,0:T(1,128)S(1)}, f32[1,8192]{1,0:T(1,128)S(1)}, u32[]{:S(2)}, u32[]{:S(2)}) collective-permute-start(f32[1,8192]{1,0:T(1,128)S(1)} %add_add_fusion.1.rest_0_), channel_id=1, source_target_pairs={{0,16},{1,17},{2,18},{3,19},{4,20},{5,21},{6,22},{7,23},{8,24},{9,... | collective-permute-start | bytes 98312 | tf_op jit(solution)/shard_map/ppermute | solution.py:42
  114.5 5.7 %collective-permute-start.28 = (f32[1,8192]{1,0:T(1,128)S(1)}, f32[1,8192]{1,0:T(1,128)S(1)}, u32[]{:S(2)}, u32[]{:S(2)}) collective-permute-start(f32[1,8192]{1,0:T(1,128)S(1)} %add_add_fusion.1.rest_0_), channel_id=1, source_target_pairs={{0,24},{1,25},{2,26},{3,27},{4,28},{5,29},{6,30},{7,31},{8,16},{9,... | collective-permute-start | bytes 98312 | tf_op jit(solution)/shard_map/ppermute | solution.py:42
  135.7 6.9 %collective-permute-start.31 = (f32[1,16384]{1,0:T(1,128)S(1)}, f32[1,16384]{1,0:T(1,128)S(1)}, u32[]{:S(2)}, u32[]{:S(2)}) collective-permute-start(f32[1,16384]{1,0:T(1,128)S(1)} %pad_maximum_fusion), channel_id=1, source_target_pairs={{0,4},{1,5},{2,6},{3,7},{4,0},{5,1},{6,2},{7,3},{8,12},{9,13},{10,... | collective-permute-start | bytes 196616 | tf_op jit(solution)/shard_map/ppermute | solution.py:42
  137.7 4.8 %collective-permute-start.32 = (f32[1,8192]{1,0:T(1,128)S(1)}, f32[1,8192]{1,0:T(1,128)S(1)}, u32[]{:S(2)}, u32[]{:S(2)}) collective-permute-start(f32[1,8192]{1,0:T(1,128)S(1)} %add.141), channel_id=1, source_target_pairs={{0,6},{1,7},{2,4},{3,5},{4,2},{5,3},{6,0},{7,1},{8,14},{9,15},{10,... | collective-permute-start | bytes 98312 | tf_op jit(solution)/shard_map/ppermute | solution.py:42
  143.6 5.7 %collective-permute-start.34 = (f32[1,16384]{1,0:T(1,128)S(1)}, f32[1,16384]{1,0:T(1,128)S(1)}, u32[]{:S(2)}, u32[]{:S(2)}) collective-permute-start(f32[1,16384]{1,0:T(1,128)S(1)} %pad_maximum_fusion.1.rest_2_), channel_id=1, source_target_pairs={{0,16},{1,17},{2,18},{3,19},{4,20},{5,21},{6,22},{7,23},{8,24},{9,... | collective-permute-start | bytes 196616 | tf_op jit(solution)/shard_map/ppermute | solution.py:42
  145.5 6.1 %collective-permute-start.35 = (f32[1,16384]{1,0:T(1,128)S(1)}, f32[1,16384]{1,0:T(1,128)S(1)}, u32[]{:S(2)}, u32[]{:S(2)}) collective-permute-start(f32[1,16384]{1,0:T(1,128)S(1)} %pad_maximum_fusion.1.rest_2_), channel_id=1, source_target_pairs={{0,24},{1,25},{2,26},{3,27},{4,28},{5,29},{6,30},{7,31},{8,16},{9,... | collective-permute-start | bytes 196616 | tf_op jit(solution)/shard_map/ppermute | solution.py:42
  168.9 19.8 %collective-permute-start.43 = (f32[64,1024]{1,0:T(8,128)}, f32[64,1024]{1,0:T(8,128)S(1)}, u32[]{:S(2)}, u32[]{:S(2)}) collective-permute-start(f32[64,1024]{1,0:T(8,128)} %centroid_update.1.refs_0_), channel_id=1, source_target_pairs={{0,16},{4,20},{8,24},{12,28},{16,0},{20,4},{24,8},{28,12},{1,17},{... | collective-permute-start | bytes 786440 | tf_op jit(solution)/shard_map/ppermute | solution.py:25
  168.9 29.6 %collective-permute-start.41 = (f32[64,1024]{1,0:T(8,128)}, f32[64,1024]{1,0:T(8,128)S(1)}, u32[]{:S(2)}, u32[]{:S(2)}) collective-permute-start(f32[64,1024]{1,0:T(8,128)} %centroid_update.1.refs_0_), channel_id=1, source_target_pairs={{0,8},{4,12},{8,0},{12,4},{16,24},{20,28},{24,16},{28,20},{1,9},{5... | collective-permute-start | bytes 786440 | tf_op jit(solution)/shard_map/ppermute | solution.py:25
  183.2 11.6 %collective-permute-start.36 = (f32[64,512]{1,0:T(8,128)}, f32[64,512]{1,0:T(8,128)S(1)}, u32[]{:S(2)}, u32[]{:S(2)}) collective-permute-start(f32[64,512]{1,0:T(8,128)} %code_gradient.3), channel_id=1, source_target_pairs={{0,1},{1,0},{2,3},{3,2},{4,5},{5,4},{6,7},{7,6},{8,9},{9,8},{10,11... | collective-permute-start | bytes 393224 | tf_op jit(solution)/shard_map/ppermute | solution.py:25
  188.6 10.3 %collective-permute-start.45 = (f32[64,1024]{1,0:T(8,128)S(1)}, f32[64,1024]{1,0:T(8,128)S(1)}, u32[]{:S(2)}, u32[]{:S(2)}) collective-permute-start(f32[64,1024]{1,0:T(8,128)S(1)} %collective-permute-done.43.refs_4_), channel_id=1, source_target_pairs={{0,8},{4,12},{8,0},{12,4},{16,24},{20,28},{24,16},{28,20},{1,9},{5... | collective-permute-start | bytes 786440 | tf_op jit(solution)/shard_map/ppermute | solution.py:25
  194.8 6.6 %collective-permute-start.37 = (f32[64,512]{1,0:T(8,128)S(1)}, f32[64,512]{1,0:T(8,128)S(1)}, u32[]{:S(2)}, u32[]{:S(2)}) collective-permute-start(f32[64,512]{1,0:T(8,128)S(1)} %add.149), channel_id=1, source_target_pairs={{0,2},{1,3},{2,0},{3,1},{4,6},{5,7},{6,4},{7,5},{8,10},{9,11},{10,... | collective-permute-start | bytes 393224 | tf_op jit(solution)/shard_map/ppermute | solution.py:25
  196.4 10.8 %collective-permute-start.40 = (f32[64,1024]{1,0:T(8,128)S(1)}, f32[64,1024]{1,0:T(8,128)S(1)}, u32[]{:S(2)}, u32[]{:S(2)}) collective-permute-start(f32[64,1024]{1,0:T(8,128)S(1)} %copy-done.2), channel_id=1, source_target_pairs={{0,4},{4,0},{8,12},{12,8},{16,20},{20,16},{24,28},{28,24},{1,5},{5... | collective-permute-start | bytes 786440 | tf_op jit(solution)/shard_map/ppermute | solution.py:25
  196.9 19.9 %collective-permute-start.44 = (f32[64,1024]{1,0:T(8,128)S(1)}, f32[64,1024]{1,0:T(8,128)S(1)}, u32[]{:S(2)}, u32[]{:S(2)}) collective-permute-start(f32[64,1024]{1,0:T(8,128)S(1)} %collective-permute-done.43.refs_4_), channel_id=1, source_target_pairs={{0,4},{4,0},{8,12},{12,8},{16,20},{20,16},{24,28},{28,24},{1,5},{5... | collective-permute-start | bytes 786440 | tf_op jit(solution)/shard_map/ppermute | solution.py:25
  198.4 18.4 %collective-permute-start.42 = (f32[64,1024]{1,0:T(8,128)S(1)}, f32[64,1024]{1,0:T(8,128)S(1)}, u32[]{:S(2)}, u32[]{:S(2)}) collective-permute-start(f32[64,1024]{1,0:T(8,128)S(1)} %collective-permute-done.41.refs_2_), channel_id=1, source_target_pairs={{0,4},{4,0},{8,12},{12,8},{16,20},{20,16},{24,28},{28,24},{1,5},{5... | collective-permute-start | bytes 786440 | tf_op jit(solution)/shard_map/ppermute | solution.py:25
  199.0 22.2 %collective-permute-start.46 = (f32[64,1024]{1,0:T(8,128)S(1)}, f32[64,1024]{1,0:T(8,128)S(1)}, u32[]{:S(2)}, u32[]{:S(2)}) collective-permute-start(f32[64,1024]{1,0:T(8,128)S(1)} %collective-permute-done.45.refs_6_), channel_id=1, source_target_pairs={{0,4},{4,0},{8,12},{12,8},{16,20},{20,16},{24,28},{28,24},{1,5},{5... | collective-permute-start | bytes 786440 | tf_op jit(solution)/shard_map/ppermute | solution.py:25
  201.4 5.0 %collective-permute-start.39 = (f32[64,512]{1,0:T(8,128)S(1)}, f32[64,512]{1,0:T(8,128)S(1)}, u32[]{:S(2)}, u32[]{:S(2)}) collective-permute-start(f32[64,512]{1,0:T(8,128)S(1)} %add.151), channel_id=1, source_target_pairs={{0,2},{1,3},{2,0},{3,1},{4,6},{5,7},{6,4},{7,5},{8,10},{9,11},{10,... | collective-permute-start | bytes 393224 | tf_op jit(solution)/shard_map/ppermute | solution.py:25
  (51 other events, 317.5 us)

commit v6 on v5

--- a/solution.py
+++ b/solution.py
@@ -16,6 +16,7 @@
 epsilon = 1e-06
 
 CHUNK = 2048
+SUB = 512
 LANES = 128
 POTS = 16
 
@@ -144,7 +145,7 @@
 
     @pl.loop(0, width // size)
     def _(step):
-        run(pl.ds(pl.multiple_of(step * size, size), size))
+        run(step, pl.ds(pl.multiple_of(step * size, size), size))
 
 
 def cases(count, run):
@@ -165,37 +166,37 @@
         run(False, True)
 
 
-def lse_kernel(l_ref, w_ref, *rest, repeat, count):
-    out_ref, y_ref, part_ref, sum_ref, wide_ref = rest[-5:]
-    block, width = y_ref.shape
-
-    def run(new, old):
-        if old:
-            highest = jnp.max(part_ref[...], axis=1, keepdims=True)
-            wide_ref[...] = jnp.broadcast_to(highest, (block, LANES))
-            sum_ref[...] = jnp.zeros(sum_ref.shape, jnp.float32)
-        if new:
-            part_ref[...] = jnp.full(part_ref.shape, -jnp.inf, jnp.float32)
-            left = left_of(l_ref, True)
-
-        def chunk(at):
-            if old:
-                terms = [jnp.exp(piece - wide_ref[...]) for piece in slices(y_ref[:, at])]
-                sum_ref[...] += folded(terms, jnp.add)
-            if new:
-                right = jnp.concatenate([w_ref[:, at]] * repeat, axis=0)
-                y = jnp.dot(left, right, preferred_element_type=jnp.float32)
-                y_ref[:, at] = y
-                part_ref[...] = jnp.maximum(part_ref[...], folded(slices(y), jnp.maximum))
-
-        chunks(width, chunk)
-        if old:
-            summed = jnp.sum(sum_ref[...], axis=1, keepdims=True)
-            lane = lax.broadcasted_iota(jnp.int32, (block, LANES), 1)
-            both = jnp.where(lane == 0, wide_ref[...], summed)
-            out_ref[...] = jnp.transpose(both)[0:2, :]
-
-    cases(count, run)
+def raised(pieces, high_ref, sum_ref):
+    was = high_ref[...]
+    high = jnp.maximum(was, folded(pieces, jnp.maximum))
+    terms = [jnp.exp(piece - high) for piece in pieces]
+    high_ref[...] = high
+    sum_ref[...] = sum_ref[...] * jnp.exp(was - high) + folded(terms, jnp.add)
+    return high, terms
+
+
+def settled(high_ref, sum_ref):
+    highest = jnp.max(high_ref[...], axis=1, keepdims=True)
+    return highest, jnp.sum(sum_ref[...] * jnp.exp(high_ref[...] - highest), axis=1, keepdims=True)
+
+
+def lse_kernel(l_ref, w_ref, *rest, repeat):
+    out_ref, high_ref, sum_ref = rest[-3:]
+    width = w_ref.shape[1]
+    left = left_of(l_ref, True)
+    high_ref[...] = jnp.full(high_ref.shape, -jnp.inf, jnp.float32)
+    sum_ref[...] = jnp.zeros(sum_ref.shape, jnp.float32)
+
+    def chunk(_, at):
+        right = jnp.concatenate([w_ref[:, at]] * repeat, axis=0)
+        for at in range(0, right.shape[1], SUB):
+            y = jnp.dot(left, right[:, at : at + SUB], preferred_element_type=jnp.float32)
+            raised(slices(y), high_ref, sum_ref)
+
+    chunks(width, chunk)
+    highest, summed = settled(high_ref, sum_ref)
+    lane = lax.broadcasted_iota(jnp.int32, high_ref.shape, 1)
+    out_ref[...] = jnp.transpose(jnp.where(lane == 0, highest, summed))[0:2, :]
 
 
 def sink_kernel(
@@ -204,14 +205,14 @@
     term_refs, rest = rest[:terms], rest[terms:]
     if not first:
         p_ref, q_ref, *rest = rest
-    sums_ref, pot_ref, row_ref, y_ref, part_ref, high_ref, wide_ref, wpot_ref, acc_ref = rest
+    sums_ref, pot_ref, row_ref, y_ref, part_ref, high_ref, highs_ref, wide_ref, wpot_ref, acc_ref = rest
     block, width = y_ref.shape
 
     def run(new, old):
         if new and not old:
             acc_ref[...] = jnp.zeros(acc_ref.shape, jnp.float32)
 
-            def prepare(at):
+            def prepare(_, at):
                 row = joined([term_ref[0:1, at] for term_ref in term_refs])
                 if not first:
                     row = q_ref[0:1, at] - jnp.log(row * float(rows_total))
@@ -222,46 +223,45 @@
         if new:
             was = jnp.zeros((1, block), jnp.float32) if first else p_ref[0:1, :]
             left = jnp.concatenate([left_of(l_ref, False), left_pots(was, block)], axis=1)
-            part_ref[...] = jnp.full(part_ref.shape, -jnp.inf if first else 0.0, jnp.float32)
-
-        def chunk(at):
+            part_ref[...] = jnp.zeros(part_ref.shape, jnp.float32)
+            if first:
+                high_ref[...] = jnp.full(high_ref.shape, -jnp.inf, jnp.float32)
+
+        def chunk(step, at):
             if old:
-                sums = [
-                    jnp.sum((piece * wide_ref[...]).reshape(block // 8, 8, LANES), axis=0)
-                    for piece in slices(y_ref[:, at])
-                ]
+                each = chunk_of(width) // SUB
+                sums = []
+                for number, piece in enumerate(slices(y_ref[:, at])):
+                    wide = wide_ref[step * each + number * LANES // SUB if first else 0]
+                    sums.append(jnp.sum((piece * wide).reshape(block // 8, 8, LANES), axis=0))
                 acc_ref[:, at] += jnp.concatenate(sums, axis=1)
             if new:
                 right = jnp.concatenate([w_ref[:, at], wpot_ref[:, at]], axis=0)
-                y = jnp.dot(left, right, preferred_element_type=jnp.float32)
                 if first:
-                    y_ref[:, at] = y
-                    part_ref[...] = jnp.maximum(part_ref[...], folded(slices(y), jnp.maximum))
+                    terms = []
+                    for number in range(right.shape[1] // SUB):
+                        piece = right[:, number * SUB : (number + 1) * SUB]
+                        y = jnp.dot(left, piece, preferred_element_type=jnp.float32)
+                        high, more = raised(slices(y), high_ref, part_ref)
+                        highs_ref[step * (right.shape[1] // SUB) + number] = high
+                        terms += more
+                    y_ref[:, at] = jnp.concatenate(terms, axis=1)
                 else:
-                    y = jnp.exp(y)
+                    y = jnp.exp(jnp.dot(left, right, preferred_element_type=jnp.float32))
                     y_ref[:, at] = y
                     part_ref[...] += folded(slices(y), jnp.add)
 
         chunks(width, chunk)
         if new and first:
-            highest = jnp.max(part_ref[...], axis=1, keepdims=True)
-            high_ref[...] = jnp.broadcast_to(highest, (block, LANES))
-            part_ref[...] = jnp.zeros(part_ref.shape, jnp.float32)
-
-            def again(at):
-                terms = [jnp.exp(piece - high_ref[...]) for piece in slices(y_ref[:, at])]
-                y_ref[:, at] = jnp.concatenate(terms, axis=1)
-                part_ref[...] += folded(terms, jnp.add)
-
-            chunks(width, again)
-        if new:
+            highest, summed = settled(high_ref, part_ref)
+            summed = summed * float(buckets_total)
+            for number in range(highs_ref.shape[0]):
+                wide_ref[number] = jnp.exp(highs_ref[number] - highest) / summed
+            pot_ref[...] = -row_of(highest + jnp.log(summed))
+        elif new:
             summed = jnp.sum(part_ref[...], axis=1, keepdims=True) * float(buckets_total)
-            wide_ref[...] = jnp.broadcast_to(1.0 / summed, (block, LANES))
-            summed = row_of(summed)
-            if first:
-                pot_ref[...] = -(row_of(high_ref[...]) + jnp.log(summed))
-            else:
-                pot_ref[...] = was - jnp.log(summed)
+            wide_ref[0] = jnp.broadcast_to(1.0 / summed, (block, LANES))
+            pot_ref[...] = was - jnp.log(row_of(summed))
         if not new:
             sums_ref[...] = jnp.sum(acc_ref[...], axis=0, keepdims=True)
 
@@ -280,7 +280,7 @@
 
     @pl.when(pl.program_id(0) == 0)
     def _():
-        def prepare(at):
+        def prepare(_, at):
             if update:
                 row = row_ref[0:1, at]
                 mass = joined([term_ref[0:1, at] for term_ref in term_refs]) * float(rows_total)
@@ -298,7 +298,7 @@
     wide_ref[...] = jnp.transpose(jnp.broadcast_to(factor_p, (LANES, block)))
     acc_ref[...] = jnp.zeros(acc_ref.shape, jnp.float32)
 
-    def chunk(at):
+    def chunk(_, at):
         right = jnp.concatenate([w_ref[:, at]] * repeat + [wpot_ref[:, at]], axis=0)
         y = jnp.dot(left, right, preferred_element_type=jnp.float32)
         delta = jnp.concatenate(
@@ -309,11 +309,11 @@
             axis=1,
         )
         acc_ref[...] += lax.dot_general(
-            delta, r_ref[:, at], (((1,), (1,)), ((), ())), preferred_element_type=jnp.float32
+            r_ref[:, at], delta, (((1,), (1,)), ((), ())), preferred_element_type=jnp.float32
         )
 
     chunks(width, chunk)
-    gradient = score_scale * jnp.transpose(acc_ref[...])
+    gradient = score_scale * acc_ref[...]
     if update:
         moved = l_ref[...].astype(jnp.float32) - step_rate * gradient
         gradient = moved * lax.rsqrt(jnp.mean(moved * moved, axis=0, keepdims=True) + epsilon)
@@ -347,13 +347,13 @@
     count = rows // parts // block
     lead = part * count
     return pl.pallas_call(
-        functools.partial(lse_kernel, repeat=repeat, count=count),
-        grid=(count + 1,),
-        in_specs=[pl.BlockSpec((dim, block), lambda k: (0, lead + jnp.minimum(k, count - 1))), full(right)]
+        functools.partial(lse_kernel, repeat=repeat),
+        grid=(count,),
+        in_specs=[pl.BlockSpec((dim, block), lambda k: (0, lead + k)), full(right)]
         + [pl.BlockSpec(memory_space=pl.ANY)] * len(before),
-        out_specs=pl.BlockSpec((2, block), lambda k: (0, lead + jnp.maximum(k - 1, 0))),
+        out_specs=pl.BlockSpec((2, block), lambda k: (0, lead + k)),
         out_shape=jax.ShapeDtypeStruct((2, rows), jnp.float32),
-        scratch_shapes=[VMEM((block, width), jnp.float32)] + [VMEM((block, LANES), jnp.float32)] * 3,
+        scratch_shapes=[VMEM((block, LANES), jnp.float32)] * 2,
         input_output_aliases={2: 0} if before else {},
         compiler_params=params(),
         cost_estimate=cost(rows // parts, width, 1),
@@ -361,72 +361,81 @@
     )(left, right, *before)
 
 
-def sink(left, right, terms, old, rows_total, buckets_total):
-    (dim, rows), width = left.shape, right.shape[1]
+def sink(left, item, rows, right, terms, old, rows_total, buckets_total):
+    dim, width = left.shape[0], right.shape[1]
     block = block_of(rows, width)
     count = rows // block
     first = not old
-    line = pl.BlockSpec((1, width), lambda k: (0, 0))
-    pot_spec = pl.BlockSpec((8, block), lambda k: (0, jnp.minimum(k, count - 1)))
+    line = pl.BlockSpec((1, width), lambda k, at: (0, 0))
+    pot_spec = pl.BlockSpec((8, block), lambda k, at: (0, jnp.minimum(k, count - 1)))
+    kernel = functools.partial(
+        sink_kernel, first=first, rows_total=rows_total, buckets_total=buckets_total, count=count,
+        terms=len(terms),
+    )
     return pl.pallas_call(
-        functools.partial(
-            sink_kernel, first=first, rows_total=rows_total, buckets_total=buckets_total, count=count,
-            terms=len(terms),
-        ),
-        grid=(count + 1,),
+        lambda at_ref, *refs: kernel(*refs),
+        grid_spec=pltpu.PrefetchScalarGridSpec(num_scalar_prefetch=1, grid=(count + 1,),
         in_specs=[
-            pl.BlockSpec((dim, block), lambda k: (0, jnp.minimum(k, count - 1))),
-            full(right),
+            pl.BlockSpec((dim, block), lambda k, at: (0, at[0] * count + jnp.minimum(k, count - 1))),
+            pl.BlockSpec(right.shape, lambda k, at: (0, 0)),
         ]
         + [line] * len(terms)
         + ([] if first else [pot_spec, line]),
         out_specs=[line, pot_spec, line],
+        scratch_shapes=[VMEM((block, width), jnp.float32)]
+        + [VMEM((block, LANES), jnp.float32)] * 2
+        + [VMEM((width // SUB if first else 1, block, LANES), jnp.float32)] * 2
+        + [VMEM((POTS, width), jnp.bfloat16), VMEM((8, width), jnp.float32)],
+        ),
         out_shape=[
             jax.ShapeDtypeStruct((1, width), jnp.float32),
             jax.ShapeDtypeStruct((8, rows), jnp.float32),
             jax.ShapeDtypeStruct((1, width), jnp.float32),
         ],
-        scratch_shapes=[VMEM((block, width), jnp.float32)]
-        + [VMEM((block, LANES), jnp.float32)] * 3
-        + [VMEM((POTS, width), jnp.bfloat16), VMEM((8, width), jnp.float32)],
         compiler_params=params(),
         cost_estimate=cost(rows, width, 1),
         name="sinkhorn_first" if first else "sinkhorn_next",
-    )(left, right, *terms, *old)
-
-
-def final(left, p_rows, right, lines, codes, repeat, update, rows_total, lead, steps, total, before):
-    (dim, rows), width = left.shape, right.shape[1]
+    )(item.reshape(1).astype(jnp.int32), left, right, *terms, *old)
+
+
+def final(left, item, rows, p_rows, right, lines, codes, repeat, update, rows_total, lead, steps, total, before):
+    dim, width = left.shape[0], right.shape[1]
     block = block_of(rows, width)
-    line = pl.BlockSpec((1, width), lambda k: (0, 0))
+    count = rows // block
     into = total - steps if before else 0
     extra = [codes] if update else []
+    kernel = functools.partial(
+        final_kernel, repeat=repeat, update=update, rows_total=rows_total, terms=len(lines) - 2
+    )
+    scalars = [item.reshape(1).astype(jnp.int32)] if update else []
+    line = pl.BlockSpec((1, width), lambda k, *at: (0, 0))
+    in_specs = [
+        pl.BlockSpec((dim, block), lambda k, *at: (0, (at[0][0] * count if at else 0) + lead + k)),
+        pl.BlockSpec((p_rows.shape[0], block), lambda k, *at: (0, lead + k)),
+        pl.BlockSpec(right.shape, lambda k, *at: (0, 0)),
+    ]
+    in_specs += [line] * len(lines) + [pl.BlockSpec(one.shape, lambda k, *at: (0, 0)) for one in extra]
+    in_specs += [pl.BlockSpec(memory_space=pl.ANY)] * len(before)
     return pl.pallas_call(
-        functools.partial(
-            final_kernel, repeat=repeat, update=update, rows_total=rows_total, terms=len(lines) - 2
+        (lambda at_ref, *refs: kernel(*refs)) if update else kernel,
+        grid_spec=pltpu.PrefetchScalarGridSpec(
+            num_scalar_prefetch=len(scalars),
+            grid=(steps,),
+            in_specs=in_specs,
+            out_specs=pl.BlockSpec((dim, block), lambda k, *at: (0, into + k)),
+            scratch_shapes=[
+                VMEM((block, LANES), jnp.float32),
+                VMEM((POTS, width), jnp.bfloat16),
+                VMEM((8, width), jnp.float32),
+                VMEM((dim, block), jnp.float32),
+            ],
         ),
-        grid=(steps,),
-        in_specs=[
-            pl.BlockSpec((dim, block), lambda k: (0, lead + k)),
-            pl.BlockSpec((p_rows.shape[0], block), lambda k: (0, lead + k)),
-            full(right),
-        ]
-        + [line] * len(lines)
-        + [full(one) for one in extra]
-        + [pl.BlockSpec(memory_space=pl.ANY)] * len(before),
-        out_specs=pl.BlockSpec((dim, block), lambda k: (0, into + k)),
         out_shape=jax.ShapeDtypeStruct((dim, total * block), jnp.float32),
-        scratch_shapes=[
-            VMEM((block, LANES), jnp.float32),
-            VMEM((POTS, width), jnp.bfloat16),
-            VMEM((8, width), jnp.float32),
-            VMEM((block, dim), jnp.float32),
-        ],
-        input_output_aliases={3 + len(lines) + len(extra): 0} if before else {},
+        input_output_aliases={len(scalars) + 3 + len(lines) + len(extra): 0} if before else {},
         compiler_params=params(),
         cost_estimate=cost(steps * block, width, 2),
         name="centroid_update" if update else "code_gradient",
-    )(left, p_rows, right, *lines, *extra, *before)
+    )(*scalars, left, p_rows, right, *lines, *extra, *before)
 
 
 def small(kernel, index, arrays, out_shape, **settings):
@@ -504,7 +513,8 @@
 
     stats = held[0]
     for flips in [[("bucket", 1)]] + [[flip] for flip in side_bits[:-1]]:
-        stats = merged(stats, joint_swap(stats, flips))
+        received = joint_swap(stats, flips)
+        stats = merged(stats, received)
     terms = exchanged(stats, groups_of([side_bits[-1], item_bits[0]])[0])
     rows = spread_rows(potential(merged(terms[0], terms[1])), item)
     rows = rows + spread_rows(potential(merged(terms[2], terms[3])), item ^ 1)
@@ -525,11 +535,10 @@
         ],
     )
 
-    own = lax.dynamic_slice_in_dim(centroids_t, item * share, share, axis=1)
     old = []
     row_first = None
     for iteration in range(ITERS):
-        total, cols, row = sink(own, right, terms, old, rows_total, buckets_total)
+        total, cols, row = sink(centroids_t, item, share, right, terms, old, rows_total, buckets_total)
         old = [cols, row]
         if row_first is None:
             row_first = row
@@ -558,7 +567,7 @@
 
     blocks = share // block_of(share, rows_total)
     update = final(
-        own, cols, right, [row, row_first, *terms], codes, 1, True, rows_total, 0, blocks, blocks, []
+        centroids_t, item, share, cols, right, [row, row_first, *terms], codes, 1, True, rows_total, 0, blocks, blocks, []
     )
     pieces = gather_blocks(update, "item")
 
@@ -572,7 +581,9 @@
         held = []
         for steps in sizes:
             held = [
-                final(codes_t, p_rows, centroids_t, [col], None, 2, False, rows_total, done, steps, sum(sizes), held)
+                final(
+                    codes_t, item, rows_own, p_rows, centroids_t, [col], None, 2, False, rows_total, done, steps, sum(sizes), held
+                )
             ]
             done += steps
         grad = held[0]

time: 226 us -> 227 us (level)
  Pallas kernels: 103 us -> 106 us
    pallas_call x9, Pallas kernels: 94.1 us -> 97.1 us  [the longest x3 43.4 us: sink(): pl.pallas_call(lambda at_ref, *refs: kernel(*refs), grid_spec=pltpu.Prefe...]
where the time goes in v6:
time: 227 us; the launch traced here: 226 us
  Pallas kernels  106 us (47%)
  starting transfers between devices  52.4 us (23%)
  waiting for transfers between devices  51.7 us (23%)
  other arithmetic  9.35 us (4%)
  local copies, waits for them, and re-layouts  5.69 us (3%)
    pallas_call x3, Pallas kernels, sink(): pl.pallas_call(lambda at_ref, *refs: kernel(*refs), grid_spec=pltpu.Prefe...  43.4 us
    pallas_call x4, Pallas kernels, final(): pl.pallas_call((lambda at_ref, *refs: kernel(*refs)) if update else kerne...  39 us
    ppermute x25, starting transfers between devices, joint_swap(): return lax.ppermute(value, ('item', 'bucket'), pairs)  32.2 us
    ppermute x22, waiting for transfers between devices, swap(): return lax.ppermute(value, axis, [(k, k ^ bit) for k in range(size)])  29.5 us
    ppermute x25, waiting for transfers between devices, joint_swap(): return lax.ppermute(value, ('item', 'bucket'), pairs)  22.2 us
    ppermute x22, starting transfers between devices, swap(): return lax.ppermute(value, axis, [(k, k ^ bit) for k in range(size)])  20.2 us
    pallas_call x2, Pallas kernels, lse(): pl.pallas_call(functools.partial(lse_kernel, repeat=repeat), grid=(count,...  14.7 us
    pallas_call x3, Pallas kernels, small(): pl.pallas_call(functools.partial(kernel, **settings), grid_spec=pltpu.Pre...  9.06 us
  transfers between devices with their start and end apart: 47, of which 24 were waited for; matrix products, arithmetic and copies ran while one was open for 3% of the time, Pallas kernels for 18%

profile of v6, /device:TPU:0, one launch (start us, length us, event | category | flops | bytes accessed | tf_op | source)
XLA Modules:
  0.0 226.3 jit_solution(2917809102395407565)
XLA Ops:
  1.5 4.1 %collective-permute-start.3 = (f32[64,512]{1,0:T(8,128)S(1)}, f32[64,512]{1,0:T(8,128)S(1)}, u32[]{:S(2)}, u32[]{:S(2)}) collective-permute-start(f32[64,512]{1,0:T(8,128)S(1)} %convert_bitcast_fusion.refs_0_), channel_id=1, source_target_pairs={{0,16},{4,20},{8,24},{12,28},{16,0},{20,4},{24,8},{28,12},{1,17},{... | collective-permute-start | bytes 393224 | tf_op jit(solution)/shard_map/ppermute | solution.py:26
  5.6 7.4 %row_lse.2.rest_0_ = f32[2,1024]{1,0:T(2,128)} custom-call(bf16[64,1024]{1,0:T(8,128)(2,1)} %bitcast.10, bf16[64,8192]{1,0:T(8,128)(2,1)} %bitcast.15), custom_call_target="tpu_custom_call" | custom-call | flops 2147483648 | bytes 4194304 | tf_op jit(solution)/shard_map/row_lse/pallas_call | solution.py:349
  13.0 7.4 %row_lse.3 = f32[2,1024]{1,0:T(2,128)} custom-call(bf16[64,1024]{1,0:T(8,128)(2,1)} %bitcast.11, bf16[64,8192]{1,0:T(8,128)(2,1)} %bitcast.16, f32[2,1024]{1,0:T(2,128)} %row_lse.2.rest_0_), custom_call_target="tpu_custom_call", output_to_operand_aliasing={{}: (2, {})} | custom-call | flops 2147483648 | bytes 4194304 | tf_op jit(solution)/shard_map/row_lse/pallas_call | solution.py:349
  32.1 3.7 %collective-permute-done.4.refs_5_ = f32[64,512]{1,0:T(8,128)S(1)} collective-permute-done((f32[64,512]{1,0:T(8,128)S(1)}, f32[64,512]{1,0:T(8,128)S(1)}, u32[]{:S(2)}, u32[]{:S(2)}) %collective-permute-start.4) | collective-permute-done | bytes 131104 | tf_op jit(solution)/shard_map/ppermute | solution.py:26
  35.8 2.5 %collective-permute-done.2.refs_3_ = f32[64,512]{1,0:T(8,128)S(1)} collective-permute-done((f32[64,512]{1,0:T(8,128)S(1)}, f32[64,512]{1,0:T(8,128)S(1)}, u32[]{:S(2)}, u32[]{:S(2)}) %collective-permute-start.2) | collective-permute-done | bytes 131104 | tf_op jit(solution)/shard_map/ppermute | solution.py:26
  40.3 2.3 %shard_map.41.mine_ref = f32[64,4096]{1,0:T(8,128)} custom-call(s32[1]{0:T(128)} %bitcast.1.item_ref.at_ref, f32[64,512]{1,0:T(8,128)} %copy-done.1, f32[64,512]{1,0:T(8,128)} %copy-done.13, f32[64,512]{1,0:T(8,128)} %copy-done.11, f32[64,512]{1,0:T(8,128)} %copy-done.15, f32[64,512]{1,0:T(8,128)} %copy-done.10, f32[64,512]{1,0:T(8,128)} %copy-done.14, ...), custom_call_target="tpu_custom_call" | custom-call | bytes 4194304 | tf_op jit(solution)/shard_map/pallas_call | solution.py:445
  42.9 1.6 collective-permute-start.12
  44.9 2.5 %collective-permute-start.14 = (f32[1,8192]{1,0:T(1,128)S(1)}, f32[1,8192]{1,0:T(1,128)S(1)}, u32[]{:S(2)}, u32[]{:S(2)}) collective-permute-start(f32[1,8192]{1,0:T(1,128)S(1)} %add.128.refs_2_), channel_id=1, source_target_pairs={{0,24},{1,25},{2,26},{3,27},{4,28},{5,29},{6,30},{7,31},{8,16},{9,... | collective-permute-start | bytes 98312 | tf_op jit(solution)/shard_map/ppermute | solution.py:43
  48.3 3.8 %shard_map.42 = (bf16[128,8192]{1,0:T(8,128)(2,1)}, bf16[64,8192]{1,0:T(8,128)(2,1)}) custom-call(s32[1]{0:T(128)} %bitcast.3.core_ref, f32[64,4096]{1,0:T(8,128)} %shard_map.41.mine_ref, f32[64,4096]{1,0:T(8,128)} %copy-done), custom_call_target="tpu_custom_call" | custom-call | bytes 4194304 | tf_op jit(solution)/shard_map/pallas_call | solution.py:445
  52.7 18.4 %sinkhorn_first.1 = (f32[1,8192]{1,0:T(1,128)}, f32[8,1024]{1,0:T(8,128)}, f32[1,8192]{1,0:T(1,128)}) custom-call(s32[1]{0:T(128)} %bitcast.1.item_ref.at_ref, bf16[64,8192]{1,0:T(8,128)(2,1)} %bitcast.17, bf16[128,8192]{1,0:T(8,128)(2,1)} %get-tuple-element.13.refs_1_.refs_2_, f32[1,8192]{1,0:T(1,128)} %copy-done.25, f32[1,8192]{1,0:T(1,128)} %copy-done.29, ...), custom_call_target="tpu_custom_call" | custom-call | flops 4294967296 | bytes 4194304 | tf_op jit(solution)/shard_map/sinkhorn_first/pallas_call | solution.py:375
  78.0 2.2 collective-permute-done.18
  82.2 2.5 %collective-permute-start.21 = (f32[1,8192]{1,0:T(1,128)S(1)}, f32[1,8192]{1,0:T(1,128)S(1)}, u32[]{:S(2)}, u32[]{:S(2)}) collective-permute-start(f32[1,8192]{1,0:T(1,128)S(1)} %add_add_fusion.2.refs_2_), channel_id=1, source_target_pairs={{0,24},{1,25},{2,26},{3,27},{4,28},{5,29},{6,30},{7,31},{8,16},{9,... | collective-permute-start | bytes 98312 | tf_op jit(solution)/shard_map/ppermute | solution.py:43
  85.8 2.1 collective-permute-done.21.refs_5_
  88.6 12.5 %sinkhorn_next.2 = (f32[1,8192]{1,0:T(1,128)}, f32[8,1024]{1,0:T(8,128)}, f32[1,8192]{1,0:T(1,128)}) custom-call(s32[1]{0:T(128)} %bitcast.1.item_ref.at_ref, bf16[64,8192]{1,0:T(8,128)(2,1)} %bitcast.18, bf16[128,8192]{1,0:T(8,128)(2,1)} %get-tuple-element.13.refs_1_.refs_2_, f32[1,8192]{1,0:T(1,128)} %copy-done.26, f32[1,8192]{1,0:T(1,128)} %copy-done.33, ...), custom_call_target="tpu_custom_call" | custom-call | flops 4294967296 | bytes 4194304 | tf_op jit(solution)/shard_map/sinkhorn_next/pallas_call | solution.py:375
  103.4 1.6 collective-permute-start.23
  110.4 3.0 %collective-permute-start.27 = (f32[1,8192]{1,0:T(1,128)S(1)}, f32[1,8192]{1,0:T(1,128)S(1)}, u32[]{:S(2)}, u32[]{:S(2)}) collective-permute-start(f32[1,8192]{1,0:T(1,128)S(1)} %add_add_fusion.1.refs_2_), channel_id=1, source_target_pairs={{0,16},{1,17},{2,18},{3,19},{4,20},{5,21},{6,22},{7,23},{8,24},{9,... | collective-permute-start | bytes 98312 | tf_op jit(solution)/shard_map/ppermute | solution.py:43
  115.4 3.8 %collective-permute-done.28.refs_5_ = f32[1,8192]{1,0:T(1,128)S(1)} collective-permute-done((f32[1,8192]{1,0:T(1,128)S(1)}, f32[1,8192]{1,0:T(1,128)S(1)}, u32[]{:S(2)}, u32[]{:S(2)}) %collective-permute-start.28) | collective-permute-done | bytes 32800 | tf_op jit(solution)/shard_map/ppermute | solution.py:43
  119.8 12.5 %sinkhorn_next.3 = (f32[1,8192]{1,0:T(1,128)}, f32[8,1024]{1,0:T(8,128)}, f32[1,8192]{1,0:T(1,128)}) custom-call(s32[1]{0:T(128)} %bitcast.1.item_ref.at_ref, bf16[64,8192]{1,0:T(8,128)(2,1)} %bitcast.19, bf16[128,8192]{1,0:T(8,128)(2,1)} %get-tuple-element.13.refs_1_.refs_2_, f32[1,8192]{1,0:T(1,128)} %copy-done.24, f32[1,8192]{1,0:T(1,128)} %copy-done.27, ...), custom_call_target="tpu_custom_call" | custom-call | flops 4294967296 | bytes 4194304 | tf_op jit(solution)/shard_map/sinkhorn_next/pallas_call | solution.py:375
  138.2 2.3 %collective-permute-done.30 = f32[1,8192]{1,0:T(1,128)S(1)} collective-permute-done((f32[1,8192]{1,0:T(1,128)S(1)}, f32[1,8192]{1,0:T(1,128)S(1)}, u32[]{:S(2)}, u32[]{:S(2)}) %collective-permute-start.30) | collective-permute-done | bytes 32800 | tf_op jit(solution)/shard_map/ppermute | solution.py:43
  142.5 1.9 collective-permute-start.34
  144.4 2.5 %collective-permute-start.35 = (f32[1,16384]{1,0:T(1,128)S(1)}, f32[1,16384]{1,0:T(1,128)S(1)}, u32[]{:S(2)}, u32[]{:S(2)}) collective-permute-start(f32[1,16384]{1,0:T(1,128)S(1)} %pad_maximum_fusion.1.refs_5_), channel_id=1, source_target_pairs={{0,24},{1,25},{2,26},{3,27},{4,28},{5,29},{6,30},{7,31},{8,16},{9,... | collective-permute-start | bytes 196616 | tf_op jit(solution)/shard_map/ppermute | solution.py:43
  148.2 2.3 %collective-permute-done.35.refs_8_ = f32[1,16384]{1,0:T(1,128)S(1)} collective-permute-done((f32[1,16384]{1,0:T(1,128)S(1)}, f32[1,16384]{1,0:T(1,128)S(1)}, u32[]{:S(2)}, u32[]{:S(2)}) %collective-permute-start.35) | collective-permute-done | bytes 65568 | tf_op jit(solution)/shard_map/ppermute | solution.py:43
  151.1 18.1 %centroid_update.1.refs_0_ = f32[64,1024]{1,0:T(8,128)} custom-call(s32[1]{0:T(128)} %bitcast.1.item_ref.at_ref, bf16[64,8192]{1,0:T(8,128)(2,1)} %bitcast.20, f32[8,1024]{1,0:T(8,128)} %get-tuple-element.22.refs_1_, bf16[128,8192]{1,0:T(8,128)(2,1)} %get-tuple-element.13.refs_1_.refs_2_, f32[1,8192]{1,0:T(1,128)} %get-tuple-element.20.refs_3_, ...), custom_call_target="tpu_custom_call" | custom-call | flops 8589934592 | bytes 4194304 | tf_op jit(solution)/shard_map/centroid_update/pallas_call | solution.py:419
  169.2 3.0 %collective-permute-start.41 = (f32[64,1024]{1,0:T(8,128)}, f32[64,1024]{1,0:T(8,128)S(1)}, u32[]{:S(2)}, u32[]{:S(2)}) collective-permute-start(f32[64,1024]{1,0:T(8,128)} %centroid_update.1.refs_0_), channel_id=1, source_target_pairs={{0,8},{4,12},{8,0},{12,4},{16,24},{20,28},{24,16},{28,20},{1,9},{5... | collective-permute-start | bytes 786440 | tf_op jit(solution)/shard_map/ppermute | solution.py:26
  174.7 9.4 %code_gradient.3 = f32[64,512]{1,0:T(8,128)} custom-call(bf16[64,1024]{1,0:T(8,128)(2,1)} %bitcast.12, f32[2,1024]{1,0:T(2,128)} %pad_maximum_fusion.3.p_ref, bf16[64,8192]{1,0:T(8,128)(2,1)} %bitcast.21, f32[1,8192]{1,0:T(1,128)} %get-tuple-element.26.rest_0_), custom_call_target="tpu_custom_call" | custom-call | flops 4294967296 | bytes 4194304 | tf_op jit(solution)/shard_map/code_gradient/pallas_call | solution.py:419
  184.1 5.7 %code_gradient.4.rest_1_ = f32[64,512]{1,0:T(8,128)} custom-call(bf16[64,1024]{1,0:T(8,128)(2,1)} %bitcast.13, f32[2,1024]{1,0:T(2,128)} %pad_maximum_fusion.3.p_ref, bf16[64,8192]{1,0:T(8,128)(2,1)} %bitcast.22, f32[1,8192]{1,0:T(1,128)} %get-tuple-element.26.rest_0_), custom_call_target="tpu_custom_call" | custom-call | flops 2147483648 | bytes 4194304 | tf_op jit(solution)/shard_map/code_gradient/pallas_call | solution.py:419
  189.9 5.8 %code_gradient.5 = f32[64,512]{1,0:T(8,128)} custom-call(bf16[64,1024]{1,0:T(8,128)(2,1)} %bitcast.14, f32[2,1024]{1,0:T(2,128)} %pad_maximum_fusion.3.p_ref, bf16[64,8192]{1,0:T(8,128)(2,1)} %bitcast.23, f32[1,8192]{1,0:T(1,128)} %get-tuple-element.26.rest_0_, f32[64,512]{1,0:T(8,128)} %code_gradient.4.rest_1_), custom_call_target="tpu_custom_call", output_to_operand_aliasing={{}: (4, {})} | custom-call | flops 2147483648 | bytes 4194304 | tf_op jit(solution)/shard_map/code_gradient/pallas_call | solution.py:419
  196.2 1.6 collective-permute-start.37
  203.4 4.4 %collective-permute-done.39 = f32[64,512]{1,0:T(8,128)S(1)} collective-permute-done((f32[64,512]{1,0:T(8,128)S(1)}, f32[64,512]{1,0:T(8,128)S(1)}, u32[]{:S(2)}, u32[]{:S(2)}) %collective-permute-start.39) | collective-permute-done | bytes 131104 | tf_op jit(solution)/shard_map/ppermute | solution.py:26
  208.6 9.6 %collective-permute-done.42.refs_3_ = f32[64,1024]{1,0:T(8,128)S(1)} collective-permute-done((f32[64,1024]{1,0:T(8,128)S(1)}, f32[64,1024]{1,0:T(8,128)S(1)}, u32[]{:S(2)}, u32[]{:S(2)}) %collective-permute-start.42) | collective-permute-done | bytes 262176 | tf_op jit(solution)/shard_map/ppermute | solution.py:26
  218.3 4.4 %collective-permute-done.46.refs_7_ = f32[64,1024]{1,0:T(8,128)S(1)} collective-permute-done((f32[64,1024]{1,0:T(8,128)S(1)}, f32[64,1024]{1,0:T(8,128)S(1)}, u32[]{:S(2)}, u32[]{:S(2)}) %collective-permute-start.46) | collective-permute-done | bytes 262176 | tf_op jit(solution)/shard_map/ppermute | solution.py:26
  223.4 3.0 %shard_map.43 = f32[64,8192]{1,0:T(8,128)} custom-call(s32[1]{0:T(128)} %bitcast.1.item_ref.at_ref, f32[64,1024]{1,0:T(8,128)} %centroid_update.1.refs_0_, f32[64,1024]{1,0:T(8,128)} %copy-done.6, f32[64,1024]{1,0:T(8,128)} %copy-done.4, f32[64,1024]{1,0:T(8,128)} %copy-done.8, f32[64,1024]{1,0:T(8,128)} %copy-done.3, f32[64,1024]{1,0:T(8,128)} %copy-done.7, ...), custom_call_target="tpu_custom_call" | custom-call | bytes 4194304 | tf_op jit(solution)/shard_map/pallas_call | solution.py:445
  (178 shorter events, 57.4 us)
Async XLA Ops:
  1.5 20.4 %collective-permute-start.3 = (f32[64,512]{1,0:T(8,128)S(1)}, f32[64,512]{1,0:T(8,128)S(1)}, u32[]{:S(2)}, u32[]{:S(2)}) collective-permute-start(f32[64,512]{1,0:T(8,128)S(1)} %convert_bitcast_fusion.refs_0_), channel_id=1, source_target_pairs={{0,16},{4,20},{8,24},{12,28},{16,0},{20,4},{24,8},{28,12},{1,17},{... | collective-permute-start | bytes 393224 | tf_op jit(solution)/shard_map/ppermute | solution.py:26
  20.4 9.6 %collective-permute-start.1 = (f32[64,512]{1,0:T(8,128)S(1)}, f32[64,512]{1,0:T(8,128)S(1)}, u32[]{:S(2)}, u32[]{:S(2)}) collective-permute-start(f32[64,512]{1,0:T(8,128)S(1)} %convert_bitcast_fusion.refs_0_), channel_id=1, source_target_pairs={{0,8},{4,12},{8,0},{12,4},{16,24},{20,28},{24,16},{28,20},{1,9},{5... | collective-permute-start | bytes 393224 | tf_op jit(solution)/shard_map/ppermute | solution.py:26
  22.0 9.5 %collective-permute-start.5 = (f32[64,512]{1,0:T(8,128)S(1)}, f32[64,512]{1,0:T(8,128)S(1)}, u32[]{:S(2)}, u32[]{:S(2)}) collective-permute-start(f32[64,512]{1,0:T(8,128)S(1)} %collective-permute-done.3.refs_4_), channel_id=1, source_target_pairs={{0,8},{4,12},{8,0},{12,4},{16,24},{20,28},{24,16},{28,20},{1,9},{5... | collective-permute-start | bytes 393224 | tf_op jit(solution)/shard_map/ppermute | solution.py:26
  26.3 5.8 %collective-permute-start = (f32[64,512]{1,0:T(8,128)S(1)}, f32[64,512]{1,0:T(8,128)S(1)}, u32[]{:S(2)}, u32[]{:S(2)}) collective-permute-start(f32[64,512]{1,0:T(8,128)S(1)} %convert_bitcast_fusion.refs_0_), channel_id=1, source_target_pairs={{0,4},{4,0},{8,12},{12,8},{16,20},{20,16},{24,28},{28,24},{1,5},{5... | collective-permute-start | bytes 393224 | tf_op jit(solution)/shard_map/ppermute | solution.py:26
  27.8 15.0 %collective-permute-start.9 = (f32[2,1024]{1,0:T(2,128)S(1)}, f32[2,1024]{1,0:T(2,128)S(1)}, u32[]{:S(2)}, u32[]{:S(2)}) collective-permute-start(f32[2,1024]{1,0:T(2,128)S(1)} %pad_maximum_fusion.2), channel_id=1, source_target_pairs={{0,2},{1,3},{2,0},{3,1},{4,6},{5,7},{6,4},{7,5},{8,10},{9,11},{10,... | collective-permute-start | bytes 24584 | tf_op jit(solution)/shard_map/ppermute | solution.py:43
  29.4 6.4 %collective-permute-start.4 = (f32[64,512]{1,0:T(8,128)S(1)}, f32[64,512]{1,0:T(8,128)S(1)}, u32[]{:S(2)}, u32[]{:S(2)}) collective-permute-start(f32[64,512]{1,0:T(8,128)S(1)} %collective-permute-done.3.refs_4_), channel_id=1, source_target_pairs={{0,4},{4,0},{8,12},{12,8},{16,20},{20,16},{24,28},{28,24},{1,5},{5... | collective-permute-start | bytes 393224 | tf_op jit(solution)/shard_map/ppermute | solution.py:26
  30.0 8.3 %collective-permute-start.2 = (f32[64,512]{1,0:T(8,128)S(1)}, f32[64,512]{1,0:T(8,128)S(1)}, u32[]{:S(2)}, u32[]{:S(2)}) collective-permute-start(f32[64,512]{1,0:T(8,128)S(1)} %collective-permute-done.1.refs_2_), channel_id=1, source_target_pairs={{0,4},{4,0},{8,12},{12,8},{16,20},{20,16},{24,28},{28,24},{1,5},{5... | collective-permute-start | bytes 393224 | tf_op jit(solution)/shard_map/ppermute | solution.py:26
  31.5 8.2 %collective-permute-start.6 = (f32[64,512]{1,0:T(8,128)S(1)}, f32[64,512]{1,0:T(8,128)S(1)}, u32[]{:S(2)}, u32[]{:S(2)}) collective-permute-start(f32[64,512]{1,0:T(8,128)S(1)} %collective-permute-done.5.refs_6_), channel_id=1, source_target_pairs={{0,4},{4,0},{8,12},{12,8},{16,20},{20,16},{24,28},{28,24},{1,5},{5... | collective-permute-start | bytes 393224 | tf_op jit(solution)/shard_map/ppermute | solution.py:26
  42.7 4.7 %collective-permute-start.7 = (f32[64,4096]{1,0:T(8,128)}, f32[64,4096]{1,0:T(8,128)S(1)}, u32[]{:S(2)}, u32[]{:S(2)}) collective-permute-start(f32[64,4096]{1,0:T(8,128)} %shard_map.41.mine_ref), channel_id=1, source_target_pairs={{0,1},{1,0},{2,3},{3,2},{4,5},{5,4},{6,7},{7,6},{8,9},{9,8},{10,11... | collective-permute-start | bytes 3145736 | tf_op jit(solution)/shard_map/ppermute | solution.py:26
  42.9 9.2 %collective-permute-start.12 = (f32[1,8192]{1,0:T(1,128)S(1)}, f32[1,8192]{1,0:T(1,128)S(1)}, u32[]{:S(2)}, u32[]{:S(2)}) collective-permute-start(f32[1,8192]{1,0:T(1,128)S(1)} %add.128.refs_2_), channel_id=1, source_target_pairs={{0,8},{1,9},{2,10},{3,11},{4,12},{5,13},{6,14},{7,15},{8,0},{9,1},... | collective-permute-start | bytes 98312 | tf_op jit(solution)/shard_map/ppermute | solution.py:43
  44.5 7.6 %collective-permute-start.13 = (f32[1,8192]{1,0:T(1,128)S(1)}, f32[1,8192]{1,0:T(1,128)S(1)}, u32[]{:S(2)}, u32[]{:S(2)}) collective-permute-start(f32[1,8192]{1,0:T(1,128)S(1)} %add.128.refs_2_), channel_id=1, source_target_pairs={{0,16},{1,17},{2,18},{3,19},{4,20},{5,21},{6,22},{7,23},{8,24},{9,... | collective-permute-start | bytes 98312 | tf_op jit(solution)/shard_map/ppermute | solution.py:43
  44.9 7.2 %collective-permute-start.14 = (f32[1,8192]{1,0:T(1,128)S(1)}, f32[1,8192]{1,0:T(1,128)S(1)}, u32[]{:S(2)}, u32[]{:S(2)}) collective-permute-start(f32[1,8192]{1,0:T(1,128)S(1)} %add.128.refs_2_), channel_id=1, source_target_pairs={{0,24},{1,25},{2,26},{3,27},{4,28},{5,29},{6,30},{7,31},{8,16},{9,... | collective-permute-start | bytes 98312 | tf_op jit(solution)/shard_map/ppermute | solution.py:43
  75.4 4.8 %collective-permute-start.18 = (f32[1,8192]{1,0:T(1,128)S(1)}, f32[1,8192]{1,0:T(1,128)S(1)}, u32[]{:S(2)}, u32[]{:S(2)}) collective-permute-start(f32[1,8192]{1,0:T(1,128)S(1)} %add.129), channel_id=1, source_target_pairs={{0,6},{1,7},{2,4},{3,5},{4,2},{5,3},{6,0},{7,1},{8,14},{9,15},{10,... | collective-permute-start | bytes 98312 | tf_op jit(solution)/shard_map/ppermute | solution.py:43
  81.0 4.8 %collective-permute-start.20 = (f32[1,8192]{1,0:T(1,128)S(1)}, f32[1,8192]{1,0:T(1,128)S(1)}, u32[]{:S(2)}, u32[]{:S(2)}) collective-permute-start(f32[1,8192]{1,0:T(1,128)S(1)} %add_add_fusion.2.refs_2_), channel_id=1, source_target_pairs={{0,16},{1,17},{2,18},{3,19},{4,20},{5,21},{6,22},{7,23},{8,24},{9,... | collective-permute-start | bytes 98312 | tf_op jit(solution)/shard_map/ppermute | solution.py:43
  82.2 5.7 %collective-permute-start.21 = (f32[1,8192]{1,0:T(1,128)S(1)}, f32[1,8192]{1,0:T(1,128)S(1)}, u32[]{:S(2)}, u32[]{:S(2)}) collective-permute-start(f32[1,8192]{1,0:T(1,128)S(1)} %add_add_fusion.2.refs_2_), channel_id=1, source_target_pairs={{0,24},{1,25},{2,26},{3,27},{4,28},{5,29},{6,30},{7,31},{8,16},{9,... | collective-permute-start | bytes 98312 | tf_op jit(solution)/shard_map/ppermute | solution.py:43
  105.5 4.8 %collective-permute-start.25 = (f32[1,8192]{1,0:T(1,128)S(1)}, f32[1,8192]{1,0:T(1,128)S(1)}, u32[]{:S(2)}, u32[]{:S(2)}) collective-permute-start(f32[1,8192]{1,0:T(1,128)S(1)} %add.133), channel_id=1, source_target_pairs={{0,6},{1,7},{2,4},{3,5},{4,2},{5,3},{6,0},{7,1},{8,14},{9,15},{10,... | collective-permute-start | bytes 98312 | tf_op jit(solution)/shard_map/ppermute | solution.py:43
  110.4 4.9 %collective-permute-start.27 = (f32[1,8192]{1,0:T(1,128)S(1)}, f32[1,8192]{1,0:T(1,128)S(1)}, u32[]{:S(2)}, u32[]{:S(2)}) collective-permute-start(f32[1,8192]{1,0:T(1,128)S(1)} %add_add_fusion.1.refs_2_), channel_id=1, source_target_pairs={{0,16},{1,17},{2,18},{3,19},{4,20},{5,21},{6,22},{7,23},{8,24},{9,... | collective-permute-start | bytes 98312 | tf_op jit(solution)/shard_map/ppermute | solution.py:43
  113.5 5.7 %collective-permute-start.28 = (f32[1,8192]{1,0:T(1,128)S(1)}, f32[1,8192]{1,0:T(1,128)S(1)}, u32[]{:S(2)}, u32[]{:S(2)}) collective-permute-start(f32[1,8192]{1,0:T(1,128)S(1)} %add_add_fusion.1.refs_2_), channel_id=1, source_target_pairs={{0,24},{1,25},{2,26},{3,27},{4,28},{5,29},{6,30},{7,31},{8,16},{9,... | collective-permute-start | bytes 98312 | tf_op jit(solution)/shard_map/ppermute | solution.py:43
  134.6 6.9 %collective-permute-start.31 = (f32[1,16384]{1,0:T(1,128)S(1)}, f32[1,16384]{1,0:T(1,128)S(1)}, u32[]{:S(2)}, u32[]{:S(2)}) collective-permute-start(f32[1,16384]{1,0:T(1,128)S(1)} %pad_maximum_fusion), channel_id=1, source_target_pairs={{0,4},{1,5},{2,6},{3,7},{4,0},{5,1},{6,2},{7,3},{8,12},{9,13},{10,... | collective-permute-start | bytes 196616 | tf_op jit(solution)/shard_map/ppermute | solution.py:43
  136.7 4.8 %collective-permute-start.32 = (f32[1,8192]{1,0:T(1,128)S(1)}, f32[1,8192]{1,0:T(1,128)S(1)}, u32[]{:S(2)}, u32[]{:S(2)}) collective-permute-start(f32[1,8192]{1,0:T(1,128)S(1)} %add.139), channel_id=1, source_target_pairs={{0,6},{1,7},{2,4},{3,5},{4,2},{5,3},{6,0},{7,1},{8,14},{9,15},{10,... | collective-permute-start | bytes 98312 | tf_op jit(solution)/shard_map/ppermute | solution.py:43
  142.5 5.7 %collective-permute-start.34 = (f32[1,16384]{1,0:T(1,128)S(1)}, f32[1,16384]{1,0:T(1,128)S(1)}, u32[]{:S(2)}, u32[]{:S(2)}) collective-permute-start(f32[1,16384]{1,0:T(1,128)S(1)} %pad_maximum_fusion.1.refs_5_), channel_id=1, source_target_pairs={{0,16},{1,17},{2,18},{3,19},{4,20},{5,21},{6,22},{7,23},{8,24},{9,... | collective-permute-start | bytes 196616 | tf_op jit(solution)/shard_map/ppermute | solution.py:43
  144.4 6.1 %collective-permute-start.35 = (f32[1,16384]{1,0:T(1,128)S(1)}, f32[1,16384]{1,0:T(1,128)S(1)}, u32[]{:S(2)}, u32[]{:S(2)}) collective-permute-start(f32[1,16384]{1,0:T(1,128)S(1)} %pad_maximum_fusion.1.refs_5_), channel_id=1, source_target_pairs={{0,24},{1,25},{2,26},{3,27},{4,28},{5,29},{6,30},{7,31},{8,16},{9,... | collective-permute-start | bytes 196616 | tf_op jit(solution)/shard_map/ppermute | solution.py:43
  169.2 20.6 %collective-permute-start.43 = (f32[64,1024]{1,0:T(8,128)}, f32[64,1024]{1,0:T(8,128)S(1)}, u32[]{:S(2)}, u32[]{:S(2)}) collective-permute-start(f32[64,1024]{1,0:T(8,128)} %centroid_update.1.refs_0_), channel_id=1, source_target_pairs={{0,16},{4,20},{8,24},{12,28},{16,0},{20,4},{24,8},{28,12},{1,17},{... | collective-permute-start | bytes 786440 | tf_op jit(solution)/shard_map/ppermute | solution.py:26
  169.2 30.7 %collective-permute-start.41 = (f32[64,1024]{1,0:T(8,128)}, f32[64,1024]{1,0:T(8,128)S(1)}, u32[]{:S(2)}, u32[]{:S(2)}) collective-permute-start(f32[64,1024]{1,0:T(8,128)} %centroid_update.1.refs_0_), channel_id=1, source_target_pairs={{0,8},{4,12},{8,0},{12,4},{16,24},{20,28},{24,16},{28,20},{1,9},{5... | collective-permute-start | bytes 786440 | tf_op jit(solution)/shard_map/ppermute | solution.py:26
  184.1 12.1 %collective-permute-start.36 = (f32[64,512]{1,0:T(8,128)}, f32[64,512]{1,0:T(8,128)S(1)}, u32[]{:S(2)}, u32[]{:S(2)}) collective-permute-start(f32[64,512]{1,0:T(8,128)} %code_gradient.3), channel_id=1, source_target_pairs={{0,1},{1,0},{2,3},{3,2},{4,5},{5,4},{6,7},{7,6},{8,9},{9,8},{10,11... | collective-permute-start | bytes 393224 | tf_op jit(solution)/shard_map/ppermute | solution.py:26
  189.8 10.6 %collective-permute-start.45 = (f32[64,1024]{1,0:T(8,128)S(1)}, f32[64,1024]{1,0:T(8,128)S(1)}, u32[]{:S(2)}, u32[]{:S(2)}) collective-permute-start(f32[64,1024]{1,0:T(8,128)S(1)} %collective-permute-done.43.refs_4_), channel_id=1, source_target_pairs={{0,8},{4,12},{8,0},{12,4},{16,24},{20,28},{24,16},{28,20},{1,9},{5... | collective-permute-start | bytes 786440 | tf_op jit(solution)/shard_map/ppermute | solution.py:26
  196.2 6.6 %collective-permute-start.37 = (f32[64,512]{1,0:T(8,128)S(1)}, f32[64,512]{1,0:T(8,128)S(1)}, u32[]{:S(2)}, u32[]{:S(2)}) collective-permute-start(f32[64,512]{1,0:T(8,128)S(1)} %add.148), channel_id=1, source_target_pairs={{0,2},{1,3},{2,0},{3,1},{4,6},{5,7},{6,4},{7,5},{8,10},{9,11},{10,... | collective-permute-start | bytes 393224 | tf_op jit(solution)/shard_map/ppermute | solution.py:26
  197.8 10.8 %collective-permute-start.40 = (f32[64,1024]{1,0:T(8,128)S(1)}, f32[64,1024]{1,0:T(8,128)S(1)}, u32[]{:S(2)}, u32[]{:S(2)}) collective-permute-start(f32[64,1024]{1,0:T(8,128)S(1)} %copy-done.2), channel_id=1, source_target_pairs={{0,4},{4,0},{8,12},{12,8},{16,20},{20,16},{24,28},{28,24},{1,5},{5... | collective-permute-start | bytes 786440 | tf_op jit(solution)/shard_map/ppermute | solution.py:26
  198.4 19.9 %collective-permute-start.44 = (f32[64,1024]{1,0:T(8,128)S(1)}, f32[64,1024]{1,0:T(8,128)S(1)}, u32[]{:S(2)}, u32[]{:S(2)}) collective-permute-start(f32[64,1024]{1,0:T(8,128)S(1)} %collective-permute-done.43.refs_4_), channel_id=1, source_target_pairs={{0,4},{4,0},{8,12},{12,8},{16,20},{20,16},{24,28},{28,24},{1,5},{5... | collective-permute-start | bytes 786440 | tf_op jit(solution)/shard_map/ppermute | solution.py:26
  199.9 18.4 %collective-permute-start.42 = (f32[64,1024]{1,0:T(8,128)S(1)}, f32[64,1024]{1,0:T(8,128)S(1)}, u32[]{:S(2)}, u32[]{:S(2)}) collective-permute-start(f32[64,1024]{1,0:T(8,128)S(1)} %collective-permute-done.41.refs_2_), channel_id=1, source_target_pairs={{0,4},{4,0},{8,12},{12,8},{16,20},{20,16},{24,28},{28,24},{1,5},{5... | collective-permute-start | bytes 786440 | tf_op jit(solution)/shard_map/ppermute | solution.py:26
  200.4 22.2 %collective-permute-start.46 = (f32[64,1024]{1,0:T(8,128)S(1)}, f32[64,1024]{1,0:T(8,128)S(1)}, u32[]{:S(2)}, u32[]{:S(2)}) collective-permute-start(f32[64,1024]{1,0:T(8,128)S(1)} %collective-permute-done.45.refs_6_), channel_id=1, source_target_pairs={{0,4},{4,0},{8,12},{12,8},{16,20},{20,16},{24,28},{28,24},{1,5},{5... | collective-permute-start | bytes 786440 | tf_op jit(solution)/shard_map/ppermute | solution.py:26
  202.8 5.0 %collective-permute-start.39 = (f32[64,512]{1,0:T(8,128)S(1)}, f32[64,512]{1,0:T(8,128)S(1)}, u32[]{:S(2)}, u32[]{:S(2)}) collective-permute-start(f32[64,512]{1,0:T(8,128)S(1)} %add.150), channel_id=1, source_target_pairs={{0,2},{1,3},{2,0},{3,1},{4,6},{5,7},{6,4},{7,5},{8,10},{9,11},{10,... | collective-permute-start | bytes 393224 | tf_op jit(solution)/shard_map/ppermute | solution.py:26
  (51 other events, 319.6 us)

commit v7 on v6

--- a/solution.py
+++ b/solution.py
@@ -15,7 +15,7 @@
 step_rate = 0.2
 epsilon = 1e-06
 
-CHUNK = 2048
+CHUNK = 4096
 SUB = 512
 LANES = 128
 POTS = 16
@@ -205,7 +205,7 @@
     term_refs, rest = rest[:terms], rest[terms:]
     if not first:
         p_ref, q_ref, *rest = rest
-    sums_ref, pot_ref, row_ref, y_ref, part_ref, high_ref, highs_ref, wide_ref, wpot_ref, acc_ref = rest
+    sums_ref, pot_ref, row_ref, y_ref, part_ref, high_ref, wide_ref, wpot_ref, acc_ref = rest
     block, width = y_ref.shape
 
     def run(new, old):
@@ -223,45 +223,46 @@
         if new:
             was = jnp.zeros((1, block), jnp.float32) if first else p_ref[0:1, :]
             left = jnp.concatenate([left_of(l_ref, False), left_pots(was, block)], axis=1)
-            part_ref[...] = jnp.zeros(part_ref.shape, jnp.float32)
-            if first:
-                high_ref[...] = jnp.full(high_ref.shape, -jnp.inf, jnp.float32)
-
-        def chunk(step, at):
+            part_ref[...] = jnp.full(part_ref.shape, -jnp.inf if first else 0.0, jnp.float32)
+
+        def chunk(_, at):
             if old:
-                each = chunk_of(width) // SUB
-                sums = []
-                for number, piece in enumerate(slices(y_ref[:, at])):
-                    wide = wide_ref[step * each + number * LANES // SUB if first else 0]
-                    sums.append(jnp.sum((piece * wide).reshape(block // 8, 8, LANES), axis=0))
+                sums = [
+                    jnp.sum((piece * wide_ref[...]).reshape(block // 8, 8, LANES), axis=0)
+                    for piece in slices(y_ref[:, at])
+                ]
                 acc_ref[:, at] += jnp.concatenate(sums, axis=1)
             if new:
                 right = jnp.concatenate([w_ref[:, at], wpot_ref[:, at]], axis=0)
+                y = jnp.dot(left, right, preferred_element_type=jnp.float32)
                 if first:
-                    terms = []
-                    for number in range(right.shape[1] // SUB):
-                        piece = right[:, number * SUB : (number + 1) * SUB]
-                        y = jnp.dot(left, piece, preferred_element_type=jnp.float32)
-                        high, more = raised(slices(y), high_ref, part_ref)
-                        highs_ref[step * (right.shape[1] // SUB) + number] = high
-                        terms += more
-                    y_ref[:, at] = jnp.concatenate(terms, axis=1)
+                    y_ref[:, at] = y
+                    part_ref[...] = jnp.maximum(part_ref[...], folded(slices(y), jnp.maximum))
                 else:
-                    y = jnp.exp(jnp.dot(left, right, preferred_element_type=jnp.float32))
+                    y = jnp.exp(y)
                     y_ref[:, at] = y
                     part_ref[...] += folded(slices(y), jnp.add)
 
         chunks(width, chunk)
         if new and first:
-            highest, summed = settled(high_ref, part_ref)
-            summed = summed * float(buckets_total)
-            for number in range(highs_ref.shape[0]):
-                wide_ref[number] = jnp.exp(highs_ref[number] - highest) / summed
-            pot_ref[...] = -row_of(highest + jnp.log(summed))
-        elif new:
+            highest = jnp.max(part_ref[...], axis=1, keepdims=True)
+            high_ref[...] = jnp.broadcast_to(highest, (block, LANES))
+            part_ref[...] = jnp.zeros(part_ref.shape, jnp.float32)
+
+            def again(_, at):
+                terms = [jnp.exp(piece - high_ref[...]) for piece in slices(y_ref[:, at])]
+                y_ref[:, at] = jnp.concatenate(terms, axis=1)
+                part_ref[...] += folded(terms, jnp.add)
+
+            chunks(width, again)
+        if new:
             summed = jnp.sum(part_ref[...], axis=1, keepdims=True) * float(buckets_total)
-            wide_ref[0] = jnp.broadcast_to(1.0 / summed, (block, LANES))
-            pot_ref[...] = was - jnp.log(row_of(summed))
+            wide_ref[...] = jnp.broadcast_to(1.0 / summed, (block, LANES))
+            summed = row_of(summed)
+            if first:
+                pot_ref[...] = -(row_of(high_ref[...]) + jnp.log(summed))
+            else:
+                pot_ref[...] = was - jnp.log(summed)
         if not new:
             sums_ref[...] = jnp.sum(acc_ref[...], axis=0, keepdims=True)
 
@@ -309,11 +310,11 @@
             axis=1,
         )
         acc_ref[...] += lax.dot_general(
-            r_ref[:, at], delta, (((1,), (1,)), ((), ())), preferred_element_type=jnp.float32
+            delta, r_ref[:, at], (((1,), (1,)), ((), ())), preferred_element_type=jnp.float32
         )
 
     chunks(width, chunk)
-    gradient = score_scale * acc_ref[...]
+    gradient = score_scale * jnp.transpose(acc_ref[...])
     if update:
         moved = l_ref[...].astype(jnp.float32) - step_rate * gradient
         gradient = moved * lax.rsqrt(jnp.mean(moved * moved, axis=0, keepdims=True) + epsilon)
@@ -324,7 +325,7 @@
 
 
 def block_of(count, width):
-    return min(count, 256 if width <= 16384 else 128)
+    return min(count, 512 if width <= 16384 else 128)
 
 
 def params():
@@ -383,8 +384,7 @@
         + ([] if first else [pot_spec, line]),
         out_specs=[line, pot_spec, line],
         scratch_shapes=[VMEM((block, width), jnp.float32)]
-        + [VMEM((block, LANES), jnp.float32)] * 2
-        + [VMEM((width // SUB if first else 1, block, LANES), jnp.float32)] * 2
+        + [VMEM((block, LANES), jnp.float32)] * 3
         + [VMEM((POTS, width), jnp.bfloat16), VMEM((8, width), jnp.float32)],
         ),
         out_shape=[
@@ -398,9 +398,8 @@
     )(item.reshape(1).astype(jnp.int32), left, right, *terms, *old)
 
 
-def final(left, item, rows, p_rows, right, lines, codes, repeat, update, rows_total, lead, steps, total, before):
+def final(left, item, rows, p_rows, right, lines, codes, repeat, update, rows_total, block, lead, steps, total, before):
     dim, width = left.shape[0], right.shape[1]
-    block = block_of(rows, width)
     count = rows // block
     into = total - steps if before else 0
     extra = [codes] if update else []
@@ -427,7 +426,7 @@
                 VMEM((block, LANES), jnp.float32),
                 VMEM((POTS, width), jnp.bfloat16),
                 VMEM((8, width), jnp.float32),
-                VMEM((dim, block), jnp.float32),
+                VMEM((block, dim), jnp.float32),
             ],
         ),
         out_shape=jax.ShapeDtypeStruct((dim, total * block), jnp.float32),
@@ -565,27 +564,27 @@
         col = functools.reduce(jnp.add, held_cols)
     terms = exchanged(jnp.concatenate([total, col], axis=1), groups[-1])
 
-    blocks = share // block_of(share, rows_total)
+    block = block_of(share, rows_total)
     update = final(
-        centroids_t, item, share, cols, right, [row, row_first, *terms], codes, 1, True, rows_total, 0, blocks, blocks, []
+        centroids_t, item, share, cols, right, [row, row_first, *terms], codes, 1, True, rows_total,
+        block, 0, share // block, share // block, [],
     )
     pieces = gather_blocks(update, "item")
 
     both = joined(terms)
     mass, col = both[:, :rows_total] * float(rows_total), both[:, rows_total:]
     p_rows = own_rows(jnp.concatenate([row + log_rows, mass * jnp.exp(row_first - row)], axis=0))
-    blocks = rows_own // block_of(rows_own, buckets_own)
     halves = []
-    done = 0
-    for sizes in [[blocks // 2], [blocks // 4, blocks // 4]]:
+    for half, calls in enumerate([1, 2]):
         held = []
-        for steps in sizes:
+        for call in range(calls):
+            block = rows_half // calls
             held = [
                 final(
-                    codes_t, item, rows_own, p_rows, centroids_t, [col], None, 2, False, rows_total, done, steps, sum(sizes), held
+                    codes_t, item, rows_own, p_rows, centroids_t, [col], None, 2, False, rows_total,
+                    block, half * calls + call, 1, calls, held,
                 )
             ]
-            done += steps
         grad = held[0]
         for bit in bits_of("bucket"):
             received = swap(grad, "bucket", bit)

time: 227 us -> 211 us (0.930)
  Pallas kernels: 106 us -> 90.2 us
    pallas_call x4, Pallas kernels: 39 us -> 30.8 us  [final(): pl.pallas_call((lambda at_ref, *refs: kernel(*refs)) if update else kerne...]
    pallas_call x3, Pallas kernels: 43.4 us -> 37.7 us  [sink(): pl.pallas_call(lambda at_ref, *refs: kernel(*refs), grid_spec=pltpu.Prefe...]
  transfers between devices with their start and end apart: 47 -> 47, of which waited for: 24 -> 24; matrix products, arithmetic and copies ran while one was open for 3% -> 3% of each run, Pallas kernels for 18% -> 17%
where the time goes in v7:
time: 211 us; the launch traced here: 210 us
  Pallas kernels  90.2 us (43%)
  starting transfers between devices  52.3 us (25%)
  waiting for transfers between devices  51.7 us (25%)
  other arithmetic  9.35 us (4%)
  local copies, waits for them, and re-layouts  5.69 us (3%)
    pallas_call x3, Pallas kernels, sink(): pl.pallas_call(lambda at_ref, *refs: kernel(*refs), grid_spec=pltpu.Prefe...  37.7 us
    ppermute x25, starting transfers between devices, joint_swap(): return lax.ppermute(value, ('item', 'bucket'), pairs)  32.2 us
    pallas_call x4, Pallas kernels, final(): pl.pallas_call((lambda at_ref, *refs: kernel(*refs)) if update else kerne...  30.8 us
    ppermute x22, waiting for transfers between devices, swap(): return lax.ppermute(value, axis, [(k, k ^ bit) for k in range(size)])  29.5 us
    ppermute x25, waiting for transfers between devices, joint_swap(): return lax.ppermute(value, ('item', 'bucket'), pairs)  22.2 us
    ppermute x22, starting transfers between devices, swap(): return lax.ppermute(value, axis, [(k, k ^ bit) for k in range(size)])  20.1 us
    pallas_call x2, Pallas kernels, lse(): pl.pallas_call(functools.partial(lse_kernel, repeat=repeat), grid=(count,...  12.6 us
    pallas_call x3, Pallas kernels, small(): pl.pallas_call(functools.partial(kernel, **settings), grid_spec=pltpu.Pre...  9.06 us
  transfers between devices with their start and end apart: 47, of which 24 were waited for; matrix products, arithmetic and copies ran while one was open for 3% of the time, Pallas kernels for 17%

profile of v7, /device:TPU:0, one launch (start us, length us, event | category | flops | bytes accessed | tf_op | source)
XLA Modules:
  0.0 210.3 jit_solution(6606667282456197140)
XLA Ops:
  1.5 4.1 %collective-permute-start.3 = (f32[64,512]{1,0:T(8,128)S(1)}, f32[64,512]{1,0:T(8,128)S(1)}, u32[]{:S(2)}, u32[]{:S(2)}) collective-permute-start(f32[64,512]{1,0:T(8,128)S(1)} %convert_bitcast_fusion.refs_0_), channel_id=1, source_target_pairs={{0,16},{4,20},{8,24},{12,28},{16,0},{20,4},{24,8},{28,12},{1,17},{... | collective-permute-start | bytes 393224 | tf_op jit(solution)/shard_map/ppermute | solution.py:26
  5.6 6.3 %row_lse.2.rest_0_ = f32[2,1024]{1,0:T(2,128)} custom-call(bf16[64,1024]{1,0:T(8,128)(2,1)} %bitcast.10, bf16[64,8192]{1,0:T(8,128)(2,1)} %bitcast.15), custom_call_target="tpu_custom_call" | custom-call | flops 2147483648 | bytes 4194304 | tf_op jit(solution)/shard_map/row_lse/pallas_call | solution.py:350
  11.9 6.3 %row_lse.3 = f32[2,1024]{1,0:T(2,128)} custom-call(bf16[64,1024]{1,0:T(8,128)(2,1)} %bitcast.11, bf16[64,8192]{1,0:T(8,128)(2,1)} %bitcast.16, f32[2,1024]{1,0:T(2,128)} %row_lse.2.rest_0_), custom_call_target="tpu_custom_call", output_to_operand_aliasing={{}: (2, {})} | custom-call | flops 2147483648 | bytes 4194304 | tf_op jit(solution)/shard_map/row_lse/pallas_call | solution.py:350
  29.9 3.7 %collective-permute-done.4.refs_5_ = f32[64,512]{1,0:T(8,128)S(1)} collective-permute-done((f32[64,512]{1,0:T(8,128)S(1)}, f32[64,512]{1,0:T(8,128)S(1)}, u32[]{:S(2)}, u32[]{:S(2)}) %collective-permute-start.4) | collective-permute-done | bytes 131104 | tf_op jit(solution)/shard_map/ppermute | solution.py:26
  33.7 2.5 %collective-permute-done.2.refs_3_ = f32[64,512]{1,0:T(8,128)S(1)} collective-permute-done((f32[64,512]{1,0:T(8,128)S(1)}, f32[64,512]{1,0:T(8,128)S(1)}, u32[]{:S(2)}, u32[]{:S(2)}) %collective-permute-start.2) | collective-permute-done | bytes 131104 | tf_op jit(solution)/shard_map/ppermute | solution.py:26
  38.2 2.3 %shard_map.41.mine_ref = f32[64,4096]{1,0:T(8,128)} custom-call(s32[1]{0:T(128)} %bitcast.1.item_ref.at_ref, f32[64,512]{1,0:T(8,128)} %copy-done.1, f32[64,512]{1,0:T(8,128)} %copy-done.13, f32[64,512]{1,0:T(8,128)} %copy-done.11, f32[64,512]{1,0:T(8,128)} %copy-done.15, f32[64,512]{1,0:T(8,128)} %copy-done.10, f32[64,512]{1,0:T(8,128)} %copy-done.14, ...), custom_call_target="tpu_custom_call" | custom-call | bytes 4194304 | tf_op jit(solution)/shard_map/pallas_call | solution.py:444
  40.8 1.6 collective-permute-start.12
  42.7 2.5 %collective-permute-start.14 = (f32[1,8192]{1,0:T(1,128)S(1)}, f32[1,8192]{1,0:T(1,128)S(1)}, u32[]{:S(2)}, u32[]{:S(2)}) collective-permute-start(f32[1,8192]{1,0:T(1,128)S(1)} %add.128.refs_2_), channel_id=1, source_target_pairs={{0,24},{1,25},{2,26},{3,27},{4,28},{5,29},{6,30},{7,31},{8,16},{9,... | collective-permute-start | bytes 98312 | tf_op jit(solution)/shard_map/ppermute | solution.py:43
  46.2 3.8 %shard_map.42 = (bf16[128,8192]{1,0:T(8,128)(2,1)}, bf16[64,8192]{1,0:T(8,128)(2,1)}) custom-call(s32[1]{0:T(128)} %bitcast.3.core_ref, f32[64,4096]{1,0:T(8,128)} %shard_map.41.mine_ref, f32[64,4096]{1,0:T(8,128)} %copy-done), custom_call_target="tpu_custom_call" | custom-call | bytes 4194304 | tf_op jit(solution)/shard_map/pallas_call | solution.py:444
  50.6 16.1 %sinkhorn_first.1 = (f32[1,8192]{1,0:T(1,128)}, f32[8,1024]{1,0:T(8,128)}, f32[1,8192]{1,0:T(1,128)}) custom-call(s32[1]{0:T(128)} %bitcast.1.item_ref.at_ref, bf16[64,8192]{1,0:T(8,128)(2,1)} %bitcast.17, bf16[128,8192]{1,0:T(8,128)(2,1)} %get-tuple-element.13.refs_1_.refs_2_, f32[1,8192]{1,0:T(1,128)} %copy-done.25, f32[1,8192]{1,0:T(1,128)} %copy-done.29, ...), custom_call_target="tpu_custom_call" | custom-call | flops 4294967296 | bytes 4194304 | tf_op jit(solution)/shard_map/sinkhorn_first/pallas_call | solution.py:376
  73.6 2.2 %collective-permute-done.18 = f32[1,8192]{1,0:T(1,128)S(1)} collective-permute-done((f32[1,8192]{1,0:T(1,128)S(1)}, f32[1,8192]{1,0:T(1,128)S(1)}, u32[]{:S(2)}, u32[]{:S(2)}) %collective-permute-start.18) | collective-permute-done | bytes 32800 | tf_op jit(solution)/shard_map/ppermute | solution.py:43
  77.9 2.5 %collective-permute-start.21 = (f32[1,8192]{1,0:T(1,128)S(1)}, f32[1,8192]{1,0:T(1,128)S(1)}, u32[]{:S(2)}, u32[]{:S(2)}) collective-permute-start(f32[1,8192]{1,0:T(1,128)S(1)} %add_add_fusion.2.refs_2_), channel_id=1, source_target_pairs={{0,24},{1,25},{2,26},{3,27},{4,28},{5,29},{6,30},{7,31},{8,16},{9,... | collective-permute-start | bytes 98312 | tf_op jit(solution)/shard_map/ppermute | solution.py:43
  81.5 2.1 %collective-permute-done.21.refs_5_ = f32[1,8192]{1,0:T(1,128)S(1)} collective-permute-done((f32[1,8192]{1,0:T(1,128)S(1)}, f32[1,8192]{1,0:T(1,128)S(1)}, u32[]{:S(2)}, u32[]{:S(2)}) %collective-permute-start.21) | collective-permute-done | bytes 32800 | tf_op jit(solution)/shard_map/ppermute | solution.py:43
  84.2 10.8 %sinkhorn_next.2 = (f32[1,8192]{1,0:T(1,128)}, f32[8,1024]{1,0:T(8,128)}, f32[1,8192]{1,0:T(1,128)}) custom-call(s32[1]{0:T(128)} %bitcast.1.item_ref.at_ref, bf16[64,8192]{1,0:T(8,128)(2,1)} %bitcast.18, bf16[128,8192]{1,0:T(8,128)(2,1)} %get-tuple-element.13.refs_1_.refs_2_, f32[1,8192]{1,0:T(1,128)} %copy-done.26, f32[1,8192]{1,0:T(1,128)} %copy-done.33, ...), custom_call_target="tpu_custom_call" | custom-call | flops 4294967296 | bytes 4194304 | tf_op jit(solution)/shard_map/sinkhorn_next/pallas_call | solution.py:376
  97.3 1.6 collective-permute-start.23
  104.4 3.0 %collective-permute-start.27 = (f32[1,8192]{1,0:T(1,128)S(1)}, f32[1,8192]{1,0:T(1,128)S(1)}, u32[]{:S(2)}, u32[]{:S(2)}) collective-permute-start(f32[1,8192]{1,0:T(1,128)S(1)} %add_add_fusion.1.refs_2_), channel_id=1, source_target_pairs={{0,16},{1,17},{2,18},{3,19},{4,20},{5,21},{6,22},{7,23},{8,24},{9,... | collective-permute-start | bytes 98312 | tf_op jit(solution)/shard_map/ppermute | solution.py:43
  109.3 3.8 %collective-permute-done.28.refs_5_ = f32[1,8192]{1,0:T(1,128)S(1)} collective-permute-done((f32[1,8192]{1,0:T(1,128)S(1)}, f32[1,8192]{1,0:T(1,128)S(1)}, u32[]{:S(2)}, u32[]{:S(2)}) %collective-permute-start.28) | collective-permute-done | bytes 32800 | tf_op jit(solution)/shard_map/ppermute | solution.py:43
  113.7 10.8 %sinkhorn_next.3 = (f32[1,8192]{1,0:T(1,128)}, f32[8,1024]{1,0:T(8,128)}, f32[1,8192]{1,0:T(1,128)}) custom-call(s32[1]{0:T(128)} %bitcast.1.item_ref.at_ref, bf16[64,8192]{1,0:T(8,128)(2,1)} %bitcast.19, bf16[128,8192]{1,0:T(8,128)(2,1)} %get-tuple-element.13.refs_1_.refs_2_, f32[1,8192]{1,0:T(1,128)} %copy-done.24, f32[1,8192]{1,0:T(1,128)} %copy-done.27, ...), custom_call_target="tpu_custom_call" | custom-call | flops 4294967296 | bytes 4194304 | tf_op jit(solution)/shard_map/sinkhorn_next/pallas_call | solution.py:376
  130.4 2.3 %collective-permute-done.30 = f32[1,8192]{1,0:T(1,128)S(1)} collective-permute-done((f32[1,8192]{1,0:T(1,128)S(1)}, f32[1,8192]{1,0:T(1,128)S(1)}, u32[]{:S(2)}, u32[]{:S(2)}) %collective-permute-start.30) | collective-permute-done | bytes 32800 | tf_op jit(solution)/shard_map/ppermute | solution.py:43
  134.7 1.9 collective-permute-start.34
  136.6 2.5 %collective-permute-start.35 = (f32[1,16384]{1,0:T(1,128)S(1)}, f32[1,16384]{1,0:T(1,128)S(1)}, u32[]{:S(2)}, u32[]{:S(2)}) collective-permute-start(f32[1,16384]{1,0:T(1,128)S(1)} %pad_maximum_fusion.1.refs_5_), channel_id=1, source_target_pairs={{0,24},{1,25},{2,26},{3,27},{4,28},{5,29},{6,30},{7,31},{8,16},{9,... | collective-permute-start | bytes 196616 | tf_op jit(solution)/shard_map/ppermute | solution.py:43
  140.4 2.3 %collective-permute-done.35.refs_8_ = f32[1,16384]{1,0:T(1,128)S(1)} collective-permute-done((f32[1,16384]{1,0:T(1,128)S(1)}, f32[1,16384]{1,0:T(1,128)S(1)}, u32[]{:S(2)}, u32[]{:S(2)}) %collective-permute-start.35) | collective-permute-done | bytes 65568 | tf_op jit(solution)/shard_map/ppermute | solution.py:43
  143.3 13.5 %centroid_update.1.refs_0_ = f32[64,1024]{1,0:T(8,128)} custom-call(s32[1]{0:T(128)} %bitcast.1.item_ref.at_ref, bf16[64,8192]{1,0:T(8,128)(2,1)} %bitcast.20, f32[8,1024]{1,0:T(8,128)} %get-tuple-element.22.refs_1_, bf16[128,8192]{1,0:T(8,128)(2,1)} %get-tuple-element.13.refs_1_.refs_2_, f32[1,8192]{1,0:T(1,128)} %get-tuple-element.20.refs_3_, ...), custom_call_target="tpu_custom_call" | custom-call | flops 8589934592 | bytes 4194304 | tf_op jit(solution)/shard_map/centroid_update/pallas_call | solution.py:418
  156.9 3.0 %collective-permute-start.41 = (f32[64,1024]{1,0:T(8,128)}, f32[64,1024]{1,0:T(8,128)S(1)}, u32[]{:S(2)}, u32[]{:S(2)}) collective-permute-start(f32[64,1024]{1,0:T(8,128)} %centroid_update.1.refs_0_), channel_id=1, source_target_pairs={{0,8},{4,12},{8,0},{12,4},{16,24},{20,28},{24,16},{28,20},{1,9},{5... | collective-permute-start | bytes 786440 | tf_op jit(solution)/shard_map/ppermute | solution.py:26
  162.3 7.2 %code_gradient.3 = f32[64,512]{1,0:T(8,128)} custom-call(bf16[64,1024]{1,0:T(8,128)(2,1)} %bitcast.12, f32[2,1024]{1,0:T(2,128)} %pad_maximum_fusion.3.p_ref, bf16[64,8192]{1,0:T(8,128)(2,1)} %bitcast.21, f32[1,8192]{1,0:T(1,128)} %get-tuple-element.26.rest_0_), custom_call_target="tpu_custom_call" | custom-call | flops 4294967296 | bytes 4194304 | tf_op jit(solution)/shard_map/code_gradient/pallas_call | solution.py:418
  169.6 4.9 %code_gradient.4.rest_1_ = f32[64,512]{1,0:T(8,128)} custom-call(bf16[64,1024]{1,0:T(8,128)(2,1)} %bitcast.13, f32[2,1024]{1,0:T(2,128)} %pad_maximum_fusion.3.p_ref, bf16[64,8192]{1,0:T(8,128)(2,1)} %bitcast.22, f32[1,8192]{1,0:T(1,128)} %get-tuple-element.26.rest_0_), custom_call_target="tpu_custom_call" | custom-call | flops 2147483648 | bytes 4194304 | tf_op jit(solution)/shard_map/code_gradient/pallas_call | solution.py:418
  174.6 5.1 %code_gradient.5 = f32[64,512]{1,0:T(8,128)} custom-call(bf16[64,1024]{1,0:T(8,128)(2,1)} %bitcast.14, f32[2,1024]{1,0:T(2,128)} %pad_maximum_fusion.3.p_ref, bf16[64,8192]{1,0:T(8,128)(2,1)} %bitcast.23, f32[1,8192]{1,0:T(1,128)} %get-tuple-element.26.rest_0_, f32[64,512]{1,0:T(8,128)} %code_gradient.4.rest_1_), custom_call_target="tpu_custom_call", output_to_operand_aliasing={{}: (4, {})} | custom-call | flops 2147483648 | bytes 4194304 | tf_op jit(solution)/shard_map/code_gradient/pallas_call | solution.py:418
  180.2 1.6 collective-permute-start.37
  187.4 4.5 %collective-permute-done.39 = f32[64,512]{1,0:T(8,128)S(1)} collective-permute-done((f32[64,512]{1,0:T(8,128)S(1)}, f32[64,512]{1,0:T(8,128)S(1)}, u32[]{:S(2)}, u32[]{:S(2)}) %collective-permute-start.39) | collective-permute-done | bytes 131104 | tf_op jit(solution)/shard_map/ppermute | solution.py:26
  192.6 9.6 %collective-permute-done.42.refs_3_ = f32[64,1024]{1,0:T(8,128)S(1)} collective-permute-done((f32[64,1024]{1,0:T(8,128)S(1)}, f32[64,1024]{1,0:T(8,128)S(1)}, u32[]{:S(2)}, u32[]{:S(2)}) %collective-permute-start.42) | collective-permute-done | bytes 262176 | tf_op jit(solution)/shard_map/ppermute | solution.py:26
  202.2 4.4 %collective-permute-done.46.refs_7_ = f32[64,1024]{1,0:T(8,128)S(1)} collective-permute-done((f32[64,1024]{1,0:T(8,128)S(1)}, f32[64,1024]{1,0:T(8,128)S(1)}, u32[]{:S(2)}, u32[]{:S(2)}) %collective-permute-start.46) | collective-permute-done | bytes 262176 | tf_op jit(solution)/shard_map/ppermute | solution.py:26
  207.3 3.0 %shard_map.43 = f32[64,8192]{1,0:T(8,128)} custom-call(s32[1]{0:T(128)} %bitcast.1.item_ref.at_ref, f32[64,1024]{1,0:T(8,128)} %centroid_update.1.refs_0_, f32[64,1024]{1,0:T(8,128)} %copy-done.6, f32[64,1024]{1,0:T(8,128)} %copy-done.4, f32[64,1024]{1,0:T(8,128)} %copy-done.8, f32[64,1024]{1,0:T(8,128)} %copy-done.3, f32[64,1024]{1,0:T(8,128)} %copy-done.7, ...), custom_call_target="tpu_custom_call" | custom-call | bytes 4194304 | tf_op jit(solution)/shard_map/pallas_call | solution.py:444
  (178 shorter events, 57.4 us)
Async XLA Ops:
  1.5 18.3 %collective-permute-start.3 = (f32[64,512]{1,0:T(8,128)S(1)}, f32[64,512]{1,0:T(8,128)S(1)}, u32[]{:S(2)}, u32[]{:S(2)}) collective-permute-start(f32[64,512]{1,0:T(8,128)S(1)} %convert_bitcast_fusion.refs_0_), channel_id=1, source_target_pairs={{0,16},{4,20},{8,24},{12,28},{16,0},{20,4},{24,8},{28,12},{1,17},{... | collective-permute-start | bytes 393224 | tf_op jit(solution)/shard_map/ppermute | solution.py:26
  18.2 9.6 %collective-permute-start.1 = (f32[64,512]{1,0:T(8,128)S(1)}, f32[64,512]{1,0:T(8,128)S(1)}, u32[]{:S(2)}, u32[]{:S(2)}) collective-permute-start(f32[64,512]{1,0:T(8,128)S(1)} %convert_bitcast_fusion.refs_0_), channel_id=1, source_target_pairs={{0,8},{4,12},{8,0},{12,4},{16,24},{20,28},{24,16},{28,20},{1,9},{5... | collective-permute-start | bytes 393224 | tf_op jit(solution)/shard_map/ppermute | solution.py:26
  19.8 9.5 %collective-permute-start.5 = (f32[64,512]{1,0:T(8,128)S(1)}, f32[64,512]{1,0:T(8,128)S(1)}, u32[]{:S(2)}, u32[]{:S(2)}) collective-permute-start(f32[64,512]{1,0:T(8,128)S(1)} %collective-permute-done.3.refs_4_), channel_id=1, source_target_pairs={{0,8},{4,12},{8,0},{12,4},{16,24},{20,28},{24,16},{28,20},{1,9},{5... | collective-permute-start | bytes 393224 | tf_op jit(solution)/shard_map/ppermute | solution.py:26
  24.1 5.8 %collective-permute-start = (f32[64,512]{1,0:T(8,128)S(1)}, f32[64,512]{1,0:T(8,128)S(1)}, u32[]{:S(2)}, u32[]{:S(2)}) collective-permute-start(f32[64,512]{1,0:T(8,128)S(1)} %convert_bitcast_fusion.refs_0_), channel_id=1, source_target_pairs={{0,4},{4,0},{8,12},{12,8},{16,20},{20,16},{24,28},{28,24},{1,5},{5... | collective-permute-start | bytes 393224 | tf_op jit(solution)/shard_map/ppermute | solution.py:26
  25.6 15.0 %collective-permute-start.9 = (f32[2,1024]{1,0:T(2,128)S(1)}, f32[2,1024]{1,0:T(2,128)S(1)}, u32[]{:S(2)}, u32[]{:S(2)}) collective-permute-start(f32[2,1024]{1,0:T(2,128)S(1)} %pad_maximum_fusion.2), channel_id=1, source_target_pairs={{0,2},{1,3},{2,0},{3,1},{4,6},{5,7},{6,4},{7,5},{8,10},{9,11},{10,... | collective-permute-start | bytes 24584 | tf_op jit(solution)/shard_map/ppermute | solution.py:43
  27.3 6.4 %collective-permute-start.4 = (f32[64,512]{1,0:T(8,128)S(1)}, f32[64,512]{1,0:T(8,128)S(1)}, u32[]{:S(2)}, u32[]{:S(2)}) collective-permute-start(f32[64,512]{1,0:T(8,128)S(1)} %collective-permute-done.3.refs_4_), channel_id=1, source_target_pairs={{0,4},{4,0},{8,12},{12,8},{16,20},{20,16},{24,28},{28,24},{1,5},{5... | collective-permute-start | bytes 393224 | tf_op jit(solution)/shard_map/ppermute | solution.py:26
  27.8 8.3 %collective-permute-start.2 = (f32[64,512]{1,0:T(8,128)S(1)}, f32[64,512]{1,0:T(8,128)S(1)}, u32[]{:S(2)}, u32[]{:S(2)}) collective-permute-start(f32[64,512]{1,0:T(8,128)S(1)} %collective-permute-done.1.refs_2_), channel_id=1, source_target_pairs={{0,4},{4,0},{8,12},{12,8},{16,20},{20,16},{24,28},{28,24},{1,5},{5... | collective-permute-start | bytes 393224 | tf_op jit(solution)/shard_map/ppermute | solution.py:26
  29.3 8.2 %collective-permute-start.6 = (f32[64,512]{1,0:T(8,128)S(1)}, f32[64,512]{1,0:T(8,128)S(1)}, u32[]{:S(2)}, u32[]{:S(2)}) collective-permute-start(f32[64,512]{1,0:T(8,128)S(1)} %collective-permute-done.5.refs_6_), channel_id=1, source_target_pairs={{0,4},{4,0},{8,12},{12,8},{16,20},{20,16},{24,28},{28,24},{1,5},{5... | collective-permute-start | bytes 393224 | tf_op jit(solution)/shard_map/ppermute | solution.py:26
  40.5 4.7 %collective-permute-start.7 = (f32[64,4096]{1,0:T(8,128)}, f32[64,4096]{1,0:T(8,128)S(1)}, u32[]{:S(2)}, u32[]{:S(2)}) collective-permute-start(f32[64,4096]{1,0:T(8,128)} %shard_map.41.mine_ref), channel_id=1, source_target_pairs={{0,1},{1,0},{2,3},{3,2},{4,5},{5,4},{6,7},{7,6},{8,9},{9,8},{10,11... | collective-permute-start | bytes 3145736 | tf_op jit(solution)/shard_map/ppermute | solution.py:26
  40.8 9.2 %collective-permute-start.12 = (f32[1,8192]{1,0:T(1,128)S(1)}, f32[1,8192]{1,0:T(1,128)S(1)}, u32[]{:S(2)}, u32[]{:S(2)}) collective-permute-start(f32[1,8192]{1,0:T(1,128)S(1)} %add.128.refs_2_), channel_id=1, source_target_pairs={{0,8},{1,9},{2,10},{3,11},{4,12},{5,13},{6,14},{7,15},{8,0},{9,1},... | collective-permute-start | bytes 98312 | tf_op jit(solution)/shard_map/ppermute | solution.py:43
  42.4 7.6 %collective-permute-start.13 = (f32[1,8192]{1,0:T(1,128)S(1)}, f32[1,8192]{1,0:T(1,128)S(1)}, u32[]{:S(2)}, u32[]{:S(2)}) collective-permute-start(f32[1,8192]{1,0:T(1,128)S(1)} %add.128.refs_2_), channel_id=1, source_target_pairs={{0,16},{1,17},{2,18},{3,19},{4,20},{5,21},{6,22},{7,23},{8,24},{9,... | collective-permute-start | bytes 98312 | tf_op jit(solution)/shard_map/ppermute | solution.py:43
  42.7 7.2 %collective-permute-start.14 = (f32[1,8192]{1,0:T(1,128)S(1)}, f32[1,8192]{1,0:T(1,128)S(1)}, u32[]{:S(2)}, u32[]{:S(2)}) collective-permute-start(f32[1,8192]{1,0:T(1,128)S(1)} %add.128.refs_2_), channel_id=1, source_target_pairs={{0,24},{1,25},{2,26},{3,27},{4,28},{5,29},{6,30},{7,31},{8,16},{9,... | collective-permute-start | bytes 98312 | tf_op jit(solution)/shard_map/ppermute | solution.py:43
  71.0 4.8 %collective-permute-start.18 = (f32[1,8192]{1,0:T(1,128)S(1)}, f32[1,8192]{1,0:T(1,128)S(1)}, u32[]{:S(2)}, u32[]{:S(2)}) collective-permute-start(f32[1,8192]{1,0:T(1,128)S(1)} %add.129), channel_id=1, source_target_pairs={{0,6},{1,7},{2,4},{3,5},{4,2},{5,3},{6,0},{7,1},{8,14},{9,15},{10,... | collective-permute-start | bytes 98312 | tf_op jit(solution)/shard_map/ppermute | solution.py:43
  76.6 4.8 %collective-permute-start.20 = (f32[1,8192]{1,0:T(1,128)S(1)}, f32[1,8192]{1,0:T(1,128)S(1)}, u32[]{:S(2)}, u32[]{:S(2)}) collective-permute-start(f32[1,8192]{1,0:T(1,128)S(1)} %add_add_fusion.2.refs_2_), channel_id=1, source_target_pairs={{0,16},{1,17},{2,18},{3,19},{4,20},{5,21},{6,22},{7,23},{8,24},{9,... | collective-permute-start | bytes 98312 | tf_op jit(solution)/shard_map/ppermute | solution.py:43
  77.9 5.7 %collective-permute-start.21 = (f32[1,8192]{1,0:T(1,128)S(1)}, f32[1,8192]{1,0:T(1,128)S(1)}, u32[]{:S(2)}, u32[]{:S(2)}) collective-permute-start(f32[1,8192]{1,0:T(1,128)S(1)} %add_add_fusion.2.refs_2_), channel_id=1, source_target_pairs={{0,24},{1,25},{2,26},{3,27},{4,28},{5,29},{6,30},{7,31},{8,16},{9,... | collective-permute-start | bytes 98312 | tf_op jit(solution)/shard_map/ppermute | solution.py:43
  99.4 4.8 %collective-permute-start.25 = (f32[1,8192]{1,0:T(1,128)S(1)}, f32[1,8192]{1,0:T(1,128)S(1)}, u32[]{:S(2)}, u32[]{:S(2)}) collective-permute-start(f32[1,8192]{1,0:T(1,128)S(1)} %add.133), channel_id=1, source_target_pairs={{0,6},{1,7},{2,4},{3,5},{4,2},{5,3},{6,0},{7,1},{8,14},{9,15},{10,... | collective-permute-start | bytes 98312 | tf_op jit(solution)/shard_map/ppermute | solution.py:43
  104.4 4.9 %collective-permute-start.27 = (f32[1,8192]{1,0:T(1,128)S(1)}, f32[1,8192]{1,0:T(1,128)S(1)}, u32[]{:S(2)}, u32[]{:S(2)}) collective-permute-start(f32[1,8192]{1,0:T(1,128)S(1)} %add_add_fusion.1.refs_2_), channel_id=1, source_target_pairs={{0,16},{1,17},{2,18},{3,19},{4,20},{5,21},{6,22},{7,23},{8,24},{9,... | collective-permute-start | bytes 98312 | tf_op jit(solution)/shard_map/ppermute | solution.py:43
  107.4 5.7 %collective-permute-start.28 = (f32[1,8192]{1,0:T(1,128)S(1)}, f32[1,8192]{1,0:T(1,128)S(1)}, u32[]{:S(2)}, u32[]{:S(2)}) collective-permute-start(f32[1,8192]{1,0:T(1,128)S(1)} %add_add_fusion.1.refs_2_), channel_id=1, source_target_pairs={{0,24},{1,25},{2,26},{3,27},{4,28},{5,29},{6,30},{7,31},{8,16},{9,... | collective-permute-start | bytes 98312 | tf_op jit(solution)/shard_map/ppermute | solution.py:43
  126.9 6.9 %collective-permute-start.31 = (f32[1,16384]{1,0:T(1,128)S(1)}, f32[1,16384]{1,0:T(1,128)S(1)}, u32[]{:S(2)}, u32[]{:S(2)}) collective-permute-start(f32[1,16384]{1,0:T(1,128)S(1)} %pad_maximum_fusion), channel_id=1, source_target_pairs={{0,4},{1,5},{2,6},{3,7},{4,0},{5,1},{6,2},{7,3},{8,12},{9,13},{10,... | collective-permute-start | bytes 196616 | tf_op jit(solution)/shard_map/ppermute | solution.py:43
  128.9 4.8 %collective-permute-start.32 = (f32[1,8192]{1,0:T(1,128)S(1)}, f32[1,8192]{1,0:T(1,128)S(1)}, u32[]{:S(2)}, u32[]{:S(2)}) collective-permute-start(f32[1,8192]{1,0:T(1,128)S(1)} %add.139), channel_id=1, source_target_pairs={{0,6},{1,7},{2,4},{3,5},{4,2},{5,3},{6,0},{7,1},{8,14},{9,15},{10,... | collective-permute-start | bytes 98312 | tf_op jit(solution)/shard_map/ppermute | solution.py:43
  134.7 5.7 %collective-permute-start.34 = (f32[1,16384]{1,0:T(1,128)S(1)}, f32[1,16384]{1,0:T(1,128)S(1)}, u32[]{:S(2)}, u32[]{:S(2)}) collective-permute-start(f32[1,16384]{1,0:T(1,128)S(1)} %pad_maximum_fusion.1.refs_5_), channel_id=1, source_target_pairs={{0,16},{1,17},{2,18},{3,19},{4,20},{5,21},{6,22},{7,23},{8,24},{9,... | collective-permute-start | bytes 196616 | tf_op jit(solution)/shard_map/ppermute | solution.py:43
  136.6 6.1 %collective-permute-start.35 = (f32[1,16384]{1,0:T(1,128)S(1)}, f32[1,16384]{1,0:T(1,128)S(1)}, u32[]{:S(2)}, u32[]{:S(2)}) collective-permute-start(f32[1,16384]{1,0:T(1,128)S(1)} %pad_maximum_fusion.1.refs_5_), channel_id=1, source_target_pairs={{0,24},{1,25},{2,26},{3,27},{4,28},{5,29},{6,30},{7,31},{8,16},{9,... | collective-permute-start | bytes 196616 | tf_op jit(solution)/shard_map/ppermute | solution.py:43
  156.9 17.6 %collective-permute-start.43 = (f32[64,1024]{1,0:T(8,128)}, f32[64,1024]{1,0:T(8,128)S(1)}, u32[]{:S(2)}, u32[]{:S(2)}) collective-permute-start(f32[64,1024]{1,0:T(8,128)} %centroid_update.1.refs_0_), channel_id=1, source_target_pairs={{0,16},{4,20},{8,24},{12,28},{16,0},{20,4},{24,8},{28,12},{1,17},{... | collective-permute-start | bytes 786440 | tf_op jit(solution)/shard_map/ppermute | solution.py:26
  156.9 27.0 %collective-permute-start.41 = (f32[64,1024]{1,0:T(8,128)}, f32[64,1024]{1,0:T(8,128)S(1)}, u32[]{:S(2)}, u32[]{:S(2)}) collective-permute-start(f32[64,1024]{1,0:T(8,128)} %centroid_update.1.refs_0_), channel_id=1, source_target_pairs={{0,8},{4,12},{8,0},{12,4},{16,24},{20,28},{24,16},{28,20},{1,9},{5... | collective-permute-start | bytes 786440 | tf_op jit(solution)/shard_map/ppermute | solution.py:26
  169.6 10.6 %collective-permute-start.36 = (f32[64,512]{1,0:T(8,128)}, f32[64,512]{1,0:T(8,128)S(1)}, u32[]{:S(2)}, u32[]{:S(2)}) collective-permute-start(f32[64,512]{1,0:T(8,128)} %code_gradient.3), channel_id=1, source_target_pairs={{0,1},{1,0},{2,3},{3,2},{4,5},{5,4},{6,7},{7,6},{8,9},{9,8},{10,11... | collective-permute-start | bytes 393224 | tf_op jit(solution)/shard_map/ppermute | solution.py:26
  174.5 9.8 %collective-permute-start.45 = (f32[64,1024]{1,0:T(8,128)S(1)}, f32[64,1024]{1,0:T(8,128)S(1)}, u32[]{:S(2)}, u32[]{:S(2)}) collective-permute-start(f32[64,1024]{1,0:T(8,128)S(1)} %collective-permute-done.43.refs_4_), channel_id=1, source_target_pairs={{0,8},{4,12},{8,0},{12,4},{16,24},{20,28},{24,16},{28,20},{1,9},{5... | collective-permute-start | bytes 786440 | tf_op jit(solution)/shard_map/ppermute | solution.py:26
  180.2 6.6 %collective-permute-start.37 = (f32[64,512]{1,0:T(8,128)S(1)}, f32[64,512]{1,0:T(8,128)S(1)}, u32[]{:S(2)}, u32[]{:S(2)}) collective-permute-start(f32[64,512]{1,0:T(8,128)S(1)} %add.148), channel_id=1, source_target_pairs={{0,2},{1,3},{2,0},{3,1},{4,6},{5,7},{6,4},{7,5},{8,10},{9,11},{10,... | collective-permute-start | bytes 393224 | tf_op jit(solution)/shard_map/ppermute | solution.py:26
  181.8 10.8 %collective-permute-start.40 = (f32[64,1024]{1,0:T(8,128)S(1)}, f32[64,1024]{1,0:T(8,128)S(1)}, u32[]{:S(2)}, u32[]{:S(2)}) collective-permute-start(f32[64,1024]{1,0:T(8,128)S(1)} %copy-done.2), channel_id=1, source_target_pairs={{0,4},{4,0},{8,12},{12,8},{16,20},{20,16},{24,28},{28,24},{1,5},{5... | collective-permute-start | bytes 786440 | tf_op jit(solution)/shard_map/ppermute | solution.py:26
  182.3 19.9 %collective-permute-start.44 = (f32[64,1024]{1,0:T(8,128)S(1)}, f32[64,1024]{1,0:T(8,128)S(1)}, u32[]{:S(2)}, u32[]{:S(2)}) collective-permute-start(f32[64,1024]{1,0:T(8,128)S(1)} %collective-permute-done.43.refs_4_), channel_id=1, source_target_pairs={{0,4},{4,0},{8,12},{12,8},{16,20},{20,16},{24,28},{28,24},{1,5},{5... | collective-permute-start | bytes 786440 | tf_op jit(solution)/shard_map/ppermute | solution.py:26
  183.9 18.4 %collective-permute-start.42 = (f32[64,1024]{1,0:T(8,128)S(1)}, f32[64,1024]{1,0:T(8,128)S(1)}, u32[]{:S(2)}, u32[]{:S(2)}) collective-permute-start(f32[64,1024]{1,0:T(8,128)S(1)} %collective-permute-done.41.refs_2_), channel_id=1, source_target_pairs={{0,4},{4,0},{8,12},{12,8},{16,20},{20,16},{24,28},{28,24},{1,5},{5... | collective-permute-start | bytes 786440 | tf_op jit(solution)/shard_map/ppermute | solution.py:26
  184.4 22.2 %collective-permute-start.46 = (f32[64,1024]{1,0:T(8,128)S(1)}, f32[64,1024]{1,0:T(8,128)S(1)}, u32[]{:S(2)}, u32[]{:S(2)}) collective-permute-start(f32[64,1024]{1,0:T(8,128)S(1)} %collective-permute-done.45.refs_6_), channel_id=1, source_target_pairs={{0,4},{4,0},{8,12},{12,8},{16,20},{20,16},{24,28},{28,24},{1,5},{5... | collective-permute-start | bytes 786440 | tf_op jit(solution)/shard_map/ppermute | solution.py:26
  186.8 5.0 %collective-permute-start.39 = (f32[64,512]{1,0:T(8,128)S(1)}, f32[64,512]{1,0:T(8,128)S(1)}, u32[]{:S(2)}, u32[]{:S(2)}) collective-permute-start(f32[64,512]{1,0:T(8,128)S(1)} %add.150), channel_id=1, source_target_pairs={{0,2},{1,3},{2,0},{3,1},{4,6},{5,7},{6,4},{7,5},{8,10},{9,11},{10,... | collective-permute-start | bytes 393224 | tf_op jit(solution)/shard_map/ppermute | solution.py:26
  (51 other events, 306.2 us)

commit v8 on v7

--- a/solution.py
+++ b/solution.py
@@ -329,7 +329,7 @@
 
 
 def params():
-    return pltpu.CompilerParams(dimension_semantics=("arbitrary",), vmem_limit_bytes=60 * 1024 * 1024)
+    return pltpu.CompilerParams(dimension_semantics=("arbitrary",), vmem_limit_bytes=48 * 1024 * 1024)
 
 
 def cost(count, width, passes):
@@ -378,11 +378,11 @@
         grid_spec=pltpu.PrefetchScalarGridSpec(num_scalar_prefetch=1, grid=(count + 1,),
         in_specs=[
             pl.BlockSpec((dim, block), lambda k, at: (0, at[0] * count + jnp.minimum(k, count - 1))),
-            pl.BlockSpec(right.shape, lambda k, at: (0, 0)),
+            pl.BlockSpec(memory_space=pltpu.VMEM),
         ]
-        + [line] * len(terms)
+        + [pl.BlockSpec(memory_space=pltpu.VMEM)] * len(terms)
         + ([] if first else [pot_spec, line]),
-        out_specs=[line, pot_spec, line],
+        out_specs=[pl.BlockSpec(memory_space=pltpu.VMEM), pot_spec, line],
         scratch_shapes=[VMEM((block, width), jnp.float32)]
         + [VMEM((block, LANES), jnp.float32)] * 3
         + [VMEM((POTS, width), jnp.bfloat16), VMEM((8, width), jnp.float32)],
@@ -411,9 +411,9 @@
     in_specs = [
         pl.BlockSpec((dim, block), lambda k, *at: (0, (at[0][0] * count if at else 0) + lead + k)),
         pl.BlockSpec((p_rows.shape[0], block), lambda k, *at: (0, lead + k)),
-        pl.BlockSpec(right.shape, lambda k, *at: (0, 0)),
+        pl.BlockSpec(memory_space=pltpu.VMEM) if update else pl.BlockSpec(right.shape, lambda k, *at: (0, 0)),
     ]
-    in_specs += [line] * len(lines) + [pl.BlockSpec(one.shape, lambda k, *at: (0, 0)) for one in extra]
+    in_specs += [line] * min(len(lines), 2) + [pl.BlockSpec(memory_space=pltpu.VMEM)] * (len(lines) - 2) + [pl.BlockSpec(memory_space=pltpu.VMEM) for one in extra]
     in_specs += [pl.BlockSpec(memory_space=pl.ANY)] * len(before)
     return pl.pallas_call(
         (lambda at_ref, *refs: kernel(*refs)) if update else kernel,
@@ -439,8 +439,9 @@
 
 def small(kernel, index, arrays, out_shape, **settings):
     several = isinstance(out_shape, list)
+    near = pl.BlockSpec(memory_space=pltpu.VMEM)
     whole = lambda shape: pl.BlockSpec(shape, lambda k, index: (0, 0))
-    specs = [whole(one.shape) for one in (out_shape if several else [out_shape])]
+    specs = [near] * 2 if several else [whole(out_shape.shape)]
     return pl.pallas_call(
         functools.partial(kernel, **settings),
         grid_spec=pltpu.PrefetchScalarGridSpec(
@@ -460,6 +461,33 @@
     dim, width = blocks[0].shape
     shape = jax.ShapeDtypeStruct((dim, width * len(keys)), jnp.float32)
     return small(place_kernel, item, [blocks[key] for key in keys], shape, keys=keys)
+
+
+def store_kernel(at_ref, *refs, count):
+    for number in range(count):
+
+        @pl.when(pl.program_id(0) == number)
+        def _():
+            refs[-1][...] = refs[number][...]
+
+
+def store(pieces, item, keys, total, before):
+    dim, width = pieces[0].shape
+    at = jnp.stack([item ^ key for key in keys]).astype(jnp.int32)
+    return pl.pallas_call(
+        functools.partial(store_kernel, count=len(keys)),
+        grid_spec=pltpu.PrefetchScalarGridSpec(
+            num_scalar_prefetch=1,
+            grid=(len(keys),),
+            in_specs=[pl.BlockSpec(memory_space=pltpu.VMEM)] * len(keys)
+            + [pl.BlockSpec(memory_space=pl.ANY)] * len(before),
+            out_specs=pl.BlockSpec((dim, width), lambda k, at: (0, at[k])),
+        ),
+        out_shape=jax.ShapeDtypeStruct((dim, width * total), jnp.float32),
+        input_output_aliases={1 + len(keys): 0} if before else {},
+        compiler_params=params(),
+        cost_estimate=pl.CostEstimate(flops=0, transcendentals=0, bytes_accessed=(1 << 19) * len(keys)),
+    )(at, *[pieces[key] for key in keys], *before)
 
 
 def step(code_rows, centroids):
@@ -590,7 +618,9 @@
             received = swap(grad, "bucket", bit)
             grad = grad + received
         halves.append(grad)
-    new_centroids = place(pieces, item)
+    keys = sorted(pieces)
+    new_centroids = store(pieces, item, keys[:-1], items, [])
+    new_centroids = store(pieces, item, keys[-1:], items, [new_centroids])
     return (jnp.concatenate(halves, axis=1).T, new_centroids.T)
 
 

time: 211 us -> 179 us (0.85)
  Pallas kernels: 90.2 us -> 66.8 us
  other arithmetic: 9.35 us -> 2.54 us
    pallas_call x4, Pallas kernels: 30.8 us -> 22.3 us  [final(): pl.pallas_call((lambda at_ref, *refs: kernel(*refs)) if update else kerne...]
    pallas_call x3 -> x2, Pallas kernels: 9.06 us -> 0.69 us  [small(): pl.pallas_call(functools.partial(kernel, **settings), grid_spec=pltpu.Pre...]
    pallas_call x3, Pallas kernels: 37.7 us -> 30.7 us  [sink(): pl.pallas_call(lambda at_ref, *refs: kernel(*refs), grid_spec=pltpu.Prefe...]
    pallas_call x0 -> x2, Pallas kernels: none -> 4.22 us  [store(): pl.pallas_call(functools.partial(store_kernel, count=len(keys)), grid_spe...]
    pallas_call x2, Pallas kernels: 12.6 us -> 8.85 us  [lse(): pl.pallas_call(functools.partial(lse_kernel, repeat=repeat), grid=(count,...]
    ppermute x25, waiting for transfers between devices: 22.2 us -> 25.8 us  [joint_swap(): return lax.ppermute(value, ('item', 'bucket'), pairs)]
    ppermute x22, waiting for transfers between devices: 29.5 us -> 26.9 us  [swap(): return lax.ppermute(value, axis, [(k, k ^ bit) for k in range(size)])]
    add x3, other arithmetic: 2.38 us -> 0.11 us  [step(): total = total + swap(total, 'bucket', 1)]
  transfers between devices with their start and end apart: 47 -> 47, of which waited for: 24 -> 29; matrix products, arithmetic and copies ran while one was open for 3% -> 1% of each run, Pallas kernels for 17% -> 14%
where the time goes in v8:
time: 179 us
  Pallas kernels  66.8 us (37%)
  waiting for transfers between devices  52.8 us (29%)
  starting transfers between devices  51.9 us (29%)
  local copies, waits for them, and re-layouts  3.59 us (2%)
  other arithmetic  2.54 us (1%)
    ppermute x25, starting transfers between devices, joint_swap(): return lax.ppermute(value, ('item', 'bucket'), pairs)  32.3 us
    pallas_call x3, Pallas kernels, sink(): pl.pallas_call(lambda at_ref, *refs: kernel(*refs), grid_spec=pltpu.Prefe...  30.7 us
    ppermute x22, waiting for transfers between devices, swap(): return lax.ppermute(value, axis, [(k, k ^ bit) for k in range(size)])  26.9 us
    ppermute x25, waiting for transfers between devices, joint_swap(): return lax.ppermute(value, ('item', 'bucket'), pairs)  25.8 us
    pallas_call x4, Pallas kernels, final(): pl.pallas_call((lambda at_ref, *refs: kernel(*refs)) if update else kerne...  22.3 us
    ppermute x22, starting transfers between devices, swap(): return lax.ppermute(value, axis, [(k, k ^ bit) for k in range(size)])  19.6 us
    pallas_call x2, Pallas kernels, lse(): pl.pallas_call(functools.partial(lse_kernel, repeat=repeat), grid=(count,...  8.85 us
    pallas_call x2, Pallas kernels, store(): pl.pallas_call(functools.partial(store_kernel, count=len(keys)), grid_spe...  4.22 us
  transfers between devices with their start and end apart: 47, of which 29 were waited for; matrix products, arithmetic and copies ran while one was open for 1% of the time, Pallas kernels for 14%

profile of v8, /device:TPU:0, one launch (start us, length us, event | category | flops | bytes accessed | tf_op | source)
XLA Modules:
  0.0 178.7 jit_solution(13877091824876983962)
XLA Ops:
  1.5 4.1 %collective-permute-start.3 = (f32[64,512]{1,0:T(8,128)S(1)}, f32[64,512]{1,0:T(8,128)S(1)}, u32[]{:S(2)}, u32[]{:S(2)}) collective-permute-start(f32[64,512]{1,0:T(8,128)S(1)} %convert_bitcast_fusion.refs_0_), channel_id=1, source_target_pairs={{0,16},{4,20},{8,24},{12,28},{16,0},{20,4},{24,8},{28,12},{1,17},{... | collective-permute-start | bytes 393224 | tf_op jit(solution)/shard_map/ppermute | solution.py:26
  7.8 4.4 %row_lse.2.rest_0_ = f32[2,1024]{1,0:T(2,128)S(1)} custom-call(bf16[64,1024]{1,0:T(8,128)(2,1)S(1)} %bitcast.16, bf16[64,8192]{1,0:T(8,128)(2,1)S(1)} %bitcast.21), custom_call_target="tpu_custom_call" | custom-call | flops 2147483648 | bytes 4194304 | tf_op jit(solution)/shard_map/row_lse/pallas_call | solution.py:350
  12.2 4.4 %row_lse.3 = f32[2,1024]{1,0:T(2,128)S(1)} custom-call(bf16[64,1024]{1,0:T(8,128)(2,1)S(1)} %bitcast.17, bf16[64,8192]{1,0:T(8,128)(2,1)S(1)} %bitcast.22, f32[2,1024]{1,0:T(2,128)S(1)} %row_lse.2.rest_0_), custom_call_target="tpu_custom_call", output_to_operand_aliasing={{}: (2, {})} | custom-call | flops 2147483648 | bytes 4194304 | tf_op jit(solution)/shard_map/row_lse/pallas_call | solution.py:350
  16.7 1.6 collective-permute-start.1
  27.7 3.7 %collective-permute-done.4.refs_5_ = f32[64,512]{1,0:T(8,128)S(1)} collective-permute-done((f32[64,512]{1,0:T(8,128)S(1)}, f32[64,512]{1,0:T(8,128)S(1)}, u32[]{:S(2)}, u32[]{:S(2)}) %collective-permute-start.4) | collective-permute-done | bytes 131104 | tf_op jit(solution)/shard_map/ppermute | solution.py:26
  31.4 2.5 %collective-permute-done.2.refs_3_ = f32[64,512]{1,0:T(8,128)S(1)} collective-permute-done((f32[64,512]{1,0:T(8,128)S(1)}, f32[64,512]{1,0:T(8,128)S(1)}, u32[]{:S(2)}, u32[]{:S(2)}) %collective-permute-start.2) | collective-permute-done | bytes 131104 | tf_op jit(solution)/shard_map/ppermute | solution.py:26
  35.6 1.6 collective-permute-start.12
  37.6 2.5 %collective-permute-start.14 = (f32[1,8192]{1,0:T(1,128)S(1)}, f32[1,8192]{1,0:T(1,128)S(1)}, u32[]{:S(2)}, u32[]{:S(2)}) collective-permute-start(f32[1,8192]{1,0:T(1,128)S(1)} %add.128.refs_2_), channel_id=1, source_target_pairs={{0,24},{1,25},{2,26},{3,27},{4,28},{5,29},{6,30},{7,31},{8,16},{9,... | collective-permute-start | bytes 98312 | tf_op jit(solution)/shard_map/ppermute | solution.py:43
  40.7 2.2 %collective-permute-done.13.refs_4_ = f32[1,8192]{1,0:T(1,128)S(1)} collective-permute-done((f32[1,8192]{1,0:T(1,128)S(1)}, f32[1,8192]{1,0:T(1,128)S(1)}, u32[]{:S(2)}, u32[]{:S(2)}) %collective-permute-start.13) | collective-permute-done | bytes 32800 | tf_op jit(solution)/shard_map/ppermute | solution.py:43
  43.4 13.6 %sinkhorn_first.1 = (f32[1,8192]{1,0:T(1,128)S(1)}, f32[8,1024]{1,0:T(8,128)S(1)}, f32[1,8192]{1,0:T(1,128)S(1)}) custom-call(s32[1]{0:T(128)} %bitcast.1.item_ref.at_ref, bf16[64,8192]{1,0:T(8,128)(2,1)S(1)} %bitcast.23, bf16[128,8192]{1,0:T(8,128)(2,1)S(1)} %get-tuple-element.13.refs_1_.refs_2_, f32[1,8192]{1,0:T(1,128)S(1)} %add.128.refs_2_, ...), custom_call_target="tpu_custom_call" | custom-call | flops 4294967296 | bytes 4194304 | tf_op jit(solution)/shard_map/sinkhorn_first/pallas_call | solution.py:376
  63.0 2.2 %collective-permute-done.18 = f32[1,8192]{1,0:T(1,128)S(1)} collective-permute-done((f32[1,8192]{1,0:T(1,128)S(1)}, f32[1,8192]{1,0:T(1,128)S(1)}, u32[]{:S(2)}, u32[]{:S(2)}) %collective-permute-start.18) | collective-permute-done | bytes 32800 | tf_op jit(solution)/shard_map/ppermute | solution.py:43
  66.2 2.1 %collective-permute-start.20 = (f32[1,8192]{1,0:T(1,128)S(1)}, f32[1,8192]{1,0:T(1,128)S(1)}, u32[]{:S(2)}, u32[]{:S(2)}) collective-permute-start(f32[1,8192]{1,0:T(1,128)S(1)} %add_add_fusion.2.refs_2_), channel_id=1, source_target_pairs={{0,16},{1,17},{2,18},{3,19},{4,20},{5,21},{6,22},{7,23},{8,24},{9,... | collective-permute-start | bytes 98312 | tf_op jit(solution)/shard_map/ppermute | solution.py:43
  69.8 1.9 %collective-permute-done.20.refs_4_ = f32[1,8192]{1,0:T(1,128)S(1)} collective-permute-done((f32[1,8192]{1,0:T(1,128)S(1)}, f32[1,8192]{1,0:T(1,128)S(1)}, u32[]{:S(2)}, u32[]{:S(2)}) %collective-permute-start.20) | collective-permute-done | bytes 32800 | tf_op jit(solution)/shard_map/ppermute | solution.py:43
  71.7 2.3 %collective-permute-done.21.refs_5_ = f32[1,8192]{1,0:T(1,128)S(1)} collective-permute-done((f32[1,8192]{1,0:T(1,128)S(1)}, f32[1,8192]{1,0:T(1,128)S(1)}, u32[]{:S(2)}, u32[]{:S(2)}) %collective-permute-start.21) | collective-permute-done | bytes 32800 | tf_op jit(solution)/shard_map/ppermute | solution.py:43
  74.0 8.7 %sinkhorn_next.2 = (f32[1,8192]{1,0:T(1,128)S(1)}, f32[8,1024]{1,0:T(8,128)S(1)}, f32[1,8192]{1,0:T(1,128)S(1)}) custom-call(s32[1]{0:T(128)} %bitcast.1.item_ref.at_ref, bf16[64,8192]{1,0:T(8,128)(2,1)S(1)} %bitcast.24, bf16[128,8192]{1,0:T(8,128)(2,1)S(1)} %get-tuple-element.13.refs_1_.refs_2_, f32[1,8192]{1,0:T(1,128)S(1)} %add_add_fusion.2.refs_2_, ...), custom_call_target="tpu_custom_call" | custom-call | flops 4294967296 | bytes 4194304 | tf_op jit(solution)/shard_map/sinkhorn_next/pallas_call | solution.py:376
  91.1 2.0 %collective-permute-start.27 = (f32[1,8192]{1,0:T(1,128)S(1)}, f32[1,8192]{1,0:T(1,128)S(1)}, u32[]{:S(2)}, u32[]{:S(2)}) collective-permute-start(f32[1,8192]{1,0:T(1,128)S(1)} %add_add_fusion.1.refs_2_), channel_id=1, source_target_pairs={{0,16},{1,17},{2,18},{3,19},{4,20},{5,21},{6,22},{7,23},{8,24},{9,... | collective-permute-start | bytes 98312 | tf_op jit(solution)/shard_map/ppermute | solution.py:43
  93.1 2.4 %collective-permute-start.28 = (f32[1,8192]{1,0:T(1,128)S(1)}, f32[1,8192]{1,0:T(1,128)S(1)}, u32[]{:S(2)}, u32[]{:S(2)}) collective-permute-start(f32[1,8192]{1,0:T(1,128)S(1)} %add_add_fusion.1.refs_2_), channel_id=1, source_target_pairs={{0,24},{1,25},{2,26},{3,27},{4,28},{5,29},{6,30},{7,31},{8,16},{9,... | collective-permute-start | bytes 98312 | tf_op jit(solution)/shard_map/ppermute | solution.py:43
  96.3 2.5 %collective-permute-done.28.refs_5_ = f32[1,8192]{1,0:T(1,128)S(1)} collective-permute-done((f32[1,8192]{1,0:T(1,128)S(1)}, f32[1,8192]{1,0:T(1,128)S(1)}, u32[]{:S(2)}, u32[]{:S(2)}) %collective-permute-start.28) | collective-permute-done | bytes 32800 | tf_op jit(solution)/shard_map/ppermute | solution.py:43
  100.0 8.5 %sinkhorn_next.3 = (f32[1,8192]{1,0:T(1,128)S(1)}, f32[8,1024]{1,0:T(8,128)S(1)}, f32[1,8192]{1,0:T(1,128)S(1)}) custom-call(s32[1]{0:T(128)} %bitcast.1.item_ref.at_ref, bf16[64,8192]{1,0:T(8,128)(2,1)S(1)} %bitcast.25, bf16[128,8192]{1,0:T(8,128)(2,1)S(1)} %get-tuple-element.13.refs_1_.refs_2_, f32[1,8192]{1,0:T(1,128)S(1)} %add_add_fusion.1.refs_2_, ...), custom_call_target="tpu_custom_call" | custom-call | flops 4294967296 | bytes 4194304 | tf_op jit(solution)/shard_map/sinkhorn_next/pallas_call | solution.py:376
  113.4 2.3 %collective-permute-done.30 = f32[1,8192]{1,0:T(1,128)S(1)} collective-permute-done((f32[1,8192]{1,0:T(1,128)S(1)}, f32[1,8192]{1,0:T(1,128)S(1)}, u32[]{:S(2)}, u32[]{:S(2)}) %collective-permute-start.30) | collective-permute-done | bytes 32800 | tf_op jit(solution)/shard_map/ppermute | solution.py:43
  117.0 2.9 %collective-permute-start.34 = (f32[1,16384]{1,0:T(1,128)S(1)}, f32[1,16384]{1,0:T(1,128)S(1)}, u32[]{:S(2)}, u32[]{:S(2)}) collective-permute-start(f32[1,16384]{1,0:T(1,128)S(1)} %pad_maximum_fusion.1.refs_5_), channel_id=1, source_target_pairs={{0,16},{1,17},{2,18},{3,19},{4,20},{5,21},{6,22},{7,23},{8,24},{9,... | collective-permute-start | bytes 196616 | tf_op jit(solution)/shard_map/ppermute | solution.py:43
  122.3 3.6 %collective-permute-done.35.refs_8_ = f32[1,16384]{1,0:T(1,128)S(1)} collective-permute-done((f32[1,16384]{1,0:T(1,128)S(1)}, f32[1,16384]{1,0:T(1,128)S(1)}, u32[]{:S(2)}, u32[]{:S(2)}) %collective-permute-start.35) | collective-permute-done | bytes 65568 | tf_op jit(solution)/shard_map/ppermute | solution.py:43
  126.0 10.7 %centroid_update.1.refs_0_ = f32[64,1024]{1,0:T(8,128)S(1)} custom-call(s32[1]{0:T(128)} %bitcast.1.item_ref.at_ref, bf16[64,8192]{1,0:T(8,128)(2,1)S(1)} %bitcast.26, f32[8,1024]{1,0:T(8,128)S(1)} %get-tuple-element.22.refs_1_, bf16[128,8192]{1,0:T(8,128)(2,1)S(1)} %get-tuple-element.13.refs_1_.refs_2_, f32[1,8192]{1,0:T(1,128)S(1)} %get-tuple-element.20.refs_3_, ...), custom_call_target="tpu_custom_call" | custom-call | flops 8589934592 | bytes 4194304 | tf_op jit(solution)/shard_map/centroid_update/pallas_call | solution.py:418
  136.7 2.0 %collective-permute-start.44 = (f32[64,1024]{1,0:T(8,128)S(1)}, f32[64,1024]{1,0:T(8,128)S(1)}, u32[]{:S(2)}, u32[]{:S(2)}) collective-permute-start(f32[64,1024]{1,0:T(8,128)S(1)} %centroid_update.1.refs_0_), channel_id=1, source_target_pairs={{0,8},{4,12},{8,0},{12,4},{16,24},{20,28},{24,16},{28,20},{1,9},{5... | collective-permute-start | bytes 786440 | tf_op jit(solution)/shard_map/ppermute | solution.py:26
  139.1 5.3 %code_gradient.3 = f32[64,512]{1,0:T(8,128)S(1)} custom-call(bf16[64,1024]{1,0:T(8,128)(2,1)S(1)} %bitcast.18, f32[2,1024]{1,0:T(2,128)S(1)} %pad_maximum_fusion.3.p_ref, bf16[64,8192]{1,0:T(8,128)(2,1)S(1)} %bitcast.27, f32[1,8192]{1,0:T(1,128)S(1)} %get-tuple-element.26.rest_0_), custom_call_target="tpu_custom_call" | custom-call | flops 4294967296 | bytes 4194304 | tf_op jit(solution)/shard_map/code_gradient/pallas_call | solution.py:418
  144.5 3.3 %code_gradient.4.rest_1_ = f32[64,512]{1,0:T(8,128)S(1)} custom-call(bf16[64,1024]{1,0:T(8,128)(2,1)S(1)} %bitcast.19, f32[2,1024]{1,0:T(2,128)S(1)} %pad_maximum_fusion.3.p_ref, bf16[64,8192]{1,0:T(8,128)(2,1)S(1)} %bitcast.28, f32[1,8192]{1,0:T(1,128)S(1)} %get-tuple-element.26.rest_0_), custom_call_target="tpu_custom_call" | custom-call | flops 2147483648 | bytes 4194304 | tf_op jit(solution)/shard_map/code_gradient/pallas_call | solution.py:418
  148.0 3.0 %code_gradient.5 = f32[64,512]{1,0:T(8,128)S(1)} custom-call(bf16[64,1024]{1,0:T(8,128)(2,1)S(1)} %bitcast.20, f32[2,1024]{1,0:T(2,128)S(1)} %pad_maximum_fusion.3.p_ref, bf16[64,8192]{1,0:T(8,128)(2,1)S(1)} %bitcast.29, f32[1,8192]{1,0:T(1,128)S(1)} %get-tuple-element.26.rest_0_, f32[64,512]{1,0:T(8,128)S(1)} %code_gradient.4.rest_1_), custom_call_target="tpu_custom_call", output_to_operand_aliasing={{}: (4, {})} | custom-call | flops 2147483648 | bytes 4194304 | tf_op jit(solution)/shard_map/code_gradient/pallas_call | solution.py:418
  151.5 1.6 collective-permute-start.37
  158.9 3.5 %collective-permute-done.39 = f32[64,512]{1,0:T(8,128)S(1)} collective-permute-done((f32[64,512]{1,0:T(8,128)S(1)}, f32[64,512]{1,0:T(8,128)S(1)}, u32[]{:S(2)}, u32[]{:S(2)}) %collective-permute-start.39) | collective-permute-done | bytes 131104 | tf_op jit(solution)/shard_map/ppermute | solution.py:26
  163.1 4.8 %collective-permute-done.45.refs_3_ = f32[64,1024]{1,0:T(8,128)S(1)} collective-permute-done((f32[64,1024]{1,0:T(8,128)S(1)}, f32[64,1024]{1,0:T(8,128)S(1)}, u32[]{:S(2)}, u32[]{:S(2)}) %collective-permute-start.45) | collective-permute-done | bytes 262176 | tf_op jit(solution)/shard_map/ppermute | solution.py:26
  167.9 5.6 %collective-permute-done.46.refs_5_ = f32[64,1024]{1,0:T(8,128)S(1)} collective-permute-done((f32[64,1024]{1,0:T(8,128)S(1)}, f32[64,1024]{1,0:T(8,128)S(1)}, u32[]{:S(2)}, u32[]{:S(2)}) %collective-permute-start.46) | collective-permute-done | bytes 262176 | tf_op jit(solution)/shard_map/ppermute | solution.py:26
  173.5 3.5 %shard_map.43.refs_1_ = f32[64,8192]{1,0:T(8,128)} custom-call(s32[7]{0:T(128)S(1)} %stack.32.at_ref, f32[64,1024]{1,0:T(8,128)S(1)} %centroid_update.1.refs_0_, f32[64,1024]{1,0:T(8,128)S(1)} %collective-permute-done.43.refs_1_, f32[64,1024]{1,0:T(8,128)S(1)} %collective-permute-done.44.refs_2_, f32[64,1024]{1,0:T(8,128)S(1)} %collective-permute-done.45.refs_3_, ...), custom_call_target="tpu_custom_call" | custom-call | bytes 3670016 | tf_op jit(solution)/shard_map/pallas_call | solution.py:477
  (124 shorter events, 52.1 us)
Async XLA Ops:
  1.5 16.8 %collective-permute-start.3 = (f32[64,512]{1,0:T(8,128)S(1)}, f32[64,512]{1,0:T(8,128)S(1)}, u32[]{:S(2)}, u32[]{:S(2)}) collective-permute-start(f32[64,512]{1,0:T(8,128)S(1)} %convert_bitcast_fusion.refs_0_), channel_id=1, source_target_pairs={{0,16},{4,20},{8,24},{12,28},{16,0},{20,4},{24,8},{28,12},{1,17},{... | collective-permute-start | bytes 393224 | tf_op jit(solution)/shard_map/ppermute | solution.py:26
  16.7 8.9 %collective-permute-start.1 = (f32[64,512]{1,0:T(8,128)S(1)}, f32[64,512]{1,0:T(8,128)S(1)}, u32[]{:S(2)}, u32[]{:S(2)}) collective-permute-start(f32[64,512]{1,0:T(8,128)S(1)} %convert_bitcast_fusion.refs_0_), channel_id=1, source_target_pairs={{0,8},{4,12},{8,0},{12,4},{16,24},{20,28},{24,16},{28,20},{1,9},{5... | collective-permute-start | bytes 393224 | tf_op jit(solution)/shard_map/ppermute | solution.py:26
  18.3 8.7 %collective-permute-start.5 = (f32[64,512]{1,0:T(8,128)S(1)}, f32[64,512]{1,0:T(8,128)S(1)}, u32[]{:S(2)}, u32[]{:S(2)}) collective-permute-start(f32[64,512]{1,0:T(8,128)S(1)} %collective-permute-done.3.refs_4_), channel_id=1, source_target_pairs={{0,8},{4,12},{8,0},{12,4},{16,24},{20,28},{24,16},{28,20},{1,9},{5... | collective-permute-start | bytes 393224 | tf_op jit(solution)/shard_map/ppermute | solution.py:26
  21.9 5.8 %collective-permute-start = (f32[64,512]{1,0:T(8,128)S(1)}, f32[64,512]{1,0:T(8,128)S(1)}, u32[]{:S(2)}, u32[]{:S(2)}) collective-permute-start(f32[64,512]{1,0:T(8,128)S(1)} %convert_bitcast_fusion.refs_0_), channel_id=1, source_target_pairs={{0,4},{4,0},{8,12},{12,8},{16,20},{20,16},{24,28},{28,24},{1,5},{5... | collective-permute-start | bytes 393224 | tf_op jit(solution)/shard_map/ppermute | solution.py:26
  23.4 12.1 %collective-permute-start.9 = (f32[2,1024]{1,0:T(2,128)S(1)}, f32[2,1024]{1,0:T(2,128)S(1)}, u32[]{:S(2)}, u32[]{:S(2)}) collective-permute-start(f32[2,1024]{1,0:T(2,128)S(1)} %pad_maximum_fusion.2), channel_id=1, source_target_pairs={{0,2},{1,3},{2,0},{3,1},{4,6},{5,7},{6,4},{7,5},{8,10},{9,11},{10,... | collective-permute-start | bytes 24584 | tf_op jit(solution)/shard_map/ppermute | solution.py:43
  25.0 6.4 %collective-permute-start.4 = (f32[64,512]{1,0:T(8,128)S(1)}, f32[64,512]{1,0:T(8,128)S(1)}, u32[]{:S(2)}, u32[]{:S(2)}) collective-permute-start(f32[64,512]{1,0:T(8,128)S(1)} %collective-permute-done.3.refs_4_), channel_id=1, source_target_pairs={{0,4},{4,0},{8,12},{12,8},{16,20},{20,16},{24,28},{28,24},{1,5},{5... | collective-permute-start | bytes 393224 | tf_op jit(solution)/shard_map/ppermute | solution.py:26
  25.6 8.3 %collective-permute-start.2 = (f32[64,512]{1,0:T(8,128)S(1)}, f32[64,512]{1,0:T(8,128)S(1)}, u32[]{:S(2)}, u32[]{:S(2)}) collective-permute-start(f32[64,512]{1,0:T(8,128)S(1)} %collective-permute-done.1.refs_2_), channel_id=1, source_target_pairs={{0,4},{4,0},{8,12},{12,8},{16,20},{20,16},{24,28},{28,24},{1,5},{5... | collective-permute-start | bytes 393224 | tf_op jit(solution)/shard_map/ppermute | solution.py:26
  27.0 8.2 %collective-permute-start.6 = (f32[64,512]{1,0:T(8,128)S(1)}, f32[64,512]{1,0:T(8,128)S(1)}, u32[]{:S(2)}, u32[]{:S(2)}) collective-permute-start(f32[64,512]{1,0:T(8,128)S(1)} %collective-permute-done.5.refs_6_), channel_id=1, source_target_pairs={{0,4},{4,0},{8,12},{12,8},{16,20},{20,16},{24,28},{28,24},{1,5},{5... | collective-permute-start | bytes 393224 | tf_op jit(solution)/shard_map/ppermute | solution.py:26
  35.3 4.8 %collective-permute-start.7 = (f32[64,4096]{1,0:T(8,128)S(1)}, f32[64,4096]{1,0:T(8,128)S(1)}, u32[]{:S(2)}, u32[]{:S(2)}) collective-permute-start(f32[64,4096]{1,0:T(8,128)S(1)} %shard_map.41.mine_ref), channel_id=1, source_target_pairs={{0,1},{1,0},{2,3},{3,2},{4,5},{5,4},{6,7},{7,6},{8,9},{9,8},{10,11... | collective-permute-start | bytes 3145736 | tf_op jit(solution)/shard_map/ppermute | solution.py:26
  35.6 5.1 %collective-permute-start.12 = (f32[1,8192]{1,0:T(1,128)S(1)}, f32[1,8192]{1,0:T(1,128)S(1)}, u32[]{:S(2)}, u32[]{:S(2)}) collective-permute-start(f32[1,8192]{1,0:T(1,128)S(1)} %add.128.refs_2_), channel_id=1, source_target_pairs={{0,8},{1,9},{2,10},{3,11},{4,12},{5,13},{6,14},{7,15},{8,0},{9,1},... | collective-permute-start | bytes 98312 | tf_op jit(solution)/shard_map/ppermute | solution.py:43
  37.3 5.7 %collective-permute-start.13 = (f32[1,8192]{1,0:T(1,128)S(1)}, f32[1,8192]{1,0:T(1,128)S(1)}, u32[]{:S(2)}, u32[]{:S(2)}) collective-permute-start(f32[1,8192]{1,0:T(1,128)S(1)} %add.128.refs_2_), channel_id=1, source_target_pairs={{0,16},{1,17},{2,18},{3,19},{4,20},{5,21},{6,22},{7,23},{8,24},{9,... | collective-permute-start | bytes 98312 | tf_op jit(solution)/shard_map/ppermute | solution.py:43
  37.6 5.8 %collective-permute-start.14 = (f32[1,8192]{1,0:T(1,128)S(1)}, f32[1,8192]{1,0:T(1,128)S(1)}, u32[]{:S(2)}, u32[]{:S(2)}) collective-permute-start(f32[1,8192]{1,0:T(1,128)S(1)} %add.128.refs_2_), channel_id=1, source_target_pairs={{0,24},{1,25},{2,26},{3,27},{4,28},{5,29},{6,30},{7,31},{8,16},{9,... | collective-permute-start | bytes 98312 | tf_op jit(solution)/shard_map/ppermute | solution.py:43
  60.4 4.8 %collective-permute-start.18 = (f32[1,8192]{1,0:T(1,128)S(1)}, f32[1,8192]{1,0:T(1,128)S(1)}, u32[]{:S(2)}, u32[]{:S(2)}) collective-permute-start(f32[1,8192]{1,0:T(1,128)S(1)} %add.129), channel_id=1, source_target_pairs={{0,6},{1,7},{2,4},{3,5},{4,2},{5,3},{6,0},{7,1},{8,14},{9,15},{10,... | collective-permute-start | bytes 98312 | tf_op jit(solution)/shard_map/ppermute | solution.py:43
  66.2 5.5 %collective-permute-start.20 = (f32[1,8192]{1,0:T(1,128)S(1)}, f32[1,8192]{1,0:T(1,128)S(1)}, u32[]{:S(2)}, u32[]{:S(2)}) collective-permute-start(f32[1,8192]{1,0:T(1,128)S(1)} %add_add_fusion.2.refs_2_), channel_id=1, source_target_pairs={{0,16},{1,17},{2,18},{3,19},{4,20},{5,21},{6,22},{7,23},{8,24},{9,... | collective-permute-start | bytes 98312 | tf_op jit(solution)/shard_map/ppermute | solution.py:43
  68.3 5.7 %collective-permute-start.21 = (f32[1,8192]{1,0:T(1,128)S(1)}, f32[1,8192]{1,0:T(1,128)S(1)}, u32[]{:S(2)}, u32[]{:S(2)}) collective-permute-start(f32[1,8192]{1,0:T(1,128)S(1)} %add_add_fusion.2.refs_2_), channel_id=1, source_target_pairs={{0,24},{1,25},{2,26},{3,27},{4,28},{5,29},{6,30},{7,31},{8,16},{9,... | collective-permute-start | bytes 98312 | tf_op jit(solution)/shard_map/ppermute | solution.py:43
  86.1 4.8 %collective-permute-start.25 = (f32[1,8192]{1,0:T(1,128)S(1)}, f32[1,8192]{1,0:T(1,128)S(1)}, u32[]{:S(2)}, u32[]{:S(2)}) collective-permute-start(f32[1,8192]{1,0:T(1,128)S(1)} %add.133), channel_id=1, source_target_pairs={{0,6},{1,7},{2,4},{3,5},{4,2},{5,3},{6,0},{7,1},{8,14},{9,15},{10,... | collective-permute-start | bytes 98312 | tf_op jit(solution)/shard_map/ppermute | solution.py:43
  91.1 5.2 %collective-permute-start.27 = (f32[1,8192]{1,0:T(1,128)S(1)}, f32[1,8192]{1,0:T(1,128)S(1)}, u32[]{:S(2)}, u32[]{:S(2)}) collective-permute-start(f32[1,8192]{1,0:T(1,128)S(1)} %add_add_fusion.1.refs_2_), channel_id=1, source_target_pairs={{0,16},{1,17},{2,18},{3,19},{4,20},{5,21},{6,22},{7,23},{8,24},{9,... | collective-permute-start | bytes 98312 | tf_op jit(solution)/shard_map/ppermute | solution.py:43
  93.1 5.7 %collective-permute-start.28 = (f32[1,8192]{1,0:T(1,128)S(1)}, f32[1,8192]{1,0:T(1,128)S(1)}, u32[]{:S(2)}, u32[]{:S(2)}) collective-permute-start(f32[1,8192]{1,0:T(1,128)S(1)} %add_add_fusion.1.refs_2_), channel_id=1, source_target_pairs={{0,24},{1,25},{2,26},{3,27},{4,28},{5,29},{6,30},{7,31},{8,16},{9,... | collective-permute-start | bytes 98312 | tf_op jit(solution)/shard_map/ppermute | solution.py:43
  109.9 6.9 %collective-permute-start.31 = (f32[1,16384]{1,0:T(1,128)S(1)}, f32[1,16384]{1,0:T(1,128)S(1)}, u32[]{:S(2)}, u32[]{:S(2)}) collective-permute-start(f32[1,16384]{1,0:T(1,128)S(1)} %pad_maximum_fusion), channel_id=1, source_target_pairs={{0,4},{1,5},{2,6},{3,7},{4,0},{5,1},{6,2},{7,3},{8,12},{9,13},{10,... | collective-permute-start | bytes 196616 | tf_op jit(solution)/shard_map/ppermute | solution.py:43
  111.9 4.8 %collective-permute-start.32 = (f32[1,8192]{1,0:T(1,128)S(1)}, f32[1,8192]{1,0:T(1,128)S(1)}, u32[]{:S(2)}, u32[]{:S(2)}) collective-permute-start(f32[1,8192]{1,0:T(1,128)S(1)} %add.139), channel_id=1, source_target_pairs={{0,6},{1,7},{2,4},{3,5},{4,2},{5,3},{6,0},{7,1},{8,14},{9,15},{10,... | collective-permute-start | bytes 98312 | tf_op jit(solution)/shard_map/ppermute | solution.py:43
  117.0 5.3 %collective-permute-start.34 = (f32[1,16384]{1,0:T(1,128)S(1)}, f32[1,16384]{1,0:T(1,128)S(1)}, u32[]{:S(2)}, u32[]{:S(2)}) collective-permute-start(f32[1,16384]{1,0:T(1,128)S(1)} %pad_maximum_fusion.1.refs_5_), channel_id=1, source_target_pairs={{0,16},{1,17},{2,18},{3,19},{4,20},{5,21},{6,22},{7,23},{8,24},{9,... | collective-permute-start | bytes 196616 | tf_op jit(solution)/shard_map/ppermute | solution.py:43
  119.9 6.1 %collective-permute-start.35 = (f32[1,16384]{1,0:T(1,128)S(1)}, f32[1,16384]{1,0:T(1,128)S(1)}, u32[]{:S(2)}, u32[]{:S(2)}) collective-permute-start(f32[1,16384]{1,0:T(1,128)S(1)} %pad_maximum_fusion.1.refs_5_), channel_id=1, source_target_pairs={{0,24},{1,25},{2,26},{3,27},{4,28},{5,29},{6,30},{7,31},{8,16},{9,... | collective-permute-start | bytes 196616 | tf_op jit(solution)/shard_map/ppermute | solution.py:43
  136.7 11.1 %collective-permute-start.40 = (f32[64,1024]{1,0:T(8,128)S(1)}, f32[64,1024]{1,0:T(8,128)S(1)}, u32[]{:S(2)}, u32[]{:S(2)}) collective-permute-start(f32[64,1024]{1,0:T(8,128)S(1)} %centroid_update.1.refs_0_), channel_id=1, source_target_pairs={{0,16},{4,20},{8,24},{12,28},{16,0},{20,4},{24,8},{28,12},{1,17},{... | collective-permute-start | bytes 786440 | tf_op jit(solution)/shard_map/ppermute | solution.py:26
  136.7 16.9 %collective-permute-start.44 = (f32[64,1024]{1,0:T(8,128)S(1)}, f32[64,1024]{1,0:T(8,128)S(1)}, u32[]{:S(2)}, u32[]{:S(2)}) collective-permute-start(f32[64,1024]{1,0:T(8,128)S(1)} %centroid_update.1.refs_0_), channel_id=1, source_target_pairs={{0,8},{4,12},{8,0},{12,4},{16,24},{20,28},{24,16},{28,20},{1,9},{5... | collective-permute-start | bytes 786440 | tf_op jit(solution)/shard_map/ppermute | solution.py:26
  144.4 7.1 %collective-permute-start.36 = (f32[64,512]{1,0:T(8,128)S(1)}, f32[64,512]{1,0:T(8,128)S(1)}, u32[]{:S(2)}, u32[]{:S(2)}) collective-permute-start(f32[64,512]{1,0:T(8,128)S(1)} %code_gradient.3), channel_id=1, source_target_pairs={{0,1},{1,0},{2,3},{3,2},{4,5},{5,4},{6,7},{7,6},{8,9},{9,8},{10,11... | collective-permute-start | bytes 393224 | tf_op jit(solution)/shard_map/ppermute | solution.py:26
  147.8 8.8 %collective-permute-start.41 = (f32[64,1024]{1,0:T(8,128)S(1)}, f32[64,1024]{1,0:T(8,128)S(1)}, u32[]{:S(2)}, u32[]{:S(2)}) collective-permute-start(f32[64,1024]{1,0:T(8,128)S(1)} %collective-permute-done.40.refs_4_), channel_id=1, source_target_pairs={{0,8},{4,12},{8,0},{12,4},{16,24},{20,28},{24,16},{28,20},{1,9},{5... | collective-permute-start | bytes 786440 | tf_op jit(solution)/shard_map/ppermute | solution.py:26
  151.5 5.8 %collective-permute-start.37 = (f32[64,512]{1,0:T(8,128)S(1)}, f32[64,512]{1,0:T(8,128)S(1)}, u32[]{:S(2)}, u32[]{:S(2)}) collective-permute-start(f32[64,512]{1,0:T(8,128)S(1)} %add.148), channel_id=1, source_target_pairs={{0,2},{1,3},{2,0},{3,1},{4,6},{5,7},{6,4},{7,5},{8,10},{9,11},{10,... | collective-permute-start | bytes 393224 | tf_op jit(solution)/shard_map/ppermute | solution.py:26
  153.1 10.0 %collective-permute-start.43 = (f32[64,1024]{1,0:T(8,128)S(1)}, f32[64,1024]{1,0:T(8,128)S(1)}, u32[]{:S(2)}, u32[]{:S(2)}) collective-permute-start(f32[64,1024]{1,0:T(8,128)S(1)} %centroid_update.1.refs_0_), channel_id=1, source_target_pairs={{0,4},{4,0},{8,12},{12,8},{16,20},{20,16},{24,28},{28,24},{1,5},{5... | collective-permute-start | bytes 786440 | tf_op jit(solution)/shard_map/ppermute | solution.py:26
  153.7 14.2 %collective-permute-start.45 = (f32[64,1024]{1,0:T(8,128)S(1)}, f32[64,1024]{1,0:T(8,128)S(1)}, u32[]{:S(2)}, u32[]{:S(2)}) collective-permute-start(f32[64,1024]{1,0:T(8,128)S(1)} %collective-permute-done.44.refs_2_), channel_id=1, source_target_pairs={{0,4},{4,0},{8,12},{12,8},{16,20},{20,16},{24,28},{28,24},{1,5},{5... | collective-permute-start | bytes 786440 | tf_op jit(solution)/shard_map/ppermute | solution.py:26
  155.1 18.4 %collective-permute-start.46 = (f32[64,1024]{1,0:T(8,128)S(1)}, f32[64,1024]{1,0:T(8,128)S(1)}, u32[]{:S(2)}, u32[]{:S(2)}) collective-permute-start(f32[64,1024]{1,0:T(8,128)S(1)} %collective-permute-done.40.refs_4_), channel_id=1, source_target_pairs={{0,4},{4,0},{8,12},{12,8},{16,20},{20,16},{24,28},{28,24},{1,5},{5... | collective-permute-start | bytes 786440 | tf_op jit(solution)/shard_map/ppermute | solution.py:26
  156.6 21.4 %collective-permute-start.42 = (f32[64,1024]{1,0:T(8,128)S(1)}, f32[64,1024]{1,0:T(8,128)S(1)}, u32[]{:S(2)}, u32[]{:S(2)}) collective-permute-start(f32[64,1024]{1,0:T(8,128)S(1)} %collective-permute-done.41.refs_6_), channel_id=1, source_target_pairs={{0,4},{4,0},{8,12},{12,8},{16,20},{20,16},{24,28},{28,24},{1,5},{5... | collective-permute-start | bytes 786440 | tf_op jit(solution)/shard_map/ppermute | solution.py:26
  157.3 5.0 %collective-permute-start.39 = (f32[64,512]{1,0:T(8,128)S(1)}, f32[64,512]{1,0:T(8,128)S(1)}, u32[]{:S(2)}, u32[]{:S(2)}) collective-permute-start(f32[64,512]{1,0:T(8,128)S(1)} %add.150), channel_id=1, source_target_pairs={{0,2},{1,3},{2,0},{3,1},{4,6},{5,7},{6,4},{7,5},{8,10},{9,11},{10,... | collective-permute-start | bytes 393224 | tf_op jit(solution)/shard_map/ppermute | solution.py:26
  (23 other events, 132.7 us)

commit v9 on v8

--- a/solution.py
+++ b/solution.py
@@ -329,7 +329,7 @@
 
 
 def params():
-    return pltpu.CompilerParams(dimension_semantics=("arbitrary",), vmem_limit_bytes=48 * 1024 * 1024)
+    return pltpu.CompilerParams(dimension_semantics=("arbitrary",), vmem_limit_bytes=40 * 1024 * 1024)
 
 
 def cost(count, width, passes):
@@ -603,7 +603,7 @@
     mass, col = both[:, :rows_total] * float(rows_total), both[:, rows_total:]
     p_rows = own_rows(jnp.concatenate([row + log_rows, mass * jnp.exp(row_first - row)], axis=0))
     halves = []
-    for half, calls in enumerate([1, 2]):
+    for half, calls in enumerate([2, 2]):
         held = []
         for call in range(calls):
             block = rows_half // calls
@@ -619,8 +619,9 @@
             grad = grad + received
         halves.append(grad)
     keys = sorted(pieces)
-    new_centroids = store(pieces, item, keys[:-1], items, [])
-    new_centroids = store(pieces, item, keys[-1:], items, [new_centroids])
+    early = [key for key in keys if not key & 1 or key < 5]
+    new_centroids = store(pieces, item, early, items, [])
+    new_centroids = store(pieces, item, [key for key in keys if key not in early], items, [new_centroids])
     return (jnp.concatenate(halves, axis=1).T, new_centroids.T)
 
 

time: 179 us -> 180 us (level)
    pallas_call x4 -> x5, Pallas kernels: 22.3 us -> 23.1 us  [final(): pl.pallas_call((lambda at_ref, *refs: kernel(*refs)) if update else kerne...]
where the time goes in v9:
time: 180 us
  Pallas kernels  67.6 us (38%)
  waiting for transfers between devices  53.4 us (30%)
  starting transfers between devices  51.9 us (29%)
  local copies, waits for them, and re-layouts  3.59 us (2%)
  other arithmetic  2.62 us (1%)
    ppermute x25, starting transfers between devices, joint_swap(): return lax.ppermute(value, ('item', 'bucket'), pairs)  32.3 us
    pallas_call x3, Pallas kernels, sink(): pl.pallas_call(lambda at_ref, *refs: kernel(*refs), grid_spec=pltpu.Prefe...  30.7 us
    ppermute x22, waiting for transfers between devices, swap(): return lax.ppermute(value, axis, [(k, k ^ bit) for k in range(size)])  27.5 us
    ppermute x25, waiting for transfers between devices, joint_swap(): return lax.ppermute(value, ('item', 'bucket'), pairs)  25.8 us
    pallas_call x5, Pallas kernels, final(): pl.pallas_call((lambda at_ref, *refs: kernel(*refs)) if update else kerne...  23.1 us
    ppermute x22, starting transfers between devices, swap(): return lax.ppermute(value, axis, [(k, k ^ bit) for k in range(size)])  19.6 us
    pallas_call x2, Pallas kernels, lse(): pl.pallas_call(functools.partial(lse_kernel, repeat=repeat), grid=(count,...  8.85 us
    pallas_call x2, Pallas kernels, store(): pl.pallas_call(functools.partial(store_kernel, count=len(keys)), grid_spe...  4.23 us
  transfers between devices with their start and end apart: 47, of which 29 were waited for; matrix products, arithmetic and copies ran while one was open for 1% of the time, Pallas kernels for 14%

profile of v9, /device:TPU:0, one launch (start us, length us, event | category | flops | bytes accessed | tf_op | source)
XLA Modules:
  0.0 180.1 jit_solution(15679643806858573808)
XLA Ops:
  1.5 4.1 %collective-permute-start.3 = (f32[64,512]{1,0:T(8,128)S(1)}, f32[64,512]{1,0:T(8,128)S(1)}, u32[]{:S(2)}, u32[]{:S(2)}) collective-permute-start(f32[64,512]{1,0:T(8,128)S(1)} %convert_bitcast_fusion.refs_0_), channel_id=1, source_target_pairs={{0,16},{4,20},{8,24},{12,28},{16,0},{20,4},{24,8},{28,12},{1,17},{... | collective-permute-start | bytes 393224 | tf_op jit(solution)/shard_map/ppermute | solution.py:26
  7.8 4.4 %row_lse.2.rest_0_ = f32[2,1024]{1,0:T(2,128)S(1)} custom-call(bf16[64,1024]{1,0:T(8,128)(2,1)S(1)} %bitcast.16, bf16[64,8192]{1,0:T(8,128)(2,1)S(1)} %bitcast.22), custom_call_target="tpu_custom_call" | custom-call | flops 2147483648 | bytes 4194304 | tf_op jit(solution)/shard_map/row_lse/pallas_call | solution.py:350
  12.2 4.4 %row_lse.3 = f32[2,1024]{1,0:T(2,128)S(1)} custom-call(bf16[64,1024]{1,0:T(8,128)(2,1)S(1)} %bitcast.17, bf16[64,8192]{1,0:T(8,128)(2,1)S(1)} %bitcast.23, f32[2,1024]{1,0:T(2,128)S(1)} %row_lse.2.rest_0_), custom_call_target="tpu_custom_call", output_to_operand_aliasing={{}: (2, {})} | custom-call | flops 2147483648 | bytes 4194304 | tf_op jit(solution)/shard_map/row_lse/pallas_call | solution.py:350
  16.7 1.6 collective-permute-start.1
  27.7 3.7 %collective-permute-done.4.refs_5_ = f32[64,512]{1,0:T(8,128)S(1)} collective-permute-done((f32[64,512]{1,0:T(8,128)S(1)}, f32[64,512]{1,0:T(8,128)S(1)}, u32[]{:S(2)}, u32[]{:S(2)}) %collective-permute-start.4) | collective-permute-done | bytes 131104 | tf_op jit(solution)/shard_map/ppermute | solution.py:26
  31.4 2.5 %collective-permute-done.2.refs_3_ = f32[64,512]{1,0:T(8,128)S(1)} collective-permute-done((f32[64,512]{1,0:T(8,128)S(1)}, f32[64,512]{1,0:T(8,128)S(1)}, u32[]{:S(2)}, u32[]{:S(2)}) %collective-permute-start.2) | collective-permute-done | bytes 131104 | tf_op jit(solution)/shard_map/ppermute | solution.py:26
  37.6 2.5 %collective-permute-start.14 = (f32[1,8192]{1,0:T(1,128)S(1)}, f32[1,8192]{1,0:T(1,128)S(1)}, u32[]{:S(2)}, u32[]{:S(2)}) collective-permute-start(f32[1,8192]{1,0:T(1,128)S(1)} %add.128.refs_2_), channel_id=1, source_target_pairs={{0,24},{1,25},{2,26},{3,27},{4,28},{5,29},{6,30},{7,31},{8,16},{9,... | collective-permute-start | bytes 98312 | tf_op jit(solution)/shard_map/ppermute | solution.py:43
  40.7 2.2 %collective-permute-done.13.refs_4_ = f32[1,8192]{1,0:T(1,128)S(1)} collective-permute-done((f32[1,8192]{1,0:T(1,128)S(1)}, f32[1,8192]{1,0:T(1,128)S(1)}, u32[]{:S(2)}, u32[]{:S(2)}) %collective-permute-start.13) | collective-permute-done | bytes 32800 | tf_op jit(solution)/shard_map/ppermute | solution.py:43
  43.4 13.6 %sinkhorn_first.1 = (f32[1,8192]{1,0:T(1,128)S(1)}, f32[8,1024]{1,0:T(8,128)S(1)}, f32[1,8192]{1,0:T(1,128)S(1)}) custom-call(s32[1]{0:T(128)} %bitcast.1.item_ref.at_ref, bf16[64,8192]{1,0:T(8,128)(2,1)S(1)} %bitcast.24, bf16[128,8192]{1,0:T(8,128)(2,1)S(1)} %get-tuple-element.13.refs_1_.refs_2_, f32[1,8192]{1,0:T(1,128)S(1)} %add.128.refs_2_, ...), custom_call_target="tpu_custom_call" | custom-call | flops 4294967296 | bytes 4194304 | tf_op jit(solution)/shard_map/sinkhorn_first/pallas_call | solution.py:376
  63.0 2.2 %collective-permute-done.18 = f32[1,8192]{1,0:T(1,128)S(1)} collective-permute-done((f32[1,8192]{1,0:T(1,128)S(1)}, f32[1,8192]{1,0:T(1,128)S(1)}, u32[]{:S(2)}, u32[]{:S(2)}) %collective-permute-start.18) | collective-permute-done | bytes 32800 | tf_op jit(solution)/shard_map/ppermute | solution.py:43
  66.2 2.1 %collective-permute-start.20 = (f32[1,8192]{1,0:T(1,128)S(1)}, f32[1,8192]{1,0:T(1,128)S(1)}, u32[]{:S(2)}, u32[]{:S(2)}) collective-permute-start(f32[1,8192]{1,0:T(1,128)S(1)} %add_add_fusion.2.refs_2_), channel_id=1, source_target_pairs={{0,16},{1,17},{2,18},{3,19},{4,20},{5,21},{6,22},{7,23},{8,24},{9,... | collective-permute-start | bytes 98312 | tf_op jit(solution)/shard_map/ppermute | solution.py:43
  69.8 1.9 %collective-permute-done.20.refs_4_ = f32[1,8192]{1,0:T(1,128)S(1)} collective-permute-done((f32[1,8192]{1,0:T(1,128)S(1)}, f32[1,8192]{1,0:T(1,128)S(1)}, u32[]{:S(2)}, u32[]{:S(2)}) %collective-permute-start.20) | collective-permute-done | bytes 32800 | tf_op jit(solution)/shard_map/ppermute | solution.py:43
  71.7 2.3 %collective-permute-done.21.refs_5_ = f32[1,8192]{1,0:T(1,128)S(1)} collective-permute-done((f32[1,8192]{1,0:T(1,128)S(1)}, f32[1,8192]{1,0:T(1,128)S(1)}, u32[]{:S(2)}, u32[]{:S(2)}) %collective-permute-start.21) | collective-permute-done | bytes 32800 | tf_op jit(solution)/shard_map/ppermute | solution.py:43
  74.0 8.7 %sinkhorn_next.2 = (f32[1,8192]{1,0:T(1,128)S(1)}, f32[8,1024]{1,0:T(8,128)S(1)}, f32[1,8192]{1,0:T(1,128)S(1)}) custom-call(s32[1]{0:T(128)} %bitcast.1.item_ref.at_ref, bf16[64,8192]{1,0:T(8,128)(2,1)S(1)} %bitcast.25, bf16[128,8192]{1,0:T(8,128)(2,1)S(1)} %get-tuple-element.13.refs_1_.refs_2_, f32[1,8192]{1,0:T(1,128)S(1)} %add_add_fusion.2.refs_2_, ...), custom_call_target="tpu_custom_call" | custom-call | flops 4294967296 | bytes 4194304 | tf_op jit(solution)/shard_map/sinkhorn_next/pallas_call | solution.py:376
  91.1 2.0 %collective-permute-start.27 = (f32[1,8192]{1,0:T(1,128)S(1)}, f32[1,8192]{1,0:T(1,128)S(1)}, u32[]{:S(2)}, u32[]{:S(2)}) collective-permute-start(f32[1,8192]{1,0:T(1,128)S(1)} %add_add_fusion.1.refs_2_), channel_id=1, source_target_pairs={{0,16},{1,17},{2,18},{3,19},{4,20},{5,21},{6,22},{7,23},{8,24},{9,... | collective-permute-start | bytes 98312 | tf_op jit(solution)/shard_map/ppermute | solution.py:43
  93.1 2.4 %collective-permute-start.28 = (f32[1,8192]{1,0:T(1,128)S(1)}, f32[1,8192]{1,0:T(1,128)S(1)}, u32[]{:S(2)}, u32[]{:S(2)}) collective-permute-start(f32[1,8192]{1,0:T(1,128)S(1)} %add_add_fusion.1.refs_2_), channel_id=1, source_target_pairs={{0,24},{1,25},{2,26},{3,27},{4,28},{5,29},{6,30},{7,31},{8,16},{9,... | collective-permute-start | bytes 98312 | tf_op jit(solution)/shard_map/ppermute | solution.py:43
  96.3 2.5 %collective-permute-done.28.refs_5_ = f32[1,8192]{1,0:T(1,128)S(1)} collective-permute-done((f32[1,8192]{1,0:T(1,128)S(1)}, f32[1,8192]{1,0:T(1,128)S(1)}, u32[]{:S(2)}, u32[]{:S(2)}) %collective-permute-start.28) | collective-permute-done | bytes 32800 | tf_op jit(solution)/shard_map/ppermute | solution.py:43
  100.0 8.5 %sinkhorn_next.3 = (f32[1,8192]{1,0:T(1,128)S(1)}, f32[8,1024]{1,0:T(8,128)S(1)}, f32[1,8192]{1,0:T(1,128)S(1)}) custom-call(s32[1]{0:T(128)} %bitcast.1.item_ref.at_ref, bf16[64,8192]{1,0:T(8,128)(2,1)S(1)} %bitcast.26, bf16[128,8192]{1,0:T(8,128)(2,1)S(1)} %get-tuple-element.13.refs_1_.refs_2_, f32[1,8192]{1,0:T(1,128)S(1)} %add_add_fusion.1.refs_2_, ...), custom_call_target="tpu_custom_call" | custom-call | flops 4294967296 | bytes 4194304 | tf_op jit(solution)/shard_map/sinkhorn_next/pallas_call | solution.py:376
  113.4 2.3 %collective-permute-done.30 = f32[1,8192]{1,0:T(1,128)S(1)} collective-permute-done((f32[1,8192]{1,0:T(1,128)S(1)}, f32[1,8192]{1,0:T(1,128)S(1)}, u32[]{:S(2)}, u32[]{:S(2)}) %collective-permute-start.30) | collective-permute-done | bytes 32800 | tf_op jit(solution)/shard_map/ppermute | solution.py:43
  117.0 2.9 %collective-permute-start.34 = (f32[1,16384]{1,0:T(1,128)S(1)}, f32[1,16384]{1,0:T(1,128)S(1)}, u32[]{:S(2)}, u32[]{:S(2)}) collective-permute-start(f32[1,16384]{1,0:T(1,128)S(1)} %pad_maximum_fusion.1.refs_5_), channel_id=1, source_target_pairs={{0,16},{1,17},{2,18},{3,19},{4,20},{5,21},{6,22},{7,23},{8,24},{9,... | collective-permute-start | bytes 196616 | tf_op jit(solution)/shard_map/ppermute | solution.py:43
  122.3 3.6 %collective-permute-done.35.refs_8_ = f32[1,16384]{1,0:T(1,128)S(1)} collective-permute-done((f32[1,16384]{1,0:T(1,128)S(1)}, f32[1,16384]{1,0:T(1,128)S(1)}, u32[]{:S(2)}, u32[]{:S(2)}) %collective-permute-start.35) | collective-permute-done | bytes 65568 | tf_op jit(solution)/shard_map/ppermute | solution.py:43
  126.0 10.7 %centroid_update.1.refs_0_ = f32[64,1024]{1,0:T(8,128)S(1)} custom-call(s32[1]{0:T(128)} %bitcast.1.item_ref.at_ref, bf16[64,8192]{1,0:T(8,128)(2,1)S(1)} %bitcast.27, f32[8,1024]{1,0:T(8,128)S(1)} %get-tuple-element.22.refs_1_, bf16[128,8192]{1,0:T(8,128)(2,1)S(1)} %get-tuple-element.13.refs_1_.refs_2_, f32[1,8192]{1,0:T(1,128)S(1)} %get-tuple-element.20.refs_3_, ...), custom_call_target="tpu_custom_call" | custom-call | flops 8589934592 | bytes 4194304 | tf_op jit(solution)/shard_map/centroid_update/pallas_call | solution.py:418
  136.7 2.0 %collective-permute-start.45 = (f32[64,1024]{1,0:T(8,128)S(1)}, f32[64,1024]{1,0:T(8,128)S(1)}, u32[]{:S(2)}, u32[]{:S(2)}) collective-permute-start(f32[64,1024]{1,0:T(8,128)S(1)} %centroid_update.1.refs_0_), channel_id=1, source_target_pairs={{0,8},{4,12},{8,0},{12,4},{16,24},{20,28},{24,16},{28,20},{1,9},{5... | collective-permute-start | bytes 786440 | tf_op jit(solution)/shard_map/ppermute | solution.py:26
  139.1 3.0 %code_gradient.4.rest_1_ = f32[64,512]{1,0:T(8,128)S(1)} custom-call(bf16[64,1024]{1,0:T(8,128)(2,1)S(1)} %bitcast.18, f32[2,1024]{1,0:T(2,128)S(1)} %pad_maximum_fusion.3.p_ref, bf16[64,8192]{1,0:T(8,128)(2,1)S(1)} %bitcast.28, f32[1,8192]{1,0:T(1,128)S(1)} %get-tuple-element.26.rest_0_), custom_call_target="tpu_custom_call" | custom-call | flops 2147483648 | bytes 4194304 | tf_op jit(solution)/shard_map/code_gradient/pallas_call | solution.py:418
  142.2 3.3 %code_gradient.5 = f32[64,512]{1,0:T(8,128)S(1)} custom-call(bf16[64,1024]{1,0:T(8,128)(2,1)S(1)} %bitcast.19, f32[2,1024]{1,0:T(2,128)S(1)} %pad_maximum_fusion.3.p_ref, bf16[64,8192]{1,0:T(8,128)(2,1)S(1)} %bitcast.29, f32[1,8192]{1,0:T(1,128)S(1)} %get-tuple-element.26.rest_0_, f32[64,512]{1,0:T(8,128)S(1)} %code_gradient.4.rest_1_), custom_call_target="tpu_custom_call", output_to_operand_aliasing={{}: (4, {})} | custom-call | flops 2147483648 | bytes 4194304 | tf_op jit(solution)/shard_map/code_gradient/pallas_call | solution.py:418
  145.5 3.0 %code_gradient.6.rest_1_ = f32[64,512]{1,0:T(8,128)S(1)} custom-call(bf16[64,1024]{1,0:T(8,128)(2,1)S(1)} %bitcast.20, f32[2,1024]{1,0:T(2,128)S(1)} %pad_maximum_fusion.3.p_ref, bf16[64,8192]{1,0:T(8,128)(2,1)S(1)} %bitcast.30, f32[1,8192]{1,0:T(1,128)S(1)} %get-tuple-element.26.rest_0_), custom_call_target="tpu_custom_call" | custom-call | flops 2147483648 | bytes 4194304 | tf_op jit(solution)/shard_map/code_gradient/pallas_call | solution.py:418
  148.7 3.0 %code_gradient.7 = f32[64,512]{1,0:T(8,128)S(1)} custom-call(bf16[64,1024]{1,0:T(8,128)(2,1)S(1)} %bitcast.21, f32[2,1024]{1,0:T(2,128)S(1)} %pad_maximum_fusion.3.p_ref, bf16[64,8192]{1,0:T(8,128)(2,1)S(1)} %bitcast.31, f32[1,8192]{1,0:T(1,128)S(1)} %get-tuple-element.26.rest_0_, f32[64,512]{1,0:T(8,128)S(1)} %code_gradient.6.rest_1_), custom_call_target="tpu_custom_call", output_to_operand_aliasing={{}: (4, {})} | custom-call | flops 2147483648 | bytes 4194304 | tf_op jit(solution)/shard_map/code_gradient/pallas_call | solution.py:418
  159.7 3.4 %collective-permute-done.39 = f32[64,512]{1,0:T(8,128)S(1)} collective-permute-done((f32[64,512]{1,0:T(8,128)S(1)}, f32[64,512]{1,0:T(8,128)S(1)}, u32[]{:S(2)}, u32[]{:S(2)}) %collective-permute-start.39) | collective-permute-done | bytes 131104 | tf_op jit(solution)/shard_map/ppermute | solution.py:26
  163.9 4.8 %collective-permute-done.46.refs_3_ = f32[64,1024]{1,0:T(8,128)S(1)} collective-permute-done((f32[64,1024]{1,0:T(8,128)S(1)}, f32[64,1024]{1,0:T(8,128)S(1)}, u32[]{:S(2)}, u32[]{:S(2)}) %collective-permute-start.46) | collective-permute-done | bytes 262176 | tf_op jit(solution)/shard_map/ppermute | solution.py:26
  168.7 2.9 %shard_map.43.refs_2_ = f32[64,8192]{1,0:T(8,128)} custom-call(s32[6]{0:T(128)S(1)} %stack.36.at_ref, f32[64,1024]{1,0:T(8,128)S(1)} %centroid_update.1.refs_0_, f32[64,1024]{1,0:T(8,128)S(1)} %collective-permute-done.44.refs_1_, f32[64,1024]{1,0:T(8,128)S(1)} %collective-permute-done.45.refs_2_, f32[64,1024]{1,0:T(8,128)S(1)} %collective-permute-done.46.refs_3_, ...), custom_call_target="tpu_custom_call" | custom-call | bytes 3145728 | tf_op jit(solution)/shard_map/pallas_call | solution.py:477
  171.5 2.8 %collective-permute-done.41.refs_0_ = f32[64,1024]{1,0:T(8,128)S(1)} collective-permute-done((f32[64,1024]{1,0:T(8,128)S(1)}, f32[64,1024]{1,0:T(8,128)S(1)}, u32[]{:S(2)}, u32[]{:S(2)}) %collective-permute-start.41) | collective-permute-done | bytes 262176 | tf_op jit(solution)/shard_map/ppermute | solution.py:26
  174.3 4.4 %collective-permute-done.43.refs_1_ = f32[64,1024]{1,0:T(8,128)S(1)} collective-permute-done((f32[64,1024]{1,0:T(8,128)S(1)}, f32[64,1024]{1,0:T(8,128)S(1)}, u32[]{:S(2)}, u32[]{:S(2)}) %collective-permute-start.43) | collective-permute-done | bytes 262176 | tf_op jit(solution)/shard_map/ppermute | solution.py:26
  (126 shorter events, 55.2 us)
Async XLA Ops:
  1.5 16.8 %collective-permute-start.3 = (f32[64,512]{1,0:T(8,128)S(1)}, f32[64,512]{1,0:T(8,128)S(1)}, u32[]{:S(2)}, u32[]{:S(2)}) collective-permute-start(f32[64,512]{1,0:T(8,128)S(1)} %convert_bitcast_fusion.refs_0_), channel_id=1, source_target_pairs={{0,16},{4,20},{8,24},{12,28},{16,0},{20,4},{24,8},{28,12},{1,17},{... | collective-permute-start | bytes 393224 | tf_op jit(solution)/shard_map/ppermute | solution.py:26
  16.7 8.9 %collective-permute-start.1 = (f32[64,512]{1,0:T(8,128)S(1)}, f32[64,512]{1,0:T(8,128)S(1)}, u32[]{:S(2)}, u32[]{:S(2)}) collective-permute-start(f32[64,512]{1,0:T(8,128)S(1)} %convert_bitcast_fusion.refs_0_), channel_id=1, source_target_pairs={{0,8},{4,12},{8,0},{12,4},{16,24},{20,28},{24,16},{28,20},{1,9},{5... | collective-permute-start | bytes 393224 | tf_op jit(solution)/shard_map/ppermute | solution.py:26
  18.3 8.7 %collective-permute-start.5 = (f32[64,512]{1,0:T(8,128)S(1)}, f32[64,512]{1,0:T(8,128)S(1)}, u32[]{:S(2)}, u32[]{:S(2)}) collective-permute-start(f32[64,512]{1,0:T(8,128)S(1)} %collective-permute-done.3.refs_4_), channel_id=1, source_target_pairs={{0,8},{4,12},{8,0},{12,4},{16,24},{20,28},{24,16},{28,20},{1,9},{5... | collective-permute-start | bytes 393224 | tf_op jit(solution)/shard_map/ppermute | solution.py:26
  21.9 5.8 %collective-permute-start = (f32[64,512]{1,0:T(8,128)S(1)}, f32[64,512]{1,0:T(8,128)S(1)}, u32[]{:S(2)}, u32[]{:S(2)}) collective-permute-start(f32[64,512]{1,0:T(8,128)S(1)} %convert_bitcast_fusion.refs_0_), channel_id=1, source_target_pairs={{0,4},{4,0},{8,12},{12,8},{16,20},{20,16},{24,28},{28,24},{1,5},{5... | collective-permute-start | bytes 393224 | tf_op jit(solution)/shard_map/ppermute | solution.py:26
  23.4 12.1 %collective-permute-start.9 = (f32[2,1024]{1,0:T(2,128)S(1)}, f32[2,1024]{1,0:T(2,128)S(1)}, u32[]{:S(2)}, u32[]{:S(2)}) collective-permute-start(f32[2,1024]{1,0:T(2,128)S(1)} %pad_maximum_fusion.2), channel_id=1, source_target_pairs={{0,2},{1,3},{2,0},{3,1},{4,6},{5,7},{6,4},{7,5},{8,10},{9,11},{10,... | collective-permute-start | bytes 24584 | tf_op jit(solution)/shard_map/ppermute | solution.py:43
  25.0 6.4 %collective-permute-start.4 = (f32[64,512]{1,0:T(8,128)S(1)}, f32[64,512]{1,0:T(8,128)S(1)}, u32[]{:S(2)}, u32[]{:S(2)}) collective-permute-start(f32[64,512]{1,0:T(8,128)S(1)} %collective-permute-done.3.refs_4_), channel_id=1, source_target_pairs={{0,4},{4,0},{8,12},{12,8},{16,20},{20,16},{24,28},{28,24},{1,5},{5... | collective-permute-start | bytes 393224 | tf_op jit(solution)/shard_map/ppermute | solution.py:26
  25.6 8.3 %collective-permute-start.2 = (f32[64,512]{1,0:T(8,128)S(1)}, f32[64,512]{1,0:T(8,128)S(1)}, u32[]{:S(2)}, u32[]{:S(2)}) collective-permute-start(f32[64,512]{1,0:T(8,128)S(1)} %collective-permute-done.1.refs_2_), channel_id=1, source_target_pairs={{0,4},{4,0},{8,12},{12,8},{16,20},{20,16},{24,28},{28,24},{1,5},{5... | collective-permute-start | bytes 393224 | tf_op jit(solution)/shard_map/ppermute | solution.py:26
  27.0 8.2 %collective-permute-start.6 = (f32[64,512]{1,0:T(8,128)S(1)}, f32[64,512]{1,0:T(8,128)S(1)}, u32[]{:S(2)}, u32[]{:S(2)}) collective-permute-start(f32[64,512]{1,0:T(8,128)S(1)} %collective-permute-done.5.refs_6_), channel_id=1, source_target_pairs={{0,4},{4,0},{8,12},{12,8},{16,20},{20,16},{24,28},{28,24},{1,5},{5... | collective-permute-start | bytes 393224 | tf_op jit(solution)/shard_map/ppermute | solution.py:26
  35.3 4.8 %collective-permute-start.7 = (f32[64,4096]{1,0:T(8,128)S(1)}, f32[64,4096]{1,0:T(8,128)S(1)}, u32[]{:S(2)}, u32[]{:S(2)}) collective-permute-start(f32[64,4096]{1,0:T(8,128)S(1)} %shard_map.41.mine_ref), channel_id=1, source_target_pairs={{0,1},{1,0},{2,3},{3,2},{4,5},{5,4},{6,7},{7,6},{8,9},{9,8},{10,11... | collective-permute-start | bytes 3145736 | tf_op jit(solution)/shard_map/ppermute | solution.py:26
  35.6 5.1 %collective-permute-start.12 = (f32[1,8192]{1,0:T(1,128)S(1)}, f32[1,8192]{1,0:T(1,128)S(1)}, u32[]{:S(2)}, u32[]{:S(2)}) collective-permute-start(f32[1,8192]{1,0:T(1,128)S(1)} %add.128.refs_2_), channel_id=1, source_target_pairs={{0,8},{1,9},{2,10},{3,11},{4,12},{5,13},{6,14},{7,15},{8,0},{9,1},... | collective-permute-start | bytes 98312 | tf_op jit(solution)/shard_map/ppermute | solution.py:43
  37.3 5.7 %collective-permute-start.13 = (f32[1,8192]{1,0:T(1,128)S(1)}, f32[1,8192]{1,0:T(1,128)S(1)}, u32[]{:S(2)}, u32[]{:S(2)}) collective-permute-start(f32[1,8192]{1,0:T(1,128)S(1)} %add.128.refs_2_), channel_id=1, source_target_pairs={{0,16},{1,17},{2,18},{3,19},{4,20},{5,21},{6,22},{7,23},{8,24},{9,... | collective-permute-start | bytes 98312 | tf_op jit(solution)/shard_map/ppermute | solution.py:43
  37.6 5.8 %collective-permute-start.14 = (f32[1,8192]{1,0:T(1,128)S(1)}, f32[1,8192]{1,0:T(1,128)S(1)}, u32[]{:S(2)}, u32[]{:S(2)}) collective-permute-start(f32[1,8192]{1,0:T(1,128)S(1)} %add.128.refs_2_), channel_id=1, source_target_pairs={{0,24},{1,25},{2,26},{3,27},{4,28},{5,29},{6,30},{7,31},{8,16},{9,... | collective-permute-start | bytes 98312 | tf_op jit(solution)/shard_map/ppermute | solution.py:43
  60.4 4.8 %collective-permute-start.18 = (f32[1,8192]{1,0:T(1,128)S(1)}, f32[1,8192]{1,0:T(1,128)S(1)}, u32[]{:S(2)}, u32[]{:S(2)}) collective-permute-start(f32[1,8192]{1,0:T(1,128)S(1)} %add.129), channel_id=1, source_target_pairs={{0,6},{1,7},{2,4},{3,5},{4,2},{5,3},{6,0},{7,1},{8,14},{9,15},{10,... | collective-permute-start | bytes 98312 | tf_op jit(solution)/shard_map/ppermute | solution.py:43
  66.2 5.5 %collective-permute-start.20 = (f32[1,8192]{1,0:T(1,128)S(1)}, f32[1,8192]{1,0:T(1,128)S(1)}, u32[]{:S(2)}, u32[]{:S(2)}) collective-permute-start(f32[1,8192]{1,0:T(1,128)S(1)} %add_add_fusion.2.refs_2_), channel_id=1, source_target_pairs={{0,16},{1,17},{2,18},{3,19},{4,20},{5,21},{6,22},{7,23},{8,24},{9,... | collective-permute-start | bytes 98312 | tf_op jit(solution)/shard_map/ppermute | solution.py:43
  68.3 5.7 %collective-permute-start.21 = (f32[1,8192]{1,0:T(1,128)S(1)}, f32[1,8192]{1,0:T(1,128)S(1)}, u32[]{:S(2)}, u32[]{:S(2)}) collective-permute-start(f32[1,8192]{1,0:T(1,128)S(1)} %add_add_fusion.2.refs_2_), channel_id=1, source_target_pairs={{0,24},{1,25},{2,26},{3,27},{4,28},{5,29},{6,30},{7,31},{8,16},{9,... | collective-permute-start | bytes 98312 | tf_op jit(solution)/shard_map/ppermute | solution.py:43
  86.1 4.8 %collective-permute-start.25 = (f32[1,8192]{1,0:T(1,128)S(1)}, f32[1,8192]{1,0:T(1,128)S(1)}, u32[]{:S(2)}, u32[]{:S(2)}) collective-permute-start(f32[1,8192]{1,0:T(1,128)S(1)} %add.133), channel_id=1, source_target_pairs={{0,6},{1,7},{2,4},{3,5},{4,2},{5,3},{6,0},{7,1},{8,14},{9,15},{10,... | collective-permute-start | bytes 98312 | tf_op jit(solution)/shard_map/ppermute | solution.py:43
  91.1 5.2 %collective-permute-start.27 = (f32[1,8192]{1,0:T(1,128)S(1)}, f32[1,8192]{1,0:T(1,128)S(1)}, u32[]{:S(2)}, u32[]{:S(2)}) collective-permute-start(f32[1,8192]{1,0:T(1,128)S(1)} %add_add_fusion.1.refs_2_), channel_id=1, source_target_pairs={{0,16},{1,17},{2,18},{3,19},{4,20},{5,21},{6,22},{7,23},{8,24},{9,... | collective-permute-start | bytes 98312 | tf_op jit(solution)/shard_map/ppermute | solution.py:43
  93.1 5.7 %collective-permute-start.28 = (f32[1,8192]{1,0:T(1,128)S(1)}, f32[1,8192]{1,0:T(1,128)S(1)}, u32[]{:S(2)}, u32[]{:S(2)}) collective-permute-start(f32[1,8192]{1,0:T(1,128)S(1)} %add_add_fusion.1.refs_2_), channel_id=1, source_target_pairs={{0,24},{1,25},{2,26},{3,27},{4,28},{5,29},{6,30},{7,31},{8,16},{9,... | collective-permute-start | bytes 98312 | tf_op jit(solution)/shard_map/ppermute | solution.py:43
  109.9 6.9 %collective-permute-start.31 = (f32[1,16384]{1,0:T(1,128)S(1)}, f32[1,16384]{1,0:T(1,128)S(1)}, u32[]{:S(2)}, u32[]{:S(2)}) collective-permute-start(f32[1,16384]{1,0:T(1,128)S(1)} %pad_maximum_fusion), channel_id=1, source_target_pairs={{0,4},{1,5},{2,6},{3,7},{4,0},{5,1},{6,2},{7,3},{8,12},{9,13},{10,... | collective-permute-start | bytes 196616 | tf_op jit(solution)/shard_map/ppermute | solution.py:43
  111.9 4.8 %collective-permute-start.32 = (f32[1,8192]{1,0:T(1,128)S(1)}, f32[1,8192]{1,0:T(1,128)S(1)}, u32[]{:S(2)}, u32[]{:S(2)}) collective-permute-start(f32[1,8192]{1,0:T(1,128)S(1)} %add.139), channel_id=1, source_target_pairs={{0,6},{1,7},{2,4},{3,5},{4,2},{5,3},{6,0},{7,1},{8,14},{9,15},{10,... | collective-permute-start | bytes 98312 | tf_op jit(solution)/shard_map/ppermute | solution.py:43
  117.0 5.3 %collective-permute-start.34 = (f32[1,16384]{1,0:T(1,128)S(1)}, f32[1,16384]{1,0:T(1,128)S(1)}, u32[]{:S(2)}, u32[]{:S(2)}) collective-permute-start(f32[1,16384]{1,0:T(1,128)S(1)} %pad_maximum_fusion.1.refs_5_), channel_id=1, source_target_pairs={{0,16},{1,17},{2,18},{3,19},{4,20},{5,21},{6,22},{7,23},{8,24},{9,... | collective-permute-start | bytes 196616 | tf_op jit(solution)/shard_map/ppermute | solution.py:43
  119.9 6.1 %collective-permute-start.35 = (f32[1,16384]{1,0:T(1,128)S(1)}, f32[1,16384]{1,0:T(1,128)S(1)}, u32[]{:S(2)}, u32[]{:S(2)}) collective-permute-start(f32[1,16384]{1,0:T(1,128)S(1)} %pad_maximum_fusion.1.refs_5_), channel_id=1, source_target_pairs={{0,24},{1,25},{2,26},{3,27},{4,28},{5,29},{6,30},{7,31},{8,16},{9,... | collective-permute-start | bytes 196616 | tf_op jit(solution)/shard_map/ppermute | solution.py:43
  136.7 11.9 %collective-permute-start.40 = (f32[64,1024]{1,0:T(8,128)S(1)}, f32[64,1024]{1,0:T(8,128)S(1)}, u32[]{:S(2)}, u32[]{:S(2)}) collective-permute-start(f32[64,1024]{1,0:T(8,128)S(1)} %centroid_update.1.refs_0_), channel_id=1, source_target_pairs={{0,16},{4,20},{8,24},{12,28},{16,0},{20,4},{24,8},{28,12},{1,17},{... | collective-permute-start | bytes 786440 | tf_op jit(solution)/shard_map/ppermute | solution.py:26
  136.7 17.7 %collective-permute-start.45 = (f32[64,1024]{1,0:T(8,128)S(1)}, f32[64,1024]{1,0:T(8,128)S(1)}, u32[]{:S(2)}, u32[]{:S(2)}) collective-permute-start(f32[64,1024]{1,0:T(8,128)S(1)} %centroid_update.1.refs_0_), channel_id=1, source_target_pairs={{0,8},{4,12},{8,0},{12,4},{16,24},{20,28},{24,16},{28,20},{1,9},{5... | collective-permute-start | bytes 786440 | tf_op jit(solution)/shard_map/ppermute | solution.py:26
  145.5 6.8 %collective-permute-start.36 = (f32[64,512]{1,0:T(8,128)S(1)}, f32[64,512]{1,0:T(8,128)S(1)}, u32[]{:S(2)}, u32[]{:S(2)}) collective-permute-start(f32[64,512]{1,0:T(8,128)S(1)} %code_gradient.5), channel_id=1, source_target_pairs={{0,1},{1,0},{2,3},{3,2},{4,5},{5,4},{6,7},{7,6},{8,9},{9,8},{10,11... | collective-permute-start | bytes 393224 | tf_op jit(solution)/shard_map/ppermute | solution.py:26
  148.6 8.8 %collective-permute-start.42 = (f32[64,1024]{1,0:T(8,128)S(1)}, f32[64,1024]{1,0:T(8,128)S(1)}, u32[]{:S(2)}, u32[]{:S(2)}) collective-permute-start(f32[64,1024]{1,0:T(8,128)S(1)} %collective-permute-done.40.refs_4_), channel_id=1, source_target_pairs={{0,8},{4,12},{8,0},{12,4},{16,24},{20,28},{24,16},{28,20},{1,9},{5... | collective-permute-start | bytes 786440 | tf_op jit(solution)/shard_map/ppermute | solution.py:26
  152.3 5.8 %collective-permute-start.37 = (f32[64,512]{1,0:T(8,128)S(1)}, f32[64,512]{1,0:T(8,128)S(1)}, u32[]{:S(2)}, u32[]{:S(2)}) collective-permute-start(f32[64,512]{1,0:T(8,128)S(1)} %add.148), channel_id=1, source_target_pairs={{0,2},{1,3},{2,0},{3,1},{4,6},{5,7},{6,4},{7,5},{8,10},{9,11},{10,... | collective-permute-start | bytes 393224 | tf_op jit(solution)/shard_map/ppermute | solution.py:26
  153.9 10.0 %collective-permute-start.44 = (f32[64,1024]{1,0:T(8,128)S(1)}, f32[64,1024]{1,0:T(8,128)S(1)}, u32[]{:S(2)}, u32[]{:S(2)}) collective-permute-start(f32[64,1024]{1,0:T(8,128)S(1)} %centroid_update.1.refs_0_), channel_id=1, source_target_pairs={{0,4},{4,0},{8,12},{12,8},{16,20},{20,16},{24,28},{28,24},{1,5},{5... | collective-permute-start | bytes 786440 | tf_op jit(solution)/shard_map/ppermute | solution.py:26
  154.4 14.2 %collective-permute-start.46 = (f32[64,1024]{1,0:T(8,128)S(1)}, f32[64,1024]{1,0:T(8,128)S(1)}, u32[]{:S(2)}, u32[]{:S(2)}) collective-permute-start(f32[64,1024]{1,0:T(8,128)S(1)} %collective-permute-done.45.refs_2_), channel_id=1, source_target_pairs={{0,4},{4,0},{8,12},{12,8},{16,20},{20,16},{24,28},{28,24},{1,5},{5... | collective-permute-start | bytes 786440 | tf_op jit(solution)/shard_map/ppermute | solution.py:26
  155.9 18.4 %collective-permute-start.41 = (f32[64,1024]{1,0:T(8,128)S(1)}, f32[64,1024]{1,0:T(8,128)S(1)}, u32[]{:S(2)}, u32[]{:S(2)}) collective-permute-start(f32[64,1024]{1,0:T(8,128)S(1)} %collective-permute-done.40.refs_4_), channel_id=1, source_target_pairs={{0,4},{4,0},{8,12},{12,8},{16,20},{20,16},{24,28},{28,24},{1,5},{5... | collective-permute-start | bytes 786440 | tf_op jit(solution)/shard_map/ppermute | solution.py:26
  157.4 21.4 %collective-permute-start.43 = (f32[64,1024]{1,0:T(8,128)S(1)}, f32[64,1024]{1,0:T(8,128)S(1)}, u32[]{:S(2)}, u32[]{:S(2)}) collective-permute-start(f32[64,1024]{1,0:T(8,128)S(1)} %collective-permute-done.42.refs_5_), channel_id=1, source_target_pairs={{0,4},{4,0},{8,12},{12,8},{16,20},{20,16},{24,28},{28,24},{1,5},{5... | collective-permute-start | bytes 786440 | tf_op jit(solution)/shard_map/ppermute | solution.py:26
  158.1 5.0 %collective-permute-start.39 = (f32[64,512]{1,0:T(8,128)S(1)}, f32[64,512]{1,0:T(8,128)S(1)}, u32[]{:S(2)}, u32[]{:S(2)}) collective-permute-start(f32[64,512]{1,0:T(8,128)S(1)} %add.150), channel_id=1, source_target_pairs={{0,2},{1,3},{2,0},{3,1},{4,6},{5,7},{6,4},{7,5},{8,10},{9,11},{10,... | collective-permute-start | bytes 393224 | tf_op jit(solution)/shard_map/ppermute | solution.py:26
  (23 other events, 132.8 us)

commit v10 on v9

--- a/solution.py
+++ b/solution.py
@@ -464,11 +464,16 @@
 
 
 def store_kernel(at_ref, *refs, count):
+    out_ref, sems = refs[-2:]
+    width = refs[0].shape[1]
+    copies = []
     for number in range(count):
-
-        @pl.when(pl.program_id(0) == number)
-        def _():
-            refs[-1][...] = refs[number][...]
+        at = pl.ds(pl.multiple_of(at_ref[number] * width, width), width)
+        copies.append(pltpu.make_async_copy(refs[number], out_ref.at[:, at], sems.at[number]))
+    for copy in copies:
+        copy.start()
+    for copy in copies:
+        copy.wait()
 
 
 def store(pieces, item, keys, total, before):
@@ -478,10 +483,11 @@
         functools.partial(store_kernel, count=len(keys)),
         grid_spec=pltpu.PrefetchScalarGridSpec(
             num_scalar_prefetch=1,
-            grid=(len(keys),),
+            grid=(1,),
             in_specs=[pl.BlockSpec(memory_space=pltpu.VMEM)] * len(keys)
             + [pl.BlockSpec(memory_space=pl.ANY)] * len(before),
-            out_specs=pl.BlockSpec((dim, width), lambda k, at: (0, at[k])),
+            out_specs=pl.BlockSpec(memory_space=pl.ANY),
+            scratch_shapes=[pltpu.SemaphoreType.DMA((len(keys),))],
         ),
         out_shape=jax.ShapeDtypeStruct((dim, width * total), jnp.float32),
         input_output_aliases={1 + len(keys): 0} if before else {},

time: 180 us -> 181 us (level)
  transfers between devices with their start and end apart: 47 -> 47, of which waited for: 29 -> 29; matrix products, arithmetic and copies ran while one was open for 1% -> 1% of each run, Pallas kernels for 14% -> 13%
where the time goes in v10:
time: 181 us; the launch traced here: 180 us
  Pallas kernels  66.5 us (37%)
  waiting for transfers between devices  54.5 us (30%)
  starting transfers between devices  51.9 us (29%)
  local copies, waits for them, and re-layouts  3.59 us (2%)
  other arithmetic  2.62 us (1%)
    ppermute x25, starting transfers between devices, joint_swap(): return lax.ppermute(value, ('item', 'bucket'), pairs)  32.3 us
    pallas_call x3, Pallas kernels, sink(): pl.pallas_call(lambda at_ref, *refs: kernel(*refs), grid_spec=pltpu.Prefe...  30.7 us
    ppermute x22, waiting for transfers between devices, swap(): return lax.ppermute(value, axis, [(k, k ^ bit) for k in range(size)])  28.6 us
    ppermute x25, waiting for transfers between devices, joint_swap(): return lax.ppermute(value, ('item', 'bucket'), pairs)  25.8 us
    pallas_call x5, Pallas kernels, final(): pl.pallas_call((lambda at_ref, *refs: kernel(*refs)) if update else kerne...  23.1 us
    ppermute x22, starting transfers between devices, swap(): return lax.ppermute(value, axis, [(k, k ^ bit) for k in range(size)])  19.6 us
    pallas_call x2, Pallas kernels, lse(): pl.pallas_call(functools.partial(lse_kernel, repeat=repeat), grid=(count,...  8.85 us
  transfers between devices with their start and end apart: 47, of which 29 were waited for; matrix products, arithmetic and copies ran while one was open for 1% of the time, Pallas kernels for 13%

profile of v10, /device:TPU:0, one launch (start us, length us, event | category | flops | bytes accessed | tf_op | source)
XLA Modules:
  0.0 180.3 jit_solution(11899931781629633119)
XLA Ops:
  1.5 4.1 %collective-permute-start.3 = (f32[64,512]{1,0:T(8,128)S(1)}, f32[64,512]{1,0:T(8,128)S(1)}, u32[]{:S(2)}, u32[]{:S(2)}) collective-permute-start(f32[64,512]{1,0:T(8,128)S(1)} %convert_bitcast_fusion.refs_0_), channel_id=1, source_target_pairs={{0,16},{4,20},{8,24},{12,28},{16,0},{20,4},{24,8},{28,12},{1,17},{... | collective-permute-start | bytes 393224 | tf_op jit(solution)/shard_map/ppermute | solution.py:26
  7.8 4.4 %row_lse.2.rest_0_ = f32[2,1024]{1,0:T(2,128)S(1)} custom-call(bf16[64,1024]{1,0:T(8,128)(2,1)S(1)} %bitcast.16, bf16[64,8192]{1,0:T(8,128)(2,1)S(1)} %bitcast.22), custom_call_target="tpu_custom_call" | custom-call | flops 2147483648 | bytes 4194304 | tf_op jit(solution)/shard_map/row_lse/pallas_call | solution.py:350
  12.2 4.4 %row_lse.3 = f32[2,1024]{1,0:T(2,128)S(1)} custom-call(bf16[64,1024]{1,0:T(8,128)(2,1)S(1)} %bitcast.17, bf16[64,8192]{1,0:T(8,128)(2,1)S(1)} %bitcast.23, f32[2,1024]{1,0:T(2,128)S(1)} %row_lse.2.rest_0_), custom_call_target="tpu_custom_call", output_to_operand_aliasing={{}: (2, {})} | custom-call | flops 2147483648 | bytes 4194304 | tf_op jit(solution)/shard_map/row_lse/pallas_call | solution.py:350
  16.7 1.6 collective-permute-start.1
  27.7 3.7 %collective-permute-done.4.refs_5_ = f32[64,512]{1,0:T(8,128)S(1)} collective-permute-done((f32[64,512]{1,0:T(8,128)S(1)}, f32[64,512]{1,0:T(8,128)S(1)}, u32[]{:S(2)}, u32[]{:S(2)}) %collective-permute-start.4) | collective-permute-done | bytes 131104 | tf_op jit(solution)/shard_map/ppermute | solution.py:26
  31.4 2.5 %collective-permute-done.2.refs_3_ = f32[64,512]{1,0:T(8,128)S(1)} collective-permute-done((f32[64,512]{1,0:T(8,128)S(1)}, f32[64,512]{1,0:T(8,128)S(1)}, u32[]{:S(2)}, u32[]{:S(2)}) %collective-permute-start.2) | collective-permute-done | bytes 131104 | tf_op jit(solution)/shard_map/ppermute | solution.py:26
  37.6 2.5 %collective-permute-start.14 = (f32[1,8192]{1,0:T(1,128)S(1)}, f32[1,8192]{1,0:T(1,128)S(1)}, u32[]{:S(2)}, u32[]{:S(2)}) collective-permute-start(f32[1,8192]{1,0:T(1,128)S(1)} %add.128.refs_2_), channel_id=1, source_target_pairs={{0,24},{1,25},{2,26},{3,27},{4,28},{5,29},{6,30},{7,31},{8,16},{9,... | collective-permute-start | bytes 98312 | tf_op jit(solution)/shard_map/ppermute | solution.py:43
  40.7 2.2 %collective-permute-done.13.refs_4_ = f32[1,8192]{1,0:T(1,128)S(1)} collective-permute-done((f32[1,8192]{1,0:T(1,128)S(1)}, f32[1,8192]{1,0:T(1,128)S(1)}, u32[]{:S(2)}, u32[]{:S(2)}) %collective-permute-start.13) | collective-permute-done | bytes 32800 | tf_op jit(solution)/shard_map/ppermute | solution.py:43
  43.4 13.6 %sinkhorn_first.1 = (f32[1,8192]{1,0:T(1,128)S(1)}, f32[8,1024]{1,0:T(8,128)S(1)}, f32[1,8192]{1,0:T(1,128)S(1)}) custom-call(s32[1]{0:T(128)} %bitcast.1.item_ref.at_ref, bf16[64,8192]{1,0:T(8,128)(2,1)S(1)} %bitcast.24, bf16[128,8192]{1,0:T(8,128)(2,1)S(1)} %get-tuple-element.13.refs_1_.refs_2_, f32[1,8192]{1,0:T(1,128)S(1)} %add.128.refs_2_, ...), custom_call_target="tpu_custom_call" | custom-call | flops 4294967296 | bytes 4194304 | tf_op jit(solution)/shard_map/sinkhorn_first/pallas_call | solution.py:376
  63.0 2.2 %collective-permute-done.18 = f32[1,8192]{1,0:T(1,128)S(1)} collective-permute-done((f32[1,8192]{1,0:T(1,128)S(1)}, f32[1,8192]{1,0:T(1,128)S(1)}, u32[]{:S(2)}, u32[]{:S(2)}) %collective-permute-start.18) | collective-permute-done | bytes 32800 | tf_op jit(solution)/shard_map/ppermute | solution.py:43
  66.2 2.1 %collective-permute-start.20 = (f32[1,8192]{1,0:T(1,128)S(1)}, f32[1,8192]{1,0:T(1,128)S(1)}, u32[]{:S(2)}, u32[]{:S(2)}) collective-permute-start(f32[1,8192]{1,0:T(1,128)S(1)} %add_add_fusion.2.refs_2_), channel_id=1, source_target_pairs={{0,16},{1,17},{2,18},{3,19},{4,20},{5,21},{6,22},{7,23},{8,24},{9,... | collective-permute-start | bytes 98312 | tf_op jit(solution)/shard_map/ppermute | solution.py:43
  69.8 1.9 %collective-permute-done.20.refs_4_ = f32[1,8192]{1,0:T(1,128)S(1)} collective-permute-done((f32[1,8192]{1,0:T(1,128)S(1)}, f32[1,8192]{1,0:T(1,128)S(1)}, u32[]{:S(2)}, u32[]{:S(2)}) %collective-permute-start.20) | collective-permute-done | bytes 32800 | tf_op jit(solution)/shard_map/ppermute | solution.py:43
  71.7 2.3 %collective-permute-done.21.refs_5_ = f32[1,8192]{1,0:T(1,128)S(1)} collective-permute-done((f32[1,8192]{1,0:T(1,128)S(1)}, f32[1,8192]{1,0:T(1,128)S(1)}, u32[]{:S(2)}, u32[]{:S(2)}) %collective-permute-start.21) | collective-permute-done | bytes 32800 | tf_op jit(solution)/shard_map/ppermute | solution.py:43
  74.0 8.7 %sinkhorn_next.2 = (f32[1,8192]{1,0:T(1,128)S(1)}, f32[8,1024]{1,0:T(8,128)S(1)}, f32[1,8192]{1,0:T(1,128)S(1)}) custom-call(s32[1]{0:T(128)} %bitcast.1.item_ref.at_ref, bf16[64,8192]{1,0:T(8,128)(2,1)S(1)} %bitcast.25, bf16[128,8192]{1,0:T(8,128)(2,1)S(1)} %get-tuple-element.13.refs_1_.refs_2_, f32[1,8192]{1,0:T(1,128)S(1)} %add_add_fusion.2.refs_2_, ...), custom_call_target="tpu_custom_call" | custom-call | flops 4294967296 | bytes 4194304 | tf_op jit(solution)/shard_map/sinkhorn_next/pallas_call | solution.py:376
  91.1 2.0 %collective-permute-start.27 = (f32[1,8192]{1,0:T(1,128)S(1)}, f32[1,8192]{1,0:T(1,128)S(1)}, u32[]{:S(2)}, u32[]{:S(2)}) collective-permute-start(f32[1,8192]{1,0:T(1,128)S(1)} %add_add_fusion.1.refs_2_), channel_id=1, source_target_pairs={{0,16},{1,17},{2,18},{3,19},{4,20},{5,21},{6,22},{7,23},{8,24},{9,... | collective-permute-start | bytes 98312 | tf_op jit(solution)/shard_map/ppermute | solution.py:43
  93.1 2.4 %collective-permute-start.28 = (f32[1,8192]{1,0:T(1,128)S(1)}, f32[1,8192]{1,0:T(1,128)S(1)}, u32[]{:S(2)}, u32[]{:S(2)}) collective-permute-start(f32[1,8192]{1,0:T(1,128)S(1)} %add_add_fusion.1.refs_2_), channel_id=1, source_target_pairs={{0,24},{1,25},{2,26},{3,27},{4,28},{5,29},{6,30},{7,31},{8,16},{9,... | collective-permute-start | bytes 98312 | tf_op jit(solution)/shard_map/ppermute | solution.py:43
  96.3 2.5 %collective-permute-done.28.refs_5_ = f32[1,8192]{1,0:T(1,128)S(1)} collective-permute-done((f32[1,8192]{1,0:T(1,128)S(1)}, f32[1,8192]{1,0:T(1,128)S(1)}, u32[]{:S(2)}, u32[]{:S(2)}) %collective-permute-start.28) | collective-permute-done | bytes 32800 | tf_op jit(solution)/shard_map/ppermute | solution.py:43
  100.0 8.5 %sinkhorn_next.3 = (f32[1,8192]{1,0:T(1,128)S(1)}, f32[8,1024]{1,0:T(8,128)S(1)}, f32[1,8192]{1,0:T(1,128)S(1)}) custom-call(s32[1]{0:T(128)} %bitcast.1.item_ref.at_ref, bf16[64,8192]{1,0:T(8,128)(2,1)S(1)} %bitcast.26, bf16[128,8192]{1,0:T(8,128)(2,1)S(1)} %get-tuple-element.13.refs_1_.refs_2_, f32[1,8192]{1,0:T(1,128)S(1)} %add_add_fusion.1.refs_2_, ...), custom_call_target="tpu_custom_call" | custom-call | flops 4294967296 | bytes 4194304 | tf_op jit(solution)/shard_map/sinkhorn_next/pallas_call | solution.py:376
  113.4 2.3 %collective-permute-done.30 = f32[1,8192]{1,0:T(1,128)S(1)} collective-permute-done((f32[1,8192]{1,0:T(1,128)S(1)}, f32[1,8192]{1,0:T(1,128)S(1)}, u32[]{:S(2)}, u32[]{:S(2)}) %collective-permute-start.30) | collective-permute-done | bytes 32800 | tf_op jit(solution)/shard_map/ppermute | solution.py:43
  117.0 2.9 %collective-permute-start.34 = (f32[1,16384]{1,0:T(1,128)S(1)}, f32[1,16384]{1,0:T(1,128)S(1)}, u32[]{:S(2)}, u32[]{:S(2)}) collective-permute-start(f32[1,16384]{1,0:T(1,128)S(1)} %pad_maximum_fusion.1.refs_5_), channel_id=1, source_target_pairs={{0,16},{1,17},{2,18},{3,19},{4,20},{5,21},{6,22},{7,23},{8,24},{9,... | collective-permute-start | bytes 196616 | tf_op jit(solution)/shard_map/ppermute | solution.py:43
  122.3 3.6 %collective-permute-done.35.refs_8_ = f32[1,16384]{1,0:T(1,128)S(1)} collective-permute-done((f32[1,16384]{1,0:T(1,128)S(1)}, f32[1,16384]{1,0:T(1,128)S(1)}, u32[]{:S(2)}, u32[]{:S(2)}) %collective-permute-start.35) | collective-permute-done | bytes 65568 | tf_op jit(solution)/shard_map/ppermute | solution.py:43
  126.0 10.7 %centroid_update.1.refs_0_ = f32[64,1024]{1,0:T(8,128)S(1)} custom-call(s32[1]{0:T(128)} %bitcast.1.item_ref.at_ref, bf16[64,8192]{1,0:T(8,128)(2,1)S(1)} %bitcast.27, f32[8,1024]{1,0:T(8,128)S(1)} %get-tuple-element.22.refs_1_, bf16[128,8192]{1,0:T(8,128)(2,1)S(1)} %get-tuple-element.13.refs_1_.refs_2_, f32[1,8192]{1,0:T(1,128)S(1)} %get-tuple-element.20.refs_3_, ...), custom_call_target="tpu_custom_call" | custom-call | flops 8589934592 | bytes 4194304 | tf_op jit(solution)/shard_map/centroid_update/pallas_call | solution.py:418
  136.7 2.0 %collective-permute-start.45 = (f32[64,1024]{1,0:T(8,128)S(1)}, f32[64,1024]{1,0:T(8,128)S(1)}, u32[]{:S(2)}, u32[]{:S(2)}) collective-permute-start(f32[64,1024]{1,0:T(8,128)S(1)} %centroid_update.1.refs_0_), channel_id=1, source_target_pairs={{0,8},{4,12},{8,0},{12,4},{16,24},{20,28},{24,16},{28,20},{1,9},{5... | collective-permute-start | bytes 786440 | tf_op jit(solution)/shard_map/ppermute | solution.py:26
  139.1 3.0 %code_gradient.4.rest_1_ = f32[64,512]{1,0:T(8,128)S(1)} custom-call(bf16[64,1024]{1,0:T(8,128)(2,1)S(1)} %bitcast.18, f32[2,1024]{1,0:T(2,128)S(1)} %pad_maximum_fusion.3.p_ref, bf16[64,8192]{1,0:T(8,128)(2,1)S(1)} %bitcast.28, f32[1,8192]{1,0:T(1,128)S(1)} %get-tuple-element.26.rest_0_), custom_call_target="tpu_custom_call" | custom-call | flops 2147483648 | bytes 4194304 | tf_op jit(solution)/shard_map/code_gradient/pallas_call | solution.py:418
  142.2 3.3 %code_gradient.5 = f32[64,512]{1,0:T(8,128)S(1)} custom-call(bf16[64,1024]{1,0:T(8,128)(2,1)S(1)} %bitcast.19, f32[2,1024]{1,0:T(2,128)S(1)} %pad_maximum_fusion.3.p_ref, bf16[64,8192]{1,0:T(8,128)(2,1)S(1)} %bitcast.29, f32[1,8192]{1,0:T(1,128)S(1)} %get-tuple-element.26.rest_0_, f32[64,512]{1,0:T(8,128)S(1)} %code_gradient.4.rest_1_), custom_call_target="tpu_custom_call", output_to_operand_aliasing={{}: (4, {})} | custom-call | flops 2147483648 | bytes 4194304 | tf_op jit(solution)/shard_map/code_gradient/pallas_call | solution.py:418
  145.5 3.0 %code_gradient.6.rest_1_ = f32[64,512]{1,0:T(8,128)S(1)} custom-call(bf16[64,1024]{1,0:T(8,128)(2,1)S(1)} %bitcast.20, f32[2,1024]{1,0:T(2,128)S(1)} %pad_maximum_fusion.3.p_ref, bf16[64,8192]{1,0:T(8,128)(2,1)S(1)} %bitcast.30, f32[1,8192]{1,0:T(1,128)S(1)} %get-tuple-element.26.rest_0_), custom_call_target="tpu_custom_call" | custom-call | flops 2147483648 | bytes 4194304 | tf_op jit(solution)/shard_map/code_gradient/pallas_call | solution.py:418
  148.7 3.0 %code_gradient.7 = f32[64,512]{1,0:T(8,128)S(1)} custom-call(bf16[64,1024]{1,0:T(8,128)(2,1)S(1)} %bitcast.21, f32[2,1024]{1,0:T(2,128)S(1)} %pad_maximum_fusion.3.p_ref, bf16[64,8192]{1,0:T(8,128)(2,1)S(1)} %bitcast.31, f32[1,8192]{1,0:T(1,128)S(1)} %get-tuple-element.26.rest_0_, f32[64,512]{1,0:T(8,128)S(1)} %code_gradient.6.rest_1_), custom_call_target="tpu_custom_call", output_to_operand_aliasing={{}: (4, {})} | custom-call | flops 2147483648 | bytes 4194304 | tf_op jit(solution)/shard_map/code_gradient/pallas_call | solution.py:418
  159.7 3.4 %collective-permute-done.39 = f32[64,512]{1,0:T(8,128)S(1)} collective-permute-done((f32[64,512]{1,0:T(8,128)S(1)}, f32[64,512]{1,0:T(8,128)S(1)}, u32[]{:S(2)}, u32[]{:S(2)}) %collective-permute-start.39) | collective-permute-done | bytes 131104 | tf_op jit(solution)/shard_map/ppermute | solution.py:26
  163.9 4.8 %collective-permute-done.46.refs_3_ = f32[64,1024]{1,0:T(8,128)S(1)} collective-permute-done((f32[64,1024]{1,0:T(8,128)S(1)}, f32[64,1024]{1,0:T(8,128)S(1)}, u32[]{:S(2)}, u32[]{:S(2)}) %collective-permute-start.46) | collective-permute-done | bytes 262176 | tf_op jit(solution)/shard_map/ppermute | solution.py:26
  168.7 1.7 shard_map.43.refs_2_
  170.4 3.9 %collective-permute-done.41.refs_0_ = f32[64,1024]{1,0:T(8,128)S(1)} collective-permute-done((f32[64,1024]{1,0:T(8,128)S(1)}, f32[64,1024]{1,0:T(8,128)S(1)}, u32[]{:S(2)}, u32[]{:S(2)}) %collective-permute-start.41) | collective-permute-done | bytes 262176 | tf_op jit(solution)/shard_map/ppermute | solution.py:26
  174.3 4.4 %collective-permute-done.43.refs_1_ = f32[64,1024]{1,0:T(8,128)S(1)} collective-permute-done((f32[64,1024]{1,0:T(8,128)S(1)}, f32[64,1024]{1,0:T(8,128)S(1)}, u32[]{:S(2)}, u32[]{:S(2)}) %collective-permute-start.43) | collective-permute-done | bytes 262176 | tf_op jit(solution)/shard_map/ppermute | solution.py:26
  (126 shorter events, 55.1 us)
Async XLA Ops:
  1.5 16.8 %collective-permute-start.3 = (f32[64,512]{1,0:T(8,128)S(1)}, f32[64,512]{1,0:T(8,128)S(1)}, u32[]{:S(2)}, u32[]{:S(2)}) collective-permute-start(f32[64,512]{1,0:T(8,128)S(1)} %convert_bitcast_fusion.refs_0_), channel_id=1, source_target_pairs={{0,16},{4,20},{8,24},{12,28},{16,0},{20,4},{24,8},{28,12},{1,17},{... | collective-permute-start | bytes 393224 | tf_op jit(solution)/shard_map/ppermute | solution.py:26
  16.7 8.9 %collective-permute-start.1 = (f32[64,512]{1,0:T(8,128)S(1)}, f32[64,512]{1,0:T(8,128)S(1)}, u32[]{:S(2)}, u32[]{:S(2)}) collective-permute-start(f32[64,512]{1,0:T(8,128)S(1)} %convert_bitcast_fusion.refs_0_), channel_id=1, source_target_pairs={{0,8},{4,12},{8,0},{12,4},{16,24},{20,28},{24,16},{28,20},{1,9},{5... | collective-permute-start | bytes 393224 | tf_op jit(solution)/shard_map/ppermute | solution.py:26
  18.3 8.7 %collective-permute-start.5 = (f32[64,512]{1,0:T(8,128)S(1)}, f32[64,512]{1,0:T(8,128)S(1)}, u32[]{:S(2)}, u32[]{:S(2)}) collective-permute-start(f32[64,512]{1,0:T(8,128)S(1)} %collective-permute-done.3.refs_4_), channel_id=1, source_target_pairs={{0,8},{4,12},{8,0},{12,4},{16,24},{20,28},{24,16},{28,20},{1,9},{5... | collective-permute-start | bytes 393224 | tf_op jit(solution)/shard_map/ppermute | solution.py:26
  21.9 5.8 %collective-permute-start = (f32[64,512]{1,0:T(8,128)S(1)}, f32[64,512]{1,0:T(8,128)S(1)}, u32[]{:S(2)}, u32[]{:S(2)}) collective-permute-start(f32[64,512]{1,0:T(8,128)S(1)} %convert_bitcast_fusion.refs_0_), channel_id=1, source_target_pairs={{0,4},{4,0},{8,12},{12,8},{16,20},{20,16},{24,28},{28,24},{1,5},{5... | collective-permute-start | bytes 393224 | tf_op jit(solution)/shard_map/ppermute | solution.py:26
  23.4 12.1 %collective-permute-start.9 = (f32[2,1024]{1,0:T(2,128)S(1)}, f32[2,1024]{1,0:T(2,128)S(1)}, u32[]{:S(2)}, u32[]{:S(2)}) collective-permute-start(f32[2,1024]{1,0:T(2,128)S(1)} %pad_maximum_fusion.2), channel_id=1, source_target_pairs={{0,2},{1,3},{2,0},{3,1},{4,6},{5,7},{6,4},{7,5},{8,10},{9,11},{10,... | collective-permute-start | bytes 24584 | tf_op jit(solution)/shard_map/ppermute | solution.py:43
  25.0 6.4 %collective-permute-start.4 = (f32[64,512]{1,0:T(8,128)S(1)}, f32[64,512]{1,0:T(8,128)S(1)}, u32[]{:S(2)}, u32[]{:S(2)}) collective-permute-start(f32[64,512]{1,0:T(8,128)S(1)} %collective-permute-done.3.refs_4_), channel_id=1, source_target_pairs={{0,4},{4,0},{8,12},{12,8},{16,20},{20,16},{24,28},{28,24},{1,5},{5... | collective-permute-start | bytes 393224 | tf_op jit(solution)/shard_map/ppermute | solution.py:26
  25.6 8.3 %collective-permute-start.2 = (f32[64,512]{1,0:T(8,128)S(1)}, f32[64,512]{1,0:T(8,128)S(1)}, u32[]{:S(2)}, u32[]{:S(2)}) collective-permute-start(f32[64,512]{1,0:T(8,128)S(1)} %collective-permute-done.1.refs_2_), channel_id=1, source_target_pairs={{0,4},{4,0},{8,12},{12,8},{16,20},{20,16},{24,28},{28,24},{1,5},{5... | collective-permute-start | bytes 393224 | tf_op jit(solution)/shard_map/ppermute | solution.py:26
  27.0 8.2 %collective-permute-start.6 = (f32[64,512]{1,0:T(8,128)S(1)}, f32[64,512]{1,0:T(8,128)S(1)}, u32[]{:S(2)}, u32[]{:S(2)}) collective-permute-start(f32[64,512]{1,0:T(8,128)S(1)} %collective-permute-done.5.refs_6_), channel_id=1, source_target_pairs={{0,4},{4,0},{8,12},{12,8},{16,20},{20,16},{24,28},{28,24},{1,5},{5... | collective-permute-start | bytes 393224 | tf_op jit(solution)/shard_map/ppermute | solution.py:26
  35.3 4.8 %collective-permute-start.7 = (f32[64,4096]{1,0:T(8,128)S(1)}, f32[64,4096]{1,0:T(8,128)S(1)}, u32[]{:S(2)}, u32[]{:S(2)}) collective-permute-start(f32[64,4096]{1,0:T(8,128)S(1)} %shard_map.41.mine_ref), channel_id=1, source_target_pairs={{0,1},{1,0},{2,3},{3,2},{4,5},{5,4},{6,7},{7,6},{8,9},{9,8},{10,11... | collective-permute-start | bytes 3145736 | tf_op jit(solution)/shard_map/ppermute | solution.py:26
  35.6 5.1 %collective-permute-start.12 = (f32[1,8192]{1,0:T(1,128)S(1)}, f32[1,8192]{1,0:T(1,128)S(1)}, u32[]{:S(2)}, u32[]{:S(2)}) collective-permute-start(f32[1,8192]{1,0:T(1,128)S(1)} %add.128.refs_2_), channel_id=1, source_target_pairs={{0,8},{1,9},{2,10},{3,11},{4,12},{5,13},{6,14},{7,15},{8,0},{9,1},... | collective-permute-start | bytes 98312 | tf_op jit(solution)/shard_map/ppermute | solution.py:43
  37.3 5.7 %collective-permute-start.13 = (f32[1,8192]{1,0:T(1,128)S(1)}, f32[1,8192]{1,0:T(1,128)S(1)}, u32[]{:S(2)}, u32[]{:S(2)}) collective-permute-start(f32[1,8192]{1,0:T(1,128)S(1)} %add.128.refs_2_), channel_id=1, source_target_pairs={{0,16},{1,17},{2,18},{3,19},{4,20},{5,21},{6,22},{7,23},{8,24},{9,... | collective-permute-start | bytes 98312 | tf_op jit(solution)/shard_map/ppermute | solution.py:43
  37.6 5.8 %collective-permute-start.14 = (f32[1,8192]{1,0:T(1,128)S(1)}, f32[1,8192]{1,0:T(1,128)S(1)}, u32[]{:S(2)}, u32[]{:S(2)}) collective-permute-start(f32[1,8192]{1,0:T(1,128)S(1)} %add.128.refs_2_), channel_id=1, source_target_pairs={{0,24},{1,25},{2,26},{3,27},{4,28},{5,29},{6,30},{7,31},{8,16},{9,... | collective-permute-start | bytes 98312 | tf_op jit(solution)/shard_map/ppermute | solution.py:43
  60.4 4.8 %collective-permute-start.18 = (f32[1,8192]{1,0:T(1,128)S(1)}, f32[1,8192]{1,0:T(1,128)S(1)}, u32[]{:S(2)}, u32[]{:S(2)}) collective-permute-start(f32[1,8192]{1,0:T(1,128)S(1)} %add.129), channel_id=1, source_target_pairs={{0,6},{1,7},{2,4},{3,5},{4,2},{5,3},{6,0},{7,1},{8,14},{9,15},{10,... | collective-permute-start | bytes 98312 | tf_op jit(solution)/shard_map/ppermute | solution.py:43
  66.2 5.5 %collective-permute-start.20 = (f32[1,8192]{1,0:T(1,128)S(1)}, f32[1,8192]{1,0:T(1,128)S(1)}, u32[]{:S(2)}, u32[]{:S(2)}) collective-permute-start(f32[1,8192]{1,0:T(1,128)S(1)} %add_add_fusion.2.refs_2_), channel_id=1, source_target_pairs={{0,16},{1,17},{2,18},{3,19},{4,20},{5,21},{6,22},{7,23},{8,24},{9,... | collective-permute-start | bytes 98312 | tf_op jit(solution)/shard_map/ppermute | solution.py:43
  68.3 5.7 %collective-permute-start.21 = (f32[1,8192]{1,0:T(1,128)S(1)}, f32[1,8192]{1,0:T(1,128)S(1)}, u32[]{:S(2)}, u32[]{:S(2)}) collective-permute-start(f32[1,8192]{1,0:T(1,128)S(1)} %add_add_fusion.2.refs_2_), channel_id=1, source_target_pairs={{0,24},{1,25},{2,26},{3,27},{4,28},{5,29},{6,30},{7,31},{8,16},{9,... | collective-permute-start | bytes 98312 | tf_op jit(solution)/shard_map/ppermute | solution.py:43
  86.1 4.8 %collective-permute-start.25 = (f32[1,8192]{1,0:T(1,128)S(1)}, f32[1,8192]{1,0:T(1,128)S(1)}, u32[]{:S(2)}, u32[]{:S(2)}) collective-permute-start(f32[1,8192]{1,0:T(1,128)S(1)} %add.133), channel_id=1, source_target_pairs={{0,6},{1,7},{2,4},{3,5},{4,2},{5,3},{6,0},{7,1},{8,14},{9,15},{10,... | collective-permute-start | bytes 98312 | tf_op jit(solution)/shard_map/ppermute | solution.py:43
  91.1 5.2 %collective-permute-start.27 = (f32[1,8192]{1,0:T(1,128)S(1)}, f32[1,8192]{1,0:T(1,128)S(1)}, u32[]{:S(2)}, u32[]{:S(2)}) collective-permute-start(f32[1,8192]{1,0:T(1,128)S(1)} %add_add_fusion.1.refs_2_), channel_id=1, source_target_pairs={{0,16},{1,17},{2,18},{3,19},{4,20},{5,21},{6,22},{7,23},{8,24},{9,... | collective-permute-start | bytes 98312 | tf_op jit(solution)/shard_map/ppermute | solution.py:43
  93.1 5.7 %collective-permute-start.28 = (f32[1,8192]{1,0:T(1,128)S(1)}, f32[1,8192]{1,0:T(1,128)S(1)}, u32[]{:S(2)}, u32[]{:S(2)}) collective-permute-start(f32[1,8192]{1,0:T(1,128)S(1)} %add_add_fusion.1.refs_2_), channel_id=1, source_target_pairs={{0,24},{1,25},{2,26},{3,27},{4,28},{5,29},{6,30},{7,31},{8,16},{9,... | collective-permute-start | bytes 98312 | tf_op jit(solution)/shard_map/ppermute | solution.py:43
  109.9 6.9 %collective-permute-start.31 = (f32[1,16384]{1,0:T(1,128)S(1)}, f32[1,16384]{1,0:T(1,128)S(1)}, u32[]{:S(2)}, u32[]{:S(2)}) collective-permute-start(f32[1,16384]{1,0:T(1,128)S(1)} %pad_maximum_fusion), channel_id=1, source_target_pairs={{0,4},{1,5},{2,6},{3,7},{4,0},{5,1},{6,2},{7,3},{8,12},{9,13},{10,... | collective-permute-start | bytes 196616 | tf_op jit(solution)/shard_map/ppermute | solution.py:43
  111.9 4.8 %collective-permute-start.32 = (f32[1,8192]{1,0:T(1,128)S(1)}, f32[1,8192]{1,0:T(1,128)S(1)}, u32[]{:S(2)}, u32[]{:S(2)}) collective-permute-start(f32[1,8192]{1,0:T(1,128)S(1)} %add.139), channel_id=1, source_target_pairs={{0,6},{1,7},{2,4},{3,5},{4,2},{5,3},{6,0},{7,1},{8,14},{9,15},{10,... | collective-permute-start | bytes 98312 | tf_op jit(solution)/shard_map/ppermute | solution.py:43
  117.0 5.3 %collective-permute-start.34 = (f32[1,16384]{1,0:T(1,128)S(1)}, f32[1,16384]{1,0:T(1,128)S(1)}, u32[]{:S(2)}, u32[]{:S(2)}) collective-permute-start(f32[1,16384]{1,0:T(1,128)S(1)} %pad_maximum_fusion.1.refs_5_), channel_id=1, source_target_pairs={{0,16},{1,17},{2,18},{3,19},{4,20},{5,21},{6,22},{7,23},{8,24},{9,... | collective-permute-start | bytes 196616 | tf_op jit(solution)/shard_map/ppermute | solution.py:43
  119.9 6.1 %collective-permute-start.35 = (f32[1,16384]{1,0:T(1,128)S(1)}, f32[1,16384]{1,0:T(1,128)S(1)}, u32[]{:S(2)}, u32[]{:S(2)}) collective-permute-start(f32[1,16384]{1,0:T(1,128)S(1)} %pad_maximum_fusion.1.refs_5_), channel_id=1, source_target_pairs={{0,24},{1,25},{2,26},{3,27},{4,28},{5,29},{6,30},{7,31},{8,16},{9,... | collective-permute-start | bytes 196616 | tf_op jit(solution)/shard_map/ppermute | solution.py:43
  136.7 11.9 %collective-permute-start.40 = (f32[64,1024]{1,0:T(8,128)S(1)}, f32[64,1024]{1,0:T(8,128)S(1)}, u32[]{:S(2)}, u32[]{:S(2)}) collective-permute-start(f32[64,1024]{1,0:T(8,128)S(1)} %centroid_update.1.refs_0_), channel_id=1, source_target_pairs={{0,16},{4,20},{8,24},{12,28},{16,0},{20,4},{24,8},{28,12},{1,17},{... | collective-permute-start | bytes 786440 | tf_op jit(solution)/shard_map/ppermute | solution.py:26
  136.7 17.7 %collective-permute-start.45 = (f32[64,1024]{1,0:T(8,128)S(1)}, f32[64,1024]{1,0:T(8,128)S(1)}, u32[]{:S(2)}, u32[]{:S(2)}) collective-permute-start(f32[64,1024]{1,0:T(8,128)S(1)} %centroid_update.1.refs_0_), channel_id=1, source_target_pairs={{0,8},{4,12},{8,0},{12,4},{16,24},{20,28},{24,16},{28,20},{1,9},{5... | collective-permute-start | bytes 786440 | tf_op jit(solution)/shard_map/ppermute | solution.py:26
  145.5 6.8 %collective-permute-start.36 = (f32[64,512]{1,0:T(8,128)S(1)}, f32[64,512]{1,0:T(8,128)S(1)}, u32[]{:S(2)}, u32[]{:S(2)}) collective-permute-start(f32[64,512]{1,0:T(8,128)S(1)} %code_gradient.5), channel_id=1, source_target_pairs={{0,1},{1,0},{2,3},{3,2},{4,5},{5,4},{6,7},{7,6},{8,9},{9,8},{10,11... | collective-permute-start | bytes 393224 | tf_op jit(solution)/shard_map/ppermute | solution.py:26
  148.6 8.8 %collective-permute-start.42 = (f32[64,1024]{1,0:T(8,128)S(1)}, f32[64,1024]{1,0:T(8,128)S(1)}, u32[]{:S(2)}, u32[]{:S(2)}) collective-permute-start(f32[64,1024]{1,0:T(8,128)S(1)} %collective-permute-done.40.refs_4_), channel_id=1, source_target_pairs={{0,8},{4,12},{8,0},{12,4},{16,24},{20,28},{24,16},{28,20},{1,9},{5... | collective-permute-start | bytes 786440 | tf_op jit(solution)/shard_map/ppermute | solution.py:26
  152.3 5.8 %collective-permute-start.37 = (f32[64,512]{1,0:T(8,128)S(1)}, f32[64,512]{1,0:T(8,128)S(1)}, u32[]{:S(2)}, u32[]{:S(2)}) collective-permute-start(f32[64,512]{1,0:T(8,128)S(1)} %add.148), channel_id=1, source_target_pairs={{0,2},{1,3},{2,0},{3,1},{4,6},{5,7},{6,4},{7,5},{8,10},{9,11},{10,... | collective-permute-start | bytes 393224 | tf_op jit(solution)/shard_map/ppermute | solution.py:26
  153.9 10.0 %collective-permute-start.44 = (f32[64,1024]{1,0:T(8,128)S(1)}, f32[64,1024]{1,0:T(8,128)S(1)}, u32[]{:S(2)}, u32[]{:S(2)}) collective-permute-start(f32[64,1024]{1,0:T(8,128)S(1)} %centroid_update.1.refs_0_), channel_id=1, source_target_pairs={{0,4},{4,0},{8,12},{12,8},{16,20},{20,16},{24,28},{28,24},{1,5},{5... | collective-permute-start | bytes 786440 | tf_op jit(solution)/shard_map/ppermute | solution.py:26
  154.4 14.2 %collective-permute-start.46 = (f32[64,1024]{1,0:T(8,128)S(1)}, f32[64,1024]{1,0:T(8,128)S(1)}, u32[]{:S(2)}, u32[]{:S(2)}) collective-permute-start(f32[64,1024]{1,0:T(8,128)S(1)} %collective-permute-done.45.refs_2_), channel_id=1, source_target_pairs={{0,4},{4,0},{8,12},{12,8},{16,20},{20,16},{24,28},{28,24},{1,5},{5... | collective-permute-start | bytes 786440 | tf_op jit(solution)/shard_map/ppermute | solution.py:26
  155.9 18.4 %collective-permute-start.41 = (f32[64,1024]{1,0:T(8,128)S(1)}, f32[64,1024]{1,0:T(8,128)S(1)}, u32[]{:S(2)}, u32[]{:S(2)}) collective-permute-start(f32[64,1024]{1,0:T(8,128)S(1)} %collective-permute-done.40.refs_4_), channel_id=1, source_target_pairs={{0,4},{4,0},{8,12},{12,8},{16,20},{20,16},{24,28},{28,24},{1,5},{5... | collective-permute-start | bytes 786440 | tf_op jit(solution)/shard_map/ppermute | solution.py:26
  157.4 21.4 %collective-permute-start.43 = (f32[64,1024]{1,0:T(8,128)S(1)}, f32[64,1024]{1,0:T(8,128)S(1)}, u32[]{:S(2)}, u32[]{:S(2)}) collective-permute-start(f32[64,1024]{1,0:T(8,128)S(1)} %collective-permute-done.42.refs_5_), channel_id=1, source_target_pairs={{0,4},{4,0},{8,12},{12,8},{16,20},{20,16},{24,28},{28,24},{1,5},{5... | collective-permute-start | bytes 786440 | tf_op jit(solution)/shard_map/ppermute | solution.py:26
  158.1 5.0 %collective-permute-start.39 = (f32[64,512]{1,0:T(8,128)S(1)}, f32[64,512]{1,0:T(8,128)S(1)}, u32[]{:S(2)}, u32[]{:S(2)}) collective-permute-start(f32[64,512]{1,0:T(8,128)S(1)} %add.150), channel_id=1, source_target_pairs={{0,2},{1,3},{2,0},{3,1},{4,6},{5,7},{6,4},{7,5},{8,10},{9,11},{10,... | collective-permute-start | bytes 393224 | tf_op jit(solution)/shard_map/ppermute | solution.py:26
  (23 other events, 132.8 us)
